TPU v7x, 256 devices: a whole 4x4x8 slice. The times are simulated.
256 devices in a mesh: seq: 64 (over x, z, core), head: 4 (over y).
Axes of the slice: x: 4, y: 4, z: 8, core: 2. Of those that a mesh axis runs over, the one named last changes fastest.
Arguments:
- latent: bfloat16 [64, 16, 1024], P('seq'), may hold values from -6 to 6
- stem_weight: bfloat16 [192, 3072], replicated, may hold values from -0.4375 to 0.4375
- stem_bias: float32 [3072], replicated, may hold values from -6 to 6
- mod_shift: float32 [3072], replicated, may hold values from -3 to 3
- mod_scale: float32 [3072], replicated, may hold values from -3 to 3
- qkv_weight: bfloat16 [3072, 3, 12, 128], P(None, None, 'head'), may hold values from -0.109375 to 0.109375
- q_gain: float32 [128], replicated, may hold values from 0.1 to 1.9
- k_gain: float32 [128], replicated, may hold values from 0.1 to 1.9
- tile_lists: int32 [128, 4], replicated, may hold values from 0 to 127, as said below
- out_grad: bfloat16 [16384, 12, 128], P('seq', 'head'), may hold values from -0.125 to 0.125
Outputs:
- qkv_weight_grad: float32 [3072, 3, 12, 128], P('seq', None, 'head')
- stem_weight_grad: float32 [192, 3072], P(None, 'head')
- vector_grad: float32 [3, 3072], P(None, 'head')
Inputs may be any that keep to these rules, and one draw needn't show every extreme that they name: `tile_lists`: row b holds 4 different tiles of tile b's own group of 8 tiles (b - b % 8 to b - b % 8 + 7), the first being b itself.
All inputs are finite; a program needn't handle non-finite values.
Results may differ from a plain program's by a relative error of at most 0.0078.
Values may be sent and summed in bfloat16 or wider, within the bound.
No kernel may reach another device: no remote copies, remote signals or barrier semaphores. Data moves between devices by JAX's collectives and lax.ppermute only.
A program may use at most 128 MiB of HBM per device.

v0:
```python
import jax
import jax.numpy as jnp
from jax import lax
from jax.sharding import PartitionSpec as P

TT = 2
TS = 8
KNB = 4
HG = 32
WG = 16


ln_eps = 1e-06


def swapped(value, axis, distance):
    mask = 2**distance
    pairs = [(source, source ^ mask) for source in range(lax.axis_size(axis))]
    return lax.ppermute(value, axis, pairs)


def from_behind(value, axis, steps):
    count = lax.axis_size(axis)
    first, last = (max(0, -steps), min(count, count - steps))
    return lax.ppermute(value, axis, [(source, source + steps) for source in range(first, last)])


def frames_to_tiles(blocks, row_total, col_total, tile_side):
    frames = blocks.shape[0]
    remain = blocks.shape[2:]
    shaped = blocks.reshape(
        (frames, row_total // tile_side, tile_side, col_total // tile_side, tile_side) + remain
    )
    shaped = jnp.transpose(shaped, (1, 3, 0, 2, 4) + tuple(range(5, 5 + len(remain))))
    return shaped.reshape(
        (row_total // tile_side * (col_total // tile_side), frames * tile_side * tile_side) + remain
    )


def tiles_to_frames(blocks, frames, row_total, col_total, tile_side):
    remain = blocks.shape[2:]
    shaped = blocks.reshape(
        (row_total // tile_side, col_total // tile_side, frames, tile_side, tile_side) + remain
    )
    shaped = jnp.transpose(shaped, (2, 0, 3, 1, 4) + tuple(range(5, 5 + len(remain))))
    return shaped.reshape((frames, row_total * col_total) + remain)


def qk_norm(raw_values, gain_vector):
    return (
        raw_values
        * lax.rsqrt(jnp.mean(raw_values * raw_values, -1, keepdims=True) + ln_eps)
        * gain_vector
    )


def norm_back(feature_grad, normed, inv_std, mod_scale):
    scaled = feature_grad * (1.0 + mod_scale)
    return (
        scaled
        - jnp.mean(scaled, -1, keepdims=True)
        - normed * jnp.mean(scaled * normed, -1, keepdims=True)
    ) * inv_std


def attend(queries, out_grads, key_vals, values, score_scale):
    scores = (
        jnp.einsum("brhe,bmhe->bhrm", queries, key_vals, preferred_element_type=jnp.float32)
        * score_scale
    )
    weights = jnp.exp(scores)
    probability = weights / jnp.sum(weights, axis=-1, keepdims=True)
    rounded = probability.astype(jnp.bfloat16)
    slopes = jnp.einsum("brhe,bmhe->bhrm", out_grads, values, preferred_element_type=jnp.float32)
    centre = jnp.sum(probability * slopes, axis=-1, keepdims=True)
    shaped = (probability * (slopes - centre)).astype(jnp.bfloat16)
    query_grad = (
        jnp.einsum("bhrm,bmhe->brhe", shaped, key_vals, preferred_element_type=jnp.float32)
        * score_scale
    )
    key_grad = (
        jnp.einsum("bhrm,brhe->bmhe", shaped, queries, preferred_element_type=jnp.float32)
        * score_scale
    )
    value_grad = jnp.einsum(
        "bhrm,brhe->bmhe", rounded, out_grads, preferred_element_type=jnp.float32
    )
    return (query_grad, key_grad, value_grad)


def group_share(blocks):
    seq_place = lax.axis_index("seq")
    for bit_index in range((2 * TT).bit_length() - 1):
        partner = swapped(blocks, "seq", bit_index)
        is_lower = seq_place // (1 << bit_index) % 2 == 0
        first_half = jnp.where(is_lower, blocks, partner)
        second_half = jnp.where(is_lower, partner, blocks)
        blocks = jnp.concatenate([first_half, second_half], 0)
    return blocks


def group_return(blocks):
    seq_place = lax.axis_index("seq")
    for bit_index in reversed(range((2 * TT).bit_length() - 1)):
        half_size = blocks.shape[0] // 2
        is_lower = seq_place // (1 << bit_index) % 2 == 0
        kept_part = jnp.where(is_lower, blocks[:half_size], blocks[half_size:])
        sent_part = jnp.where(is_lower, blocks[half_size:], blocks[:half_size])
        blocks = kept_part + swapped(sent_part, "seq", bit_index)
    return blocks[0]


def seq_total(stem_part, vector_part):
    return lax.psum((stem_part, vector_part), "seq")


def per_device(
    latent,
    stem_weight,
    stem_bias,
    mod_shift,
    mod_scale,
    qkv_weight,
    q_gain,
    k_gain,
    tile_lists,
    out_grad,
):
    half_rows = HG // 2
    tok_count = half_rows * WG
    frame_tokens = HG * WG
    model_width = qkv_weight.shape[0]
    heads_here = qkv_weight.shape[2]
    head_dim = qkv_weight.shape[3]
    score_scale = head_dim ** (-0.5)
    before = from_behind(latent, "seq", 2)
    after = from_behind(latent, "seq", -2)
    padded = jnp.concatenate([before, latent, after], 0)
    channels = latent.shape[1]
    patches = padded.reshape(3, channels, half_rows, 2, WG, 2)
    patches = jnp.transpose(patches, (2, 4, 0, 1, 3, 5)).reshape(tok_count, 12 * channels)
    embedded = jnp.dot(patches, stem_weight, preferred_element_type=jnp.float32) + stem_bias
    centred = embedded - jnp.mean(embedded, -1, keepdims=True)
    inv_std = lax.rsqrt(jnp.mean(centred * centred, -1, keepdims=True) + ln_eps)
    normed = centred * inv_std
    hidden = (normed * (1.0 + mod_scale) + mod_shift).astype(jnp.bfloat16)
    columns = 3 * heads_here * head_dim
    flat_weight = qkv_weight.reshape(model_width, columns)
    projected = jnp.dot(hidden, flat_weight, preferred_element_type=jnp.float32).reshape(
        tok_count, 3, heads_here, head_dim
    )
    q_normed, q_back = jax.vjp(lambda raw_values: qk_norm(raw_values, q_gain), projected[:, 0])
    k_normed, k_back = jax.vjp(lambda raw_values: qk_norm(raw_values, k_gain), projected[:, 1])
    queries = q_normed.astype(jnp.bfloat16)
    key_vals = k_normed.astype(jnp.bfloat16)
    values = projected[:, 2].astype(jnp.bfloat16)
    seq_place = lax.axis_index("seq")
    group_devs = 2 * TT
    my_group = seq_place // group_devs
    my_half = seq_place % 2
    tiles_group = HG // TS * (WG // TS)
    half_tiles = tiles_group // 2
    local_lists = (
        lax.dynamic_slice_in_dim(tile_lists, my_group * tiles_group, tiles_group, 0)
        - my_group * tiles_group
    )
    shared = group_share(jnp.stack([key_vals, values], 1)[None])
    shared = shared.reshape((TT, frame_tokens) + shared.shape[2:])
    tiles = frames_to_tiles(shared, HG, WG, TS)
    tile_len = tiles.shape[1]
    my_lists = lax.dynamic_slice_in_dim(local_lists, my_half * half_tiles, half_tiles, 0)
    near_tiles = jnp.take(tiles, my_lists.reshape(-1), axis=0)
    near_tiles = near_tiles.reshape(half_tiles, KNB * tile_len, 2, heads_here, head_dim)
    own_queries = frames_to_tiles(queries[None], half_rows, WG, TS)
    own_grads = frames_to_tiles(out_grad[None], half_rows, WG, TS)
    query_part, key_part, value_part = attend(
        own_queries, own_grads, near_tiles[:, :, 0], near_tiles[:, :, 1], score_scale
    )
    query_grad = tiles_to_frames(query_part, 1, half_rows, WG, TS)[0]
    pair_part = jnp.stack([key_part, value_part], 2).reshape(
        half_tiles * KNB, tile_len, 2, heads_here, head_dim
    )
    pair_tiles = (
        jnp.zeros((tiles_group, tile_len, 2, heads_here, head_dim), jnp.float32)
        .at[my_lists.reshape(-1)]
        .add(pair_part)
    )
    framed = tiles_to_frames(pair_tiles, TT, HG, WG, TS)
    returned = group_return(framed.reshape((group_devs, tok_count) + framed.shape[2:]))
    key_grad = returned[:, 0]
    value_grad = returned[:, 1]
    raw_q = q_back(query_grad)[0]
    raw_k = k_back(key_grad)[0]
    mixed_grad = (
        jnp.stack([raw_q, raw_k, value_grad], 1).astype(jnp.bfloat16).reshape(tok_count, columns)
    )
    weight_grad = lax.psum_scatter(
        lax.dot_general(
            hidden, mixed_grad, (((0,), (0,)), ((), ())), preferred_element_type=jnp.float32
        ),
        "seq",
        scatter_dimension=0,
        tiled=True,
    )
    weight_grad = weight_grad.reshape(-1, 3, heads_here, head_dim)
    feature_grad = lax.dot_general(
        mixed_grad, flat_weight, (((1,), (1,)), ((), ())), preferred_element_type=jnp.float32
    )
    patch_rows = patches.astype(jnp.float32)
    feature_grad = lax.psum(feature_grad, "head")
    embed_grad = norm_back(feature_grad, normed, inv_std, mod_scale)
    share_cols = model_width // lax.axis_size("head")
    offset = lax.axis_index("head") * share_cols
    grad_slice = lax.dynamic_slice_in_dim(feature_grad, offset, share_cols, 1)
    normed_slice = lax.dynamic_slice_in_dim(normed, offset, share_cols, 1)
    embed_slice = lax.dynamic_slice_in_dim(embed_grad, offset, share_cols, 1)
    stem_part = lax.dot_general(
        patch_rows, embed_slice, (((0,), (0,)), ((), ())), precision=lax.Precision.HIGHEST
    )
    vector_part = jnp.stack(
        [jnp.sum(grad_slice, 0), jnp.sum(grad_slice * normed_slice, 0), jnp.sum(embed_slice, 0)]
    )
    stem_grad, vector_grad = seq_total(stem_part, vector_part)
    return (weight_grad, stem_grad, vector_grad)


def solution(mesh):
    return jax.shard_map(
        per_device,
        mesh=mesh,
        in_specs=(
            P("seq", None, None),
            P(),
            P(),
            P(),
            P(),
            P(None, None, "head", None),
            P(),
            P(),
            P(),
            P("seq", "head", None),
        ),
        out_specs=(P("seq", None, "head", None), P(None, "head"), P(None, "head")),
        check_vma=False,
    )
```

profile of v0, /device:TPU:1, one launch (start us, length us, event | category | flops | bytes accessed | tf_op | source)
XLA Modules:
  0.0 514.0 jit_solution(13901229938263370222)
XLA Ops:
  8.1 4.5 collective-permute-start
  12.6 1.3 collective-permute-start.1
  13.9 0.7 broadcast_add_fusion
  14.6 10.3 %copy.44 = bf16[3072,3,3,128]{0,3,2,1:T(8,128)(2,1)} copy(bf16[3072,3,3,128]{3,0,2,1:T(8,128)(2,1)} %param.15) | data formatting | bytes 14155776 | tf_op args[5]
  24.9 0.4 copy.41
  25.3 1.7 copy.42
  26.9 0.7 reshape.189
  27.7 0.7 fusion.29
  28.4 0.5 multiply_reduce_fusion.1
  28.8 1.1 copy-done.2
  30.0 0.5 subtract_multiply_fusion
  30.5 0.5 slice-done.2
  31.0 0.9 slice-done.3
  31.9 2.3 fusion
  34.2 0.3 fusion.20
  34.5 0.7 copy-done.8
  35.5 1.0 collective-permute-start.2
  37.1 0.8 collective-permute-done.2
  38.0 2.6 collective-permute-start.3
  41.0 17.3 %collective-permute-done.3 = bf16[2,256,2,3,128]{4,1,3,2,0:T(8,128)(2,1)} collective-permute-done((bf16[2,256,2,3,128]{4,1,3,2,0:T(8,128)(2,1)S(1)}, bf16[2,256,2,3,128]{4,1,3,2,0:T(8,128)(2,1)}, u32[]{:S(2)}, u32[]{:S(2)}) %collective-permute-start.3) | collective-permute-done | bytes 786464 | tf_op jit(solution)/shard_map/ppermute | solution.py:19
  58.4 1.2 broadcast_select_fusion.1
  59.9 0.4 copy.46
  60.3 2.6 gather_fusion
  62.9 2.3 copy.48
  65.2 0.5 copy_select_fusion
  65.8 0.7 fusion.2
  66.4 1.0 copy-done.6
  67.4 0.7 multiply_exponential_fusion
  68.1 3.3 convolution_bitcast_fusion.1
  71.5 2.1 fusion.4
  73.6 1.9 copy.54
  75.4 0.3 fusion.6
  75.8 0.9 copy-done.11
  76.7 0.6 multiply_bitcast_fusion
  77.3 2.3 copy.53
  79.6 3.3 pad_maximum_fusion
  82.9 3.1 copy.55
  86.0 0.4 broadcast_in_dim.47
  86.3 9.3 %scatter_fusion = f32[8,128,2,3,128]{4,1,3,2,0:T(8,128)S(1)} fusion(f32[8,128,2,3,128]{4,1,3,2,0:T(8,128)S(1)} %broadcast_in_dim.47, s32[16]{0:T(128)S(1)} %fusion.24, f32[16,128,2,3,128]{4,1,3,2,0:T(8,128)} %copy.55), kind=kCustom, calls=%fused_computation.1 | custom fusion | flops 1572864 | bytes 18874432 | tf_op jit(solution)/shard_map/scatter-add | solution.py:186
  95.7 0.3 copy.68
  96.0 0.4 slice_select_fusion.1
  96.5 1.2 collective-permute-start.4
  97.7 33.9 %collective-permute-done.4 = f32[2,256,2,3,128]{4,1,3,2,0:T(8,128)S(1)} collective-permute-done((f32[2,256,2,3,128]{4,1,3,2,0:T(8,128)S(1)}, f32[2,256,2,3,128]{4,1,3,2,0:T(8,128)S(1)}, u32[]{:S(2)}, u32[]{:S(2)}) %collective-permute-start.4) | collective-permute-done | bytes 1572896 | tf_op jit(solution)/shard_map/ppermute | solution.py:19
  131.6 0.2 copy_add_fusion
  132.0 1.9 collective-permute-start.5
  133.8 0.4 fusion.8
  134.3 1.4 collective-permute-done.5
  135.9 0.3 fusion.19
  136.2 0.5 add_add_fusion.1
  136.7 0.6 copy-done.13
  137.5 4.0 convolution_bitcast_fusion
  141.5 0.3 reduce-scatter.2.cloned.1.call-start
  141.7 2.1 maximum_convert_fusion
  143.8 2.1 copy.59
  145.9 8.4 %fusion.14 = f32[3072,1152]{1,0:T(8,128)} fusion(bf16[256,1152]{0,1:T(8,128)(2,1)} %bitcast.148, f32[256,3072]{1,0:T(8,128)S(1)} %copy-done.5, f32[3072]{0:T(1024)S(1)} %copy-done.17, f32[3072]{0:T(1024)S(1)} %broadcast_add_fusion), kind=kOutput, calls=%fused_computation.48 | convolution fusion | flops 1814298624 | bytes 17915904 | tf_op jit(solution)/shard_map/dot_general | solution.py:198
  154.4 71.5 %all-reduce.3.cloned.1.call-done = f32[256,3072]{1,0:T(8,128)} async-done(((f32[256,3072]{1,0:T(8,128)}), f32[256,3072]{1,0:T(8,128)}) %all-reduce.3.cloned.1.call-update) | async-done | bytes 3145744 | tf_op jit(solution)/shard_map/psum | solution.py:210
  226.0 2.8 fusion.26
  228.8 1.7 dynamic-slice_reduce_fusion
  230.6 1.3 fusion.30
  231.9 247.0 %psum.23 = f32[3,768]{1,0:T(4,128)} all-reduce(f32[3,768]{1,0:T(4,128)S(1)} %pad_maximum_fusion.4), channel_id=1, replica_groups=mesh['seq'=64,'head'=4] {'seq'}, use_global_device_ids=true, to_apply=%region_17.18 | all-reduce | flops 2304 | bytes 18432 | tf_op jit(solution)/shard_map/psum | solution.py:114
  479.0 1.0 reshape.197
  480.0 0.7 copy.60
  480.7 23.9 %all-reduce.5.cloned.1.call-done = f32[192,768]{1,0:T(8,128)} async-done(((f32[192,768]{1,0:T(8,128)}), f32[192,768]{1,0:T(8,128)}) %all-reduce.5.cloned.1.call-update) | async-done | bytes 589840 | tf_op jit(solution)/shard_map/psum | solution.py:114
  504.6 1.9 copy.73
  (93 shorter events, 2.4 us)
Async XLA Ops:
  8.0 19.6 %copy-start = (bf16[192,3072]{1,0:T(8,128)(2,1)S(1)}, bf16[192,3072]{1,0:T(8,128)(2,1)}, u32[]{:S(2)}) copy-start(bf16[192,3072]{1,0:T(8,128)(2,1)} %param.11) | copy-start | bytes 3538948
  8.0 217.9 %all-reduce.3.cloned.1.call-start = ((), (), s32[]{:S(2)}) async-start(), calls=%async_computation.2 | async-start | bytes 6291456 | tf_op jit(solution)/shard_map/psum | solution.py:210
  8.1 16.8 %collective-permute-start = (bf16[1,16,1024]{2,1,0:T(8,128)(2,1)}, bf16[1,16,1024]{2,1,0:T(8,128)(2,1)S(1)}, u32[]{:S(2)}, u32[]{:S(2)}) collective-permute-start(bf16[1,16,1024]{2,1,0:T(8,128)(2,1)} %param.10), channel_id=1, source_target_pairs={{0,8},{4,12},{8,16},{12,20},{16,24},{20,28},{24,32},{28,36},{32,40... | collective-permute-start | bytes 98312 | tf_op jit(solution)/shard_map/ppermute | solution.py:25
  12.6 12.3 %collective-permute-start.1 = (bf16[1,16,1024]{2,1,0:T(8,128)(2,1)}, bf16[1,16,1024]{2,1,0:T(8,128)(2,1)S(1)}, u32[]{:S(2)}, u32[]{:S(2)}) collective-permute-start(bf16[1,16,1024]{2,1,0:T(8,128)(2,1)} %param.10), channel_id=1, source_target_pairs={{8,0},{12,4},{16,8},{20,12},{24,16},{28,20},{32,24},{36,28},{40,32... | collective-permute-start | bytes 98312 | tf_op jit(solution)/shard_map/ppermute | solution.py:25
  14.6 10.3 %copy-start.18 = (bf16[1,16,1024]{2,1,0:T(8,128)(2,1)S(1)}, bf16[1,16,1024]{2,1,0:T(8,128)(2,1)}, u32[]{:S(2)}) copy-start(bf16[1,16,1024]{2,1,0:T(8,128)(2,1)} %param.10) | copy-start | bytes 98308
  24.9 2.8 copy-start.19
  27.7 3.3 slice-start.2
  28.3 1.6 copy-start.2
  28.4 3.5 slice-start.3
  30.0 1.9 copy-start.17
  31.9 2.3 copy-start.4
  31.9 3.4 copy-start.20
  34.2 1.1 copy-start.8
  34.2 2.4 copy-start.22
  34.2 2.9 copy-start.16
  34.5 6.3 %copy-start.21 = (f32[128]{0:T(128)S(1)}, f32[128]{0:T(128)}, u32[]{:S(2)}) copy-start(f32[128]{0:T(128)} %param.16) | copy-start | bytes 1540
  35.5 2.4 collective-permute-start.2
  37.1 28.6 %copy-start.15 = (bf16[2,2,1,8,8,3,128]{6,4,3,5,1,0,2:T(8,128)(2,1)}, bf16[2,2,1,8,8,3,128]{6,4,3,5,1,0,2:T(8,128)(2,1)S(1)}, u32[]{:S(2)}) copy-start(bf16[2,2,1,8,8,3,128]{6,4,3,5,1,0,2:T(8,128)(2,1)S(1)} %copy.51) | copy-start | bytes 589828
  38.0 20.4 %collective-permute-start.3 = (bf16[2,256,2,3,128]{4,1,3,2,0:T(8,128)(2,1)S(1)}, bf16[2,256,2,3,128]{4,1,3,2,0:T(8,128)(2,1)}, u32[]{:S(2)}, u32[]{:S(2)}) collective-permute-start(bf16[2,256,2,3,128]{4,1,3,2,0:T(8,128)(2,1)S(1)} %pad_maximum_fusion.2), channel_id=1, source_target_pairs={{0,8},{4,12},{8,0},{12,4},{16,24},{20,28},{24,16},{28,20},{32,40},... | collective-permute-start | bytes 2359304 | tf_op jit(solution)/shard_map/ppermute | solution.py:19
  65.7 1.7 copy-start.6
  71.5 2.1 copy-start.10
  75.8 0.9 copy-start.11
  96.4 37.5 %copy-start.12 = (bf16[4,3,64,512]{3,2,1,0:T(8,128)(2,1)S(1)}, bf16[4,3,64,512]{3,2,1,0:T(8,128)(2,1)}, u32[]{:S(2)}) copy-start(bf16[4,3,64,512]{3,2,1,0:T(8,128)(2,1)} %copy-done.11) | copy-start | bytes 2359300
  96.5 35.1 %collective-permute-start.4 = (f32[2,256,2,3,128]{4,1,3,2,0:T(8,128)S(1)}, f32[2,256,2,3,128]{4,1,3,2,0:T(8,128)S(1)}, u32[]{:S(2)}, u32[]{:S(2)}) collective-permute-start(f32[2,256,2,3,128]{4,1,3,2,0:T(8,128)S(1)} %copy.57), channel_id=1, source_target_pairs={{0,8},{4,12},{8,0},{12,4},{16,24},{20,28},{24,16},{28,20},{32,40},... | collective-permute-start | bytes 4718600 | tf_op jit(solution)/shard_map/ppermute | solution.py:19
  131.6 2.2 copy-start.7
  131.6 5.9 %slice-start = ((s8[7077888]{0:T(1024)(128)(4,1)}), s8[4194304]{0:T(1024)(128)(4,1)S(1)}, s32[]{:S(2)}) async-start(s8[7077888]{0:T(1024)(128)(4,1)} %bitcast.139), calls=%async_computation.4 | async-start | bytes 8388608
  131.9 4.0 copy-start.9
  131.9 5.5 %slice-start.1 = ((s8[7077888]{0:T(1024)(128)(4,1)}), s8[2883584]{0:T(1024)(128)(4,1)S(1)}, s32[]{:S(2)}) async-start(s8[7077888]{0:T(1024)(128)(4,1)} %bitcast.139), calls=%async_computation.5 | async-start | bytes 5767168
  132.0 3.8 collective-permute-start.5
  136.7 0.7 copy-start.13
  136.7 0.7 copy-start.14
  141.4 4.5 copy-start.5
  141.5 337.5 %reduce-scatter.2.cloned.1.call-start = ((), (), s32[]{:S(2)}) async-start(), calls=%async_computation.1 | async-start | bytes 14376960 | tf_op jit(solution)/shard_map/reduce_scatter | solution.py:197
  154.3 71.6 %copy-start.3 = (f32[256,3072]{1,0:T(8,128)S(1)}, f32[256,3072]{1,0:T(8,128)}, u32[]{:S(2)}) copy-start(f32[256,3072]{1,0:T(8,128)} %copy-done.2) | copy-start | bytes 9437188
  154.3 350.3 %all-reduce.5.cloned.1.call-start = ((), (), s32[]{:S(2)}) async-start(), calls=%async_computation.3 | async-start | bytes 1179648 | tf_op jit(solution)/shard_map/psum | solution.py:114
  228.8 277.8 %copy-start.1 = (bf16[192,3072]{1,0:T(8,128)(2,1)S(1)}, bf16[192,3072]{1,0:T(8,128)(2,1)}, u32[]{:S(2)}) copy-start(bf16[192,3072]{1,0:T(8,128)(2,1)} %param.11) | copy-start | bytes 3538948
Sparse Core Ops, SparseCore 0:
  141.6 84.3 all-reduce.2
Sparse Core Ops, SparseCore 1:
  154.4 163.4 reduce-scatter.1
  321.8 182.7 all-reduce.4
where the time goes:
time: 516 us; the launch traced here: 514 us
  blocking collectives  247 us (48%)
  waiting for transfers between devices  149 us (29%)
  local copies, waits for them, and re-layouts  38.8 us (8%)
  other arithmetic  27.9 us (5%)
  matrix products  22.3 us (4%)
  between operations  16.1 us (3%)
  starting transfers between devices  12.9 us (2%)
    psum x1, blocking collectives, seq_total(): return lax.psum((stem_part, vector_part), 'seq')  247 us
    psum x1, waiting for transfers between devices, per_device(): feature_grad = lax.psum(feature_grad, 'head')  71.5 us
    ppermute x4, waiting for transfers between devices, swapped(): return lax.ppermute(value, axis, pairs)  53.4 us
    psum x1, waiting for transfers between devices, seq_total(): return lax.psum((stem_part, vector_part), 'seq')  23.9 us
    unnamed x59, local copies, waits for them, and re-layouts  18.9 us
  transfers between devices with their start and end apart: 9, of which 6 were waited for; matrix products, arithmetic and copies ran while one was open for 6% of the time, Pallas kernels for 0%

commit v1 on v0

v1 whole, which is shorter than its diff:
```python
import functools

import jax
import jax.numpy as jnp
from jax import lax
from jax.experimental import pallas as pl
from jax.experimental.pallas import tpu as pltpu
from jax.sharding import PartitionSpec as P

TT = 2
TS = 8
KNB = 4
HG = 32
WG = 16

ln_eps = 1e-06
F32 = jnp.float32
BF16 = jnp.bfloat16

NN = (((1,), (0,)), ((), ()))
NT = (((1,), (1,)), ((), ()))
TN = (((0,), (0,)), ((), ()))


def mm(a, b, dims=NN):
    return lax.dot_general(a, b, dims, preferred_element_type=F32)


def split2(v):
    hi = v.astype(BF16)
    return hi, (v - hi.astype(F32)).astype(BF16)


def split3(v):
    hi = v.astype(BF16)
    return (hi,) + split2(v - hi.astype(F32))


BLOCK = 512


def forward_kernel(
    ids, pext, stem, bias, scale, shift, w9, proj, hid, nrm, inv_out, wv, scale_out, emb, hid_all, sw, w, sc, sh, sems
):
    width, block = emb.shape
    share = hid.shape[0]
    rows = share // 16
    pin = stem.shape[0]
    hd = w9.shape[2]
    j = ids[0]
    first = pl.program_id(0) == 0
    copies = [
        pltpu.make_async_copy(w9.at[n], w.at[:, n * hd : (n + 1) * hd], sems.at[n]) for n in range(w9.shape[0])
    ]

    @pl.when(first)
    def _():
        for copy in copies:
            copy.start()
        row = lax.broadcasted_iota(jnp.int32, (256 - pin, width), 0)
        parts = split3(bias[...])
        fill = jnp.zeros((256 - pin, width), F32)
        for n in range(3):
            fill = jnp.where(row == n, parts[n].astype(F32), fill)
        sw[0:pin, :] = stem[...]
        sw[pin:256, :] = fill.astype(BF16)
        ones = jnp.ones((8, 128), BF16)
        row = lax.broadcasted_iota(jnp.int32, (8, width), 0)
        for value, column in ((1.0 + scale[...], sc), (shift[...], sh)):
            parts = split3(value)
            fill = jnp.zeros((8, width), F32)
            for n in range(3):
                fill = jnp.where(row == n, parts[n].astype(F32), fill)
            column[...] = mm(fill.astype(BF16), ones, TN)
        for g in range(16):
            at = pl.ds(pl.multiple_of(4 * rows * g + rows * j, 16), rows)
            scale_out[g * rows : (g + 1) * rows, :] = sc[at, :]

    step = width // 4
    for n in range(4):
        emb[n * step : (n + 1) * step, :] = mm(sw[:, n * step : (n + 1) * step], pext[...], TN)
    chunk = 64

    def add(i, acc):
        x = emb[pl.ds(pl.multiple_of(i * chunk, chunk), chunk), :]
        return acc + jnp.sum(x.reshape(chunk // 8, 8, block), axis=0)

    total = lax.fori_loop(0, width // chunk, add, jnp.zeros((8, block), F32), unroll=2)
    mu = jnp.sum(total, axis=0, keepdims=True) * (1.0 / width)

    def add_squares(i, acc):
        x = emb[pl.ds(pl.multiple_of(i * chunk, chunk), chunk), :] - mu
        return acc + jnp.sum((x * x).reshape(chunk // 8, 8, block), axis=0)

    total = lax.fori_loop(0, width // chunk, add_squares, jnp.zeros((8, block), F32), unroll=2)
    inv = lax.rsqrt(jnp.sum(total, axis=0, keepdims=True) * (1.0 / width) + ln_eps)
    inv_out[...] = jnp.broadcast_to(inv, (8, block))

    def normalise(i, carry):
        at = pl.ds(pl.multiple_of(i * chunk, chunk), chunk)
        n = (emb[at, :] - mu) * inv
        emb[at, :] = n
        wide = lambda ref: jnp.concatenate([ref[at, :]] * (block // 128), 1)
        hid_all[at, :] = (n * wide(sc) + wide(sh)).astype(BF16)
        return carry

    lax.fori_loop(0, width // chunk, normalise, 0, unroll=2)
    for g in range(16):
        at = pl.ds(pl.multiple_of(4 * rows * g + rows * j, 16), rows)
        hid[g * rows : (g + 1) * rows, :] = hid_all[at, :]
        nrm[g * rows : (g + 1) * rows, :] = emb[at, :]

    @pl.when(first)
    def _():
        for copy in copies:
            copy.wait()
        row = lax.broadcasted_iota(jnp.int32, (8, width), 0)
        fill = jnp.zeros((8, width), F32)
        for n, part in enumerate(split2(1.0 + scale[...]) + split2(shift[...])):
            fill = jnp.where(row == n, part.astype(F32), fill)
        wv[...] = mm(fill.astype(BF16), w[...])

    proj[...] = mm(hid_all[...], w[...], TN)


def forward(ids, pext, stem, bias, scale, shift, w9, block=BLOCK):
    tokens = pext.shape[1]
    count, width, hd = w9.shape
    columns = count * hd
    share = width // 4
    whole = lambda i, ids: (0, 0)
    rows = lambda i, ids: (i, 0)
    lanes = lambda i, ids: (0, i)
    once = pl.Buffered(1)
    vec = pl.BlockSpec((1, width), whole, pipeline_mode=once)
    return pl.pallas_call(
        forward_kernel,
        grid_spec=pltpu.PrefetchScalarGridSpec(
            num_scalar_prefetch=1,
            grid=(tokens // block,),
            in_specs=[
                pl.BlockSpec((256, block), lanes),
                pl.BlockSpec(stem.shape, whole, pipeline_mode=once),
                vec,
                vec,
                vec,
                pl.BlockSpec(memory_space=pl.ANY),
            ],
            out_specs=[
                pl.BlockSpec((block, columns), rows),
                pl.BlockSpec((share, block), lanes),
                pl.BlockSpec((share, block), lanes),
                pl.BlockSpec((8, block), lanes),
                pl.BlockSpec((8, columns), whole),
                pl.BlockSpec((share, 128), whole),
            ],
            scratch_shapes=[
                pltpu.VMEM((width, block), F32),
                pltpu.VMEM((width, block), BF16),
                pltpu.VMEM((256, width), BF16),
                pltpu.VMEM((width, columns), BF16),
                pltpu.VMEM((width, 128), F32),
                pltpu.VMEM((width, 128), F32),
                pltpu.SemaphoreType.DMA((count,)),
            ],
        ),
        out_shape=[
            jax.ShapeDtypeStruct((tokens, columns), F32),
            jax.ShapeDtypeStruct((share, tokens), BF16),
            jax.ShapeDtypeStruct((share, tokens), F32),
            jax.ShapeDtypeStruct((8, tokens), F32),
            jax.ShapeDtypeStruct((8, columns), F32),
            jax.ShapeDtypeStruct((share, 128), F32),
        ],
        compiler_params=pltpu.CompilerParams(vmem_limit_bytes=60 * 2**20),
        cost_estimate=pl.CostEstimate(
            flops=2 * tokens * width * (columns + 256), bytes_accessed=24 * 2**20, transcendentals=0
        ),
        name="forward",
    )(ids, pext, stem, bias, scale, shift, w9)


def attention_kernel(
    ids, lists, pq, pk, pv, og, qg, kg, wq, wk, wv, mixed, means, q_s, k_s, v_s, o_s, iq_s, ik_s, dq_s, dk_s, dv_s, a1_s, a2_s
):
    tokens, hd = pq.shape
    score_scale = hd ** (-0.5)
    j, g = ids[0], ids[1]
    tile = TT * TS * TS
    count = tokens // tile
    frame_tile = TS * TS
    for raw, gain, keep, store in ((pq, qg, iq_s, q_s), (pk, kg, ik_s, k_s)):
        r = raw[...]
        inv = lax.rsqrt(jnp.mean(r * r, -1, keepdims=True) + ln_eps)
        keep[...] = inv
        store[...] = (r * inv * gain[...]).astype(BF16)
    v_s[...] = pv[...].astype(BF16)
    dk_s[...] = jnp.zeros_like(dk_s)
    dv_s[...] = jnp.zeros_like(dv_s)
    for half in range(2):
        for t in range(count // 2):
            for frame in range(2):
                at = ((half * (count // 2) + t) * 2 + frame) * frame_tile
                o_s[at : at + frame_tile, :] = og[jnp.bitwise_xor(j, 2 * frame + half), 0, t]

    def visit(b, carry):
        mine = pl.ds(pl.multiple_of(b * tile, tile), tile)
        q_b = q_s[mine, :]
        o_b = o_s[mine, :]
        near = [
            pl.ds(pl.multiple_of((lists[g * count + b, n] - g * count) * tile, tile), tile)
            for n in range(KNB)
        ]
        keys = jnp.concatenate([k_s[at, :] for at in near], 0)
        vals = jnp.concatenate([v_s[at, :] for at in near], 0)
        e = jnp.exp(mm(q_b, keys, NT) * score_scale)
        prob = e * (1.0 / jnp.sum(e, -1, keepdims=True))
        slope = mm(o_b, vals, NT)
        centre = jnp.sum(prob * slope, -1, keepdims=True)
        shaped = (prob * (slope - centre)).astype(BF16)
        rounded = prob.astype(BF16)
        dq_s[mine, :] = mm(shaped, keys) * score_scale
        dk = mm(shaped, q_b, TN)
        dv = mm(rounded, o_b, TN)
        for n, at in enumerate(near):
            dk_s[at, :] += dk[n * tile : (n + 1) * tile, :]
            dv_s[at, :] += dv[n * tile : (n + 1) * tile, :]
        return carry

    lax.fori_loop(0, count, visit, 0, unroll=2)

    @pl.when(pl.program_id(0) == 0)
    def _():
        a1_s[...] = jnp.zeros_like(a1_s)
        a2_s[...] = jnp.zeros_like(a2_s)

    m1 = a1_s[...]
    m2 = a2_s[...]
    for i, (raw, gain, keep, grad, factor, vec) in enumerate(
        (
            (pq, qg, iq_s, dq_s, 1.0, wq),
            (pk, kg, ik_s, dk_s, score_scale, wk),
            (pv, None, None, dv_s, 1.0, wv),
        )
    ):
        r = raw[...]
        if gain is None:
            out = grad[...]
        else:
            inv = keep[...]
            u = grad[...] * (gain[...] * factor)
            out = inv * (u - r * (inv * inv * jnp.mean(r * u, -1, keepdims=True)))
        out = out.astype(BF16)
        mixed[i] = out
        out = out.astype(F32)
        m1 = m1 + out * (vec[0:1, :] + vec[1:2, :])
        m2 = m2 + out * (r - (vec[2:3, :] + vec[3:4, :]))
    a1_s[...] = m1
    a2_s[...] = m2

    @pl.when(pl.program_id(0) == pl.num_programs(0) - 1)
    def _():
        for n, total in enumerate((m1, m2)):
            row = jnp.sum(jnp.transpose(total), axis=0, keepdims=True)
            means[n] = jnp.broadcast_to(row, (8, tokens))


def attention(ids, lists, proj, og, q_gain, k_gain, wv):
    tokens, columns = proj.shape
    hd = q_gain.shape[-1]
    heads = columns // 3 // hd
    pick = lambda i: pl.BlockSpec((tokens, hd), lambda h, *_: (0, i * heads + h))
    vec = lambda i: pl.BlockSpec((8, hd), lambda h, *_: (0, i * heads + h))
    gain = pl.BlockSpec((1, hd), lambda h, *_: (0, 0))
    return pl.pallas_call(
        attention_kernel,
        grid_spec=pltpu.PrefetchScalarGridSpec(
            num_scalar_prefetch=2,
            grid=(heads,),
            in_specs=[
                pick(0),
                pick(1),
                pick(2),
                pl.BlockSpec((4, 1) + og.shape[2:], lambda h, *_: (0, h, 0, 0, 0)),
                gain,
                gain,
                vec(0),
                vec(1),
                vec(2),
            ],
            out_specs=[
                pl.BlockSpec((3, tokens, hd), lambda h, *_: (0, 0, h)),
                pl.BlockSpec((2, 8, tokens), lambda h, *_: (0, 0, 0)),
            ],
            scratch_shapes=[pltpu.VMEM((tokens, hd), BF16)] * 4
            + [pltpu.VMEM((tokens, 1), F32)] * 2
            + [pltpu.VMEM((tokens, hd), F32)] * 5,
        ),
        out_shape=[
            jax.ShapeDtypeStruct((3, tokens, heads * hd), BF16),
            jax.ShapeDtypeStruct((2, 8, tokens), F32),
        ],
        compiler_params=pltpu.CompilerParams(vmem_limit_bytes=48 * 2**20),
        cost_estimate=pl.CostEstimate(
            flops=10 * tokens * 512 * hd * heads, bytes_accessed=10 * 2**20, transcendentals=tokens * 512 * heads
        ),
        name="attention",
    )(ids, lists, proj, proj, proj, og, q_gain, k_gain, wv, wv, wv)


def weight_kernel(ids, hid, mixed, *outs):
    rows, hd = outs[0].shape[2:]
    block = 4 * rows
    x = ids[1] // 4
    for k in range(4):
        at = pl.ds(pl.multiple_of((x + k) % 4 * block, block), block)
        mine = hid[at, :]
        for i in range(3):
            part = mm(mine, mixed[i]).astype(BF16)
            for n in range(3):
                for z in range(4):
                    outs[k][z, 3 * i + n] = part[z * rows : (z + 1) * rows, n * hd : (n + 1) * hd]


def weight_part(ids, hid, mixed, hd):
    share, tokens = hid.shape
    third = mixed.shape[2]
    out = jax.ShapeDtypeStruct((4, 3 * third // hd, share // 16, hd), BF16)
    vmem = pl.BlockSpec(memory_space=pltpu.VMEM)
    return pl.pallas_call(
        weight_kernel,
        in_specs=[pl.BlockSpec(memory_space=pltpu.SMEM), vmem, vmem],
        out_specs=[vmem] * 4,
        out_shape=[out] * 4,
        compiler_params=pltpu.CompilerParams(vmem_limit_bytes=40 * 2**20),
        cost_estimate=pl.CostEstimate(
            flops=2 * share * tokens * 3 * third, bytes_accessed=6 * 2**20, transcendentals=0
        ),
        name="weight_part",
    )(ids, hid, mixed)


def stem_kernel(ids, w9, mixed, nrm, sc, means, inv, pext, own, *others):
    third = mixed.shape[2]
    block, tokens = nrm.shape
    count, _, _, _, hd = w9.shape
    w = jnp.concatenate([w9[n, :, 0].reshape(block, hd) for n in range(count)], 1)
    fg = mm(w[:, 0:third], mixed[0], NT)
    for i in range(1, 3):
        fg = fg + mm(w[:, i * third : (i + 1) * third], mixed[i], NT)
    n = nrm[...]
    scale = 1.0 / (4 * 4 * block)
    m1 = means[0, 0:1, :] * scale
    m2 = means[1, 0:1, :] * scale
    eg = (fg * jnp.concatenate([sc[...]] * (tokens // 128), 1) - m1 - n * m2) * inv[0:1, :]
    hi, lo = split2(eg)
    grad = mm(hi, pext[...], NT) + mm(lo, pext[...], NT)
    shift_grad = jnp.sum(fg, -1, keepdims=True)
    scale_grad = jnp.sum(fg * n, -1, keepdims=True)
    lane = lax.broadcasted_iota(jnp.int32, grad.shape, 1)
    grad = jnp.where(lane == 193, shift_grad, grad)
    grad = jnp.where(lane == 194, scale_grad, grad)
    for k, out in enumerate((own,) + others):

        @pl.when(pl.program_id(0) == k)
        def _():
            out[...] = grad.astype(out.dtype)


def stem_part(ids, w9, mixed, nrm, sc, means, inv, pext):
    share, tokens = nrm.shape
    block = share // 4
    count, width, hd = w9.shape
    w9 = w9.reshape(count, 16, 4, share // 16, hd)
    rows = lambda i, ids: ((i + ids[2]) % 4, 0)
    once = pl.Buffered(1)
    shape = (block, 256)
    return pl.pallas_call(
        stem_kernel,
        grid_spec=pltpu.PrefetchScalarGridSpec(
            num_scalar_prefetch=1,
            grid=(4,),
            in_specs=[
                pl.BlockSpec((count, 4, 1, share // 16, hd), lambda i, ids: (0, (i + ids[2]) % 4, ids[0], 0, 0)),
                pl.BlockSpec(mixed.shape, lambda i, ids: (0, 0, 0), pipeline_mode=once),
                pl.BlockSpec((block, tokens), rows),
                pl.BlockSpec((block, 128), rows),
                pl.BlockSpec(means.shape, lambda i, ids: (0, 0, 0), pipeline_mode=once),
                pl.BlockSpec(inv.shape, lambda i, ids: (0, 0), pipeline_mode=once),
                pl.BlockSpec(pext.shape, lambda i, ids: (0, 0), pipeline_mode=once),
            ],
            out_specs=[pl.BlockSpec(shape, lambda i, ids: (0, 0))] * 4,
        ),
        out_shape=[jax.ShapeDtypeStruct(shape, F32)] + [jax.ShapeDtypeStruct(shape, BF16)] * 3,
        compiler_params=pltpu.CompilerParams(vmem_limit_bytes=40 * 2**20),
        cost_estimate=pl.CostEstimate(
            flops=2 * share * tokens * (count * hd + 512), bytes_accessed=10 * 2**20, transcendentals=0
        ),
        name="stem_part",
    )(ids, w9, mixed, nrm, sc, means, inv, pext)


def per_device(
    latent,
    stem_weight,
    stem_bias,
    mod_shift,
    mod_scale,
    qkv_weight,
    q_gain,
    k_gain,
    tile_lists,
    out_grad,
):
    width = qkv_weight.shape[0]
    heads, hd = qkv_weight.shape[2:]
    columns = 3 * heads * hd
    channels = latent.shape[1]
    seq = lax.axis_size("seq")
    groups = seq // 4
    rows = width // seq
    s = lax.axis_index("seq")
    h = lax.axis_index("head")
    g, j = s // 4, s % 4
    half_rows = HG // 2
    tr, tc = half_rows // TS, WG // TS
    tiles = tr * tc
    cell = TS * TS
    x, z = g // 4, g % 4

    def xor(value, mask):
        return lax.ppermute(value, "seq", [(a, a ^ mask) for a in range(seq)])

    piece = latent.reshape(channels, tr, TS, 2, tc, TS, 2)
    piece = jnp.transpose(piece, (0, 3, 6, 1, 4, 2, 5)).reshape(4 * channels, tiles * cell)
    other = xor(piece, 1)
    is_low = s % 2 == 0
    frame = jnp.concatenate([jnp.where(is_low, piece, other), jnp.where(is_low, other, piece)], 1)
    behind = lax.ppermute(frame, "seq", [(a, a + 2) for a in range(seq - 2)])
    ahead = lax.ppermute(frame, "seq", [(a, a - 2) for a in range(2, seq)])
    far_pairs = [(a, a - 4 if a % 4 < 2 else a + 4) for a in range(seq)]
    far = lax.ppermute(frame, "seq", [(a, b) for a, b in far_pairs if 0 <= b < seq])
    even = j < 2
    window = [
        jnp.where(even, behind, far),
        jnp.where(even, frame, behind),
        jnp.where(even, ahead, frame),
        jnp.where(even, far, ahead),
    ]
    fill = jnp.zeros((256 - 12 * channels, 2 * tiles * cell), BF16).at[:3].set(1)
    pext = jnp.stack(
        [
            jnp.concatenate(window[k : k + 3] + [fill], 0).reshape(256, 2 * tiles, cell)
            for k in range(2)
        ],
        2,
    ).reshape(256, 4 * tiles * cell)

    grads = jnp.transpose(out_grad, (1, 0, 2)).reshape(heads, tr, TS, tc, TS, hd)
    grads = jnp.transpose(grads, (0, 1, 3, 2, 4, 5)).reshape(heads, tiles, cell, hd)
    grads = jnp.stack([grads] + [xor(grads, mask) for mask in (1, 2, 3)])

    w9 = jnp.transpose(qkv_weight, (1, 2, 0, 3)).reshape(3 * heads, width, hd)
    ids = jnp.stack([j, g, h]).astype(jnp.int32)

    proj, hid, nrm, inv, wv, sc = forward(
        ids, pext, stem_weight, stem_bias[None], mod_scale[None], mod_shift[None], w9
    )
    mixed, means = attention(ids, tile_lists, proj, grads, q_gain[None], k_gain[None], wv)
    weight = weight_part(ids, hid, mixed, hd)
    stem = stem_part(ids, w9, mixed, nrm, sc, means, inv, pext)

    def shift(value, step, place):
        def target(a):
            ax, az, aj = a // 16, a // 4 % 4, a % 4
            if place == "x":
                ax = (ax + step) % 4
            else:
                az = (az + step) % 4
            return ax * 16 + az * 4 + aj

        return lax.ppermute(value, "seq", [(a, target(a)) for a in range(seq)])

    total = weight[0].astype(F32)
    for k in range(1, 4):
        total = total + shift(weight[k], k, "x").astype(F32)
    total = total.astype(BF16)

    def part(k):
        return lax.dynamic_index_in_dim(total, (z + k) % 4, 0, keepdims=False)

    weight_grad = part(0).astype(F32)
    for k in range(1, 4):
        weight_grad = weight_grad + shift(part(k), k, "z").astype(F32)
    weight_grad = jnp.transpose(weight_grad.reshape(3, heads, rows, hd), (2, 0, 1, 3))

    total = stem[0]
    count = lax.axis_size("head")
    for k in range(1, count):
        pairs = [(a, (a + k) % count) for a in range(count)]
        total = total + lax.ppermute(stem[k], "head", pairs).astype(F32)
    for mask in (16, 32, 4, 8):
        held = lax.reduce_precision(total, 8, 7)
        total = held + xor(held.astype(BF16), mask).astype(F32)
    full = total.astype(BF16)[None]
    for mask in (1, 2):
        other = xor(full, mask)
        low = (s // mask) % 2 == 0
        full = jnp.concatenate([jnp.where(low, full, other), jnp.where(low, other, full)])
    full = full.reshape(4, groups // 4, rows, 256)
    full = jnp.transpose(full, (1, 0, 2, 3)).reshape(width // 4, 256).T.astype(F32)
    base = 12 * channels
    stem_grad = full[:base]
    vector_grad = jnp.stack([full[base + 1], full[base + 2], full[base]])
    return (weight_grad, stem_grad, vector_grad)


def solution(mesh):
    return jax.shard_map(
        per_device,
        mesh=mesh,
        in_specs=(
            P("seq", None, None),
            P(),
            P(),
            P(),
            P(),
            P(None, None, "head", None),
            P(),
            P(),
            P(),
            P("seq", "head", None),
        ),
        out_specs=(P("seq", None, "head", None), P(None, "head"), P(None, "head")),
        check_vma=False,
    )
```

time: 516 us -> 150 us (0.29)
  blocking collectives: 247 us -> 0 us
  waiting for transfers between devices: 149 us -> 31.7 us
  Pallas kernels: 0 us -> 54.5 us
  starting transfers between devices: 12.9 us -> 43.3 us
  local copies, waits for them, and re-layouts: 38.8 us -> 12.5 us
  matrix products: 22.3 us -> 0 us
  other arithmetic: 27.9 us -> 6.07 us
  between operations: 16.1 us -> 1.01 us
    psum x1 -> x0, blocking collectives: 247 us -> none  [seq_total(): return lax.psum((stem_part, vector_part), 'seq')]
    psum x2 -> x0, waiting for transfers between devices: 95.5 us -> none  [the longest x1 71.5 us: per_device(): feature_grad = lax.psum(feature_grad, 'head')]
    pallas_call x0 -> x4, Pallas kernels: none -> 54.5 us  [the longest x1 22.3 us: attention(): pl.pallas_call(attention_kernel, grid_spec=pltpu.PrefetchScalarGridSpec(n...]
    ppermute x6 -> x22, starting transfers between devices: 12.6 us -> 43.3 us  [the longest x10 22.6 us: xor(): return lax.ppermute(value, 'seq', [(a, a ^ mask) for a in range(seq)])]
    dot_general x10 -> x0, matrix products: 22.3 us -> none  [the longest x1 8.41 us: per_device(): lax.dot_general(hidden, mixed_grad, (((0,), (0,)), ((), ())), preferred_e...]
    ppermute x6 -> x22, waiting for transfers between devices: 53.4 us -> 31.7 us  [the longest x6 18.6 us: shift(): return lax.ppermute(value, 'seq', [(a, target(a)) for a in range(seq)])]
    unnamed x59 -> x29, local copies, waits for them, and re-layouts: 18.9 us -> 7.82 us
    scatter-add x1 -> x0, other arithmetic: 9.34 us -> none  [per_device(): pair_tiles = jnp.zeros((tiles_group, tile_len, 2, heads_here, head_dim),...]
  transfers between devices with their start and end apart: 9 -> 22, of which waited for: 6 -> 11; matrix products, arithmetic and copies ran while one was open for 6% -> 5% of each run, Pallas kernels for 0% -> 16%
where the time goes in v1:
time: 150 us; the launch traced here: 149 us
  Pallas kernels  54.5 us (36%)
  starting transfers between devices  43.3 us (29%)
  waiting for transfers between devices  31.7 us (21%)
  local copies, waits for them, and re-layouts  12.5 us (8%)
  other arithmetic  6.07 us (4%)
    ppermute x10, starting transfers between devices, xor(): return lax.ppermute(value, 'seq', [(a, a ^ mask) for a in range(seq)])  22.6 us
    pallas_call x1, Pallas kernels, attention(): pl.pallas_call(attention_kernel, grid_spec=pltpu.PrefetchScalarGridSpec(n...  22.3 us
    pallas_call x1, Pallas kernels, forward(): pl.pallas_call(forward_kernel, grid_spec=pltpu.PrefetchScalarGridSpec(num...  21.4 us
    ppermute x6, waiting for transfers between devices, shift(): return lax.ppermute(value, 'seq', [(a, target(a)) for a in range(seq)])  18.6 us
    ppermute x6, starting transfers between devices, shift(): return lax.ppermute(value, 'seq', [(a, target(a)) for a in range(seq)])  8.2 us
    unnamed x29, local copies, waits for them, and re-layouts  7.82 us
    pallas_call x1, Pallas kernels, stem_part(): pl.pallas_call(stem_kernel, grid_spec=pltpu.PrefetchScalarGridSpec(num_sc...  7.64 us
    ppermute x10, waiting for transfers between devices, xor(): return lax.ppermute(value, 'seq', [(a, a ^ mask) for a in range(seq)])  7.51 us
  transfers between devices with their start and end apart: 22, of which 11 were waited for; matrix products, arithmetic and copies ran while one was open for 5% of the time, Pallas kernels for 16%

profile of v1, /device:TPU:1, one launch (start us, length us, event | category | flops | bytes accessed | tf_op | source)
XLA Modules:
  0.0 149.0 jit_solution(7607852429122477700)
XLA Ops:
  0.6 0.9 copy.28
  1.6 1.0 copy.29
  2.5 0.7 reshape.60
  3.2 3.3 %collective-permute-start = (bf16[64,256]{1,0:T(8,128)(2,1)S(1)}, bf16[64,256]{1,0:T(8,128)(2,1)S(1)}, u32[]{:S(2)}, u32[]{:S(2)}) collective-permute-start(bf16[64,256]{1,0:T(8,128)(2,1)S(1)} %reshape.60), channel_id=1, source_target_pairs={{0,4},{4,0},{8,12},{12,8},{16,20},{20,16},{24,28},{28,24},{32,36},... | collective-permute-start | bytes 98312 | tf_op jit(solution)/shard_map/ppermute | solution.py:432
  6.5 1.0 copy.34
  7.5 0.1 collective-permute-start.6
  7.6 1.4 collective-permute-start.5
  9.0 0.8 copy.35.lists
  9.8 1.3 collective-permute-start.3
  11.1 1.3 collective-permute-start.2
  12.4 6.2 %collective-permute-start.1 = (bf16[64,512]{1,0:T(8,128)(2,1)S(1)}, bf16[64,512]{1,0:T(8,128)(2,1)S(1)}, u32[]{:S(2)}, u32[]{:S(2)}) collective-permute-start(bf16[64,512]{1,0:T(8,128)(2,1)S(1)} %pad_maximum_fusion.6), channel_id=1, source_target_pairs={{0,8},{4,12},{8,16},{12,20},{16,24},{20,28},{24,32},{28,36},{32,40... | collective-permute-start | bytes 196616 | tf_op jit(solution)/shard_map/ppermute | solution.py:439
  18.6 0.6 pad_add_fusion.ids
  19.2 1.6 %collective-permute-done.3 = bf16[64,512]{1,0:T(8,128)(2,1)S(1)} collective-permute-done((bf16[64,512]{1,0:T(8,128)(2,1)S(1)}, bf16[64,512]{1,0:T(8,128)(2,1)S(1)}, u32[]{:S(2)}, u32[]{:S(2)}) %collective-permute-start.3) | collective-permute-done | bytes 65568 | tf_op jit(solution)/shard_map/ppermute | solution.py:440
  20.8 1.0 collective-permute-start.4
  21.9 0.9 pad_maximum_fusion.4
  22.8 0.1 copy.30
  22.9 0.1 copy.31
  23.2 1.0 copy.33.pext
  24.2 21.4 %forward.1 = (f32[1024,1152]{1,0:T(8,128)}, bf16[768,1024]{1,0:T(8,128)(2,1)}, f32[768,1024]{1,0:T(8,128)}, f32[8,1024]{1,0:T(8,128)}, f32[8,1152]{1,0:T(8,128)}, /*index=5*/f32[768,128]{1,0:T(8,128)}) custom-call(s32[3]{0:T(128)} %pad_add_fusion.ids, bf16[256,1024]{1,0:T(8,128)(2,1)} %copy.33.pext, bf16[192,3072]{1,0:T(8,128)(2,1)} %stem.1, ...), custom_call_target="tpu_custom_call" | custom-call | flops 8858370048 | bytes 25165824 | tf_op jit(solution)/shard_map/forward/pallas_call | solution.py:136
  45.6 0.1 pad_maximum_fusion.og
  45.8 0.9 copy-done.5
  46.7 22.3 %attention.1 = (bf16[3,1024,384]{2,1,0:T(8,128)(2,1)S(1)}, f32[2,8,1024]{2,1,0:T(8,128)S(1)}) custom-call(s32[3]{0:T(128)S(1)} %copy-done.7, s32[128,4]{1,0:T(8,128)S(1)} %copy.35.lists, f32[1024,1152]{1,0:T(8,128)} %get-tuple-element.32.pq.pk.pv, f32[1024,1152]{1,0:T(8,128)} %get-tuple-element.32.pq.pk.pv, f32[1024,1152]{1,0:T(8,128)} %get-tuple-element.32.pq.pk.pv, ...), custom_call_target="tpu_custom_call" | custom-call | flops 2013265920 | bytes 10485760 | tf_op jit(solution)/shard_map/attention/pallas_call | solution.py:275
  69.0 1.4 copy-done.1
  70.4 1.7 %copy-done.2 = bf16[3,1024,384]{2,1,0:T(8,128)(2,1)S(1)} copy-done((bf16[3,1024,384]{2,1,0:T(8,128)(2,1)S(1)}, bf16[3,1024,384]{2,1,0:T(8,128)(2,1)}, u32[]{:S(2)}) %copy-start.2) | copy-done | bytes 2359320
  72.1 1.0 copy-done.4
  73.1 7.6 %stem_part.1 = (f32[192,256]{1,0:T(8,128)S(1)}, bf16[192,256]{1,0:T(8,128)(2,1)S(1)}, bf16[192,256]{1,0:T(8,128)(2,1)S(1)}, bf16[192,256]{1,0:T(8,128)(2,1)S(1)}) custom-call(s32[3]{0:T(128)S(1)} %copy-done.7, bf16[9,16,4,48,128]{4,3,2,1,0:T(8,128)(2,1)S(1)} %bitcast.57, bf16[3,1024,384]{2,1,0:T(8,128)(2,1)S(1)} %copy-done.2, f32[768,1024]{1,0:T(8,128)S(1)} %copy-done, ...), custom_call_target="tpu_custom_call" | custom-call | flops 2617245696 | bytes 10485760 | tf_op jit(solution)/shard_map/stem_part/pallas_call | solution.py:378
  80.7 0.1 collective-permute-start.13
  80.8 2.6 %collective-permute-start.14 = (bf16[192,256]{1,0:T(8,128)(2,1)S(1)}, bf16[192,256]{1,0:T(8,128)(2,1)S(1)}, u32[]{:S(2)}, u32[]{:S(2)}) collective-permute-start(bf16[192,256]{1,0:T(8,128)(2,1)S(1)} %get-tuple-element.45), channel_id=1, source_target_pairs={{0,2},{1,3},{2,0},{3,1},{4,6},{5,7},{6,4},{7,5},{8,10},{9,11},{10,... | collective-permute-start | bytes 294920 | tf_op jit(solution)/shard_map/ppermute | solution.py:501
  83.4 1.1 collective-permute-start.15
  84.5 3.0 %collective-permute-done.13 = bf16[192,256]{1,0:T(8,128)(2,1)S(1)} collective-permute-done((bf16[192,256]{1,0:T(8,128)(2,1)S(1)}, bf16[192,256]{1,0:T(8,128)(2,1)S(1)}, u32[]{:S(2)}, u32[]{:S(2)}) %collective-permute-start.13) | collective-permute-done | bytes 98336 | tf_op jit(solution)/shard_map/ppermute | solution.py:501
  87.5 1.0 collective-permute-done.15
  88.5 0.1 fusion.6
  88.5 5.2 %collective-permute-start.16 = (bf16[192,256]{1,0:T(8,128)(2,1)S(1)}, bf16[192,256]{1,0:T(8,128)(2,1)S(1)}, u32[]{:S(2)}, u32[]{:S(2)}) collective-permute-start(bf16[192,256]{1,0:T(8,128)(2,1)S(1)} %get-tuple-element.53), channel_id=1, source_target_pairs={{0,64},{4,68},{8,72},{12,76},{16,80},{20,84},{24,88},{28,92},{32,9... | collective-permute-start | bytes 294920 | tf_op jit(solution)/shard_map/ppermute | solution.py:432
  93.7 2.0 %collective-permute-done.16 = bf16[192,256]{1,0:T(8,128)(2,1)S(1)} collective-permute-done((bf16[192,256]{1,0:T(8,128)(2,1)S(1)}, bf16[192,256]{1,0:T(8,128)(2,1)S(1)}, u32[]{:S(2)}, u32[]{:S(2)}) %collective-permute-start.16) | collective-permute-done | bytes 98336 | tf_op jit(solution)/shard_map/ppermute | solution.py:432
  95.8 3.1 %collective-permute-start.17 = (bf16[192,256]{1,0:T(8,128)(2,1)S(1)}, bf16[192,256]{1,0:T(8,128)(2,1)S(1)}, u32[]{:S(2)}, u32[]{:S(2)}) collective-permute-start(bf16[192,256]{1,0:T(8,128)(2,1)S(1)} %fusion.2), channel_id=1, source_target_pairs={{0,128},{4,132},{8,136},{12,140},{16,144},{20,148},{24,152},{28,15... | collective-permute-start | bytes 294920 | tf_op jit(solution)/shard_map/ppermute | solution.py:432
  98.9 3.2 %weight_part.1 = (bf16[4,9,48,128]{3,2,1,0:T(8,128)(2,1)S(1)}, bf16[4,9,48,128]{3,2,1,0:T(8,128)(2,1)S(1)}, bf16[4,9,48,128]{3,2,1,0:T(8,128)(2,1)S(1)}, bf16[4,9,48,128]{3,2,1,0:T(8,128)(2,1)S(1)}) custom-call(s32[3]{0:T(128)S(1)} %copy-done.7, bf16[768,1024]{1,0:T(8,128)(2,1)S(1)} %copy-done.10, bf16[3,1024,384]{2,1,0:T(8,128)(2,1)S(1)} %copy-done.2), custom_call_target="tpu_custom_call" | custom-call | flops 1811939328 | bytes 6291456 | tf_op jit(solution)/shard_map/weight_part/pallas_call | solution.py:330
  102.1 0.7 collective-permute-start.7
  102.7 1.4 collective-permute-start.8
  104.2 1.1 collective-permute-start.9
  105.2 0.7 fusion.5
  105.9 4.8 %collective-permute-done.18 = bf16[192,256]{1,0:T(8,128)(2,1)} collective-permute-done((bf16[192,256]{1,0:T(8,128)(2,1)}, bf16[192,256]{1,0:T(8,128)(2,1)}, u32[]{:S(2)}, u32[]{:S(2)}) %collective-permute-start.18) | collective-permute-done | bytes 98336 | tf_op jit(solution)/shard_map/ppermute | solution.py:432
  110.7 1.0 fusion.3
  111.7 3.0 %collective-permute-start.19 = (bf16[192,256]{1,0:T(8,128)(2,1)S(1)}, bf16[192,256]{1,0:T(8,128)(2,1)S(1)}, u32[]{:S(2)}, u32[]{:S(2)}) collective-permute-start(bf16[192,256]{1,0:T(8,128)(2,1)S(1)} %fusion.3), channel_id=1, source_target_pairs={{0,32},{4,36},{8,40},{12,44},{16,48},{20,52},{24,56},{28,60},{32,0... | collective-permute-start | bytes 294920 | tf_op jit(solution)/shard_map/ppermute | solution.py:432
  114.6 5.4 %collective-permute-done.8 = bf16[4,9,48,128]{3,2,1,0:T(8,128)(2,1)S(1)} collective-permute-done((bf16[4,9,48,128]{3,2,1,0:T(8,128)(2,1)S(1)}, bf16[4,9,48,128]{3,2,1,0:T(8,128)(2,1)S(1)}, u32[]{:S(2)}, u32[]{:S(2)}) %collective-permute-start.8) | collective-permute-done | bytes 442400 | tf_op jit(solution)/shard_map/ppermute | solution.py:482
  120.0 3.8 %collective-permute-done.9 = bf16[4,9,48,128]{3,2,1,0:T(8,128)(2,1)S(1)} collective-permute-done((bf16[4,9,48,128]{3,2,1,0:T(8,128)(2,1)S(1)}, bf16[4,9,48,128]{3,2,1,0:T(8,128)(2,1)S(1)}, u32[]{:S(2)}, u32[]{:S(2)}) %collective-permute-start.9) | collective-permute-done | bytes 442400 | tf_op jit(solution)/shard_map/ppermute | solution.py:482
  123.9 0.2 add_convert_fusion
  124.1 1.0 fusion.4
  125.1 5.4 %collective-permute-start.20 = (bf16[1,192,256]{2,1,0:T(8,128)(2,1)S(1)}, bf16[1,192,256]{2,1,0:T(8,128)(2,1)S(1)}, u32[]{:S(2)}, u32[]{:S(2)}) collective-permute-start(bf16[1,192,256]{2,1,0:T(8,128)(2,1)S(1)} %fusion.4), channel_id=1, source_target_pairs={{0,4},{4,0},{8,12},{12,8},{16,20},{20,16},{24,28},{28,24},{32,36},... | collective-permute-start | bytes 294920 | tf_op jit(solution)/shard_map/ppermute | solution.py:432
  130.5 0.1 collective-permute-start.10
  130.6 3.6 %collective-permute-start.12 = (bf16[9,48,128]{2,1,0:T(8,128)(2,1)S(1)}, bf16[9,48,128]{2,1,0:T(8,128)(2,1)S(1)}, u32[]{:S(2)}, u32[]{:S(2)}) collective-permute-start(bf16[9,48,128]{2,1,0:T(8,128)(2,1)S(1)} %get-tuple-element.56), channel_id=1, source_target_pairs={{0,48},{4,52},{8,56},{12,60},{16,0},{20,4},{24,8},{28,12},{32,16},... | collective-permute-start | bytes 331784 | tf_op jit(solution)/shard_map/ppermute | solution.py:482
  134.2 1.4 collective-permute-start.11
  135.6 0.1 collective-permute-start.21
  135.7 3.1 %collective-permute-done.10 = bf16[9,48,128]{2,1,0:T(8,128)(2,1)S(1)} collective-permute-done((bf16[9,48,128]{2,1,0:T(8,128)(2,1)S(1)}, bf16[9,48,128]{2,1,0:T(8,128)(2,1)S(1)}, u32[]{:S(2)}, u32[]{:S(2)}) %collective-permute-start.10) | collective-permute-done | bytes 110624 | tf_op jit(solution)/shard_map/ppermute | solution.py:482
  138.8 1.2 collective-permute-done.12
  140.0 5.1 %collective-permute-done.11 = bf16[9,48,128]{2,1,0:T(8,128)(2,1)S(1)} collective-permute-done((bf16[9,48,128]{2,1,0:T(8,128)(2,1)S(1)}, bf16[9,48,128]{2,1,0:T(8,128)(2,1)S(1)}, u32[]{:S(2)}, u32[]{:S(2)}) %collective-permute-start.11) | collective-permute-done | bytes 110624 | tf_op jit(solution)/shard_map/ppermute | solution.py:482
  145.1 0.7 fusion.1
  145.8 0.7 collective-permute-done.21
  146.6 0.1 copy.37
  146.7 0.2 slice.32
  146.9 0.2 slice.31
  147.0 0.2 copy.39
  147.2 0.2 copy.38
  147.4 1.1 copy.40
  148.4 0.6 pad_maximum_fusion.7
  (46 shorter events, 0.4 us)
Async XLA Ops:
  3.2 6.5 %collective-permute-start = (bf16[64,256]{1,0:T(8,128)(2,1)S(1)}, bf16[64,256]{1,0:T(8,128)(2,1)S(1)}, u32[]{:S(2)}, u32[]{:S(2)}) collective-permute-start(bf16[64,256]{1,0:T(8,128)(2,1)S(1)} %reshape.60), channel_id=1, source_target_pairs={{0,4},{4,0},{8,12},{12,8},{16,20},{20,16},{24,28},{28,24},{32,36},... | collective-permute-start | bytes 98312 | tf_op jit(solution)/shard_map/ppermute | solution.py:432
  7.5 38.0 %collective-permute-start.6 = (bf16[3,4,64,128]{3,2,1,0:T(8,128)(2,1)S(1)}, bf16[3,4,64,128]{3,2,1,0:T(8,128)(2,1)S(1)}, u32[]{:S(2)}, u32[]{:S(2)}) collective-permute-start(bf16[3,4,64,128]{3,2,1,0:T(8,128)(2,1)S(1)} %bitcast.68), channel_id=1, source_target_pairs={{0,12},{4,8},{8,4},{12,0},{16,28},{20,24},{24,20},{28,16},{32,44},... | collective-permute-start | bytes 589832 | tf_op jit(solution)/shard_map/ppermute | solution.py:432
  7.6 38.0 %collective-permute-start.5 = (bf16[3,4,64,128]{3,2,1,0:T(8,128)(2,1)S(1)}, bf16[3,4,64,128]{3,2,1,0:T(8,128)(2,1)S(1)}, u32[]{:S(2)}, u32[]{:S(2)}) collective-permute-start(bf16[3,4,64,128]{3,2,1,0:T(8,128)(2,1)S(1)} %bitcast.69), channel_id=1, source_target_pairs={{0,8},{4,12},{8,0},{12,4},{16,24},{20,28},{24,16},{28,20},{32,40},... | collective-permute-start | bytes 589832 | tf_op jit(solution)/shard_map/ppermute | solution.py:432
  9.8 11.0 %collective-permute-start.3 = (bf16[64,512]{1,0:T(8,128)(2,1)S(1)}, bf16[64,512]{1,0:T(8,128)(2,1)S(1)}, u32[]{:S(2)}, u32[]{:S(2)}) collective-permute-start(bf16[64,512]{1,0:T(8,128)(2,1)S(1)} %pad_maximum_fusion.6), channel_id=1, source_target_pairs={{8,0},{12,4},{16,8},{20,12},{24,16},{28,20},{32,24},{36,28},{40,32... | collective-permute-start | bytes 196616 | tf_op jit(solution)/shard_map/ppermute | solution.py:440
  11.1 10.7 %collective-permute-start.2 = (bf16[64,512]{1,0:T(8,128)(2,1)S(1)}, bf16[64,512]{1,0:T(8,128)(2,1)S(1)}, u32[]{:S(2)}, u32[]{:S(2)}) collective-permute-start(bf16[64,512]{1,0:T(8,128)(2,1)S(1)} %pad_maximum_fusion.6), channel_id=1, source_target_pairs={{8,24},{12,28},{16,0},{20,4},{24,40},{28,44},{32,16},{36,20},{40,5... | collective-permute-start | bytes 196616 | tf_op jit(solution)/shard_map/ppermute | solution.py:442
  12.4 9.4 %collective-permute-start.1 = (bf16[64,512]{1,0:T(8,128)(2,1)S(1)}, bf16[64,512]{1,0:T(8,128)(2,1)S(1)}, u32[]{:S(2)}, u32[]{:S(2)}) collective-permute-start(bf16[64,512]{1,0:T(8,128)(2,1)S(1)} %pad_maximum_fusion.6), channel_id=1, source_target_pairs={{0,8},{4,12},{8,16},{12,20},{16,24},{20,28},{24,32},{28,36},{32,40... | collective-permute-start | bytes 196616 | tf_op jit(solution)/shard_map/ppermute | solution.py:439
  20.8 24.8 %collective-permute-start.4 = (bf16[3,4,64,128]{3,2,1,0:T(8,128)(2,1)S(1)}, bf16[3,4,64,128]{3,2,1,0:T(8,128)(2,1)S(1)}, u32[]{:S(2)}, u32[]{:S(2)}) collective-permute-start(bf16[3,4,64,128]{3,2,1,0:T(8,128)(2,1)S(1)} %bitcast.70), channel_id=1, source_target_pairs={{0,4},{4,0},{8,12},{12,8},{16,20},{20,16},{24,28},{28,24},{32,36},... | collective-permute-start | bytes 589832 | tf_op jit(solution)/shard_map/ppermute | solution.py:432
  24.2 21.5 %copy-start.7 = (s32[3]{0:T(128)S(1)}, s32[3]{0:T(128)}, u32[]{:S(2)}) copy-start(s32[3]{0:T(128)} %pad_add_fusion.ids) | copy-start | bytes 40
  24.2 21.6 %copy-start.8 = (f32[128]{0:T(128)S(1)}, f32[128]{0:T(128)}, u32[]{:S(2)}) copy-start(f32[128]{0:T(128)} %param.18) | copy-start | bytes 1540
  24.2 21.6 %copy-start.9 = (f32[128]{0:T(128)S(1)}, f32[128]{0:T(128)}, u32[]{:S(2)}) copy-start(f32[128]{0:T(128)} %param.19) | copy-start | bytes 1540
  45.7 24.7 %slice-start = ((s8[7077888]{0:T(1024)(128)(4,1)}), s8[4194304]{0:T(1024)(128)(4,1)S(1)}, s32[]{:S(2)}) async-start(s8[7077888]{0:T(1024)(128)(4,1)} %bitcast.55), calls=%async_computation | async-start | bytes 8388608
  45.7 0.9 copy-start.5
  46.7 23.7 %slice-start.1 = ((s8[7077888]{0:T(1024)(128)(4,1)}), s8[2883584]{0:T(1024)(128)(4,1)S(1)}, s32[]{:S(2)}) async-start(s8[7077888]{0:T(1024)(128)(4,1)} %bitcast.55), calls=%async_computation.1 | async-start | bytes 5767168
  46.7 23.7 %copy-start = (f32[768,1024]{1,0:T(8,128)S(1)}, f32[768,1024]{1,0:T(8,128)}, u32[]{:S(2)}) copy-start(f32[768,1024]{1,0:T(8,128)} %get-tuple-element.39.nrm) | copy-start | bytes 9437188
  46.7 23.7 %copy-start.3 = (bf16[256,1024]{1,0:T(8,128)(2,1)S(1)}, bf16[256,1024]{1,0:T(8,128)(2,1)}, u32[]{:S(2)}) copy-start(bf16[256,1024]{1,0:T(8,128)(2,1)} %copy.33.pext) | copy-start | bytes 1572868
  46.7 23.7 %copy-start.6 = (f32[8,1024]{1,0:T(8,128)S(1)}, f32[8,1024]{1,0:T(8,128)}, u32[]{:S(2)}) copy-start(f32[8,1024]{1,0:T(8,128)} %get-tuple-element.42.inv) | copy-start | bytes 98308
  69.0 1.4 copy-start.1
  70.4 1.7 %copy-start.2 = (bf16[3,1024,384]{2,1,0:T(8,128)(2,1)S(1)}, bf16[3,1024,384]{2,1,0:T(8,128)(2,1)}, u32[]{:S(2)}) copy-start(bf16[3,1024,384]{2,1,0:T(8,128)(2,1)} %copy-done.1) | copy-start | bytes 7077892
  72.1 1.0 copy-start.4
  73.1 25.8 %copy-start.10 = (bf16[768,1024]{1,0:T(8,128)(2,1)S(1)}, bf16[768,1024]{1,0:T(8,128)(2,1)}, u32[]{:S(2)}) copy-start(bf16[768,1024]{1,0:T(8,128)(2,1)} %get-tuple-element.31.hid) | copy-start | bytes 4718596
  80.7 6.8 %collective-permute-start.13 = (bf16[192,256]{1,0:T(8,128)(2,1)S(1)}, bf16[192,256]{1,0:T(8,128)(2,1)S(1)}, u32[]{:S(2)}, u32[]{:S(2)}) collective-permute-start(bf16[192,256]{1,0:T(8,128)(2,1)S(1)} %get-tuple-element.44), channel_id=1, source_target_pairs={{0,1},{1,2},{2,3},{3,0},{4,5},{5,6},{6,7},{7,4},{8,9},{9,10},{10,1... | collective-permute-start | bytes 294920 | tf_op jit(solution)/shard_map/ppermute | solution.py:501
  80.8 6.7 %collective-permute-start.14 = (bf16[192,256]{1,0:T(8,128)(2,1)S(1)}, bf16[192,256]{1,0:T(8,128)(2,1)S(1)}, u32[]{:S(2)}, u32[]{:S(2)}) collective-permute-start(bf16[192,256]{1,0:T(8,128)(2,1)S(1)} %get-tuple-element.45), channel_id=1, source_target_pairs={{0,2},{1,3},{2,0},{3,1},{4,6},{5,7},{6,4},{7,5},{8,10},{9,11},{10,... | collective-permute-start | bytes 294920 | tf_op jit(solution)/shard_map/ppermute | solution.py:501
  83.4 5.1 %collective-permute-start.15 = (bf16[192,256]{1,0:T(8,128)(2,1)S(1)}, bf16[192,256]{1,0:T(8,128)(2,1)S(1)}, u32[]{:S(2)}, u32[]{:S(2)}) collective-permute-start(bf16[192,256]{1,0:T(8,128)(2,1)S(1)} %get-tuple-element.46), channel_id=1, source_target_pairs={{0,3},{1,0},{2,1},{3,2},{4,7},{5,4},{6,5},{7,6},{8,11},{9,8},{10,9... | collective-permute-start | bytes 294920 | tf_op jit(solution)/shard_map/ppermute | solution.py:501
  88.5 7.2 %collective-permute-start.16 = (bf16[192,256]{1,0:T(8,128)(2,1)S(1)}, bf16[192,256]{1,0:T(8,128)(2,1)S(1)}, u32[]{:S(2)}, u32[]{:S(2)}) collective-permute-start(bf16[192,256]{1,0:T(8,128)(2,1)S(1)} %get-tuple-element.53), channel_id=1, source_target_pairs={{0,64},{4,68},{8,72},{12,76},{16,80},{20,84},{24,88},{28,92},{32,9... | collective-permute-start | bytes 294920 | tf_op jit(solution)/shard_map/ppermute | solution.py:432
  95.8 9.5 %collective-permute-start.17 = (bf16[192,256]{1,0:T(8,128)(2,1)S(1)}, bf16[192,256]{1,0:T(8,128)(2,1)S(1)}, u32[]{:S(2)}, u32[]{:S(2)}) collective-permute-start(bf16[192,256]{1,0:T(8,128)(2,1)S(1)} %fusion.2), channel_id=1, source_target_pairs={{0,128},{4,132},{8,136},{12,140},{16,144},{20,148},{24,152},{28,15... | collective-permute-start | bytes 294920 | tf_op jit(solution)/shard_map/ppermute | solution.py:432
  102.1 12.6 %collective-permute-start.7 = (bf16[4,9,48,128]{3,2,1,0:T(8,128)(2,1)S(1)}, bf16[4,9,48,128]{3,2,1,0:T(8,128)(2,1)S(1)}, u32[]{:S(2)}, u32[]{:S(2)}) collective-permute-start(bf16[4,9,48,128]{3,2,1,0:T(8,128)(2,1)S(1)} %get-tuple-element.36), channel_id=1, source_target_pairs={{0,64},{4,68},{8,72},{12,76},{16,80},{20,84},{24,88},{28,92},{32,9... | collective-permute-start | bytes 1327112 | tf_op jit(solution)/shard_map/ppermute | solution.py:482
  102.7 17.3 %collective-permute-start.8 = (bf16[4,9,48,128]{3,2,1,0:T(8,128)(2,1)S(1)}, bf16[4,9,48,128]{3,2,1,0:T(8,128)(2,1)S(1)}, u32[]{:S(2)}, u32[]{:S(2)}) collective-permute-start(bf16[4,9,48,128]{3,2,1,0:T(8,128)(2,1)S(1)} %get-tuple-element.37), channel_id=1, source_target_pairs={{0,128},{4,132},{8,136},{12,140},{16,144},{20,148},{24,152},{28,15... | collective-permute-start | bytes 1327112 | tf_op jit(solution)/shard_map/ppermute | solution.py:482
  104.2 19.7 %collective-permute-start.9 = (bf16[4,9,48,128]{3,2,1,0:T(8,128)(2,1)S(1)}, bf16[4,9,48,128]{3,2,1,0:T(8,128)(2,1)S(1)}, u32[]{:S(2)}, u32[]{:S(2)}) collective-permute-start(bf16[4,9,48,128]{3,2,1,0:T(8,128)(2,1)S(1)} %get-tuple-element.38), channel_id=1, source_target_pairs={{0,192},{4,196},{8,200},{12,204},{16,208},{20,212},{24,216},{28,22... | collective-permute-start | bytes 1327112 | tf_op jit(solution)/shard_map/ppermute | solution.py:482
  105.9 4.8 %collective-permute-start.18 = (bf16[192,256]{1,0:T(8,128)(2,1)}, bf16[192,256]{1,0:T(8,128)(2,1)}, u32[]{:S(2)}, u32[]{:S(2)}) collective-permute-start(bf16[192,256]{1,0:T(8,128)(2,1)} %fusion.5), channel_id=1, source_target_pairs={{0,16},{4,20},{8,24},{12,28},{16,0},{20,4},{24,8},{28,12},{32,48},... | collective-permute-start | bytes 294920 | tf_op jit(solution)/shard_map/ppermute | solution.py:432
  111.7 12.4 %collective-permute-start.19 = (bf16[192,256]{1,0:T(8,128)(2,1)S(1)}, bf16[192,256]{1,0:T(8,128)(2,1)S(1)}, u32[]{:S(2)}, u32[]{:S(2)}) collective-permute-start(bf16[192,256]{1,0:T(8,128)(2,1)S(1)} %fusion.3), channel_id=1, source_target_pairs={{0,32},{4,36},{8,40},{12,44},{16,48},{20,52},{24,56},{28,60},{32,0... | collective-permute-start | bytes 294920 | tf_op jit(solution)/shard_map/ppermute | solution.py:432
  125.1 10.5 %collective-permute-start.20 = (bf16[1,192,256]{2,1,0:T(8,128)(2,1)S(1)}, bf16[1,192,256]{2,1,0:T(8,128)(2,1)S(1)}, u32[]{:S(2)}, u32[]{:S(2)}) collective-permute-start(bf16[1,192,256]{2,1,0:T(8,128)(2,1)S(1)} %fusion.4), channel_id=1, source_target_pairs={{0,4},{4,0},{8,12},{12,8},{16,20},{20,16},{24,28},{28,24},{32,36},... | collective-permute-start | bytes 294920 | tf_op jit(solution)/shard_map/ppermute | solution.py:432
  130.5 8.3 %collective-permute-start.10 = (bf16[9,48,128]{2,1,0:T(8,128)(2,1)S(1)}, bf16[9,48,128]{2,1,0:T(8,128)(2,1)S(1)}, u32[]{:S(2)}, u32[]{:S(2)}) collective-permute-start(bf16[9,48,128]{2,1,0:T(8,128)(2,1)S(1)} %get-tuple-element.55), channel_id=1, source_target_pairs={{0,16},{4,20},{8,24},{12,28},{16,32},{20,36},{24,40},{28,44},{32,4... | collective-permute-start | bytes 331784 | tf_op jit(solution)/shard_map/ppermute | solution.py:482
  130.6 9.4 %collective-permute-start.12 = (bf16[9,48,128]{2,1,0:T(8,128)(2,1)S(1)}, bf16[9,48,128]{2,1,0:T(8,128)(2,1)S(1)}, u32[]{:S(2)}, u32[]{:S(2)}) collective-permute-start(bf16[9,48,128]{2,1,0:T(8,128)(2,1)S(1)} %get-tuple-element.56), channel_id=1, source_target_pairs={{0,48},{4,52},{8,56},{12,60},{16,0},{20,4},{24,8},{28,12},{32,16},... | collective-permute-start | bytes 331784 | tf_op jit(solution)/shard_map/ppermute | solution.py:482
  134.2 10.9 %collective-permute-start.11 = (bf16[9,48,128]{2,1,0:T(8,128)(2,1)S(1)}, bf16[9,48,128]{2,1,0:T(8,128)(2,1)S(1)}, u32[]{:S(2)}, u32[]{:S(2)}) collective-permute-start(bf16[9,48,128]{2,1,0:T(8,128)(2,1)S(1)} %get-tuple-element.57), channel_id=1, source_target_pairs={{0,32},{4,36},{8,40},{12,44},{16,48},{20,52},{24,56},{28,60},{32,0... | collective-permute-start | bytes 331784 | tf_op jit(solution)/shard_map/ppermute | solution.py:482
  135.6 10.9 %collective-permute-start.21 = (bf16[2,192,256]{2,1,0:T(8,128)(2,1)S(1)}, bf16[2,192,256]{2,1,0:T(8,128)(2,1)S(1)}, u32[]{:S(2)}, u32[]{:S(2)}) collective-permute-start(bf16[2,192,256]{2,1,0:T(8,128)(2,1)S(1)} %pad_maximum_fusion.5), channel_id=1, source_target_pairs={{0,8},{4,12},{8,0},{12,4},{16,24},{20,28},{24,16},{28,20},{32,40},... | collective-permute-start | bytes 589832 | tf_op jit(solution)/shard_map/ppermute | solution.py:432

commit v2 on v1

--- a/solution.py
+++ b/solution.py
@@ -14,6 +14,7 @@
 WG = 16
 
 ln_eps = 1e-06
+LOG2E = 1.4426950408889634
 F32 = jnp.float32
 BF16 = jnp.bfloat16
 
@@ -213,21 +214,21 @@
         ]
         keys = jnp.concatenate([k_s[at, :] for at in near], 0)
         vals = jnp.concatenate([v_s[at, :] for at in near], 0)
-        e = jnp.exp(mm(q_b, keys, NT) * score_scale)
+        e = jnp.exp2(mm(q_b, keys, NT) * (score_scale * LOG2E))
         prob = e * (1.0 / jnp.sum(e, -1, keepdims=True))
         slope = mm(o_b, vals, NT)
         centre = jnp.sum(prob * slope, -1, keepdims=True)
         shaped = (prob * (slope - centre)).astype(BF16)
         rounded = prob.astype(BF16)
         dq_s[mine, :] = mm(shaped, keys) * score_scale
-        dk = mm(shaped, q_b, TN)
-        dv = mm(rounded, o_b, TN)
+        dk = mm(q_b, shaped, TN)
+        dv = mm(o_b, rounded, TN)
         for n, at in enumerate(near):
-            dk_s[at, :] += dk[n * tile : (n + 1) * tile, :]
-            dv_s[at, :] += dv[n * tile : (n + 1) * tile, :]
+            dk_s[:, at] += dk[:, n * tile : (n + 1) * tile]
+            dv_s[:, at] += dv[:, n * tile : (n + 1) * tile]
         return carry
 
-    lax.fori_loop(0, count, visit, 0, unroll=2)
+    lax.fori_loop(0, count, visit, 0, unroll=8)
 
     @pl.when(pl.program_id(0) == 0)
     def _():
@@ -238,17 +239,17 @@
     m2 = a2_s[...]
     for i, (raw, gain, keep, grad, factor, vec) in enumerate(
         (
-            (pq, qg, iq_s, dq_s, 1.0, wq),
-            (pk, kg, ik_s, dk_s, score_scale, wk),
-            (pv, None, None, dv_s, 1.0, wv),
+            (pq, qg, iq_s, dq_s[...], 1.0, wq),
+            (pk, kg, ik_s, jnp.transpose(dk_s[...]), score_scale, wk),
+            (pv, None, None, jnp.transpose(dv_s[...]), 1.0, wv),
         )
     ):
         r = raw[...]
         if gain is None:
-            out = grad[...]
+            out = grad
         else:
             inv = keep[...]
-            u = grad[...] * (gain[...] * factor)
+            u = grad * (gain[...] * factor)
             out = inv * (u - r * (inv * inv * jnp.mean(r * u, -1, keepdims=True)))
         out = out.astype(BF16)
         mixed[i] = out
@@ -294,7 +295,9 @@
             ],
             scratch_shapes=[pltpu.VMEM((tokens, hd), BF16)] * 4
             + [pltpu.VMEM((tokens, 1), F32)] * 2
-            + [pltpu.VMEM((tokens, hd), F32)] * 5,
+            + [pltpu.VMEM((tokens, hd), F32)]
+            + [pltpu.VMEM((hd, tokens), F32)] * 2
+            + [pltpu.VMEM((tokens, hd), F32)] * 2,
         ),
         out_shape=[
             jax.ShapeDtypeStruct((3, tokens, heads * hd), BF16),
@@ -394,7 +397,7 @@
         out_shape=[jax.ShapeDtypeStruct(shape, F32)] + [jax.ShapeDtypeStruct(shape, BF16)] * 3,
         compiler_params=pltpu.CompilerParams(vmem_limit_bytes=40 * 2**20),
         cost_estimate=pl.CostEstimate(
-            flops=2 * share * tokens * (count * hd + 512), bytes_accessed=10 * 2**20, transcendentals=0
+            flops=1000, bytes_accessed=1000, transcendentals=0
         ),
         name="stem_part",
     )(ids, w9, mixed, nrm, sc, means, inv, pext)
@@ -426,7 +429,6 @@
     tr, tc = half_rows // TS, WG // TS
     tiles = tr * tc
     cell = TS * TS
-    x, z = g // 4, g % 4
 
     def xor(value, mask):
         return lax.ppermute(value, "seq", [(a, a ^ mask) for a in range(seq)])
@@ -468,40 +470,36 @@
     )
     mixed, means = attention(ids, tile_lists, proj, grads, q_gain[None], k_gain[None], wv)
     weight = weight_part(ids, hid, mixed, hd)
+    mixed, *weight = lax.optimization_barrier((mixed, *weight))
     stem = stem_part(ids, w9, mixed, nrm, sc, means, inv, pext)
 
-    def shift(value, step, place):
-        def target(a):
-            ax, az, aj = a // 16, a // 4 % 4, a % 4
-            if place == "x":
-                ax = (ax + step) % 4
-            else:
-                az = (az + step) % 4
-            return ax * 16 + az * 4 + aj
-
-        return lax.ppermute(value, "seq", [(a, target(a)) for a in range(seq)])
-
-    total = weight[0].astype(F32)
+    weight_total = weight[0].astype(F32)
     for k in range(1, 4):
-        total = total + shift(weight[k], k, "x").astype(F32)
-    total = total.astype(BF16)
-
-    def part(k):
-        return lax.dynamic_index_in_dim(total, (z + k) % 4, 0, keepdims=False)
-
-    weight_grad = part(0).astype(F32)
-    for k in range(1, 4):
-        weight_grad = weight_grad + shift(part(k), k, "z").astype(F32)
-    weight_grad = jnp.transpose(weight_grad.reshape(3, heads, rows, hd), (2, 0, 1, 3))
+        pairs = [(a, (a + 16 * k) % seq) for a in range(seq)]
+        weight_total = weight_total + lax.ppermute(weight[k], "seq", pairs).astype(F32)
 
     total = stem[0]
     count = lax.axis_size("head")
     for k in range(1, count):
         pairs = [(a, (a + k) % count) for a in range(count)]
         total = total + lax.ppermute(stem[k], "head", pairs).astype(F32)
-    for mask in (16, 32, 4, 8):
-        held = lax.reduce_precision(total, 8, 7)
-        total = held + xor(held.astype(BF16), mask).astype(F32)
+
+    def pair_sum(value, mask):
+        held = lax.reduce_precision(value, 8, 7)
+        return held + xor(held.astype(BF16), mask).astype(F32)
+
+    def half_sum(value, mask):
+        side = s // mask % 2
+        half = value.shape[0] // 2
+        kept = lax.dynamic_slice_in_dim(value, side * half, half, 0)
+        sent = lax.dynamic_slice_in_dim(value, (1 - side) * half, half, 0)
+        return kept + xor(sent.astype(BF16), mask).astype(F32)
+
+    total, weight_total = lax.optimization_barrier((total, weight_total))
+    weight_grad = half_sum(half_sum(weight_total, 8), 4)[0]
+    weight_grad = jnp.transpose(weight_grad.reshape(3, heads, rows, hd), (2, 0, 1, 3))
+    for mask in (4, 8, 16, 32):
+        total = pair_sum(total, mask)
     full = total.astype(BF16)[None]
     for mask in (1, 2):
         other = xor(full, mask)

time: 150 us -> 142 us (0.947)
  local copies, waits for them, and re-layouts: 12.5 us -> 8.42 us
  starting transfers between devices: 43.3 us -> 46.3 us
  waiting for transfers between devices: 31.7 us -> 29 us
  other arithmetic: 6.07 us -> 3.69 us
  Pallas kernels: 54.5 us -> 52.7 us
    ppermute x6 -> x3, waiting for transfers between devices: 18.6 us -> 1.33 us  [per_device(): lax.ppermute(weight[k], 'seq', pairs).astype(F32)]
    ppermute x10 -> x12, waiting for transfers between devices: 7.51 us -> 23 us  [xor(): return lax.ppermute(value, 'seq', [(a, a ^ mask) for a in range(seq)])]
    unnamed x29 -> x25, local copies, waits for them, and re-layouts: 7.82 us -> 3.75 us
    pallas_call x1, Pallas kernels: 22.3 us -> 20.4 us  [attention(): pl.pallas_call(attention_kernel, grid_spec=pltpu.PrefetchScalarGridSpec(n...]
    convert_element_type x5 -> x4, other arithmetic: 1.94 us -> 0.15 us  [pair_sum(): return held + xor(held.astype(BF16), mask).astype(F32)]
    ppermute x3, starting transfers between devices: 3.73 us -> 5.45 us  [per_device(): total = total + lax.ppermute(stem[k], 'head', pairs).astype(F32)]
    ppermute x10 -> x12, starting transfers between devices: 22.6 us -> 23.2 us  [xor(): return lax.ppermute(value, 'seq', [(a, a ^ mask) for a in range(seq)])]
    ppermute x6 -> x3, starting transfers between devices: 8.2 us -> 8.78 us  [per_device(): lax.ppermute(weight[k], 'seq', pairs).astype(F32)]
  transfers between devices with their start and end apart: 22 -> 21, of which waited for: 11 -> 12; matrix products, arithmetic and copies ran while one was open for 5% -> 4% of each run, Pallas kernels for 16% -> 21%
where the time goes in v2:
time: 142 us; the launch traced here: 141 us
  Pallas kernels  52.7 us (37%)
  starting transfers between devices  46.3 us (33%)
  waiting for transfers between devices  29 us (20%)
  local copies, waits for them, and re-layouts  8.42 us (6%)
  other arithmetic  3.69 us (3%)
    ppermute x12, starting transfers between devices, xor(): return lax.ppermute(value, 'seq', [(a, a ^ mask) for a in range(seq)])  23.2 us
    ppermute x12, waiting for transfers between devices, xor(): return lax.ppermute(value, 'seq', [(a, a ^ mask) for a in range(seq)])  23 us
    pallas_call x1, Pallas kernels, forward(): pl.pallas_call(forward_kernel, grid_spec=pltpu.PrefetchScalarGridSpec(num...  21.4 us
    pallas_call x1, Pallas kernels, attention(): pl.pallas_call(attention_kernel, grid_spec=pltpu.PrefetchScalarGridSpec(n...  20.4 us
    ppermute x3, starting transfers between devices, per_device(): lax.ppermute(weight[k], 'seq', pairs).astype(F32)  8.78 us
    pallas_call x1, Pallas kernels, stem_part(): pl.pallas_call(stem_kernel, grid_spec=pltpu.PrefetchScalarGridSpec(num_sc...  7.65 us
    ppermute x1, starting transfers between devices, per_device(): behind = lax.ppermute(frame, 'seq', [(a, a + 2) for a in range(seq - 2)])  6.23 us
    ppermute x3, starting transfers between devices, per_device(): total = total + lax.ppermute(stem[k], 'head', pairs).astype(F32)  5.45 us
  transfers between devices with their start and end apart: 21, of which 12 were waited for; matrix products, arithmetic and copies ran while one was open for 4% of the time, Pallas kernels for 21%

profile of v2, /device:TPU:1, one launch (start us, length us, event | category | flops | bytes accessed | tf_op | source)
XLA Modules:
  0.0 141.1 jit_solution(12327611011449865524)
XLA Ops:
  0.6 0.9 copy.28
  1.6 1.0 copy.29
  2.5 0.7 reshape.55
  3.2 3.3 %collective-permute-start = (bf16[64,256]{1,0:T(8,128)(2,1)S(1)}, bf16[64,256]{1,0:T(8,128)(2,1)S(1)}, u32[]{:S(2)}, u32[]{:S(2)}) collective-permute-start(bf16[64,256]{1,0:T(8,128)(2,1)S(1)} %reshape.55), channel_id=1, source_target_pairs={{0,4},{4,0},{8,12},{12,8},{16,20},{20,16},{24,28},{28,24},{32,36},... | collective-permute-start | bytes 98312 | tf_op jit(solution)/shard_map/ppermute | solution.py:434
  6.5 1.0 copy.34
  7.5 0.1 collective-permute-start.6
  7.6 1.4 collective-permute-start.5
  9.0 0.8 copy.35.lists
  9.8 1.3 collective-permute-start.3
  11.1 1.3 collective-permute-start.2
  12.4 6.2 %collective-permute-start.1 = (bf16[64,512]{1,0:T(8,128)(2,1)S(1)}, bf16[64,512]{1,0:T(8,128)(2,1)S(1)}, u32[]{:S(2)}, u32[]{:S(2)}) collective-permute-start(bf16[64,512]{1,0:T(8,128)(2,1)S(1)} %pad_maximum_fusion.6), channel_id=1, source_target_pairs={{0,8},{4,12},{8,16},{12,20},{16,24},{20,28},{24,32},{28,36},{32,40... | collective-permute-start | bytes 196616 | tf_op jit(solution)/shard_map/ppermute | solution.py:441
  18.6 0.6 pad_add_fusion.ids
  19.2 1.6 %collective-permute-done.3 = bf16[64,512]{1,0:T(8,128)(2,1)S(1)} collective-permute-done((bf16[64,512]{1,0:T(8,128)(2,1)S(1)}, bf16[64,512]{1,0:T(8,128)(2,1)S(1)}, u32[]{:S(2)}, u32[]{:S(2)}) %collective-permute-start.3) | collective-permute-done | bytes 65568 | tf_op jit(solution)/shard_map/ppermute | solution.py:442
  20.8 1.0 collective-permute-start.4
  21.9 0.9 pad_maximum_fusion.4
  22.8 0.1 copy.30
  22.9 0.1 copy.31
  23.1 0.1 pad_maximum_fusion.1
  23.2 1.0 copy.33.pext
  24.2 21.4 %forward.1 = (f32[1024,1152]{1,0:T(8,128)}, bf16[768,1024]{1,0:T(8,128)(2,1)}, f32[768,1024]{1,0:T(8,128)}, f32[8,1024]{1,0:T(8,128)}, f32[8,1152]{1,0:T(8,128)}, /*index=5*/f32[768,128]{1,0:T(8,128)}) custom-call(s32[3]{0:T(128)} %pad_add_fusion.ids, bf16[256,1024]{1,0:T(8,128)(2,1)} %copy.33.pext, bf16[192,3072]{1,0:T(8,128)(2,1)} %stem.1, ...), custom_call_target="tpu_custom_call" | custom-call | flops 8858370048 | bytes 25165824 | tf_op jit(solution)/shard_map/forward/pallas_call | solution.py:137
  45.6 0.1 pad_maximum_fusion.og
  45.7 0.0 slice-start
  45.7 0.0 copy-start.3
  45.7 0.9 copy-done.3
  46.7 20.4 %attention.1 = (bf16[3,1024,384]{2,1,0:T(8,128)(2,1)S(1)}, f32[2,8,1024]{2,1,0:T(8,128)S(1)}) custom-call(s32[3]{0:T(128)S(1)} %copy-done.5, s32[128,4]{1,0:T(8,128)S(1)} %copy.35.lists, f32[1024,1152]{1,0:T(8,128)} %get-tuple-element.38.pq.pk.pv, f32[1024,1152]{1,0:T(8,128)} %get-tuple-element.38.pq.pk.pv, f32[1024,1152]{1,0:T(8,128)} %get-tuple-element.38.pq.pk.pv, ...), custom_call_target="tpu_custom_call" | custom-call | flops 2013265920 | bytes 10485760 | tf_op jit(solution)/shard_map/attention/pallas_call | solution.py:276
  67.2 3.2 %weight_part.1 = (bf16[4,9,48,128]{3,2,1,0:T(8,128)(2,1)S(1)}, bf16[4,9,48,128]{3,2,1,0:T(8,128)(2,1)S(1)}, bf16[4,9,48,128]{3,2,1,0:T(8,128)(2,1)S(1)}, bf16[4,9,48,128]{3,2,1,0:T(8,128)(2,1)S(1)}) custom-call(s32[3]{0:T(128)S(1)} %copy-done.5, bf16[768,1024]{1,0:T(8,128)(2,1)S(1)} %copy-done.8, bf16[3,1024,384]{2,1,0:T(8,128)(2,1)S(1)} %get-tuple-element.46.mixed), custom_call_target="tpu_custom_call" | custom-call | flops 1811939328 | bytes 6291456 | tf_op jit(solution)/shard_map/weight_part/pallas_call | solution.py:333
  70.4 5.1 %collective-permute-start.10 = (bf16[4,9,48,128]{3,2,1,0:T(8,128)(2,1)S(1)}, bf16[4,9,48,128]{3,2,1,0:T(8,128)(2,1)S(1)}, u32[]{:S(2)}, u32[]{:S(2)}) collective-permute-start(bf16[4,9,48,128]{3,2,1,0:T(8,128)(2,1)S(1)} %get-tuple-element.56), channel_id=1, source_target_pairs={{0,64},{4,68},{8,72},{12,76},{16,80},{20,84},{24,88},{28,92},{32,9... | collective-permute-start | bytes 1327112 | tf_op jit(solution)/shard_map/ppermute | solution.py:479
  75.5 2.7 %collective-permute-start.11 = (bf16[4,9,48,128]{3,2,1,0:T(8,128)(2,1)S(1)}, bf16[4,9,48,128]{3,2,1,0:T(8,128)(2,1)S(1)}, u32[]{:S(2)}, u32[]{:S(2)}) collective-permute-start(bf16[4,9,48,128]{3,2,1,0:T(8,128)(2,1)S(1)} %get-tuple-element.57), channel_id=1, source_target_pairs={{0,128},{4,132},{8,136},{12,140},{16,144},{20,148},{24,152},{28,15... | collective-permute-start | bytes 1327112 | tf_op jit(solution)/shard_map/ppermute | solution.py:479
  78.2 0.9 collective-permute-start.12
  79.2 7.7 %stem_part.1 = (f32[192,256]{1,0:T(8,128)S(1)}, bf16[192,256]{1,0:T(8,128)(2,1)S(1)}, bf16[192,256]{1,0:T(8,128)(2,1)S(1)}, bf16[192,256]{1,0:T(8,128)(2,1)S(1)}) custom-call(s32[3]{0:T(128)S(1)} %copy-done.5, bf16[9,16,4,48,128]{4,3,2,1,0:T(8,128)(2,1)S(1)} %bitcast.48, bf16[3,1024,384]{2,1,0:T(8,128)(2,1)S(1)} %get-tuple-element.46.mixed, ...), custom_call_target="tpu_custom_call" | custom-call | flops 1000 | bytes 1000 | tf_op jit(solution)/shard_map/stem_part/pallas_call | solution.py:381
  86.8 1.4 collective-permute-start.7
  88.2 2.6 %collective-permute-start.8 = (bf16[192,256]{1,0:T(8,128)(2,1)S(1)}, bf16[192,256]{1,0:T(8,128)(2,1)S(1)}, u32[]{:S(2)}, u32[]{:S(2)}) collective-permute-start(bf16[192,256]{1,0:T(8,128)(2,1)S(1)} %get-tuple-element.53), channel_id=1, source_target_pairs={{0,2},{1,3},{2,0},{3,1},{4,6},{5,7},{6,4},{7,5},{8,10},{9,11},{10,... | collective-permute-start | bytes 294920 | tf_op jit(solution)/shard_map/ppermute | solution.py:485
  90.8 0.8 collective-permute-done.7
  91.7 1.5 %collective-permute-start.9 = (bf16[192,256]{1,0:T(8,128)(2,1)S(1)}, bf16[192,256]{1,0:T(8,128)(2,1)S(1)}, u32[]{:S(2)}, u32[]{:S(2)}) collective-permute-start(bf16[192,256]{1,0:T(8,128)(2,1)S(1)} %get-tuple-element.54), channel_id=1, source_target_pairs={{0,3},{1,0},{2,1},{3,2},{4,7},{5,4},{6,5},{7,6},{8,11},{9,8},{10,9... | collective-permute-start | bytes 294920 | tf_op jit(solution)/shard_map/ppermute | solution.py:485
  93.1 1.1 collective-permute-done.8
  94.2 1.2 collective-permute-done.9
  95.4 0.1 convert_add_fusion.3
  95.5 1.3 collective-permute-done.12
  96.8 0.2 convert_add_fusion
  97.1 0.1 collective-permute-start.15
  97.2 4.4 %collective-permute-done.15 = bf16[192,256]{1,0:T(8,128)(2,1)S(1)} collective-permute-done((bf16[192,256]{1,0:T(8,128)(2,1)S(1)}, bf16[192,256]{1,0:T(8,128)(2,1)S(1)}, u32[]{:S(2)}, u32[]{:S(2)}) %collective-permute-start.15) | collective-permute-done | bytes 98336 | tf_op jit(solution)/shard_map/ppermute | solution.py:434
  101.6 2.3 %collective-permute-start.16 = (bf16[192,256]{1,0:T(8,128)(2,1)S(1)}, bf16[192,256]{1,0:T(8,128)(2,1)S(1)}, u32[]{:S(2)}, u32[]{:S(2)}) collective-permute-start(bf16[192,256]{1,0:T(8,128)(2,1)S(1)} %fusion.3), channel_id=1, source_target_pairs={{0,32},{4,36},{8,40},{12,44},{16,48},{20,52},{24,56},{28,60},{32,0... | collective-permute-start | bytes 294920 | tf_op jit(solution)/shard_map/ppermute | solution.py:434
  103.8 5.6 %collective-permute-done.16 = bf16[192,256]{1,0:T(8,128)(2,1)S(1)} collective-permute-done((bf16[192,256]{1,0:T(8,128)(2,1)S(1)}, bf16[192,256]{1,0:T(8,128)(2,1)S(1)}, u32[]{:S(2)}, u32[]{:S(2)}) %collective-permute-start.16) | collective-permute-done | bytes 98336 | tf_op jit(solution)/shard_map/ppermute | solution.py:434
  109.5 2.6 %collective-permute-start.17 = (bf16[192,256]{1,0:T(8,128)(2,1)S(1)}, bf16[192,256]{1,0:T(8,128)(2,1)S(1)}, u32[]{:S(2)}, u32[]{:S(2)}) collective-permute-start(bf16[192,256]{1,0:T(8,128)(2,1)S(1)} %fusion), channel_id=1, source_target_pairs={{0,64},{4,68},{8,72},{12,76},{16,80},{20,84},{24,88},{28,92},{32,9... | collective-permute-start | bytes 294920 | tf_op jit(solution)/shard_map/ppermute | solution.py:434
  112.2 1.0 collective-permute-start.13
  113.2 1.2 collective-permute-done.17
  114.4 0.1 fusion.2
  114.5 6.2 %collective-permute-start.18 = (bf16[192,256]{1,0:T(8,128)(2,1)S(1)}, bf16[192,256]{1,0:T(8,128)(2,1)S(1)}, u32[]{:S(2)}, u32[]{:S(2)}) collective-permute-start(bf16[192,256]{1,0:T(8,128)(2,1)S(1)} %fusion.2), channel_id=1, source_target_pairs={{0,128},{4,132},{8,136},{12,140},{16,144},{20,148},{24,152},{28,15... | collective-permute-start | bytes 294920 | tf_op jit(solution)/shard_map/ppermute | solution.py:434
  120.7 2.5 %collective-permute-done.13 = bf16[2,9,48,128]{3,2,1,0:T(8,128)(2,1)S(1)} collective-permute-done((bf16[2,9,48,128]{3,2,1,0:T(8,128)(2,1)S(1)}, bf16[2,9,48,128]{3,2,1,0:T(8,128)(2,1)S(1)}, u32[]{:S(2)}, u32[]{:S(2)}) %collective-permute-start.13) | collective-permute-done | bytes 221216 | tf_op jit(solution)/shard_map/ppermute | solution.py:434
  123.3 0.1 fusion.1
  123.4 5.0 %collective-permute-start.19 = (bf16[1,192,256]{2,1,0:T(8,128)(2,1)S(1)}, bf16[1,192,256]{2,1,0:T(8,128)(2,1)S(1)}, u32[]{:S(2)}, u32[]{:S(2)}) collective-permute-start(bf16[1,192,256]{2,1,0:T(8,128)(2,1)S(1)} %fusion.1), channel_id=1, source_target_pairs={{0,4},{4,0},{8,12},{12,8},{16,20},{20,16},{24,28},{28,24},{32,36},... | collective-permute-start | bytes 294920 | tf_op jit(solution)/shard_map/ppermute | solution.py:434
  128.3 0.1 collective-permute-start.14
  128.5 0.8 collective-permute-done.19
  129.3 0.1 collective-permute-start.20
  129.4 4.8 %collective-permute-done.14 = bf16[1,9,48,128]{3,2,1,0:T(8,128)(2,1)S(1)} collective-permute-done((bf16[1,9,48,128]{3,2,1,0:T(8,128)(2,1)S(1)}, bf16[1,9,48,128]{3,2,1,0:T(8,128)(2,1)S(1)}, u32[]{:S(2)}, u32[]{:S(2)}) %collective-permute-start.14) | collective-permute-done | bytes 110624 | tf_op jit(solution)/shard_map/ppermute | solution.py:434
  134.2 0.7 convert_add_fusion.2
  134.9 3.7 %collective-permute-done.20 = bf16[2,192,256]{2,1,0:T(8,128)(2,1)S(1)} collective-permute-done((bf16[2,192,256]{2,1,0:T(8,128)(2,1)S(1)}, bf16[2,192,256]{2,1,0:T(8,128)(2,1)S(1)}, u32[]{:S(2)}, u32[]{:S(2)}) %collective-permute-start.20) | collective-permute-done | bytes 196640 | tf_op jit(solution)/shard_map/ppermute | solution.py:434
  138.7 0.1 copy.37
  138.8 0.2 slice.32
  138.9 0.2 slice.31
  139.1 0.2 copy.39
  139.3 0.2 copy.38
  139.4 1.1 copy.40
  140.5 0.6 pad_maximum_fusion.7
  (43 shorter events, 0.5 us)
Async XLA Ops:
  3.2 6.5 %collective-permute-start = (bf16[64,256]{1,0:T(8,128)(2,1)S(1)}, bf16[64,256]{1,0:T(8,128)(2,1)S(1)}, u32[]{:S(2)}, u32[]{:S(2)}) collective-permute-start(bf16[64,256]{1,0:T(8,128)(2,1)S(1)} %reshape.55), channel_id=1, source_target_pairs={{0,4},{4,0},{8,12},{12,8},{16,20},{20,16},{24,28},{28,24},{32,36},... | collective-permute-start | bytes 98312 | tf_op jit(solution)/shard_map/ppermute | solution.py:434
  7.5 38.0 %collective-permute-start.6 = (bf16[3,4,64,128]{3,2,1,0:T(8,128)(2,1)S(1)}, bf16[3,4,64,128]{3,2,1,0:T(8,128)(2,1)S(1)}, u32[]{:S(2)}, u32[]{:S(2)}) collective-permute-start(bf16[3,4,64,128]{3,2,1,0:T(8,128)(2,1)S(1)} %bitcast.59), channel_id=1, source_target_pairs={{0,12},{4,8},{8,4},{12,0},{16,28},{20,24},{24,20},{28,16},{32,44},... | collective-permute-start | bytes 589832 | tf_op jit(solution)/shard_map/ppermute | solution.py:434
  7.6 38.0 %collective-permute-start.5 = (bf16[3,4,64,128]{3,2,1,0:T(8,128)(2,1)S(1)}, bf16[3,4,64,128]{3,2,1,0:T(8,128)(2,1)S(1)}, u32[]{:S(2)}, u32[]{:S(2)}) collective-permute-start(bf16[3,4,64,128]{3,2,1,0:T(8,128)(2,1)S(1)} %bitcast.60), channel_id=1, source_target_pairs={{0,8},{4,12},{8,0},{12,4},{16,24},{20,28},{24,16},{28,20},{32,40},... | collective-permute-start | bytes 589832 | tf_op jit(solution)/shard_map/ppermute | solution.py:434
  9.8 11.0 %collective-permute-start.3 = (bf16[64,512]{1,0:T(8,128)(2,1)S(1)}, bf16[64,512]{1,0:T(8,128)(2,1)S(1)}, u32[]{:S(2)}, u32[]{:S(2)}) collective-permute-start(bf16[64,512]{1,0:T(8,128)(2,1)S(1)} %pad_maximum_fusion.6), channel_id=1, source_target_pairs={{8,0},{12,4},{16,8},{20,12},{24,16},{28,20},{32,24},{36,28},{40,32... | collective-permute-start | bytes 196616 | tf_op jit(solution)/shard_map/ppermute | solution.py:442
  11.1 10.7 %collective-permute-start.2 = (bf16[64,512]{1,0:T(8,128)(2,1)S(1)}, bf16[64,512]{1,0:T(8,128)(2,1)S(1)}, u32[]{:S(2)}, u32[]{:S(2)}) collective-permute-start(bf16[64,512]{1,0:T(8,128)(2,1)S(1)} %pad_maximum_fusion.6), channel_id=1, source_target_pairs={{8,24},{12,28},{16,0},{20,4},{24,40},{28,44},{32,16},{36,20},{40,5... | collective-permute-start | bytes 196616 | tf_op jit(solution)/shard_map/ppermute | solution.py:444
  12.4 9.4 %collective-permute-start.1 = (bf16[64,512]{1,0:T(8,128)(2,1)S(1)}, bf16[64,512]{1,0:T(8,128)(2,1)S(1)}, u32[]{:S(2)}, u32[]{:S(2)}) collective-permute-start(bf16[64,512]{1,0:T(8,128)(2,1)S(1)} %pad_maximum_fusion.6), channel_id=1, source_target_pairs={{0,8},{4,12},{8,16},{12,20},{16,24},{20,28},{24,32},{28,36},{32,40... | collective-permute-start | bytes 196616 | tf_op jit(solution)/shard_map/ppermute | solution.py:441
  20.8 24.8 %collective-permute-start.4 = (bf16[3,4,64,128]{3,2,1,0:T(8,128)(2,1)S(1)}, bf16[3,4,64,128]{3,2,1,0:T(8,128)(2,1)S(1)}, u32[]{:S(2)}, u32[]{:S(2)}) collective-permute-start(bf16[3,4,64,128]{3,2,1,0:T(8,128)(2,1)S(1)} %bitcast.61), channel_id=1, source_target_pairs={{0,4},{4,0},{8,12},{12,8},{16,20},{20,16},{24,28},{28,24},{32,36},... | collective-permute-start | bytes 589832 | tf_op jit(solution)/shard_map/ppermute | solution.py:434
  24.2 21.5 %copy-start.5 = (s32[3]{0:T(128)S(1)}, s32[3]{0:T(128)}, u32[]{:S(2)}) copy-start(s32[3]{0:T(128)} %pad_add_fusion.ids) | copy-start | bytes 40
  24.2 21.5 %copy-start.6 = (f32[128]{0:T(128)S(1)}, f32[128]{0:T(128)}, u32[]{:S(2)}) copy-start(f32[128]{0:T(128)} %param.18) | copy-start | bytes 1540
  24.2 21.6 %copy-start.7 = (f32[128]{0:T(128)S(1)}, f32[128]{0:T(128)}, u32[]{:S(2)}) copy-start(f32[128]{0:T(128)} %param.19) | copy-start | bytes 1540
  45.7 33.5 %slice-start = ((s8[7077888]{0:T(1024)(128)(4,1)}), s8[4194304]{0:T(1024)(128)(4,1)S(1)}, s32[]{:S(2)}) async-start(s8[7077888]{0:T(1024)(128)(4,1)} %bitcast.46), calls=%async_computation | async-start | bytes 8388608
  45.7 0.9 copy-start.3
  46.7 20.5 %copy-start.8 = (bf16[768,1024]{1,0:T(8,128)(2,1)S(1)}, bf16[768,1024]{1,0:T(8,128)(2,1)}, u32[]{:S(2)}) copy-start(bf16[768,1024]{1,0:T(8,128)(2,1)} %get-tuple-element.41.hid) | copy-start | bytes 4718596
  46.7 32.5 %slice-start.1 = ((s8[7077888]{0:T(1024)(128)(4,1)}), s8[2883584]{0:T(1024)(128)(4,1)S(1)}, s32[]{:S(2)}) async-start(s8[7077888]{0:T(1024)(128)(4,1)} %bitcast.46), calls=%async_computation.1 | async-start | bytes 5767168
  67.1 12.0 %copy-start = (f32[768,1024]{1,0:T(8,128)S(1)}, f32[768,1024]{1,0:T(8,128)}, u32[]{:S(2)}) copy-start(f32[768,1024]{1,0:T(8,128)} %get-tuple-element.47.nrm) | copy-start | bytes 9437188
  67.1 12.0 %copy-start.1 = (bf16[256,1024]{1,0:T(8,128)(2,1)S(1)}, bf16[256,1024]{1,0:T(8,128)(2,1)}, u32[]{:S(2)}) copy-start(bf16[256,1024]{1,0:T(8,128)(2,1)} %copy.33.pext) | copy-start | bytes 1572868
  67.1 12.0 %copy-start.2 = (f32[768,128]{1,0:T(8,128)S(1)}, f32[768,128]{1,0:T(8,128)}, u32[]{:S(2)}) copy-start(f32[768,128]{1,0:T(8,128)} %get-tuple-element.48.sc) | copy-start | bytes 1179652
  67.2 12.0 %copy-start.4 = (f32[8,1024]{1,0:T(8,128)S(1)}, f32[8,1024]{1,0:T(8,128)}, u32[]{:S(2)}) copy-start(f32[8,1024]{1,0:T(8,128)} %get-tuple-element.50.inv) | copy-start | bytes 98308
  70.4 25.1 %collective-permute-start.10 = (bf16[4,9,48,128]{3,2,1,0:T(8,128)(2,1)S(1)}, bf16[4,9,48,128]{3,2,1,0:T(8,128)(2,1)S(1)}, u32[]{:S(2)}, u32[]{:S(2)}) collective-permute-start(bf16[4,9,48,128]{3,2,1,0:T(8,128)(2,1)S(1)} %get-tuple-element.56), channel_id=1, source_target_pairs={{0,64},{4,68},{8,72},{12,76},{16,80},{20,84},{24,88},{28,92},{32,9... | collective-permute-start | bytes 1327112 | tf_op jit(solution)/shard_map/ppermute | solution.py:479
  75.5 20.0 %collective-permute-start.11 = (bf16[4,9,48,128]{3,2,1,0:T(8,128)(2,1)S(1)}, bf16[4,9,48,128]{3,2,1,0:T(8,128)(2,1)S(1)}, u32[]{:S(2)}, u32[]{:S(2)}) collective-permute-start(bf16[4,9,48,128]{3,2,1,0:T(8,128)(2,1)S(1)} %get-tuple-element.57), channel_id=1, source_target_pairs={{0,128},{4,132},{8,136},{12,140},{16,144},{20,148},{24,152},{28,15... | collective-permute-start | bytes 1327112 | tf_op jit(solution)/shard_map/ppermute | solution.py:479
  78.2 18.6 %collective-permute-start.12 = (bf16[4,9,48,128]{3,2,1,0:T(8,128)(2,1)S(1)}, bf16[4,9,48,128]{3,2,1,0:T(8,128)(2,1)S(1)}, u32[]{:S(2)}, u32[]{:S(2)}) collective-permute-start(bf16[4,9,48,128]{3,2,1,0:T(8,128)(2,1)S(1)} %get-tuple-element.58), channel_id=1, source_target_pairs={{0,192},{4,196},{8,200},{12,204},{16,208},{20,212},{24,216},{28,22... | collective-permute-start | bytes 1327112 | tf_op jit(solution)/shard_map/ppermute | solution.py:479
  86.8 4.8 %collective-permute-start.7 = (bf16[192,256]{1,0:T(8,128)(2,1)S(1)}, bf16[192,256]{1,0:T(8,128)(2,1)S(1)}, u32[]{:S(2)}, u32[]{:S(2)}) collective-permute-start(bf16[192,256]{1,0:T(8,128)(2,1)S(1)} %get-tuple-element.52), channel_id=1, source_target_pairs={{0,1},{1,2},{2,3},{3,0},{4,5},{5,6},{6,7},{7,4},{8,9},{9,10},{10,1... | collective-permute-start | bytes 294920 | tf_op jit(solution)/shard_map/ppermute | solution.py:485
  88.2 6.0 %collective-permute-start.8 = (bf16[192,256]{1,0:T(8,128)(2,1)S(1)}, bf16[192,256]{1,0:T(8,128)(2,1)S(1)}, u32[]{:S(2)}, u32[]{:S(2)}) collective-permute-start(bf16[192,256]{1,0:T(8,128)(2,1)S(1)} %get-tuple-element.53), channel_id=1, source_target_pairs={{0,2},{1,3},{2,0},{3,1},{4,6},{5,7},{6,4},{7,5},{8,10},{9,11},{10,... | collective-permute-start | bytes 294920 | tf_op jit(solution)/shard_map/ppermute | solution.py:485
  91.7 3.8 %collective-permute-start.9 = (bf16[192,256]{1,0:T(8,128)(2,1)S(1)}, bf16[192,256]{1,0:T(8,128)(2,1)S(1)}, u32[]{:S(2)}, u32[]{:S(2)}) collective-permute-start(bf16[192,256]{1,0:T(8,128)(2,1)S(1)} %get-tuple-element.54), channel_id=1, source_target_pairs={{0,3},{1,0},{2,1},{3,2},{4,7},{5,4},{6,5},{7,6},{8,11},{9,8},{10,9... | collective-permute-start | bytes 294920 | tf_op jit(solution)/shard_map/ppermute | solution.py:485
  97.1 4.5 %collective-permute-start.15 = (bf16[192,256]{1,0:T(8,128)(2,1)S(1)}, bf16[192,256]{1,0:T(8,128)(2,1)S(1)}, u32[]{:S(2)}, u32[]{:S(2)}) collective-permute-start(bf16[192,256]{1,0:T(8,128)(2,1)S(1)} %reduce-precision_convert_fusion), channel_id=1, source_target_pairs={{0,16},{4,20},{8,24},{12,28},{16,0},{20,4},{24,8},{28,12},{32,48},... | collective-permute-start | bytes 294920 | tf_op jit(solution)/shard_map/ppermute | solution.py:434
  101.6 7.9 %collective-permute-start.16 = (bf16[192,256]{1,0:T(8,128)(2,1)S(1)}, bf16[192,256]{1,0:T(8,128)(2,1)S(1)}, u32[]{:S(2)}, u32[]{:S(2)}) collective-permute-start(bf16[192,256]{1,0:T(8,128)(2,1)S(1)} %fusion.3), channel_id=1, source_target_pairs={{0,32},{4,36},{8,40},{12,44},{16,48},{20,52},{24,56},{28,60},{32,0... | collective-permute-start | bytes 294920 | tf_op jit(solution)/shard_map/ppermute | solution.py:434
  109.5 4.9 %collective-permute-start.17 = (bf16[192,256]{1,0:T(8,128)(2,1)S(1)}, bf16[192,256]{1,0:T(8,128)(2,1)S(1)}, u32[]{:S(2)}, u32[]{:S(2)}) collective-permute-start(bf16[192,256]{1,0:T(8,128)(2,1)S(1)} %fusion), channel_id=1, source_target_pairs={{0,64},{4,68},{8,72},{12,76},{16,80},{20,84},{24,88},{28,92},{32,9... | collective-permute-start | bytes 294920 | tf_op jit(solution)/shard_map/ppermute | solution.py:434
  112.2 11.1 %collective-permute-start.13 = (bf16[2,9,48,128]{3,2,1,0:T(8,128)(2,1)S(1)}, bf16[2,9,48,128]{3,2,1,0:T(8,128)(2,1)S(1)}, u32[]{:S(2)}, u32[]{:S(2)}) collective-permute-start(bf16[2,9,48,128]{3,2,1,0:T(8,128)(2,1)S(1)} %dynamic-slice_convert_fusion), channel_id=1, source_target_pairs={{0,32},{4,36},{8,40},{12,44},{16,48},{20,52},{24,56},{28,60},{32,0... | collective-permute-start | bytes 663560 | tf_op jit(solution)/shard_map/ppermute | solution.py:434
  114.5 8.8 %collective-permute-start.18 = (bf16[192,256]{1,0:T(8,128)(2,1)S(1)}, bf16[192,256]{1,0:T(8,128)(2,1)S(1)}, u32[]{:S(2)}, u32[]{:S(2)}) collective-permute-start(bf16[192,256]{1,0:T(8,128)(2,1)S(1)} %fusion.2), channel_id=1, source_target_pairs={{0,128},{4,132},{8,136},{12,140},{16,144},{20,148},{24,152},{28,15... | collective-permute-start | bytes 294920 | tf_op jit(solution)/shard_map/ppermute | solution.py:434
  123.4 5.9 %collective-permute-start.19 = (bf16[1,192,256]{2,1,0:T(8,128)(2,1)S(1)}, bf16[1,192,256]{2,1,0:T(8,128)(2,1)S(1)}, u32[]{:S(2)}, u32[]{:S(2)}) collective-permute-start(bf16[1,192,256]{2,1,0:T(8,128)(2,1)S(1)} %fusion.1), channel_id=1, source_target_pairs={{0,4},{4,0},{8,12},{12,8},{16,20},{20,16},{24,28},{28,24},{32,36},... | collective-permute-start | bytes 294920 | tf_op jit(solution)/shard_map/ppermute | solution.py:434
  128.3 5.8 %collective-permute-start.14 = (bf16[1,9,48,128]{3,2,1,0:T(8,128)(2,1)S(1)}, bf16[1,9,48,128]{3,2,1,0:T(8,128)(2,1)S(1)}, u32[]{:S(2)}, u32[]{:S(2)}) collective-permute-start(bf16[1,9,48,128]{3,2,1,0:T(8,128)(2,1)S(1)} %dynamic-slice_convert_fusion.1), channel_id=1, source_target_pairs={{0,16},{4,20},{8,24},{12,28},{16,0},{20,4},{24,8},{28,12},{32,48},... | collective-permute-start | bytes 331784 | tf_op jit(solution)/shard_map/ppermute | solution.py:434
  129.3 9.3 %collective-permute-start.20 = (bf16[2,192,256]{2,1,0:T(8,128)(2,1)S(1)}, bf16[2,192,256]{2,1,0:T(8,128)(2,1)S(1)}, u32[]{:S(2)}, u32[]{:S(2)}) collective-permute-start(bf16[2,192,256]{2,1,0:T(8,128)(2,1)S(1)} %pad_maximum_fusion.5), channel_id=1, source_target_pairs={{0,8},{4,12},{8,0},{12,4},{16,24},{20,28},{24,16},{28,20},{32,40},... | collective-permute-start | bytes 589832 | tf_op jit(solution)/shard_map/ppermute | solution.py:434

commit v3 on v2

--- a/solution.py
+++ b/solution.py
@@ -109,7 +109,7 @@
     for g in range(16):
         at = pl.ds(pl.multiple_of(4 * rows * g + rows * j, 16), rows)
         hid[g * rows : (g + 1) * rows, :] = hid_all[at, :]
-        nrm[g * rows : (g + 1) * rows, :] = emb[at, :]
+        nrm[g * rows : (g + 1) * rows, :] = emb[at, :].astype(BF16)
 
     @pl.when(first)
     def _():
@@ -168,7 +168,7 @@
         out_shape=[
             jax.ShapeDtypeStruct((tokens, columns), F32),
             jax.ShapeDtypeStruct((share, tokens), BF16),
-            jax.ShapeDtypeStruct((share, tokens), F32),
+            jax.ShapeDtypeStruct((share, tokens), BF16),
             jax.ShapeDtypeStruct((8, tokens), F32),
             jax.ShapeDtypeStruct((8, columns), F32),
             jax.ShapeDtypeStruct((share, 128), F32),
@@ -182,7 +182,31 @@
 
 
 def attention_kernel(
-    ids, lists, pq, pk, pv, og, qg, kg, wq, wk, wv, mixed, means, q_s, k_s, v_s, o_s, iq_s, ik_s, dq_s, dk_s, dv_s, a1_s, a2_s
+    ids,
+    lists,
+    pq,
+    pk,
+    pv,
+    og,
+    qg,
+    kg,
+    wq,
+    wk,
+    wv,
+    mixed,
+    means,
+    q_s,
+    k_s,
+    v_s,
+    o_s,
+    kt_s,
+    iq_s,
+    ik_s,
+    dq_s,
+    dk_s,
+    dv_s,
+    a1_s,
+    a2_s,
 ):
     tokens, hd = pq.shape
     score_scale = hd ** (-0.5)
@@ -190,80 +214,96 @@
     tile = TT * TS * TS
     count = tokens // tile
     frame_tile = TS * TS
-    for raw, gain, keep, store in ((pq, qg, iq_s, q_s), (pk, kg, ik_s, k_s)):
-        r = raw[...]
-        inv = lax.rsqrt(jnp.mean(r * r, -1, keepdims=True) + ln_eps)
-        keep[...] = inv
-        store[...] = (r * inv * gain[...]).astype(BF16)
-    v_s[...] = pv[...].astype(BF16)
-    dk_s[...] = jnp.zeros_like(dk_s)
-    dv_s[...] = jnp.zeros_like(dv_s)
-    for half in range(2):
-        for t in range(count // 2):
-            for frame in range(2):
-                at = ((half * (count // 2) + t) * 2 + frame) * frame_tile
-                o_s[at : at + frame_tile, :] = og[jnp.bitwise_xor(j, 2 * frame + half), 0, t]
+    first = pl.program_id(0) == 0
+    last = pl.program_id(0) == pl.num_programs(0) - 1
+
+    def rows(b):
+        return pl.ds(pl.multiple_of(b * tile, tile), tile)
+
+    def prepare(b, carry):
+        at = rows(b)
+        for raw, gain, keep, store in ((pq, qg, iq_s, q_s), (pk, kg, ik_s, k_s)):
+            r = raw[at, :]
+            inv = lax.rsqrt(jnp.mean(r * r, -1, keepdims=True) + ln_eps)
+            keep[at, :] = inv
+            value = r * inv * gain[...]
+            store[at, :] = value.astype(BF16)
+        kt_s[:, at] = jnp.transpose(value).astype(BF16)
+        v_s[at, :] = pv[at, :].astype(BF16)
+        half, t = b // (count // 2), b % (count // 2)
+        for frame in range(2):
+            to = pl.ds(pl.multiple_of(b * tile + frame * frame_tile, frame_tile), frame_tile)
+            o_s[to, :] = og[jnp.bitwise_xor(j, 2 * frame + half), 0, t]
+        dk_s[at, :] = jnp.zeros((tile, hd), F32)
+        dv_s[at, :] = jnp.zeros((tile, hd), F32)
+        return carry
+
+    lax.fori_loop(0, count, prepare, 0, unroll=8)
 
     def visit(b, carry):
-        mine = pl.ds(pl.multiple_of(b * tile, tile), tile)
+        mine = rows(b)
         q_b = q_s[mine, :]
         o_b = o_s[mine, :]
-        near = [
-            pl.ds(pl.multiple_of((lists[g * count + b, n] - g * count) * tile, tile), tile)
-            for n in range(KNB)
-        ]
+        near = [rows(lists[g * count + b, n] - g * count) for n in range(KNB)]
         keys = jnp.concatenate([k_s[at, :] for at in near], 0)
+        keys_t = jnp.concatenate([kt_s[:, at] for at in near], 1)
         vals = jnp.concatenate([v_s[at, :] for at in near], 0)
-        e = jnp.exp2(mm(q_b, keys, NT) * (score_scale * LOG2E))
-        prob = e * (1.0 / jnp.sum(e, -1, keepdims=True))
-        slope = mm(o_b, vals, NT)
-        centre = jnp.sum(prob * slope, -1, keepdims=True)
+        e = jnp.exp2(mm(keys, q_b, NT) * (score_scale * LOG2E))
+        prob = e * (1.0 / jnp.sum(e, 0, keepdims=True))
+        slope = mm(vals, o_b, NT)
+        centre = jnp.sum(prob * slope, 0, keepdims=True)
         shaped = (prob * (slope - centre)).astype(BF16)
         rounded = prob.astype(BF16)
-        dq_s[mine, :] = mm(shaped, keys) * score_scale
-        dk = mm(q_b, shaped, TN)
-        dv = mm(o_b, rounded, TN)
+        dq_s[:, mine] = mm(keys_t, shaped)
+        dk = mm(shaped, q_b)
+        dv = mm(rounded, o_b)
         for n, at in enumerate(near):
-            dk_s[:, at] += dk[:, n * tile : (n + 1) * tile]
-            dv_s[:, at] += dv[:, n * tile : (n + 1) * tile]
+            dk_s[at, :] += dk[n * tile : (n + 1) * tile, :]
+            dv_s[at, :] += dv[n * tile : (n + 1) * tile, :]
         return carry
 
     lax.fori_loop(0, count, visit, 0, unroll=8)
 
-    @pl.when(pl.program_id(0) == 0)
+    @pl.when(first)
     def _():
         a1_s[...] = jnp.zeros_like(a1_s)
         a2_s[...] = jnp.zeros_like(a2_s)
 
-    m1 = a1_s[...]
-    m2 = a2_s[...]
-    for i, (raw, gain, keep, grad, factor, vec) in enumerate(
-        (
-            (pq, qg, iq_s, dq_s[...], 1.0, wq),
-            (pk, kg, ik_s, jnp.transpose(dk_s[...]), score_scale, wk),
-            (pv, None, None, jnp.transpose(dv_s[...]), 1.0, wv),
-        )
-    ):
-        r = raw[...]
-        if gain is None:
+    def finish(b, carry):
+        at = rows(b)
+        m1 = a1_s[at, :]
+        m2 = a2_s[at, :]
+        for i, (raw, gain, keep, grad, vec) in enumerate(
+            (
+                (pq, qg, iq_s, jnp.transpose(dq_s[:, at]), wq),
+                (pk, kg, ik_s, dk_s[at, :], wk),
+                (pv, None, None, dv_s[at, :], wv),
+            )
+        ):
+            r = raw[at, :]
             out = grad
-        else:
-            inv = keep[...]
-            u = grad * (gain[...] * factor)
-            out = inv * (u - r * (inv * inv * jnp.mean(r * u, -1, keepdims=True)))
-        out = out.astype(BF16)
-        mixed[i] = out
-        out = out.astype(F32)
-        m1 = m1 + out * (vec[0:1, :] + vec[1:2, :])
-        m2 = m2 + out * (r - (vec[2:3, :] + vec[3:4, :]))
-    a1_s[...] = m1
-    a2_s[...] = m2
-
-    @pl.when(pl.program_id(0) == pl.num_programs(0) - 1)
+            if gain is not None:
+                inv = keep[at, :]
+                u = grad * (gain[...] * score_scale)
+                out = inv * (u - r * (inv * inv * jnp.mean(r * u, -1, keepdims=True)))
+            out = out.astype(BF16)
+            mixed[i, at, :] = out
+            out = out.astype(F32)
+            m1 = m1 + out * (vec[0:1, :] + vec[1:2, :])
+            m2 = m2 + out * (r - (vec[2:3, :] + vec[3:4, :]))
+        a1_s[at, :] = m1
+        a2_s[at, :] = m2
+        return carry
+
+    lax.fori_loop(0, count, finish, 0, unroll=8)
+
+    @pl.when(last)
     def _():
-        for n, total in enumerate((m1, m2)):
-            row = jnp.sum(jnp.transpose(total), axis=0, keepdims=True)
-            means[n] = jnp.broadcast_to(row, (8, tokens))
+        for n, total in enumerate((a1_s, a2_s)):
+            for b in range(count):
+                at = slice(b * tile, (b + 1) * tile)
+                row = jnp.sum(jnp.transpose(total[at, :]), axis=0, keepdims=True)
+                means[n, :, at] = jnp.broadcast_to(row, (8, tile))
 
 
 def attention(ids, lists, proj, og, q_gain, k_gain, wv):
@@ -294,10 +334,10 @@
                 pl.BlockSpec((2, 8, tokens), lambda h, *_: (0, 0, 0)),
             ],
             scratch_shapes=[pltpu.VMEM((tokens, hd), BF16)] * 4
+            + [pltpu.VMEM((hd, tokens), BF16)]
             + [pltpu.VMEM((tokens, 1), F32)] * 2
-            + [pltpu.VMEM((tokens, hd), F32)]
-            + [pltpu.VMEM((hd, tokens), F32)] * 2
-            + [pltpu.VMEM((tokens, hd), F32)] * 2,
+            + [pltpu.VMEM((hd, tokens), F32)]
+            + [pltpu.VMEM((tokens, hd), F32)] * 4,
         ),
         out_shape=[
             jax.ShapeDtypeStruct((3, tokens, heads * hd), BF16),
@@ -343,15 +383,20 @@
     )(ids, hid, mixed)
 
 
-def stem_kernel(ids, w9, mixed, nrm, sc, means, inv, pext, own, *others):
+def stem_kernel(ids, w9, mixed, nrm, sc, means, inv, pext, own, *rest):
+    others, (mixed_t,) = rest[:3], rest[3:]
     third = mixed.shape[2]
     block, tokens = nrm.shape
     count, _, _, _, hd = w9.shape
     w = jnp.concatenate([w9[n, :, 0].reshape(block, hd) for n in range(count)], 1)
-    fg = mm(w[:, 0:third], mixed[0], NT)
-    for i in range(1, 3):
-        fg = fg + mm(w[:, i * third : (i + 1) * third], mixed[i], NT)
-    n = nrm[...]
+
+    @pl.when(pl.program_id(0) == 0)
+    def _():
+        for i in range(3):
+            mixed_t[i * third : (i + 1) * third, :] = jnp.transpose(mixed[i])
+
+    fg = mm(w, mixed_t[...])
+    n = nrm[...].astype(F32)
     scale = 1.0 / (4 * 4 * block)
     m1 = means[0, 0:1, :] * scale
     m2 = means[1, 0:1, :] * scale
@@ -393,6 +438,7 @@
                 pl.BlockSpec(pext.shape, lambda i, ids: (0, 0), pipeline_mode=once),
             ],
             out_specs=[pl.BlockSpec(shape, lambda i, ids: (0, 0))] * 4,
+            scratch_shapes=[pltpu.VMEM((count * hd, tokens), BF16)],
         ),
         out_shape=[jax.ShapeDtypeStruct(shape, F32)] + [jax.ShapeDtypeStruct(shape, BF16)] * 3,
         compiler_params=pltpu.CompilerParams(vmem_limit_bytes=40 * 2**20),
@@ -433,34 +479,39 @@
     def xor(value, mask):
         return lax.ppermute(value, "seq", [(a, a ^ mask) for a in range(seq)])
 
+    is_low = s % 2 == 0
+    even = j < 2
     piece = latent.reshape(channels, tr, TS, 2, tc, TS, 2)
     piece = jnp.transpose(piece, (0, 3, 6, 1, 4, 2, 5)).reshape(4 * channels, tiles * cell)
-    other = xor(piece, 1)
-    is_low = s % 2 == 0
-    frame = jnp.concatenate([jnp.where(is_low, piece, other), jnp.where(is_low, other, piece)], 1)
-    behind = lax.ppermute(frame, "seq", [(a, a + 2) for a in range(seq - 2)])
-    ahead = lax.ppermute(frame, "seq", [(a, a - 2) for a in range(2, seq)])
-    far_pairs = [(a, a - 4 if a % 4 < 2 else a + 4) for a in range(seq)]
-    far = lax.ppermute(frame, "seq", [(a, b) for a, b in far_pairs if 0 <= b < seq])
-    even = j < 2
-    window = [
-        jnp.where(even, behind, far),
-        jnp.where(even, frame, behind),
-        jnp.where(even, ahead, frame),
-        jnp.where(even, far, ahead),
-    ]
+    border = [(a, a - 2 if a % 4 < 2 else a + 2) for a in range(seq)]
+    outer = lax.ppermute(piece, "seq", [(a, b) for a, b in border if 0 <= b < seq])
+    pair = jnp.stack([outer, piece])
+    facing = xor(pair, 2)
+    window = jnp.stack(
+        [
+            jnp.where(even, outer, facing[0]),
+            jnp.where(even, piece, facing[1]),
+            jnp.where(even, facing[1], piece),
+            jnp.where(even, facing[0], outer),
+        ]
+    )
+    grads = jnp.transpose(out_grad, (1, 0, 2)).reshape(heads, tr, TS, tc, TS, hd)
+    grads = jnp.transpose(grads, (0, 1, 3, 2, 4, 5)).reshape(heads, tiles, cell, hd)
+    grads = jnp.stack([grads, xor(grads, 1)])
+    other = xor(window, 1)
+    other, grads = lax.optimization_barrier((other, grads))
+    grads = jnp.concatenate([grads, xor(grads, 2)])
+    window = jnp.concatenate([jnp.where(is_low, window, other), jnp.where(is_low, other, window)], 2)
     fill = jnp.zeros((256 - 12 * channels, 2 * tiles * cell), BF16).at[:3].set(1)
     pext = jnp.stack(
         [
-            jnp.concatenate(window[k : k + 3] + [fill], 0).reshape(256, 2 * tiles, cell)
+            jnp.concatenate([window[k], window[k + 1], window[k + 2], fill], 0).reshape(
+                256, 2 * tiles, cell
+            )
             for k in range(2)
         ],
         2,
     ).reshape(256, 4 * tiles * cell)
-
-    grads = jnp.transpose(out_grad, (1, 0, 2)).reshape(heads, tr, TS, tc, TS, hd)
-    grads = jnp.transpose(grads, (0, 1, 3, 2, 4, 5)).reshape(heads, tiles, cell, hd)
-    grads = jnp.stack([grads] + [xor(grads, mask) for mask in (1, 2, 3)])
 
     w9 = jnp.transpose(qkv_weight, (1, 2, 0, 3)).reshape(3 * heads, width, hd)
     ids = jnp.stack([j, g, h]).astype(jnp.int32)

time: 142 us -> 137 us (0.965)
  waiting for transfers between devices: 29 us -> 25.3 us
  starting transfers between devices: 46.3 us -> 48.7 us
  Pallas kernels: 52.7 us -> 50.5 us
    ppermute x12, starting transfers between devices: 23.2 us -> 35.7 us  [xor(): return lax.ppermute(value, 'seq', [(a, a ^ mask) for a in range(seq)])]
    ppermute x3 -> x1, starting transfers between devices: 8.81 us -> 0.66 us  [per_device(): lax.ppermute(piece, 'seq', [(a, b) for a, b in border if 0 <= b < seq])]
    ppermute x12, waiting for transfers between devices: 23 us -> 18.3 us  [xor(): return lax.ppermute(value, 'seq', [(a, a ^ mask) for a in range(seq)])]
    ppermute x3, waiting for transfers between devices: 1.33 us -> 3.27 us  [per_device(): lax.ppermute(weight[k], 'seq', pairs).astype(F32)]
    ppermute x3 -> x1, waiting for transfers between devices: 1.59 us -> 0.01 us  [per_device(): lax.ppermute(piece, 'seq', [(a, b) for a, b in border if 0 <= b < seq])]
    ppermute x3, starting transfers between devices: 8.78 us -> 7.24 us  [per_device(): lax.ppermute(weight[k], 'seq', pairs).astype(F32)]
    unnamed x25 -> x31, local copies, waits for them, and re-layouts: 3.75 us -> 3.13 us
  transfers between devices with their start and end apart: 21 -> 19, of which waited for: 12 -> 11; matrix products, arithmetic and copies ran while one was open for 4% -> 3% of each run, Pallas kernels for 21% -> 20%
where the time goes in v3:
time: 137 us
  Pallas kernels  50.5 us (37%)
  starting transfers between devices  48.7 us (36%)
  waiting for transfers between devices  25.3 us (18%)
  local copies, waits for them, and re-layouts  8.48 us (6%)
  other arithmetic  3.1 us (2%)
    ppermute x12, starting transfers between devices, xor(): return lax.ppermute(value, 'seq', [(a, a ^ mask) for a in range(seq)])  35.7 us
    pallas_call x1, Pallas kernels, forward(): pl.pallas_call(forward_kernel, grid_spec=pltpu.PrefetchScalarGridSpec(num...  21.3 us
    pallas_call x1, Pallas kernels, attention(): pl.pallas_call(attention_kernel, grid_spec=pltpu.PrefetchScalarGridSpec(n...  19.7 us
    ppermute x12, waiting for transfers between devices, xor(): return lax.ppermute(value, 'seq', [(a, a ^ mask) for a in range(seq)])  18.3 us
    ppermute x3, starting transfers between devices, per_device(): lax.ppermute(weight[k], 'seq', pairs).astype(F32)  7.24 us
    pallas_call x1, Pallas kernels, stem_part(): pl.pallas_call(stem_kernel, grid_spec=pltpu.PrefetchScalarGridSpec(num_sc...  6.25 us
    ppermute x3, starting transfers between devices, per_device(): total = total + lax.ppermute(stem[k], 'head', pairs).astype(F32)  5.16 us
    ppermute x3, waiting for transfers between devices, per_device(): total = total + lax.ppermute(stem[k], 'head', pairs).astype(F32)  3.71 us
  transfers between devices with their start and end apart: 19, of which 11 were waited for; matrix products, arithmetic and copies ran while one was open for 3% of the time, Pallas kernels for 20%

profile of v3, /device:TPU:1, one launch (start us, length us, event | category | flops | bytes accessed | tf_op | source)
XLA Modules:
  0.0 137.1 jit_solution(5572315782745327693)
XLA Ops:
  0.7 1.0 copy.27
  1.6 1.0 copy.28
  2.6 0.0 copy-start.10
  2.6 0.7 reshape.71
  3.3 0.7 collective-permute-start
  4.0 0.7 stack_reshape.8
  4.6 6.0 %collective-permute-start.1 = (bf16[2,64,256]{2,1,0:T(8,128)(2,1)S(1)}, bf16[2,64,256]{2,1,0:T(8,128)(2,1)S(1)}, u32[]{:S(2)}, u32[]{:S(2)}) collective-permute-start(bf16[2,64,256]{2,1,0:T(8,128)(2,1)S(1)} %pad_maximum_fusion.6), channel_id=1, source_target_pairs={{0,8},{4,12},{8,0},{12,4},{16,24},{20,28},{24,16},{28,20},{32,40},... | collective-permute-start | bytes 196616 | tf_op jit(solution)/shard_map/ppermute | solution.py:480
  10.7 2.0 %collective-permute-start.3 = (bf16[3,4,64,128]{3,2,1,0:T(8,128)(2,1)S(1)}, bf16[3,4,64,128]{3,2,1,0:T(8,128)(2,1)S(1)}, u32[]{:S(2)}, u32[]{:S(2)}) collective-permute-start(bf16[3,4,64,128]{3,2,1,0:T(8,128)(2,1)S(1)} %bitcast.66), channel_id=1, source_target_pairs={{0,4},{4,0},{8,12},{12,8},{16,20},{20,16},{24,28},{28,24},{32,36},... | collective-permute-start | bytes 589832 | tf_op jit(solution)/shard_map/ppermute | solution.py:480
  12.8 2.2 %collective-permute-start.2 = (bf16[4,64,256]{2,1,0:T(8,128)(2,1)S(1)}, bf16[4,64,256]{2,1,0:T(8,128)(2,1)S(1)}, u32[]{:S(2)}, u32[]{:S(2)}) collective-permute-start(bf16[4,64,256]{2,1,0:T(8,128)(2,1)S(1)} %pad_maximum_fusion.4), channel_id=1, source_target_pairs={{0,4},{4,0},{8,12},{12,8},{16,20},{20,16},{24,28},{28,24},{32,36},... | collective-permute-start | bytes 393224 | tf_op jit(solution)/shard_map/ppermute | solution.py:480
  15.0 0.7 pad_add_fusion.ids
  15.7 0.1 copy.33.lists
  15.8 0.2 collective-permute-done.2
  16.0 0.1 concatenate.31
  16.2 0.1 concatenate.32
  16.3 0.1 concatenate.35
  16.5 0.1 concatenate.33
  16.6 2.0 %collective-permute-start.4 = (bf16[2,3,4,64,128]{4,3,2,1,0:T(8,128)(2,1)S(1)}, bf16[2,3,4,64,128]{4,3,2,1,0:T(8,128)(2,1)S(1)}, u32[]{:S(2)}, u32[]{:S(2)}) collective-permute-start(bf16[2,3,4,64,128]{4,3,2,1,0:T(8,128)(2,1)S(1)} %pad_maximum_fusion.1), channel_id=1, source_target_pairs={{0,8},{4,12},{8,0},{12,4},{16,24},{20,28},{24,16},{28,20},{32,40},... | collective-permute-start | bytes 1179656 | tf_op jit(solution)/shard_map/ppermute | solution.py:480
  18.6 0.2 maximum_maximum_fusion
  18.8 0.7 copy.31
  19.6 1.0 copy.32.pext
  20.6 21.3 %forward.1 = (f32[1024,1152]{1,0:T(8,128)}, bf16[768,1024]{1,0:T(8,128)(2,1)}, bf16[768,1024]{1,0:T(8,128)(2,1)}, f32[8,1024]{1,0:T(8,128)}, f32[8,1152]{1,0:T(8,128)}, /*index=5*/f32[768,128]{1,0:T(8,128)}) custom-call(s32[3]{0:T(128)} %pad_add_fusion.ids, bf16[256,1024]{1,0:T(8,128)(2,1)} %copy.32.pext, bf16[192,3072]{1,0:T(8,128)(2,1)} %stem.1, ...), custom_call_target="tpu_custom_call" | custom-call | flops 8858370048 | bytes 25165824 | tf_op jit(solution)/shard_map/forward/pallas_call | solution.py:137
  41.9 0.1 pad_maximum_fusion.og
  42.0 0.0 slice-start
  42.1 0.0 copy-start.3
  42.1 0.9 copy-done.3
  43.0 19.7 %attention.1 = (bf16[3,1024,384]{2,1,0:T(8,128)(2,1)S(1)}, f32[2,8,1024]{2,1,0:T(8,128)S(1)}) custom-call(s32[3]{0:T(128)S(1)} %copy-done.5, s32[128,4]{1,0:T(8,128)S(1)} %copy.33.lists, f32[1024,1152]{1,0:T(8,128)} %get-tuple-element.41.pq.pk.pv, f32[1024,1152]{1,0:T(8,128)} %get-tuple-element.41.pq.pk.pv, f32[1024,1152]{1,0:T(8,128)} %get-tuple-element.41.pq.pk.pv, ...), custom_call_target="tpu_custom_call" | custom-call | flops 2013265920 | bytes 10485760 | tf_op jit(solution)/shard_map/attention/pallas_call | solution.py:316
  62.7 0.0 copy-start
  62.7 3.2 %weight_part.1 = (bf16[4,9,48,128]{3,2,1,0:T(8,128)(2,1)S(1)}, bf16[4,9,48,128]{3,2,1,0:T(8,128)(2,1)S(1)}, bf16[4,9,48,128]{3,2,1,0:T(8,128)(2,1)S(1)}, bf16[4,9,48,128]{3,2,1,0:T(8,128)(2,1)S(1)}) custom-call(s32[3]{0:T(128)S(1)} %copy-done.5, bf16[768,1024]{1,0:T(8,128)(2,1)S(1)} %copy-done.8, bf16[3,1024,384]{2,1,0:T(8,128)(2,1)S(1)} %get-tuple-element.50.mixed), custom_call_target="tpu_custom_call" | custom-call | flops 1811939328 | bytes 6291456 | tf_op jit(solution)/shard_map/weight_part/pallas_call | solution.py:373
  65.9 3.6 %collective-permute-start.8 = (bf16[4,9,48,128]{3,2,1,0:T(8,128)(2,1)S(1)}, bf16[4,9,48,128]{3,2,1,0:T(8,128)(2,1)S(1)}, u32[]{:S(2)}, u32[]{:S(2)}) collective-permute-start(bf16[4,9,48,128]{3,2,1,0:T(8,128)(2,1)S(1)} %get-tuple-element.60), channel_id=1, source_target_pairs={{0,64},{4,68},{8,72},{12,76},{16,80},{20,84},{24,88},{28,92},{32,9... | collective-permute-start | bytes 1327112 | tf_op jit(solution)/shard_map/ppermute | solution.py:530
  69.5 2.8 %collective-permute-start.9 = (bf16[4,9,48,128]{3,2,1,0:T(8,128)(2,1)S(1)}, bf16[4,9,48,128]{3,2,1,0:T(8,128)(2,1)S(1)}, u32[]{:S(2)}, u32[]{:S(2)}) collective-permute-start(bf16[4,9,48,128]{3,2,1,0:T(8,128)(2,1)S(1)} %get-tuple-element.61), channel_id=1, source_target_pairs={{0,128},{4,132},{8,136},{12,140},{16,144},{20,148},{24,152},{28,15... | collective-permute-start | bytes 1327112 | tf_op jit(solution)/shard_map/ppermute | solution.py:530
  72.3 0.9 collective-permute-start.10
  73.2 6.3 %stem_part.1 = (f32[192,256]{1,0:T(8,128)S(1)}, bf16[192,256]{1,0:T(8,128)(2,1)S(1)}, bf16[192,256]{1,0:T(8,128)(2,1)S(1)}, bf16[192,256]{1,0:T(8,128)(2,1)S(1)}) custom-call(s32[3]{0:T(128)S(1)} %copy-done.5, bf16[9,16,4,48,128]{4,3,2,1,0:T(8,128)(2,1)S(1)} %bitcast.57, bf16[3,1024,384]{2,1,0:T(8,128)(2,1)S(1)} %get-tuple-element.50.mixed, ...), custom_call_target="tpu_custom_call" | custom-call | flops 1000 | bytes 1000 | tf_op jit(solution)/shard_map/stem_part/pallas_call | solution.py:426
  79.5 1.4 %collective-permute-start.5 = (bf16[192,256]{1,0:T(8,128)(2,1)S(1)}, bf16[192,256]{1,0:T(8,128)(2,1)S(1)}, u32[]{:S(2)}, u32[]{:S(2)}) collective-permute-start(bf16[192,256]{1,0:T(8,128)(2,1)S(1)} %get-tuple-element.56), channel_id=1, source_target_pairs={{0,1},{1,2},{2,3},{3,0},{4,5},{5,6},{6,7},{7,4},{8,9},{9,10},{10,1... | collective-permute-start | bytes 294920 | tf_op jit(solution)/shard_map/ppermute | solution.py:536
  80.9 2.6 %collective-permute-start.6 = (bf16[192,256]{1,0:T(8,128)(2,1)S(1)}, bf16[192,256]{1,0:T(8,128)(2,1)S(1)}, u32[]{:S(2)}, u32[]{:S(2)}) collective-permute-start(bf16[192,256]{1,0:T(8,128)(2,1)S(1)} %get-tuple-element.57), channel_id=1, source_target_pairs={{0,2},{1,3},{2,0},{3,1},{4,6},{5,7},{6,4},{7,5},{8,10},{9,11},{10,... | collective-permute-start | bytes 294920 | tf_op jit(solution)/shard_map/ppermute | solution.py:536
  83.5 1.1 collective-permute-done.5
  84.6 1.2 collective-permute-start.7
  85.8 1.4 %collective-permute-done.6 = bf16[192,256]{1,0:T(8,128)(2,1)S(1)} collective-permute-done((bf16[192,256]{1,0:T(8,128)(2,1)S(1)}, bf16[192,256]{1,0:T(8,128)(2,1)S(1)}, u32[]{:S(2)}, u32[]{:S(2)}) %collective-permute-start.6) | collective-permute-done | bytes 98336 | tf_op jit(solution)/shard_map/ppermute | solution.py:536
  87.2 1.2 collective-permute-done.7
  88.4 3.3 %collective-permute-done.9 = bf16[4,9,48,128]{3,2,1,0:T(8,128)(2,1)S(1)} collective-permute-done((bf16[4,9,48,128]{3,2,1,0:T(8,128)(2,1)S(1)}, bf16[4,9,48,128]{3,2,1,0:T(8,128)(2,1)S(1)}, u32[]{:S(2)}, u32[]{:S(2)}) %collective-permute-start.9) | collective-permute-done | bytes 442400 | tf_op jit(solution)/shard_map/ppermute | solution.py:530
  91.7 0.2 convert_add_fusion
  91.9 1.5 %collective-permute-start.13 = (bf16[192,256]{1,0:T(8,128)(2,1)S(1)}, bf16[192,256]{1,0:T(8,128)(2,1)S(1)}, u32[]{:S(2)}, u32[]{:S(2)}) collective-permute-start(bf16[192,256]{1,0:T(8,128)(2,1)S(1)} %reduce-precision_convert_fusion), channel_id=1, source_target_pairs={{0,16},{4,20},{8,24},{12,28},{16,0},{20,4},{24,8},{28,12},{32,48},... | collective-permute-start | bytes 294920 | tf_op jit(solution)/shard_map/ppermute | solution.py:480
  93.4 4.4 %collective-permute-done.13 = bf16[192,256]{1,0:T(8,128)(2,1)S(1)} collective-permute-done((bf16[192,256]{1,0:T(8,128)(2,1)S(1)}, bf16[192,256]{1,0:T(8,128)(2,1)S(1)}, u32[]{:S(2)}, u32[]{:S(2)}) %collective-permute-start.13) | collective-permute-done | bytes 98336 | tf_op jit(solution)/shard_map/ppermute | solution.py:480
  97.8 4.0 %collective-permute-start.14 = (bf16[192,256]{1,0:T(8,128)(2,1)S(1)}, bf16[192,256]{1,0:T(8,128)(2,1)S(1)}, u32[]{:S(2)}, u32[]{:S(2)}) collective-permute-start(bf16[192,256]{1,0:T(8,128)(2,1)S(1)} %fusion.6), channel_id=1, source_target_pairs={{0,32},{4,36},{8,40},{12,44},{16,48},{20,52},{24,56},{28,60},{32,0... | collective-permute-start | bytes 294920 | tf_op jit(solution)/shard_map/ppermute | solution.py:480
  101.9 3.4 %collective-permute-done.14 = bf16[192,256]{1,0:T(8,128)(2,1)S(1)} collective-permute-done((bf16[192,256]{1,0:T(8,128)(2,1)S(1)}, bf16[192,256]{1,0:T(8,128)(2,1)S(1)}, u32[]{:S(2)}, u32[]{:S(2)}) %collective-permute-start.14) | collective-permute-done | bytes 98336 | tf_op jit(solution)/shard_map/ppermute | solution.py:480
  105.3 0.3 collective-permute-start.15
  105.7 5.8 %collective-permute-start.11 = (bf16[2,9,48,128]{3,2,1,0:T(8,128)(2,1)S(1)}, bf16[2,9,48,128]{3,2,1,0:T(8,128)(2,1)S(1)}, u32[]{:S(2)}, u32[]{:S(2)}) collective-permute-start(bf16[2,9,48,128]{3,2,1,0:T(8,128)(2,1)S(1)} %dynamic-slice_convert_fusion), channel_id=1, source_target_pairs={{0,32},{4,36},{8,40},{12,44},{16,48},{20,52},{24,56},{28,60},{32,0... | collective-permute-start | bytes 663560 | tf_op jit(solution)/shard_map/ppermute | solution.py:480
  111.5 0.1 fusion.5
  111.6 5.1 %collective-permute-start.16 = (bf16[192,256]{1,0:T(8,128)(2,1)S(1)}, bf16[192,256]{1,0:T(8,128)(2,1)S(1)}, u32[]{:S(2)}, u32[]{:S(2)}) collective-permute-start(bf16[192,256]{1,0:T(8,128)(2,1)S(1)} %fusion.5), channel_id=1, source_target_pairs={{0,128},{4,132},{8,136},{12,140},{16,144},{20,148},{24,152},{28,15... | collective-permute-start | bytes 294920 | tf_op jit(solution)/shard_map/ppermute | solution.py:480
  116.7 2.3 %collective-permute-done.16 = bf16[192,256]{1,0:T(8,128)(2,1)S(1)} collective-permute-done((bf16[192,256]{1,0:T(8,128)(2,1)S(1)}, bf16[192,256]{1,0:T(8,128)(2,1)S(1)}, u32[]{:S(2)}, u32[]{:S(2)}) %collective-permute-start.16) | collective-permute-done | bytes 98336 | tf_op jit(solution)/shard_map/ppermute | solution.py:480
  119.0 0.1 fusion.1
  119.0 5.9 %collective-permute-start.17 = (bf16[1,192,256]{2,1,0:T(8,128)(2,1)S(1)}, bf16[1,192,256]{2,1,0:T(8,128)(2,1)S(1)}, u32[]{:S(2)}, u32[]{:S(2)}) collective-permute-start(bf16[1,192,256]{2,1,0:T(8,128)(2,1)S(1)} %fusion.1), channel_id=1, source_target_pairs={{0,4},{4,0},{8,12},{12,8},{16,20},{20,16},{24,28},{28,24},{32,36},... | collective-permute-start | bytes 294920 | tf_op jit(solution)/shard_map/ppermute | solution.py:480
  125.0 0.1 collective-permute-start.12
  125.1 0.8 collective-permute-done.17
  126.0 0.7 collective-permute-start.18
  126.6 5.6 %collective-permute-done.12 = bf16[1,9,48,128]{3,2,1,0:T(8,128)(2,1)S(1)} collective-permute-done((bf16[1,9,48,128]{3,2,1,0:T(8,128)(2,1)S(1)}, bf16[1,9,48,128]{3,2,1,0:T(8,128)(2,1)S(1)}, u32[]{:S(2)}, u32[]{:S(2)}) %collective-permute-start.12) | collective-permute-done | bytes 110624 | tf_op jit(solution)/shard_map/ppermute | solution.py:480
  132.2 0.7 convert_add_fusion.2
  132.9 1.7 %collective-permute-done.18 = bf16[2,192,256]{2,1,0:T(8,128)(2,1)S(1)} collective-permute-done((bf16[2,192,256]{2,1,0:T(8,128)(2,1)S(1)}, bf16[2,192,256]{2,1,0:T(8,128)(2,1)S(1)}, u32[]{:S(2)}, u32[]{:S(2)}) %collective-permute-start.18) | collective-permute-done | bytes 196640 | tf_op jit(solution)/shard_map/ppermute | solution.py:480
  134.7 0.1 copy.35
  134.8 0.2 slice.68
  135.0 0.2 slice.67
  135.1 0.2 copy.37
  135.3 0.2 copy.36
  135.4 1.1 copy.38
  136.5 0.6 pad_maximum_fusion.7
  (51 shorter events, 0.6 us)
Async XLA Ops:
  0.6 10.1 %copy-start.9 = (bf16[256,3,128]{2,0,1:T(8,128)(2,1)S(1)}, bf16[256,3,128]{2,0,1:T(8,128)(2,1)}, u32[]{:S(2)}) copy-start(bf16[256,3,128]{2,0,1:T(8,128)(2,1)} %param.21) | copy-start | bytes 589828
  0.6 15.0 %copy-start.11 = (s32[128,4]{0,1:T(4,128)S(1)}, s32[128,4]{0,1:T(4,128)}, u32[]{:S(2)}) copy-start(s32[128,4]{0,1:T(4,128)} %param.20) | copy-start | bytes 6148
  2.6 16.0 %copy-start.10 = (bf16[64,8,1,64]{3,1,0,2:T(8,128)(2,1)S(1)}, bf16[64,8,1,64]{3,1,0,2:T(8,128)(2,1)}, u32[]{:S(2)}) copy-start(bf16[64,8,1,64]{3,1,0,2:T(8,128)(2,1)} %constant.121.clone.1) | copy-start | bytes 196612
  3.3 1.3 collective-permute-start
  4.6 8.1 %collective-permute-start.1 = (bf16[2,64,256]{2,1,0:T(8,128)(2,1)S(1)}, bf16[2,64,256]{2,1,0:T(8,128)(2,1)S(1)}, u32[]{:S(2)}, u32[]{:S(2)}) collective-permute-start(bf16[2,64,256]{2,1,0:T(8,128)(2,1)S(1)} %pad_maximum_fusion.6), channel_id=1, source_target_pairs={{0,8},{4,12},{8,0},{12,4},{16,24},{20,28},{24,16},{28,20},{32,40},... | collective-permute-start | bytes 196616 | tf_op jit(solution)/shard_map/ppermute | solution.py:480
  10.7 5.1 %collective-permute-start.3 = (bf16[3,4,64,128]{3,2,1,0:T(8,128)(2,1)S(1)}, bf16[3,4,64,128]{3,2,1,0:T(8,128)(2,1)S(1)}, u32[]{:S(2)}, u32[]{:S(2)}) collective-permute-start(bf16[3,4,64,128]{3,2,1,0:T(8,128)(2,1)S(1)} %bitcast.66), channel_id=1, source_target_pairs={{0,4},{4,0},{8,12},{12,8},{16,20},{20,16},{24,28},{28,24},{32,36},... | collective-permute-start | bytes 589832 | tf_op jit(solution)/shard_map/ppermute | solution.py:480
  12.8 3.2 %collective-permute-start.2 = (bf16[4,64,256]{2,1,0:T(8,128)(2,1)S(1)}, bf16[4,64,256]{2,1,0:T(8,128)(2,1)S(1)}, u32[]{:S(2)}, u32[]{:S(2)}) collective-permute-start(bf16[4,64,256]{2,1,0:T(8,128)(2,1)S(1)} %pad_maximum_fusion.4), channel_id=1, source_target_pairs={{0,4},{4,0},{8,12},{12,8},{16,20},{20,16},{24,28},{28,24},{32,36},... | collective-permute-start | bytes 393224 | tf_op jit(solution)/shard_map/ppermute | solution.py:480
  16.6 25.3 %collective-permute-start.4 = (bf16[2,3,4,64,128]{4,3,2,1,0:T(8,128)(2,1)S(1)}, bf16[2,3,4,64,128]{4,3,2,1,0:T(8,128)(2,1)S(1)}, u32[]{:S(2)}, u32[]{:S(2)}) collective-permute-start(bf16[2,3,4,64,128]{4,3,2,1,0:T(8,128)(2,1)S(1)} %pad_maximum_fusion.1), channel_id=1, source_target_pairs={{0,8},{4,12},{8,0},{12,4},{16,24},{20,28},{24,16},{28,20},{32,40},... | collective-permute-start | bytes 1179656 | tf_op jit(solution)/shard_map/ppermute | solution.py:480
  20.6 21.4 %copy-start.5 = (s32[3]{0:T(128)S(1)}, s32[3]{0:T(128)}, u32[]{:S(2)}) copy-start(s32[3]{0:T(128)} %pad_add_fusion.ids) | copy-start | bytes 40
  20.6 21.4 %copy-start.6 = (f32[128]{0:T(128)S(1)}, f32[128]{0:T(128)}, u32[]{:S(2)}) copy-start(f32[128]{0:T(128)} %param.18) | copy-start | bytes 1540
  20.6 21.5 %copy-start.7 = (f32[128]{0:T(128)S(1)}, f32[128]{0:T(128)}, u32[]{:S(2)}) copy-start(f32[128]{0:T(128)} %param.19) | copy-start | bytes 1540
  42.0 31.2 %slice-start = ((s8[7077888]{0:T(1024)(128)(4,1)}), s8[4194304]{0:T(1024)(128)(4,1)S(1)}, s32[]{:S(2)}) async-start(s8[7077888]{0:T(1024)(128)(4,1)} %bitcast.55), calls=%async_computation | async-start | bytes 8388608
  42.1 0.9 copy-start.3
  43.0 19.7 %copy-start.8 = (bf16[768,1024]{1,0:T(8,128)(2,1)S(1)}, bf16[768,1024]{1,0:T(8,128)(2,1)}, u32[]{:S(2)}) copy-start(bf16[768,1024]{1,0:T(8,128)(2,1)} %get-tuple-element.45.hid) | copy-start | bytes 4718596
  43.0 30.2 %slice-start.1 = ((s8[7077888]{0:T(1024)(128)(4,1)}), s8[2883584]{0:T(1024)(128)(4,1)S(1)}, s32[]{:S(2)}) async-start(s8[7077888]{0:T(1024)(128)(4,1)} %bitcast.55), calls=%async_computation.1 | async-start | bytes 5767168
  62.7 10.5 %copy-start = (bf16[256,1024]{1,0:T(8,128)(2,1)S(1)}, bf16[256,1024]{1,0:T(8,128)(2,1)}, u32[]{:S(2)}) copy-start(bf16[256,1024]{1,0:T(8,128)(2,1)} %copy.32.pext) | copy-start | bytes 1572868
  62.7 10.5 %copy-start.1 = (bf16[768,1024]{1,0:T(8,128)(2,1)S(1)}, bf16[768,1024]{1,0:T(8,128)(2,1)}, u32[]{:S(2)}) copy-start(bf16[768,1024]{1,0:T(8,128)(2,1)} %get-tuple-element.51.nrm) | copy-start | bytes 4718596
  62.7 10.5 %copy-start.2 = (f32[768,128]{1,0:T(8,128)S(1)}, f32[768,128]{1,0:T(8,128)}, u32[]{:S(2)}) copy-start(f32[768,128]{1,0:T(8,128)} %get-tuple-element.52.sc) | copy-start | bytes 1179652
  62.7 10.5 %copy-start.4 = (f32[8,1024]{1,0:T(8,128)S(1)}, f32[8,1024]{1,0:T(8,128)}, u32[]{:S(2)}) copy-start(f32[8,1024]{1,0:T(8,128)} %get-tuple-element.54.inv) | copy-start | bytes 98308
  65.9 22.5 %collective-permute-start.8 = (bf16[4,9,48,128]{3,2,1,0:T(8,128)(2,1)S(1)}, bf16[4,9,48,128]{3,2,1,0:T(8,128)(2,1)S(1)}, u32[]{:S(2)}, u32[]{:S(2)}) collective-permute-start(bf16[4,9,48,128]{3,2,1,0:T(8,128)(2,1)S(1)} %get-tuple-element.60), channel_id=1, source_target_pairs={{0,64},{4,68},{8,72},{12,76},{16,80},{20,84},{24,88},{28,92},{32,9... | collective-permute-start | bytes 1327112 | tf_op jit(solution)/shard_map/ppermute | solution.py:530
  69.5 22.2 %collective-permute-start.9 = (bf16[4,9,48,128]{3,2,1,0:T(8,128)(2,1)S(1)}, bf16[4,9,48,128]{3,2,1,0:T(8,128)(2,1)S(1)}, u32[]{:S(2)}, u32[]{:S(2)}) collective-permute-start(bf16[4,9,48,128]{3,2,1,0:T(8,128)(2,1)S(1)} %get-tuple-element.61), channel_id=1, source_target_pairs={{0,128},{4,132},{8,136},{12,140},{16,144},{20,148},{24,152},{28,15... | collective-permute-start | bytes 1327112 | tf_op jit(solution)/shard_map/ppermute | solution.py:530
  72.3 19.4 %collective-permute-start.10 = (bf16[4,9,48,128]{3,2,1,0:T(8,128)(2,1)S(1)}, bf16[4,9,48,128]{3,2,1,0:T(8,128)(2,1)S(1)}, u32[]{:S(2)}, u32[]{:S(2)}) collective-permute-start(bf16[4,9,48,128]{3,2,1,0:T(8,128)(2,1)S(1)} %get-tuple-element.62), channel_id=1, source_target_pairs={{0,192},{4,196},{8,200},{12,204},{16,208},{20,212},{24,216},{28,22... | collective-permute-start | bytes 1327112 | tf_op jit(solution)/shard_map/ppermute | solution.py:530
  79.5 5.1 %collective-permute-start.5 = (bf16[192,256]{1,0:T(8,128)(2,1)S(1)}, bf16[192,256]{1,0:T(8,128)(2,1)S(1)}, u32[]{:S(2)}, u32[]{:S(2)}) collective-permute-start(bf16[192,256]{1,0:T(8,128)(2,1)S(1)} %get-tuple-element.56), channel_id=1, source_target_pairs={{0,1},{1,2},{2,3},{3,0},{4,5},{5,6},{6,7},{7,4},{8,9},{9,10},{10,1... | collective-permute-start | bytes 294920 | tf_op jit(solution)/shard_map/ppermute | solution.py:536
  80.9 6.3 %collective-permute-start.6 = (bf16[192,256]{1,0:T(8,128)(2,1)S(1)}, bf16[192,256]{1,0:T(8,128)(2,1)S(1)}, u32[]{:S(2)}, u32[]{:S(2)}) collective-permute-start(bf16[192,256]{1,0:T(8,128)(2,1)S(1)} %get-tuple-element.57), channel_id=1, source_target_pairs={{0,2},{1,3},{2,0},{3,1},{4,6},{5,7},{6,4},{7,5},{8,10},{9,11},{10,... | collective-permute-start | bytes 294920 | tf_op jit(solution)/shard_map/ppermute | solution.py:536
  84.6 3.8 %collective-permute-start.7 = (bf16[192,256]{1,0:T(8,128)(2,1)S(1)}, bf16[192,256]{1,0:T(8,128)(2,1)S(1)}, u32[]{:S(2)}, u32[]{:S(2)}) collective-permute-start(bf16[192,256]{1,0:T(8,128)(2,1)S(1)} %get-tuple-element.58), channel_id=1, source_target_pairs={{0,3},{1,0},{2,1},{3,2},{4,7},{5,4},{6,5},{7,6},{8,11},{9,8},{10,9... | collective-permute-start | bytes 294920 | tf_op jit(solution)/shard_map/ppermute | solution.py:536
  91.9 5.8 %collective-permute-start.13 = (bf16[192,256]{1,0:T(8,128)(2,1)S(1)}, bf16[192,256]{1,0:T(8,128)(2,1)S(1)}, u32[]{:S(2)}, u32[]{:S(2)}) collective-permute-start(bf16[192,256]{1,0:T(8,128)(2,1)S(1)} %reduce-precision_convert_fusion), channel_id=1, source_target_pairs={{0,16},{4,20},{8,24},{12,28},{16,0},{20,4},{24,8},{28,12},{32,48},... | collective-permute-start | bytes 294920 | tf_op jit(solution)/shard_map/ppermute | solution.py:480
  97.8 7.5 %collective-permute-start.14 = (bf16[192,256]{1,0:T(8,128)(2,1)S(1)}, bf16[192,256]{1,0:T(8,128)(2,1)S(1)}, u32[]{:S(2)}, u32[]{:S(2)}) collective-permute-start(bf16[192,256]{1,0:T(8,128)(2,1)S(1)} %fusion.6), channel_id=1, source_target_pairs={{0,32},{4,36},{8,40},{12,44},{16,48},{20,52},{24,56},{28,60},{32,0... | collective-permute-start | bytes 294920 | tf_op jit(solution)/shard_map/ppermute | solution.py:480
  105.3 6.2 %collective-permute-start.15 = (bf16[192,256]{1,0:T(8,128)(2,1)S(1)}, bf16[192,256]{1,0:T(8,128)(2,1)S(1)}, u32[]{:S(2)}, u32[]{:S(2)}) collective-permute-start(bf16[192,256]{1,0:T(8,128)(2,1)S(1)} %fusion), channel_id=1, source_target_pairs={{0,64},{4,68},{8,72},{12,76},{16,80},{20,84},{24,88},{28,92},{32,9... | collective-permute-start | bytes 294920 | tf_op jit(solution)/shard_map/ppermute | solution.py:480
  105.7 11.0 %collective-permute-start.11 = (bf16[2,9,48,128]{3,2,1,0:T(8,128)(2,1)S(1)}, bf16[2,9,48,128]{3,2,1,0:T(8,128)(2,1)S(1)}, u32[]{:S(2)}, u32[]{:S(2)}) collective-permute-start(bf16[2,9,48,128]{3,2,1,0:T(8,128)(2,1)S(1)} %dynamic-slice_convert_fusion), channel_id=1, source_target_pairs={{0,32},{4,36},{8,40},{12,44},{16,48},{20,52},{24,56},{28,60},{32,0... | collective-permute-start | bytes 663560 | tf_op jit(solution)/shard_map/ppermute | solution.py:480
  111.6 7.4 %collective-permute-start.16 = (bf16[192,256]{1,0:T(8,128)(2,1)S(1)}, bf16[192,256]{1,0:T(8,128)(2,1)S(1)}, u32[]{:S(2)}, u32[]{:S(2)}) collective-permute-start(bf16[192,256]{1,0:T(8,128)(2,1)S(1)} %fusion.5), channel_id=1, source_target_pairs={{0,128},{4,132},{8,136},{12,140},{16,144},{20,148},{24,152},{28,15... | collective-permute-start | bytes 294920 | tf_op jit(solution)/shard_map/ppermute | solution.py:480
  119.0 6.9 %collective-permute-start.17 = (bf16[1,192,256]{2,1,0:T(8,128)(2,1)S(1)}, bf16[1,192,256]{2,1,0:T(8,128)(2,1)S(1)}, u32[]{:S(2)}, u32[]{:S(2)}) collective-permute-start(bf16[1,192,256]{2,1,0:T(8,128)(2,1)S(1)} %fusion.1), channel_id=1, source_target_pairs={{0,4},{4,0},{8,12},{12,8},{16,20},{20,16},{24,28},{28,24},{32,36},... | collective-permute-start | bytes 294920 | tf_op jit(solution)/shard_map/ppermute | solution.py:480
  125.0 7.2 %collective-permute-start.12 = (bf16[1,9,48,128]{3,2,1,0:T(8,128)(2,1)S(1)}, bf16[1,9,48,128]{3,2,1,0:T(8,128)(2,1)S(1)}, u32[]{:S(2)}, u32[]{:S(2)}) collective-permute-start(bf16[1,9,48,128]{3,2,1,0:T(8,128)(2,1)S(1)} %dynamic-slice_convert_fusion.1), channel_id=1, source_target_pairs={{0,16},{4,20},{8,24},{12,28},{16,0},{20,4},{24,8},{28,12},{32,48},... | collective-permute-start | bytes 331784 | tf_op jit(solution)/shard_map/ppermute | solution.py:480
  126.0 8.7 %collective-permute-start.18 = (bf16[2,192,256]{2,1,0:T(8,128)(2,1)S(1)}, bf16[2,192,256]{2,1,0:T(8,128)(2,1)S(1)}, u32[]{:S(2)}, u32[]{:S(2)}) collective-permute-start(bf16[2,192,256]{2,1,0:T(8,128)(2,1)S(1)} %pad_maximum_fusion.3), channel_id=1, source_target_pairs={{0,8},{4,12},{8,0},{12,4},{16,24},{20,28},{24,16},{28,20},{32,40},... | collective-permute-start | bytes 589832 | tf_op jit(solution)/shard_map/ppermute | solution.py:480

commit v4 on v3

--- a/solution.py
+++ b/solution.py
@@ -520,14 +520,12 @@
         ids, pext, stem_weight, stem_bias[None], mod_scale[None], mod_shift[None], w9
     )
     mixed, means = attention(ids, tile_lists, proj, grads, q_gain[None], k_gain[None], wv)
-    weight = weight_part(ids, hid, mixed, hd)
-    mixed, *weight = lax.optimization_barrier((mixed, *weight))
+    weight = list(weight_part(ids, hid, mixed, hd))
     stem = stem_part(ids, w9, mixed, nrm, sc, means, inv, pext)
 
-    weight_total = weight[0].astype(F32)
     for k in range(1, 4):
         pairs = [(a, (a + 16 * k) % seq) for a in range(seq)]
-        weight_total = weight_total + lax.ppermute(weight[k], "seq", pairs).astype(F32)
+        weight[k] = lax.ppermute(weight[k], "seq", pairs)
 
     total = stem[0]
     count = lax.axis_size("head")
@@ -546,10 +544,13 @@
         sent = lax.dynamic_slice_in_dim(value, (1 - side) * half, half, 0)
         return kept + xor(sent.astype(BF16), mask).astype(F32)
 
-    total, weight_total = lax.optimization_barrier((total, weight_total))
+    total, weight[1], weight[2] = lax.optimization_barrier((total, weight[1], weight[2]))
+    total = pair_sum(pair_sum(total, 4), 8)
+    total, weight[3] = lax.optimization_barrier((total, weight[3]))
+    weight_total = sum(part.astype(F32) for part in weight)
     weight_grad = half_sum(half_sum(weight_total, 8), 4)[0]
     weight_grad = jnp.transpose(weight_grad.reshape(3, heads, rows, hd), (2, 0, 1, 3))
-    for mask in (4, 8, 16, 32):
+    for mask in (16, 32):
         total = pair_sum(total, mask)
     full = total.astype(BF16)[None]
     for mask in (1, 2):

time: 137 us -> 137 us (level)
  the two profiles are of different devices: /device:TPU:1 before, /device:TPU:14 now
where the time goes in v4:
time: 137 us
  Pallas kernels  50.6 us (37%)
  starting transfers between devices  41.5 us (30%)
  waiting for transfers between devices  32.3 us (24%)
  local copies, waits for them, and re-layouts  8.49 us (6%)
  other arithmetic  3.04 us (2%)
    ppermute x12, waiting for transfers between devices, xor(): return lax.ppermute(value, 'seq', [(a, a ^ mask) for a in range(seq)])  26.3 us
    pallas_call x1, Pallas kernels, forward(): pl.pallas_call(forward_kernel, grid_spec=pltpu.PrefetchScalarGridSpec(num...  21.3 us
    ppermute x12, starting transfers between devices, xor(): return lax.ppermute(value, 'seq', [(a, a ^ mask) for a in range(seq)])  21 us
    pallas_call x1, Pallas kernels, attention(): pl.pallas_call(attention_kernel, grid_spec=pltpu.PrefetchScalarGridSpec(n...  19.8 us
    ppermute x1, starting transfers between devices, per_device(): lax.ppermute(piece, 'seq', [(a, b) for a, b in border if 0 <= b < seq])  8.02 us
    ppermute x3, starting transfers between devices, per_device(): weight[k] = lax.ppermute(weight[k], 'seq', pairs)  7.43 us
    pallas_call x1, Pallas kernels, stem_part(): pl.pallas_call(stem_kernel, grid_spec=pltpu.PrefetchScalarGridSpec(num_sc...  6.25 us
    ppermute x3, starting transfers between devices, per_device(): total = total + lax.ppermute(stem[k], 'head', pairs).astype(F32)  5 us
  transfers between devices with their start and end apart: 19, of which 11 were waited for; matrix products, arithmetic and copies ran while one was open for 3% of the time, Pallas kernels for 20%

profile of v4, /device:TPU:14, one launch (start us, length us, event | category | flops | bytes accessed | tf_op | source)
XLA Modules:
  0.0 137.0 jit_solution(7221960472473447907)
XLA Ops:
  0.7 1.0 copy.27
  1.6 1.0 copy.28
  2.6 0.0 copy-start.10
  2.6 0.7 reshape.71
  3.3 8.0 %collective-permute-start = (bf16[64,256]{1,0:T(8,128)(2,1)S(1)}, bf16[64,256]{1,0:T(8,128)(2,1)S(1)}, u32[]{:S(2)}, u32[]{:S(2)}) collective-permute-start(bf16[64,256]{1,0:T(8,128)(2,1)S(1)} %reshape.71), channel_id=1, source_target_pairs={{8,16},{12,20},{16,8},{20,12},{24,32},{28,36},{32,24},{36,28},{40,... | collective-permute-start | bytes 98312 | tf_op jit(solution)/shard_map/ppermute | solution.py:487
  11.3 0.7 stack_reshape.8
  12.0 1.2 collective-permute-done
  13.2 0.1 collective-permute-start.1
  13.4 0.1 collective-permute-start.3
  13.5 4.1 %collective-permute-done.1 = bf16[2,64,256]{2,1,0:T(8,128)(2,1)S(1)} collective-permute-done((bf16[2,64,256]{2,1,0:T(8,128)(2,1)S(1)}, bf16[2,64,256]{2,1,0:T(8,128)(2,1)S(1)}, u32[]{:S(2)}, u32[]{:S(2)}) %collective-permute-start.1) | collective-permute-done | bytes 65568 | tf_op jit(solution)/shard_map/ppermute | solution.py:480
  17.6 0.1 collective-permute-start.2
  17.7 0.7 pad_add_fusion.ids
  18.4 0.1 copy.33.lists
  18.6 0.5 collective-permute-done.2
  19.1 0.1 concatenate.31
  19.3 0.1 concatenate.32
  19.4 0.1 concatenate.35
  19.5 0.1 concatenate.33
  19.7 0.3 collective-permute-start.4
  19.9 0.2 maximum_maximum_fusion
  20.2 0.7 copy.31
  20.9 1.0 copy.32.pext
  21.9 21.3 %forward.1 = (f32[1024,1152]{1,0:T(8,128)}, bf16[768,1024]{1,0:T(8,128)(2,1)}, bf16[768,1024]{1,0:T(8,128)(2,1)}, f32[8,1024]{1,0:T(8,128)}, f32[8,1152]{1,0:T(8,128)}, /*index=5*/f32[768,128]{1,0:T(8,128)}) custom-call(s32[3]{0:T(128)} %pad_add_fusion.ids, bf16[256,1024]{1,0:T(8,128)(2,1)} %copy.32.pext, bf16[192,3072]{1,0:T(8,128)(2,1)} %stem.1, ...), custom_call_target="tpu_custom_call" | custom-call | flops 8858370048 | bytes 25165824 | tf_op jit(solution)/shard_map/forward/pallas_call | solution.py:137
  43.3 0.1 pad_maximum_fusion.og
  43.4 0.0 slice-start
  43.4 0.0 copy-start.3
  43.4 0.9 copy-done.3
  44.3 19.8 %attention.1 = (bf16[3,1024,384]{2,1,0:T(8,128)(2,1)S(1)}, f32[2,8,1024]{2,1,0:T(8,128)S(1)}) custom-call(s32[3]{0:T(128)S(1)} %copy-done.5, s32[128,4]{1,0:T(8,128)S(1)} %copy.33.lists, f32[1024,1152]{1,0:T(8,128)} %get-tuple-element.40.pq.pk.pv, f32[1024,1152]{1,0:T(8,128)} %get-tuple-element.40.pq.pk.pv, f32[1024,1152]{1,0:T(8,128)} %get-tuple-element.40.pq.pk.pv, ...), custom_call_target="tpu_custom_call" | custom-call | flops 2013265920 | bytes 10485760 | tf_op jit(solution)/shard_map/attention/pallas_call | solution.py:316
  64.2 0.0 copy-start
  64.2 3.2 %weight_part.1 = (bf16[4,9,48,128]{3,2,1,0:T(8,128)(2,1)S(1)}, bf16[4,9,48,128]{3,2,1,0:T(8,128)(2,1)S(1)}, bf16[4,9,48,128]{3,2,1,0:T(8,128)(2,1)S(1)}, bf16[4,9,48,128]{3,2,1,0:T(8,128)(2,1)S(1)}) custom-call(s32[3]{0:T(128)S(1)} %copy-done.5, bf16[768,1024]{1,0:T(8,128)(2,1)S(1)} %copy-done.8, bf16[3,1024,384]{2,1,0:T(8,128)(2,1)S(1)} %get-tuple-element.43.mixed), custom_call_target="tpu_custom_call" | custom-call | flops 1811939328 | bytes 6291456 | tf_op jit(solution)/shard_map/weight_part/pallas_call | solution.py:373
  67.4 0.1 collective-permute-start.8
  67.5 2.6 %collective-permute-start.9 = (bf16[4,9,48,128]{3,2,1,0:T(8,128)(2,1)S(1)}, bf16[4,9,48,128]{3,2,1,0:T(8,128)(2,1)S(1)}, u32[]{:S(2)}, u32[]{:S(2)}) collective-permute-start(bf16[4,9,48,128]{3,2,1,0:T(8,128)(2,1)S(1)} %get-tuple-element.54), channel_id=1, source_target_pairs={{0,128},{4,132},{8,136},{12,140},{16,144},{20,148},{24,152},{28,15... | collective-permute-start | bytes 1327112 | tf_op jit(solution)/shard_map/ppermute | solution.py:528
  70.2 6.3 %stem_part.1 = (f32[192,256]{1,0:T(8,128)S(1)}, bf16[192,256]{1,0:T(8,128)(2,1)S(1)}, bf16[192,256]{1,0:T(8,128)(2,1)S(1)}, bf16[192,256]{1,0:T(8,128)(2,1)S(1)}) custom-call(s32[3]{0:T(128)S(1)} %copy-done.5, bf16[9,16,4,48,128]{4,3,2,1,0:T(8,128)(2,1)S(1)} %bitcast.57, bf16[3,1024,384]{2,1,0:T(8,128)(2,1)S(1)} %get-tuple-element.43.mixed, ...), custom_call_target="tpu_custom_call" | custom-call | flops 1000 | bytes 1000 | tf_op jit(solution)/shard_map/stem_part/pallas_call | solution.py:426
  76.5 1.6 %collective-permute-start.5 = (bf16[192,256]{1,0:T(8,128)(2,1)S(1)}, bf16[192,256]{1,0:T(8,128)(2,1)S(1)}, u32[]{:S(2)}, u32[]{:S(2)}) collective-permute-start(bf16[192,256]{1,0:T(8,128)(2,1)S(1)} %get-tuple-element.50), channel_id=1, source_target_pairs={{0,1},{1,2},{2,3},{3,0},{4,5},{5,6},{6,7},{7,4},{8,9},{9,10},{10,1... | collective-permute-start | bytes 294920 | tf_op jit(solution)/shard_map/ppermute | solution.py:534
  78.1 1.0 collective-permute-start.6
  79.1 2.4 %collective-permute-start.7 = (bf16[192,256]{1,0:T(8,128)(2,1)S(1)}, bf16[192,256]{1,0:T(8,128)(2,1)S(1)}, u32[]{:S(2)}, u32[]{:S(2)}) collective-permute-start(bf16[192,256]{1,0:T(8,128)(2,1)S(1)} %get-tuple-element.52), channel_id=1, source_target_pairs={{0,3},{1,0},{2,1},{3,2},{4,7},{5,4},{6,5},{7,6},{8,11},{9,8},{10,9... | collective-permute-start | bytes 294920 | tf_op jit(solution)/shard_map/ppermute | solution.py:534
  81.5 3.4 %collective-permute-done.6 = bf16[192,256]{1,0:T(8,128)(2,1)S(1)} collective-permute-done((bf16[192,256]{1,0:T(8,128)(2,1)S(1)}, bf16[192,256]{1,0:T(8,128)(2,1)S(1)}, u32[]{:S(2)}, u32[]{:S(2)}) %collective-permute-start.6) | collective-permute-done | bytes 98336 | tf_op jit(solution)/shard_map/ppermute | solution.py:534
  84.8 0.2 collective-permute-done.7
  85.1 0.1 convert_add_fusion.4
  85.2 2.2 %collective-permute-start.10 = (bf16[192,256]{1,0:T(8,128)(2,1)S(1)}, bf16[192,256]{1,0:T(8,128)(2,1)S(1)}, u32[]{:S(2)}, u32[]{:S(2)}) collective-permute-start(bf16[192,256]{1,0:T(8,128)(2,1)S(1)} %reduce-precision_convert_fusion.1), channel_id=1, source_target_pairs={{0,16},{4,20},{8,24},{12,28},{16,0},{20,4},{24,8},{28,12},{32,48},... | collective-permute-start | bytes 294920 | tf_op jit(solution)/shard_map/ppermute | solution.py:480
  87.4 4.7 %collective-permute-start.12 = (bf16[4,9,48,128]{3,2,1,0:T(8,128)(2,1)S(1)}, bf16[4,9,48,128]{3,2,1,0:T(8,128)(2,1)S(1)}, u32[]{:S(2)}, u32[]{:S(2)}) collective-permute-start(bf16[4,9,48,128]{3,2,1,0:T(8,128)(2,1)S(1)} %get-tuple-element.58), channel_id=1, source_target_pairs={{0,192},{4,196},{8,200},{12,204},{16,208},{20,212},{24,216},{28,22... | collective-permute-start | bytes 1327112 | tf_op jit(solution)/shard_map/ppermute | solution.py:528
  92.1 5.5 %collective-permute-start.11 = (bf16[192,256]{1,0:T(8,128)(2,1)S(1)}, bf16[192,256]{1,0:T(8,128)(2,1)S(1)}, u32[]{:S(2)}, u32[]{:S(2)}) collective-permute-start(bf16[192,256]{1,0:T(8,128)(2,1)S(1)} %fusion), channel_id=1, source_target_pairs={{0,32},{4,36},{8,40},{12,44},{16,48},{20,52},{24,56},{28,60},{32,0... | collective-permute-start | bytes 294920 | tf_op jit(solution)/shard_map/ppermute | solution.py:480
  97.6 4.2 %collective-permute-done.11 = bf16[192,256]{1,0:T(8,128)(2,1)S(1)} collective-permute-done((bf16[192,256]{1,0:T(8,128)(2,1)S(1)}, bf16[192,256]{1,0:T(8,128)(2,1)S(1)}, u32[]{:S(2)}, u32[]{:S(2)}) %collective-permute-start.11) | collective-permute-done | bytes 98336 | tf_op jit(solution)/shard_map/ppermute | solution.py:480
  101.8 1.2 collective-permute-done.12
  103.0 3.7 %collective-permute-start.15 = (bf16[192,256]{1,0:T(8,128)(2,1)S(1)}, bf16[192,256]{1,0:T(8,128)(2,1)S(1)}, u32[]{:S(2)}, u32[]{:S(2)}) collective-permute-start(bf16[192,256]{1,0:T(8,128)(2,1)S(1)} %reduce-precision_convert_fusion), channel_id=1, source_target_pairs={{0,64},{4,68},{8,72},{12,76},{16,80},{20,84},{24,88},{28,92},{32,9... | collective-permute-start | bytes 294920 | tf_op jit(solution)/shard_map/ppermute | solution.py:480
  106.7 0.2 convert_add_fusion
  106.9 2.7 %collective-permute-done.15 = bf16[192,256]{1,0:T(8,128)(2,1)S(1)} collective-permute-done((bf16[192,256]{1,0:T(8,128)(2,1)S(1)}, bf16[192,256]{1,0:T(8,128)(2,1)S(1)}, u32[]{:S(2)}, u32[]{:S(2)}) %collective-permute-start.15) | collective-permute-done | bytes 98336 | tf_op jit(solution)/shard_map/ppermute | solution.py:480
  109.7 3.7 %collective-permute-start.16 = (bf16[192,256]{1,0:T(8,128)(2,1)S(1)}, bf16[192,256]{1,0:T(8,128)(2,1)S(1)}, u32[]{:S(2)}, u32[]{:S(2)}) collective-permute-start(bf16[192,256]{1,0:T(8,128)(2,1)S(1)} %fusion.1), channel_id=1, source_target_pairs={{0,128},{4,132},{8,136},{12,140},{16,144},{20,148},{24,152},{28,15... | collective-permute-start | bytes 294920 | tf_op jit(solution)/shard_map/ppermute | solution.py:480
  113.4 4.1 %collective-permute-start.13 = (bf16[2,9,48,128]{3,2,1,0:T(8,128)(2,1)S(1)}, bf16[2,9,48,128]{3,2,1,0:T(8,128)(2,1)S(1)}, u32[]{:S(2)}, u32[]{:S(2)}) collective-permute-start(bf16[2,9,48,128]{3,2,1,0:T(8,128)(2,1)S(1)} %dynamic-slice_convert_fusion), channel_id=1, source_target_pairs={{0,32},{4,36},{8,40},{12,44},{16,48},{20,52},{24,56},{28,60},{32,0... | collective-permute-start | bytes 663560 | tf_op jit(solution)/shard_map/ppermute | solution.py:480
  117.5 0.1 fusion.2
  117.5 0.1 collective-permute-start.17
  117.6 9.7 %collective-permute-done.13 = bf16[2,9,48,128]{3,2,1,0:T(8,128)(2,1)S(1)} collective-permute-done((bf16[2,9,48,128]{3,2,1,0:T(8,128)(2,1)S(1)}, bf16[2,9,48,128]{3,2,1,0:T(8,128)(2,1)S(1)}, u32[]{:S(2)}, u32[]{:S(2)}) %collective-permute-start.13) | collective-permute-done | bytes 221216 | tf_op jit(solution)/shard_map/ppermute | solution.py:480
  127.4 0.1 collective-permute-start.14
  127.6 1.1 collective-permute-start.18
  128.8 4.5 %collective-permute-done.14 = bf16[1,9,48,128]{3,2,1,0:T(8,128)(2,1)S(1)} collective-permute-done((bf16[1,9,48,128]{3,2,1,0:T(8,128)(2,1)S(1)}, bf16[1,9,48,128]{3,2,1,0:T(8,128)(2,1)S(1)}, u32[]{:S(2)}, u32[]{:S(2)}) %collective-permute-start.14) | collective-permute-done | bytes 110624 | tf_op jit(solution)/shard_map/ppermute | solution.py:480
  133.3 0.7 convert_add_fusion.2
  134.0 0.6 collective-permute-done.18
  134.6 0.1 copy.35
  134.7 0.2 slice.68
  134.9 0.2 slice.67
  135.1 0.2 copy.37
  135.2 0.2 copy.36
  135.4 1.1 copy.38
  136.4 0.6 pad_maximum_fusion.7
  (52 shorter events, 0.6 us)
Async XLA Ops:
  0.6 12.7 %copy-start.9 = (bf16[256,3,128]{2,0,1:T(8,128)(2,1)S(1)}, bf16[256,3,128]{2,0,1:T(8,128)(2,1)}, u32[]{:S(2)}) copy-start(bf16[256,3,128]{2,0,1:T(8,128)(2,1)} %param.21) | copy-start | bytes 589828
  0.6 17.8 %copy-start.11 = (s32[128,4]{0,1:T(4,128)S(1)}, s32[128,4]{0,1:T(4,128)}, u32[]{:S(2)}) copy-start(s32[128,4]{0,1:T(4,128)} %param.20) | copy-start | bytes 6148
  2.6 17.3 %copy-start.10 = (bf16[64,8,1,64]{3,1,0,2:T(8,128)(2,1)S(1)}, bf16[64,8,1,64]{3,1,0,2:T(8,128)(2,1)}, u32[]{:S(2)}) copy-start(bf16[64,8,1,64]{3,1,0,2:T(8,128)(2,1)} %constant.121.clone.1) | copy-start | bytes 196612
  3.3 9.9 %collective-permute-start = (bf16[64,256]{1,0:T(8,128)(2,1)S(1)}, bf16[64,256]{1,0:T(8,128)(2,1)S(1)}, u32[]{:S(2)}, u32[]{:S(2)}) collective-permute-start(bf16[64,256]{1,0:T(8,128)(2,1)S(1)} %reshape.71), channel_id=1, source_target_pairs={{8,16},{12,20},{16,8},{20,12},{24,32},{28,36},{32,24},{36,28},{40,... | collective-permute-start | bytes 98312 | tf_op jit(solution)/shard_map/ppermute | solution.py:487
  13.2 4.4 %collective-permute-start.1 = (bf16[2,64,256]{2,1,0:T(8,128)(2,1)S(1)}, bf16[2,64,256]{2,1,0:T(8,128)(2,1)S(1)}, u32[]{:S(2)}, u32[]{:S(2)}) collective-permute-start(bf16[2,64,256]{2,1,0:T(8,128)(2,1)S(1)} %pad_maximum_fusion.6), channel_id=1, source_target_pairs={{0,8},{4,12},{8,0},{12,4},{16,24},{20,28},{24,16},{28,20},{32,40},... | collective-permute-start | bytes 196616 | tf_op jit(solution)/shard_map/ppermute | solution.py:480
  13.4 5.1 %collective-permute-start.3 = (bf16[3,4,64,128]{3,2,1,0:T(8,128)(2,1)S(1)}, bf16[3,4,64,128]{3,2,1,0:T(8,128)(2,1)S(1)}, u32[]{:S(2)}, u32[]{:S(2)}) collective-permute-start(bf16[3,4,64,128]{3,2,1,0:T(8,128)(2,1)S(1)} %bitcast.66), channel_id=1, source_target_pairs={{0,4},{4,0},{8,12},{12,8},{16,20},{20,16},{24,28},{28,24},{32,36},... | collective-permute-start | bytes 589832 | tf_op jit(solution)/shard_map/ppermute | solution.py:480
  17.6 1.4 %collective-permute-start.2 = (bf16[4,64,256]{2,1,0:T(8,128)(2,1)S(1)}, bf16[4,64,256]{2,1,0:T(8,128)(2,1)S(1)}, u32[]{:S(2)}, u32[]{:S(2)}) collective-permute-start(bf16[4,64,256]{2,1,0:T(8,128)(2,1)S(1)} %pad_maximum_fusion.4), channel_id=1, source_target_pairs={{0,4},{4,0},{8,12},{12,8},{16,20},{20,16},{24,28},{28,24},{32,36},... | collective-permute-start | bytes 393224 | tf_op jit(solution)/shard_map/ppermute | solution.py:480
  19.7 23.6 %collective-permute-start.4 = (bf16[2,3,4,64,128]{4,3,2,1,0:T(8,128)(2,1)S(1)}, bf16[2,3,4,64,128]{4,3,2,1,0:T(8,128)(2,1)S(1)}, u32[]{:S(2)}, u32[]{:S(2)}) collective-permute-start(bf16[2,3,4,64,128]{4,3,2,1,0:T(8,128)(2,1)S(1)} %pad_maximum_fusion.1), channel_id=1, source_target_pairs={{0,8},{4,12},{8,0},{12,4},{16,24},{20,28},{24,16},{28,20},{32,40},... | collective-permute-start | bytes 1179656 | tf_op jit(solution)/shard_map/ppermute | solution.py:480
  21.9 21.4 %copy-start.5 = (s32[3]{0:T(128)S(1)}, s32[3]{0:T(128)}, u32[]{:S(2)}) copy-start(s32[3]{0:T(128)} %pad_add_fusion.ids) | copy-start | bytes 40
  21.9 21.4 %copy-start.6 = (f32[128]{0:T(128)S(1)}, f32[128]{0:T(128)}, u32[]{:S(2)}) copy-start(f32[128]{0:T(128)} %param.18) | copy-start | bytes 1540
  21.9 21.5 %copy-start.7 = (f32[128]{0:T(128)S(1)}, f32[128]{0:T(128)}, u32[]{:S(2)}) copy-start(f32[128]{0:T(128)} %param.19) | copy-start | bytes 1540
  43.4 26.8 %slice-start = ((s8[7077888]{0:T(1024)(128)(4,1)}), s8[4194304]{0:T(1024)(128)(4,1)S(1)}, s32[]{:S(2)}) async-start(s8[7077888]{0:T(1024)(128)(4,1)} %bitcast.55), calls=%async_computation | async-start | bytes 8388608
  43.4 0.9 copy-start.3
  44.3 19.8 %copy-start.8 = (bf16[768,1024]{1,0:T(8,128)(2,1)S(1)}, bf16[768,1024]{1,0:T(8,128)(2,1)}, u32[]{:S(2)}) copy-start(bf16[768,1024]{1,0:T(8,128)(2,1)} %get-tuple-element.39.hid) | copy-start | bytes 4718596
  44.3 25.8 %slice-start.1 = ((s8[7077888]{0:T(1024)(128)(4,1)}), s8[2883584]{0:T(1024)(128)(4,1)S(1)}, s32[]{:S(2)}) async-start(s8[7077888]{0:T(1024)(128)(4,1)} %bitcast.55), calls=%async_computation.1 | async-start | bytes 5767168
  64.2 6.0 %copy-start = (bf16[256,1024]{1,0:T(8,128)(2,1)S(1)}, bf16[256,1024]{1,0:T(8,128)(2,1)}, u32[]{:S(2)}) copy-start(bf16[256,1024]{1,0:T(8,128)(2,1)} %copy.32.pext) | copy-start | bytes 1572868
  64.2 6.0 %copy-start.1 = (bf16[768,1024]{1,0:T(8,128)(2,1)S(1)}, bf16[768,1024]{1,0:T(8,128)(2,1)}, u32[]{:S(2)}) copy-start(bf16[768,1024]{1,0:T(8,128)(2,1)} %get-tuple-element.45.nrm) | copy-start | bytes 4718596
  64.2 6.0 %copy-start.2 = (f32[768,128]{1,0:T(8,128)S(1)}, f32[768,128]{1,0:T(8,128)}, u32[]{:S(2)}) copy-start(f32[768,128]{1,0:T(8,128)} %get-tuple-element.46.sc) | copy-start | bytes 1179652
  64.2 6.0 %copy-start.4 = (f32[8,1024]{1,0:T(8,128)S(1)}, f32[8,1024]{1,0:T(8,128)}, u32[]{:S(2)}) copy-start(f32[8,1024]{1,0:T(8,128)} %get-tuple-element.48.inv) | copy-start | bytes 98308
  67.4 17.7 %collective-permute-start.8 = (bf16[4,9,48,128]{3,2,1,0:T(8,128)(2,1)S(1)}, bf16[4,9,48,128]{3,2,1,0:T(8,128)(2,1)S(1)}, u32[]{:S(2)}, u32[]{:S(2)}) collective-permute-start(bf16[4,9,48,128]{3,2,1,0:T(8,128)(2,1)S(1)} %get-tuple-element.53), channel_id=1, source_target_pairs={{0,64},{4,68},{8,72},{12,76},{16,80},{20,84},{24,88},{28,92},{32,9... | collective-permute-start | bytes 1327112 | tf_op jit(solution)/shard_map/ppermute | solution.py:528
  67.5 17.6 %collective-permute-start.9 = (bf16[4,9,48,128]{3,2,1,0:T(8,128)(2,1)S(1)}, bf16[4,9,48,128]{3,2,1,0:T(8,128)(2,1)S(1)}, u32[]{:S(2)}, u32[]{:S(2)}) collective-permute-start(bf16[4,9,48,128]{3,2,1,0:T(8,128)(2,1)S(1)} %get-tuple-element.54), channel_id=1, source_target_pairs={{0,128},{4,132},{8,136},{12,140},{16,144},{20,148},{24,152},{28,15... | collective-permute-start | bytes 1327112 | tf_op jit(solution)/shard_map/ppermute | solution.py:528
  76.5 5.0 %collective-permute-start.5 = (bf16[192,256]{1,0:T(8,128)(2,1)S(1)}, bf16[192,256]{1,0:T(8,128)(2,1)S(1)}, u32[]{:S(2)}, u32[]{:S(2)}) collective-permute-start(bf16[192,256]{1,0:T(8,128)(2,1)S(1)} %get-tuple-element.50), channel_id=1, source_target_pairs={{0,1},{1,2},{2,3},{3,0},{4,5},{5,6},{6,7},{7,4},{8,9},{9,10},{10,1... | collective-permute-start | bytes 294920 | tf_op jit(solution)/shard_map/ppermute | solution.py:534
  78.1 6.7 %collective-permute-start.6 = (bf16[192,256]{1,0:T(8,128)(2,1)S(1)}, bf16[192,256]{1,0:T(8,128)(2,1)S(1)}, u32[]{:S(2)}, u32[]{:S(2)}) collective-permute-start(bf16[192,256]{1,0:T(8,128)(2,1)S(1)} %get-tuple-element.51), channel_id=1, source_target_pairs={{0,2},{1,3},{2,0},{3,1},{4,6},{5,7},{6,4},{7,5},{8,10},{9,11},{10,... | collective-permute-start | bytes 294920 | tf_op jit(solution)/shard_map/ppermute | solution.py:534
  79.1 6.0 %collective-permute-start.7 = (bf16[192,256]{1,0:T(8,128)(2,1)S(1)}, bf16[192,256]{1,0:T(8,128)(2,1)S(1)}, u32[]{:S(2)}, u32[]{:S(2)}) collective-permute-start(bf16[192,256]{1,0:T(8,128)(2,1)S(1)} %get-tuple-element.52), channel_id=1, source_target_pairs={{0,3},{1,0},{2,1},{3,2},{4,7},{5,4},{6,5},{7,6},{8,11},{9,8},{10,9... | collective-permute-start | bytes 294920 | tf_op jit(solution)/shard_map/ppermute | solution.py:534
  85.2 6.9 %collective-permute-start.10 = (bf16[192,256]{1,0:T(8,128)(2,1)S(1)}, bf16[192,256]{1,0:T(8,128)(2,1)S(1)}, u32[]{:S(2)}, u32[]{:S(2)}) collective-permute-start(bf16[192,256]{1,0:T(8,128)(2,1)S(1)} %reduce-precision_convert_fusion.1), channel_id=1, source_target_pairs={{0,16},{4,20},{8,24},{12,28},{16,0},{20,4},{24,8},{28,12},{32,48},... | collective-permute-start | bytes 294920 | tf_op jit(solution)/shard_map/ppermute | solution.py:480
  87.4 15.6 %collective-permute-start.12 = (bf16[4,9,48,128]{3,2,1,0:T(8,128)(2,1)S(1)}, bf16[4,9,48,128]{3,2,1,0:T(8,128)(2,1)S(1)}, u32[]{:S(2)}, u32[]{:S(2)}) collective-permute-start(bf16[4,9,48,128]{3,2,1,0:T(8,128)(2,1)S(1)} %get-tuple-element.58), channel_id=1, source_target_pairs={{0,192},{4,196},{8,200},{12,204},{16,208},{20,212},{24,216},{28,22... | collective-permute-start | bytes 1327112 | tf_op jit(solution)/shard_map/ppermute | solution.py:528
  92.1 9.7 %collective-permute-start.11 = (bf16[192,256]{1,0:T(8,128)(2,1)S(1)}, bf16[192,256]{1,0:T(8,128)(2,1)S(1)}, u32[]{:S(2)}, u32[]{:S(2)}) collective-permute-start(bf16[192,256]{1,0:T(8,128)(2,1)S(1)} %fusion), channel_id=1, source_target_pairs={{0,32},{4,36},{8,40},{12,44},{16,48},{20,52},{24,56},{28,60},{32,0... | collective-permute-start | bytes 294920 | tf_op jit(solution)/shard_map/ppermute | solution.py:480
  103.0 6.6 %collective-permute-start.15 = (bf16[192,256]{1,0:T(8,128)(2,1)S(1)}, bf16[192,256]{1,0:T(8,128)(2,1)S(1)}, u32[]{:S(2)}, u32[]{:S(2)}) collective-permute-start(bf16[192,256]{1,0:T(8,128)(2,1)S(1)} %reduce-precision_convert_fusion), channel_id=1, source_target_pairs={{0,64},{4,68},{8,72},{12,76},{16,80},{20,84},{24,88},{28,92},{32,9... | collective-permute-start | bytes 294920 | tf_op jit(solution)/shard_map/ppermute | solution.py:480
  109.7 7.8 %collective-permute-start.16 = (bf16[192,256]{1,0:T(8,128)(2,1)S(1)}, bf16[192,256]{1,0:T(8,128)(2,1)S(1)}, u32[]{:S(2)}, u32[]{:S(2)}) collective-permute-start(bf16[192,256]{1,0:T(8,128)(2,1)S(1)} %fusion.1), channel_id=1, source_target_pairs={{0,128},{4,132},{8,136},{12,140},{16,144},{20,148},{24,152},{28,15... | collective-permute-start | bytes 294920 | tf_op jit(solution)/shard_map/ppermute | solution.py:480
  113.4 14.0 %collective-permute-start.13 = (bf16[2,9,48,128]{3,2,1,0:T(8,128)(2,1)S(1)}, bf16[2,9,48,128]{3,2,1,0:T(8,128)(2,1)S(1)}, u32[]{:S(2)}, u32[]{:S(2)}) collective-permute-start(bf16[2,9,48,128]{3,2,1,0:T(8,128)(2,1)S(1)} %dynamic-slice_convert_fusion), channel_id=1, source_target_pairs={{0,32},{4,36},{8,40},{12,44},{16,48},{20,52},{24,56},{28,60},{32,0... | collective-permute-start | bytes 663560 | tf_op jit(solution)/shard_map/ppermute | solution.py:480
  117.5 10.0 %collective-permute-start.17 = (bf16[1,192,256]{2,1,0:T(8,128)(2,1)S(1)}, bf16[1,192,256]{2,1,0:T(8,128)(2,1)S(1)}, u32[]{:S(2)}, u32[]{:S(2)}) collective-permute-start(bf16[1,192,256]{2,1,0:T(8,128)(2,1)S(1)} %fusion.2), channel_id=1, source_target_pairs={{0,4},{4,0},{8,12},{12,8},{16,20},{20,16},{24,28},{28,24},{32,36},... | collective-permute-start | bytes 294920 | tf_op jit(solution)/shard_map/ppermute | solution.py:480
  127.4 5.8 %collective-permute-start.14 = (bf16[1,9,48,128]{3,2,1,0:T(8,128)(2,1)S(1)}, bf16[1,9,48,128]{3,2,1,0:T(8,128)(2,1)S(1)}, u32[]{:S(2)}, u32[]{:S(2)}) collective-permute-start(bf16[1,9,48,128]{3,2,1,0:T(8,128)(2,1)S(1)} %dynamic-slice_convert_fusion.1), channel_id=1, source_target_pairs={{0,16},{4,20},{8,24},{12,28},{16,0},{20,4},{24,8},{28,12},{32,48},... | collective-permute-start | bytes 331784 | tf_op jit(solution)/shard_map/ppermute | solution.py:480
  127.6 6.9 %collective-permute-start.18 = (bf16[2,192,256]{2,1,0:T(8,128)(2,1)S(1)}, bf16[2,192,256]{2,1,0:T(8,128)(2,1)S(1)}, u32[]{:S(2)}, u32[]{:S(2)}) collective-permute-start(bf16[2,192,256]{2,1,0:T(8,128)(2,1)S(1)} %pad_maximum_fusion.3), channel_id=1, source_target_pairs={{0,8},{4,12},{8,0},{12,4},{16,24},{20,28},{24,16},{28,20},{32,40},... | collective-permute-start | bytes 589832 | tf_op jit(solution)/shard_map/ppermute | solution.py:480

commit v5 on v4

--- a/solution.py
+++ b/solution.py
@@ -533,30 +533,35 @@
         pairs = [(a, (a + k) % count) for a in range(count)]
         total = total + lax.ppermute(stem[k], "head", pairs).astype(F32)
 
-    def pair_sum(value, mask):
+    def quad_sum(value, low, high):
         held = lax.reduce_precision(value, 8, 7)
-        return held + xor(held.astype(BF16), mask).astype(F32)
-
-    def half_sum(value, mask):
-        side = s // mask % 2
-        half = value.shape[0] // 2
-        kept = lax.dynamic_slice_in_dim(value, side * half, half, 0)
-        sent = lax.dynamic_slice_in_dim(value, (1 - side) * half, half, 0)
-        return kept + xor(sent.astype(BF16), mask).astype(F32)
+        sent = held.astype(BF16)
+        near, far, both = (xor(sent, mask).astype(F32) for mask in (low, high, low + high))
+        return (held + near) + (far + both)
 
     total, weight[1], weight[2] = lax.optimization_barrier((total, weight[1], weight[2]))
-    total = pair_sum(pair_sum(total, 4), 8)
+    total = quad_sum(total, 4, 8)
     total, weight[3] = lax.optimization_barrier((total, weight[3]))
     weight_total = sum(part.astype(F32) for part in weight)
-    weight_grad = half_sum(half_sum(weight_total, 8), 4)[0]
+
+    zhi = g % 4
+    parts = []
+    for k in range(4):
+        part = lax.dynamic_index_in_dim(weight_total, (zhi + k) % 4, 0, keepdims=False)
+        if k > 0:
+            pairs = [(a, a - a % 16 + (a + 4 * k) % 16) for a in range(seq)]
+            part = lax.ppermute(part.astype(BF16), "seq", pairs)
+        parts.append(part)
+    total = quad_sum(total, 16, 32)
+    total, parts[1], parts[2] = lax.optimization_barrier((total, parts[1], parts[2]))
+    weight_grad = sum(part.astype(F32) for part in parts)
     weight_grad = jnp.transpose(weight_grad.reshape(3, heads, rows, hd), (2, 0, 1, 3))
-    for mask in (16, 32):
-        total = pair_sum(total, mask)
-    full = total.astype(BF16)[None]
-    for mask in (1, 2):
-        other = xor(full, mask)
-        low = (s // mask) % 2 == 0
-        full = jnp.concatenate([jnp.where(low, full, other), jnp.where(low, other, full)])
+
+    held = total.astype(BF16)
+    found = [held] + [xor(held, mask) for mask in (1, 2, 3)]
+    low, high = j % 2 == 0, j < 2
+    swapped = [jnp.where(low, found[m], found[m ^ 1]) for m in range(4)]
+    full = jnp.stack([jnp.where(high, swapped[m], swapped[m ^ 2]) for m in range(4)])
     full = full.reshape(4, groups // 4, rows, 256)
     full = jnp.transpose(full, (1, 0, 2, 3)).reshape(width // 4, 256).T.astype(F32)
     base = 12 * channels

time: 137 us -> 137 us (level)
  the two profiles are of different devices: /device:TPU:14 before, /device:TPU:1 now
where the time goes in v5:
time: 137 us
  Pallas kernels  50.5 us (37%)
  starting transfers between devices  47.3 us (35%)
  waiting for transfers between devices  27.2 us (20%)
  local copies, waits for them, and re-layouts  8.41 us (6%)
  other arithmetic  2.95 us (2%)
    ppermute x13, starting transfers between devices, xor(): return lax.ppermute(value, 'seq', [(a, a ^ mask) for a in range(seq)])  27.7 us
    pallas_call x1, Pallas kernels, forward(): pl.pallas_call(forward_kernel, grid_spec=pltpu.PrefetchScalarGridSpec(num...  21.3 us
    pallas_call x1, Pallas kernels, attention(): pl.pallas_call(attention_kernel, grid_spec=pltpu.PrefetchScalarGridSpec(n...  19.7 us
    ppermute x13, waiting for transfers between devices, xor(): return lax.ppermute(value, 'seq', [(a, a ^ mask) for a in range(seq)])  13.1 us
    ppermute x3, starting transfers between devices, per_device(): weight[k] = lax.ppermute(weight[k], 'seq', pairs)  7.18 us
    ppermute x3, waiting for transfers between devices, per_device(): part = lax.ppermute(part.astype(BF16), 'seq', pairs)  7 us
    ppermute x3, starting transfers between devices, per_device(): part = lax.ppermute(part.astype(BF16), 'seq', pairs)  6.73 us
    pallas_call x1, Pallas kernels, stem_part(): pl.pallas_call(stem_kernel, grid_spec=pltpu.PrefetchScalarGridSpec(num_sc...  6.26 us
  transfers between devices with their start and end apart: 23, of which 10 were waited for; matrix products, arithmetic and copies ran while one was open for 2% of the time, Pallas kernels for 20%

profile of v5, /device:TPU:1, one launch (start us, length us, event | category | flops | bytes accessed | tf_op | source)
XLA Modules:
  0.0 137.4 jit_solution(17660737268515405506)
XLA Ops:
  0.7 1.0 copy.30
  1.6 1.0 copy.31
  2.6 0.0 copy-start.10
  2.6 0.7 reshape.83
  3.3 0.7 collective-permute-start
  4.0 0.7 stack_reshape.8
  4.6 6.0 %collective-permute-start.1 = (bf16[2,64,256]{2,1,0:T(8,128)(2,1)S(1)}, bf16[2,64,256]{2,1,0:T(8,128)(2,1)S(1)}, u32[]{:S(2)}, u32[]{:S(2)}) collective-permute-start(bf16[2,64,256]{2,1,0:T(8,128)(2,1)S(1)} %pad_maximum_fusion.4), channel_id=1, source_target_pairs={{0,8},{4,12},{8,0},{12,4},{16,24},{20,28},{24,16},{28,20},{32,40},... | collective-permute-start | bytes 196616 | tf_op jit(solution)/shard_map/ppermute | solution.py:480
  10.7 2.0 %collective-permute-start.3 = (bf16[3,4,64,128]{3,2,1,0:T(8,128)(2,1)S(1)}, bf16[3,4,64,128]{3,2,1,0:T(8,128)(2,1)S(1)}, u32[]{:S(2)}, u32[]{:S(2)}) collective-permute-start(bf16[3,4,64,128]{3,2,1,0:T(8,128)(2,1)S(1)} %bitcast.85), channel_id=1, source_target_pairs={{0,4},{4,0},{8,12},{12,8},{16,20},{20,16},{24,28},{28,24},{32,36},... | collective-permute-start | bytes 589832 | tf_op jit(solution)/shard_map/ppermute | solution.py:480
  12.8 2.2 %collective-permute-start.2 = (bf16[4,64,256]{2,1,0:T(8,128)(2,1)S(1)}, bf16[4,64,256]{2,1,0:T(8,128)(2,1)S(1)}, u32[]{:S(2)}, u32[]{:S(2)}) collective-permute-start(bf16[4,64,256]{2,1,0:T(8,128)(2,1)S(1)} %pad_maximum_fusion.2), channel_id=1, source_target_pairs={{0,4},{4,0},{8,12},{12,8},{16,20},{20,16},{24,28},{28,24},{32,36},... | collective-permute-start | bytes 393224 | tf_op jit(solution)/shard_map/ppermute | solution.py:480
  15.0 0.6 pad_add_fusion.ids
  15.6 0.1 copy.36.lists
  15.8 0.2 collective-permute-done.2
  16.0 0.1 concatenate.26
  16.2 0.1 concatenate.27
  16.3 0.1 concatenate.28
  16.5 0.1 concatenate.30
  16.6 0.2 maximum_maximum_fusion
  16.8 0.7 copy.34
  17.6 1.0 copy.35.pext
  18.6 1.7 %collective-permute-start.4 = (bf16[2,3,4,64,128]{4,3,2,1,0:T(8,128)(2,1)S(1)}, bf16[2,3,4,64,128]{4,3,2,1,0:T(8,128)(2,1)S(1)}, u32[]{:S(2)}, u32[]{:S(2)}) collective-permute-start(bf16[2,3,4,64,128]{4,3,2,1,0:T(8,128)(2,1)S(1)} %pad_maximum_fusion.1), channel_id=1, source_target_pairs={{0,8},{4,12},{8,0},{12,4},{16,24},{20,28},{24,16},{28,20},{32,40},... | collective-permute-start | bytes 1179656 | tf_op jit(solution)/shard_map/ppermute | solution.py:480
  20.3 21.3 %forward.1 = (f32[1024,1152]{1,0:T(8,128)}, bf16[768,1024]{1,0:T(8,128)(2,1)}, bf16[768,1024]{1,0:T(8,128)(2,1)}, f32[8,1024]{1,0:T(8,128)}, f32[8,1152]{1,0:T(8,128)}, /*index=5*/f32[768,128]{1,0:T(8,128)}) custom-call(s32[3]{0:T(128)} %pad_add_fusion.ids, bf16[256,1024]{1,0:T(8,128)(2,1)} %copy.35.pext, bf16[192,3072]{1,0:T(8,128)(2,1)} %stem.1, ...), custom_call_target="tpu_custom_call" | custom-call | flops 8858370048 | bytes 25165824 | tf_op jit(solution)/shard_map/forward/pallas_call | solution.py:137
  41.7 0.1 pad_maximum_fusion.og
  41.7 0.0 slice-start
  41.8 0.9 copy-done.3
  42.7 19.7 %attention.1 = (bf16[3,1024,384]{2,1,0:T(8,128)(2,1)S(1)}, f32[2,8,1024]{2,1,0:T(8,128)S(1)}) custom-call(s32[3]{0:T(128)S(1)} %copy-done.5, s32[128,4]{1,0:T(8,128)S(1)} %copy.36.lists, f32[1024,1152]{1,0:T(8,128)} %get-tuple-element.43.pq.pk.pv, f32[1024,1152]{1,0:T(8,128)} %get-tuple-element.43.pq.pk.pv, f32[1024,1152]{1,0:T(8,128)} %get-tuple-element.43.pq.pk.pv, ...), custom_call_target="tpu_custom_call" | custom-call | flops 2013265920 | bytes 10485760 | tf_op jit(solution)/shard_map/attention/pallas_call | solution.py:316
  62.5 3.2 %weight_part.1 = (bf16[4,9,48,128]{3,2,1,0:T(8,128)(2,1)S(1)}, bf16[4,9,48,128]{3,2,1,0:T(8,128)(2,1)S(1)}, bf16[4,9,48,128]{3,2,1,0:T(8,128)(2,1)S(1)}, bf16[4,9,48,128]{3,2,1,0:T(8,128)(2,1)S(1)}) custom-call(s32[3]{0:T(128)S(1)} %copy-done.5, bf16[768,1024]{1,0:T(8,128)(2,1)S(1)} %copy-done.8, bf16[3,1024,384]{2,1,0:T(8,128)(2,1)S(1)} %get-tuple-element.46.mixed), custom_call_target="tpu_custom_call" | custom-call | flops 1811939328 | bytes 6291456 | tf_op jit(solution)/shard_map/weight_part/pallas_call | solution.py:373
  65.7 3.5 %collective-permute-start.8 = (bf16[4,9,48,128]{3,2,1,0:T(8,128)(2,1)S(1)}, bf16[4,9,48,128]{3,2,1,0:T(8,128)(2,1)S(1)}, u32[]{:S(2)}, u32[]{:S(2)}) collective-permute-start(bf16[4,9,48,128]{3,2,1,0:T(8,128)(2,1)S(1)} %get-tuple-element.56), channel_id=1, source_target_pairs={{0,64},{4,68},{8,72},{12,76},{16,80},{20,84},{24,88},{28,92},{32,9... | collective-permute-start | bytes 1327112 | tf_op jit(solution)/shard_map/ppermute | solution.py:528
  69.2 2.8 %collective-permute-start.9 = (bf16[4,9,48,128]{3,2,1,0:T(8,128)(2,1)S(1)}, bf16[4,9,48,128]{3,2,1,0:T(8,128)(2,1)S(1)}, u32[]{:S(2)}, u32[]{:S(2)}) collective-permute-start(bf16[4,9,48,128]{3,2,1,0:T(8,128)(2,1)S(1)} %get-tuple-element.57), channel_id=1, source_target_pairs={{0,128},{4,132},{8,136},{12,140},{16,144},{20,148},{24,152},{28,15... | collective-permute-start | bytes 1327112 | tf_op jit(solution)/shard_map/ppermute | solution.py:528
  72.0 6.3 %stem_part.1 = (f32[192,256]{1,0:T(8,128)S(1)}, bf16[192,256]{1,0:T(8,128)(2,1)S(1)}, bf16[192,256]{1,0:T(8,128)(2,1)S(1)}, bf16[192,256]{1,0:T(8,128)(2,1)S(1)}) custom-call(s32[3]{0:T(128)S(1)} %copy-done.5, bf16[9,16,4,48,128]{4,3,2,1,0:T(8,128)(2,1)S(1)} %bitcast.77, bf16[3,1024,384]{2,1,0:T(8,128)(2,1)S(1)} %get-tuple-element.46.mixed, ...), custom_call_target="tpu_custom_call" | custom-call | flops 1000 | bytes 1000 | tf_op jit(solution)/shard_map/stem_part/pallas_call | solution.py:426
  78.3 1.4 %collective-permute-start.5 = (bf16[192,256]{1,0:T(8,128)(2,1)S(1)}, bf16[192,256]{1,0:T(8,128)(2,1)S(1)}, u32[]{:S(2)}, u32[]{:S(2)}) collective-permute-start(bf16[192,256]{1,0:T(8,128)(2,1)S(1)} %get-tuple-element.53), channel_id=1, source_target_pairs={{0,1},{1,2},{2,3},{3,0},{4,5},{5,6},{6,7},{7,4},{8,9},{9,10},{10,1... | collective-permute-start | bytes 294920 | tf_op jit(solution)/shard_map/ppermute | solution.py:534
  79.7 2.6 %collective-permute-start.6 = (bf16[192,256]{1,0:T(8,128)(2,1)S(1)}, bf16[192,256]{1,0:T(8,128)(2,1)S(1)}, u32[]{:S(2)}, u32[]{:S(2)}) collective-permute-start(bf16[192,256]{1,0:T(8,128)(2,1)S(1)} %get-tuple-element.54), channel_id=1, source_target_pairs={{0,2},{1,3},{2,0},{3,1},{4,6},{5,7},{6,4},{7,5},{8,10},{9,11},{10,... | collective-permute-start | bytes 294920 | tf_op jit(solution)/shard_map/ppermute | solution.py:534
  82.3 1.1 collective-permute-start.7
  83.3 0.9 collective-permute-start.13
  84.3 2.0 %collective-permute-done.6 = bf16[192,256]{1,0:T(8,128)(2,1)S(1)} collective-permute-done((bf16[192,256]{1,0:T(8,128)(2,1)S(1)}, bf16[192,256]{1,0:T(8,128)(2,1)S(1)}, u32[]{:S(2)}, u32[]{:S(2)}) %collective-permute-start.6) | collective-permute-done | bytes 98336 | tf_op jit(solution)/shard_map/ppermute | solution.py:534
  86.3 0.3 collective-permute-done.7
  86.6 0.1 convert_add_fusion.1
  86.7 4.7 %collective-permute-done.9 = bf16[4,9,48,128]{3,2,1,0:T(8,128)(2,1)S(1)} collective-permute-done((bf16[4,9,48,128]{3,2,1,0:T(8,128)(2,1)S(1)}, bf16[4,9,48,128]{3,2,1,0:T(8,128)(2,1)S(1)}, u32[]{:S(2)}, u32[]{:S(2)}) %collective-permute-start.9) | collective-permute-done | bytes 442400 | tf_op jit(solution)/shard_map/ppermute | solution.py:528
  91.4 1.5 %collective-permute-start.10 = (bf16[192,256]{1,0:T(8,128)(2,1)S(1)}, bf16[192,256]{1,0:T(8,128)(2,1)S(1)}, u32[]{:S(2)}, u32[]{:S(2)}) collective-permute-start(bf16[192,256]{1,0:T(8,128)(2,1)S(1)} %reduce-precision_convert_fusion.1), channel_id=1, source_target_pairs={{0,16},{4,20},{8,24},{12,28},{16,0},{20,4},{24,8},{28,12},{32,48},... | collective-permute-start | bytes 294920 | tf_op jit(solution)/shard_map/ppermute | solution.py:480
  92.9 4.5 %collective-permute-start.11 = (bf16[192,256]{1,0:T(8,128)(2,1)S(1)}, bf16[192,256]{1,0:T(8,128)(2,1)S(1)}, u32[]{:S(2)}, u32[]{:S(2)}) collective-permute-start(bf16[192,256]{1,0:T(8,128)(2,1)S(1)} %reduce-precision_convert_fusion.1), channel_id=1, source_target_pairs={{0,32},{4,36},{8,40},{12,44},{16,48},{20,52},{24,56},{28,60},{32,0... | collective-permute-start | bytes 294920 | tf_op jit(solution)/shard_map/ppermute | solution.py:480
  97.4 3.6 %collective-permute-done.11 = bf16[192,256]{1,0:T(8,128)(2,1)S(1)} collective-permute-done((bf16[192,256]{1,0:T(8,128)(2,1)S(1)}, bf16[192,256]{1,0:T(8,128)(2,1)S(1)}, u32[]{:S(2)}, u32[]{:S(2)}) %collective-permute-start.11) | collective-permute-done | bytes 98336 | tf_op jit(solution)/shard_map/ppermute | solution.py:480
  101.0 5.1 %collective-permute-done.12 = bf16[192,256]{1,0:T(8,128)(2,1)S(1)} collective-permute-done((bf16[192,256]{1,0:T(8,128)(2,1)S(1)}, bf16[192,256]{1,0:T(8,128)(2,1)S(1)}, u32[]{:S(2)}, u32[]{:S(2)}) %collective-permute-start.12) | collective-permute-done | bytes 98336 | tf_op jit(solution)/shard_map/ppermute | solution.py:480
  106.1 0.1 add_add_fusion.1
  106.2 0.1 collective-permute-start.14
  106.3 1.3 collective-permute-start.15
  107.6 2.5 %collective-permute-start.16 = (bf16[192,256]{1,0:T(8,128)(2,1)S(1)}, bf16[192,256]{1,0:T(8,128)(2,1)S(1)}, u32[]{:S(2)}, u32[]{:S(2)}) collective-permute-start(bf16[192,256]{1,0:T(8,128)(2,1)S(1)} %reduce-precision_convert_fusion), channel_id=1, source_target_pairs={{0,192},{4,196},{8,200},{12,204},{16,208},{20,212},{24,216},{28,22... | collective-permute-start | bytes 294920 | tf_op jit(solution)/shard_map/ppermute | solution.py:480
  110.1 0.2 convert_add_fusion
  110.3 0.1 fusion.3
  110.4 2.5 %collective-permute-start.17 = (bf16[9,48,128]{2,1,0:T(8,128)(2,1)S(1)}, bf16[9,48,128]{2,1,0:T(8,128)(2,1)S(1)}, u32[]{:S(2)}, u32[]{:S(2)}) collective-permute-start(bf16[9,48,128]{2,1,0:T(8,128)(2,1)S(1)} %get-tuple-element.75), channel_id=1, source_target_pairs={{0,16},{4,20},{8,24},{12,28},{16,32},{20,36},{24,40},{28,44},{32,4... | collective-permute-start | bytes 331784 | tf_op jit(solution)/shard_map/ppermute | solution.py:553
  112.9 4.3 %collective-permute-start.18 = (bf16[9,48,128]{2,1,0:T(8,128)(2,1)S(1)}, bf16[9,48,128]{2,1,0:T(8,128)(2,1)S(1)}, u32[]{:S(2)}, u32[]{:S(2)}) collective-permute-start(bf16[9,48,128]{2,1,0:T(8,128)(2,1)S(1)} %get-tuple-element.73), channel_id=1, source_target_pairs={{0,32},{4,36},{8,40},{12,44},{16,48},{20,52},{24,56},{28,60},{32,0... | collective-permute-start | bytes 331784 | tf_op jit(solution)/shard_map/ppermute | solution.py:553
  117.2 0.1 add_add_fusion
  117.2 2.5 %collective-permute-done.17 = bf16[9,48,128]{2,1,0:T(8,128)(2,1)S(1)} collective-permute-done((bf16[9,48,128]{2,1,0:T(8,128)(2,1)S(1)}, bf16[9,48,128]{2,1,0:T(8,128)(2,1)S(1)}, u32[]{:S(2)}, u32[]{:S(2)}) %collective-permute-start.17) | collective-permute-done | bytes 110624 | tf_op jit(solution)/shard_map/ppermute | solution.py:553
  119.7 4.5 %collective-permute-done.18 = bf16[9,48,128]{2,1,0:T(8,128)(2,1)S(1)} collective-permute-done((bf16[9,48,128]{2,1,0:T(8,128)(2,1)S(1)}, bf16[9,48,128]{2,1,0:T(8,128)(2,1)S(1)}, u32[]{:S(2)}, u32[]{:S(2)}) %collective-permute-start.18) | collective-permute-done | bytes 110624 | tf_op jit(solution)/shard_map/ppermute | solution.py:553
  124.2 4.1 %collective-permute-start.20 = (bf16[192,256]{1,0:T(8,128)(2,1)S(1)}, bf16[192,256]{1,0:T(8,128)(2,1)S(1)}, u32[]{:S(2)}, u32[]{:S(2)}) collective-permute-start(bf16[192,256]{1,0:T(8,128)(2,1)S(1)} %add_add_fusion), channel_id=1, source_target_pairs={{0,4},{4,0},{8,12},{12,8},{16,20},{20,16},{24,28},{28,24},{32,36},... | collective-permute-start | bytes 294920 | tf_op jit(solution)/shard_map/ppermute | solution.py:480
  128.3 1.6 %collective-permute-start.22 = (bf16[192,256]{1,0:T(8,128)(2,1)S(1)}, bf16[192,256]{1,0:T(8,128)(2,1)S(1)}, u32[]{:S(2)}, u32[]{:S(2)}) collective-permute-start(bf16[192,256]{1,0:T(8,128)(2,1)S(1)} %add_add_fusion), channel_id=1, source_target_pairs={{0,12},{4,8},{8,4},{12,0},{16,28},{20,24},{24,20},{28,16},{32,44},... | collective-permute-start | bytes 294920 | tf_op jit(solution)/shard_map/ppermute | solution.py:480
  129.9 0.7 fusion.1
  130.7 2.0 %collective-permute-done.21 = bf16[192,256]{1,0:T(8,128)(2,1)S(1)} collective-permute-done((bf16[192,256]{1,0:T(8,128)(2,1)S(1)}, bf16[192,256]{1,0:T(8,128)(2,1)S(1)}, u32[]{:S(2)}, u32[]{:S(2)}) %collective-permute-start.21) | collective-permute-done | bytes 98336 | tf_op jit(solution)/shard_map/ppermute | solution.py:480
  132.7 2.2 %collective-permute-done.22 = bf16[192,256]{1,0:T(8,128)(2,1)S(1)} collective-permute-done((bf16[192,256]{1,0:T(8,128)(2,1)S(1)}, bf16[192,256]{1,0:T(8,128)(2,1)S(1)}, u32[]{:S(2)}, u32[]{:S(2)}) %collective-permute-start.22) | collective-permute-done | bytes 98336 | tf_op jit(solution)/shard_map/ppermute | solution.py:480
  135.0 0.1 maximum_convert_fusion
  135.0 0.2 slice.67
  135.2 0.2 slice.68
  135.4 0.2 copy.42
  135.5 0.2 copy.43
  135.7 1.1 copy.44
  136.8 0.6 pad_maximum_fusion.5
  (53 shorter events, 0.3 us)
Async XLA Ops:
  0.6 10.1 %copy-start.9 = (bf16[256,3,128]{2,0,1:T(8,128)(2,1)S(1)}, bf16[256,3,128]{2,0,1:T(8,128)(2,1)}, u32[]{:S(2)}) copy-start(bf16[256,3,128]{2,0,1:T(8,128)(2,1)} %param.21) | copy-start | bytes 589828
  0.6 15.0 %copy-start.11 = (s32[128,4]{0,1:T(4,128)S(1)}, s32[128,4]{0,1:T(4,128)}, u32[]{:S(2)}) copy-start(s32[128,4]{0,1:T(4,128)} %param.20) | copy-start | bytes 6148
  2.6 14.0 %copy-start.10 = (bf16[64,8,1,64]{3,1,0,2:T(8,128)(2,1)S(1)}, bf16[64,8,1,64]{3,1,0,2:T(8,128)(2,1)}, u32[]{:S(2)}) copy-start(bf16[64,8,1,64]{3,1,0,2:T(8,128)(2,1)} %constant.112.clone.1) | copy-start | bytes 196612
  3.3 1.3 collective-permute-start
  4.6 8.1 %collective-permute-start.1 = (bf16[2,64,256]{2,1,0:T(8,128)(2,1)S(1)}, bf16[2,64,256]{2,1,0:T(8,128)(2,1)S(1)}, u32[]{:S(2)}, u32[]{:S(2)}) collective-permute-start(bf16[2,64,256]{2,1,0:T(8,128)(2,1)S(1)} %pad_maximum_fusion.4), channel_id=1, source_target_pairs={{0,8},{4,12},{8,0},{12,4},{16,24},{20,28},{24,16},{28,20},{32,40},... | collective-permute-start | bytes 196616 | tf_op jit(solution)/shard_map/ppermute | solution.py:480
  10.7 5.0 %collective-permute-start.3 = (bf16[3,4,64,128]{3,2,1,0:T(8,128)(2,1)S(1)}, bf16[3,4,64,128]{3,2,1,0:T(8,128)(2,1)S(1)}, u32[]{:S(2)}, u32[]{:S(2)}) collective-permute-start(bf16[3,4,64,128]{3,2,1,0:T(8,128)(2,1)S(1)} %bitcast.85), channel_id=1, source_target_pairs={{0,4},{4,0},{8,12},{12,8},{16,20},{20,16},{24,28},{28,24},{32,36},... | collective-permute-start | bytes 589832 | tf_op jit(solution)/shard_map/ppermute | solution.py:480
  12.8 3.2 %collective-permute-start.2 = (bf16[4,64,256]{2,1,0:T(8,128)(2,1)S(1)}, bf16[4,64,256]{2,1,0:T(8,128)(2,1)S(1)}, u32[]{:S(2)}, u32[]{:S(2)}) collective-permute-start(bf16[4,64,256]{2,1,0:T(8,128)(2,1)S(1)} %pad_maximum_fusion.2), channel_id=1, source_target_pairs={{0,4},{4,0},{8,12},{12,8},{16,20},{20,16},{24,28},{28,24},{32,36},... | collective-permute-start | bytes 393224 | tf_op jit(solution)/shard_map/ppermute | solution.py:480
  18.6 23.1 %collective-permute-start.4 = (bf16[2,3,4,64,128]{4,3,2,1,0:T(8,128)(2,1)S(1)}, bf16[2,3,4,64,128]{4,3,2,1,0:T(8,128)(2,1)S(1)}, u32[]{:S(2)}, u32[]{:S(2)}) collective-permute-start(bf16[2,3,4,64,128]{4,3,2,1,0:T(8,128)(2,1)S(1)} %pad_maximum_fusion.1), channel_id=1, source_target_pairs={{0,8},{4,12},{8,0},{12,4},{16,24},{20,28},{24,16},{28,20},{32,40},... | collective-permute-start | bytes 1179656 | tf_op jit(solution)/shard_map/ppermute | solution.py:480
  20.3 21.4 %copy-start.5 = (s32[3]{0:T(128)S(1)}, s32[3]{0:T(128)}, u32[]{:S(2)}) copy-start(s32[3]{0:T(128)} %pad_add_fusion.ids) | copy-start | bytes 40
  20.3 21.4 %copy-start.6 = (f32[128]{0:T(128)S(1)}, f32[128]{0:T(128)}, u32[]{:S(2)}) copy-start(f32[128]{0:T(128)} %param.18) | copy-start | bytes 1540
  20.3 21.4 %copy-start.7 = (f32[128]{0:T(128)S(1)}, f32[128]{0:T(128)}, u32[]{:S(2)}) copy-start(f32[128]{0:T(128)} %param.19) | copy-start | bytes 1540
  41.7 30.2 %slice-start = ((s8[7077888]{0:T(1024)(128)(4,1)}), s8[4194304]{0:T(1024)(128)(4,1)S(1)}, s32[]{:S(2)}) async-start(s8[7077888]{0:T(1024)(128)(4,1)} %bitcast.75), calls=%async_computation | async-start | bytes 8388608
  41.8 0.9 copy-start.3
  42.7 19.7 %copy-start.8 = (bf16[768,1024]{1,0:T(8,128)(2,1)S(1)}, bf16[768,1024]{1,0:T(8,128)(2,1)}, u32[]{:S(2)}) copy-start(bf16[768,1024]{1,0:T(8,128)(2,1)} %get-tuple-element.42.hid) | copy-start | bytes 4718596
  42.7 29.3 %slice-start.1 = ((s8[7077888]{0:T(1024)(128)(4,1)}), s8[2883584]{0:T(1024)(128)(4,1)S(1)}, s32[]{:S(2)}) async-start(s8[7077888]{0:T(1024)(128)(4,1)} %bitcast.75), calls=%async_computation.1 | async-start | bytes 5767168
  62.4 9.5 %copy-start = (bf16[256,1024]{1,0:T(8,128)(2,1)S(1)}, bf16[256,1024]{1,0:T(8,128)(2,1)}, u32[]{:S(2)}) copy-start(bf16[256,1024]{1,0:T(8,128)(2,1)} %copy.35.pext) | copy-start | bytes 1572868
  62.5 9.5 %copy-start.1 = (bf16[768,1024]{1,0:T(8,128)(2,1)S(1)}, bf16[768,1024]{1,0:T(8,128)(2,1)}, u32[]{:S(2)}) copy-start(bf16[768,1024]{1,0:T(8,128)(2,1)} %get-tuple-element.48.nrm) | copy-start | bytes 4718596
  62.5 9.5 %copy-start.2 = (f32[768,128]{1,0:T(8,128)S(1)}, f32[768,128]{1,0:T(8,128)}, u32[]{:S(2)}) copy-start(f32[768,128]{1,0:T(8,128)} %get-tuple-element.49.sc) | copy-start | bytes 1179652
  62.5 9.5 %copy-start.4 = (f32[8,1024]{1,0:T(8,128)S(1)}, f32[8,1024]{1,0:T(8,128)}, u32[]{:S(2)}) copy-start(f32[8,1024]{1,0:T(8,128)} %get-tuple-element.51.inv) | copy-start | bytes 98308
  65.7 21.0 %collective-permute-start.8 = (bf16[4,9,48,128]{3,2,1,0:T(8,128)(2,1)S(1)}, bf16[4,9,48,128]{3,2,1,0:T(8,128)(2,1)S(1)}, u32[]{:S(2)}, u32[]{:S(2)}) collective-permute-start(bf16[4,9,48,128]{3,2,1,0:T(8,128)(2,1)S(1)} %get-tuple-element.56), channel_id=1, source_target_pairs={{0,64},{4,68},{8,72},{12,76},{16,80},{20,84},{24,88},{28,92},{32,9... | collective-permute-start | bytes 1327112 | tf_op jit(solution)/shard_map/ppermute | solution.py:528
  69.2 22.2 %collective-permute-start.9 = (bf16[4,9,48,128]{3,2,1,0:T(8,128)(2,1)S(1)}, bf16[4,9,48,128]{3,2,1,0:T(8,128)(2,1)S(1)}, u32[]{:S(2)}, u32[]{:S(2)}) collective-permute-start(bf16[4,9,48,128]{3,2,1,0:T(8,128)(2,1)S(1)} %get-tuple-element.57), channel_id=1, source_target_pairs={{0,128},{4,132},{8,136},{12,140},{16,144},{20,148},{24,152},{28,15... | collective-permute-start | bytes 1327112 | tf_op jit(solution)/shard_map/ppermute | solution.py:528
  78.3 5.1 %collective-permute-start.5 = (bf16[192,256]{1,0:T(8,128)(2,1)S(1)}, bf16[192,256]{1,0:T(8,128)(2,1)S(1)}, u32[]{:S(2)}, u32[]{:S(2)}) collective-permute-start(bf16[192,256]{1,0:T(8,128)(2,1)S(1)} %get-tuple-element.53), channel_id=1, source_target_pairs={{0,1},{1,2},{2,3},{3,0},{4,5},{5,6},{6,7},{7,4},{8,9},{9,10},{10,1... | collective-permute-start | bytes 294920 | tf_op jit(solution)/shard_map/ppermute | solution.py:534
  79.7 6.6 %collective-permute-start.6 = (bf16[192,256]{1,0:T(8,128)(2,1)S(1)}, bf16[192,256]{1,0:T(8,128)(2,1)S(1)}, u32[]{:S(2)}, u32[]{:S(2)}) collective-permute-start(bf16[192,256]{1,0:T(8,128)(2,1)S(1)} %get-tuple-element.54), channel_id=1, source_target_pairs={{0,2},{1,3},{2,0},{3,1},{4,6},{5,7},{6,4},{7,5},{8,10},{9,11},{10,... | collective-permute-start | bytes 294920 | tf_op jit(solution)/shard_map/ppermute | solution.py:534
  82.3 4.3 %collective-permute-start.7 = (bf16[192,256]{1,0:T(8,128)(2,1)S(1)}, bf16[192,256]{1,0:T(8,128)(2,1)S(1)}, u32[]{:S(2)}, u32[]{:S(2)}) collective-permute-start(bf16[192,256]{1,0:T(8,128)(2,1)S(1)} %get-tuple-element.55), channel_id=1, source_target_pairs={{0,3},{1,0},{2,1},{3,2},{4,7},{5,4},{6,5},{7,6},{8,11},{9,8},{10,9... | collective-permute-start | bytes 294920 | tf_op jit(solution)/shard_map/ppermute | solution.py:534
  83.3 22.8 %collective-permute-start.13 = (bf16[4,9,48,128]{3,2,1,0:T(8,128)(2,1)S(1)}, bf16[4,9,48,128]{3,2,1,0:T(8,128)(2,1)S(1)}, u32[]{:S(2)}, u32[]{:S(2)}) collective-permute-start(bf16[4,9,48,128]{3,2,1,0:T(8,128)(2,1)S(1)} %get-tuple-element.61), channel_id=1, source_target_pairs={{0,192},{4,196},{8,200},{12,204},{16,208},{20,212},{24,216},{28,22... | collective-permute-start | bytes 1327112 | tf_op jit(solution)/shard_map/ppermute | solution.py:528
  91.4 6.0 %collective-permute-start.10 = (bf16[192,256]{1,0:T(8,128)(2,1)S(1)}, bf16[192,256]{1,0:T(8,128)(2,1)S(1)}, u32[]{:S(2)}, u32[]{:S(2)}) collective-permute-start(bf16[192,256]{1,0:T(8,128)(2,1)S(1)} %reduce-precision_convert_fusion.1), channel_id=1, source_target_pairs={{0,16},{4,20},{8,24},{12,28},{16,0},{20,4},{24,8},{28,12},{32,48},... | collective-permute-start | bytes 294920 | tf_op jit(solution)/shard_map/ppermute | solution.py:480
  92.9 8.1 %collective-permute-start.11 = (bf16[192,256]{1,0:T(8,128)(2,1)S(1)}, bf16[192,256]{1,0:T(8,128)(2,1)S(1)}, u32[]{:S(2)}, u32[]{:S(2)}) collective-permute-start(bf16[192,256]{1,0:T(8,128)(2,1)S(1)} %reduce-precision_convert_fusion.1), channel_id=1, source_target_pairs={{0,32},{4,36},{8,40},{12,44},{16,48},{20,52},{24,56},{28,60},{32,0... | collective-permute-start | bytes 294920 | tf_op jit(solution)/shard_map/ppermute | solution.py:480
  97.4 8.7 %collective-permute-start.12 = (bf16[192,256]{1,0:T(8,128)(2,1)S(1)}, bf16[192,256]{1,0:T(8,128)(2,1)S(1)}, u32[]{:S(2)}, u32[]{:S(2)}) collective-permute-start(bf16[192,256]{1,0:T(8,128)(2,1)S(1)} %reduce-precision_convert_fusion.1), channel_id=1, source_target_pairs={{0,48},{4,52},{8,56},{12,60},{16,32},{20,36},{24,40},{28,44},{32,1... | collective-permute-start | bytes 294920 | tf_op jit(solution)/shard_map/ppermute | solution.py:480
  106.2 11.0 %collective-permute-start.14 = (bf16[192,256]{1,0:T(8,128)(2,1)S(1)}, bf16[192,256]{1,0:T(8,128)(2,1)S(1)}, u32[]{:S(2)}, u32[]{:S(2)}) collective-permute-start(bf16[192,256]{1,0:T(8,128)(2,1)S(1)} %reduce-precision_convert_fusion), channel_id=1, source_target_pairs={{0,64},{4,68},{8,72},{12,76},{16,80},{20,84},{24,88},{28,92},{32,9... | collective-permute-start | bytes 294920 | tf_op jit(solution)/shard_map/ppermute | solution.py:480
  106.3 10.9 %collective-permute-start.15 = (bf16[192,256]{1,0:T(8,128)(2,1)S(1)}, bf16[192,256]{1,0:T(8,128)(2,1)S(1)}, u32[]{:S(2)}, u32[]{:S(2)}) collective-permute-start(bf16[192,256]{1,0:T(8,128)(2,1)S(1)} %reduce-precision_convert_fusion), channel_id=1, source_target_pairs={{0,128},{4,132},{8,136},{12,140},{16,144},{20,148},{24,152},{28,15... | collective-permute-start | bytes 294920 | tf_op jit(solution)/shard_map/ppermute | solution.py:480
  107.6 9.6 %collective-permute-start.16 = (bf16[192,256]{1,0:T(8,128)(2,1)S(1)}, bf16[192,256]{1,0:T(8,128)(2,1)S(1)}, u32[]{:S(2)}, u32[]{:S(2)}) collective-permute-start(bf16[192,256]{1,0:T(8,128)(2,1)S(1)} %reduce-precision_convert_fusion), channel_id=1, source_target_pairs={{0,192},{4,196},{8,200},{12,204},{16,208},{20,212},{24,216},{28,22... | collective-permute-start | bytes 294920 | tf_op jit(solution)/shard_map/ppermute | solution.py:480
  110.4 9.3 %collective-permute-start.17 = (bf16[9,48,128]{2,1,0:T(8,128)(2,1)S(1)}, bf16[9,48,128]{2,1,0:T(8,128)(2,1)S(1)}, u32[]{:S(2)}, u32[]{:S(2)}) collective-permute-start(bf16[9,48,128]{2,1,0:T(8,128)(2,1)S(1)} %get-tuple-element.75), channel_id=1, source_target_pairs={{0,16},{4,20},{8,24},{12,28},{16,32},{20,36},{24,40},{28,44},{32,4... | collective-permute-start | bytes 331784 | tf_op jit(solution)/shard_map/ppermute | solution.py:553
  112.9 11.3 %collective-permute-start.18 = (bf16[9,48,128]{2,1,0:T(8,128)(2,1)S(1)}, bf16[9,48,128]{2,1,0:T(8,128)(2,1)S(1)}, u32[]{:S(2)}, u32[]{:S(2)}) collective-permute-start(bf16[9,48,128]{2,1,0:T(8,128)(2,1)S(1)} %get-tuple-element.73), channel_id=1, source_target_pairs={{0,32},{4,36},{8,40},{12,44},{16,48},{20,52},{24,56},{28,60},{32,0... | collective-permute-start | bytes 331784 | tf_op jit(solution)/shard_map/ppermute | solution.py:553
  117.1 12.8 %collective-permute-start.19 = (bf16[9,48,128]{2,1,0:T(8,128)(2,1)S(1)}, bf16[9,48,128]{2,1,0:T(8,128)(2,1)S(1)}, u32[]{:S(2)}, u32[]{:S(2)}) collective-permute-start(bf16[9,48,128]{2,1,0:T(8,128)(2,1)S(1)} %get-tuple-element.74), channel_id=1, source_target_pairs={{0,48},{4,52},{8,56},{12,60},{16,0},{20,4},{24,8},{28,12},{32,16},... | collective-permute-start | bytes 331784 | tf_op jit(solution)/shard_map/ppermute | solution.py:553
  124.2 6.5 %collective-permute-start.20 = (bf16[192,256]{1,0:T(8,128)(2,1)S(1)}, bf16[192,256]{1,0:T(8,128)(2,1)S(1)}, u32[]{:S(2)}, u32[]{:S(2)}) collective-permute-start(bf16[192,256]{1,0:T(8,128)(2,1)S(1)} %add_add_fusion), channel_id=1, source_target_pairs={{0,4},{4,0},{8,12},{12,8},{16,20},{20,16},{24,28},{28,24},{32,36},... | collective-permute-start | bytes 294920 | tf_op jit(solution)/shard_map/ppermute | solution.py:480
  128.3 4.4 %collective-permute-start.21 = (bf16[192,256]{1,0:T(8,128)(2,1)S(1)}, bf16[192,256]{1,0:T(8,128)(2,1)S(1)}, u32[]{:S(2)}, u32[]{:S(2)}) collective-permute-start(bf16[192,256]{1,0:T(8,128)(2,1)S(1)} %add_add_fusion), channel_id=1, source_target_pairs={{0,8},{4,12},{8,0},{12,4},{16,24},{20,28},{24,16},{28,20},{32,40},... | collective-permute-start | bytes 294920 | tf_op jit(solution)/shard_map/ppermute | solution.py:480
  128.3 6.6 %collective-permute-start.22 = (bf16[192,256]{1,0:T(8,128)(2,1)S(1)}, bf16[192,256]{1,0:T(8,128)(2,1)S(1)}, u32[]{:S(2)}, u32[]{:S(2)}) collective-permute-start(bf16[192,256]{1,0:T(8,128)(2,1)S(1)} %add_add_fusion), channel_id=1, source_target_pairs={{0,12},{4,8},{8,4},{12,0},{16,28},{20,24},{24,20},{28,16},{32,44},... | collective-permute-start | bytes 294920 | tf_op jit(solution)/shard_map/ppermute | solution.py:480

commit v6 on v5

--- a/solution.py
+++ b/solution.py
@@ -41,7 +41,7 @@
 
 
 def forward_kernel(
-    ids, pext, stem, bias, scale, shift, w9, proj, hid, nrm, inv_out, wv, scale_out, emb, hid_all, sw, w, sc, sh, sems
+    ids, pext, stem, bias, scale, shift, w9, proj, hid, nrm, inv_out, wv, scale_out, emb, hid_all, sw, w, sc, sh, px, sums, sems
 ):
     width, block = emb.shape
     share = hid.shape[0]
@@ -63,8 +63,16 @@
         fill = jnp.zeros((256 - pin, width), F32)
         for n in range(3):
             fill = jnp.where(row == n, parts[n].astype(F32), fill)
+        fill = jnp.where((row >= 8) & (row < 11), 1.0, fill)
         sw[0:pin, :] = stem[...]
         sw[pin:256, :] = fill.astype(BF16)
+        total = mm(jnp.ones((8, width), BF16), sw[...], NT) * (-1.0 / width)
+        row = lax.broadcasted_iota(jnp.int32, (8, 256), 0)
+        lane = lax.broadcasted_iota(jnp.int32, (8, 256), 1)
+        fill = jnp.zeros((8, 256), F32)
+        for n, part in enumerate(split3(total)):
+            fill = jnp.where(row == n, part.astype(F32), fill)
+        sums[...] = jnp.where(lane < pin + 3, fill, 0.0).astype(BF16)
         ones = jnp.ones((8, 128), BF16)
         row = lax.broadcasted_iota(jnp.int32, (8, width), 0)
         for value, column in ((1.0 + scale[...], sc), (shift[...], sh)):
@@ -77,39 +85,34 @@
             at = pl.ds(pl.multiple_of(4 * rows * g + rows * j, 16), rows)
             scale_out[g * rows : (g + 1) * rows, :] = sc[at, :]
 
-    step = width // 4
-    for n in range(4):
-        emb[n * step : (n + 1) * step, :] = mm(sw[:, n * step : (n + 1) * step], pext[...], TN)
-    chunk = 64
-
-    def add(i, acc):
-        x = emb[pl.ds(pl.multiple_of(i * chunk, chunk), chunk), :]
-        return acc + jnp.sum(x.reshape(chunk // 8, 8, block), axis=0)
-
-    total = lax.fori_loop(0, width // chunk, add, jnp.zeros((8, block), F32), unroll=2)
-    mu = jnp.sum(total, axis=0, keepdims=True) * (1.0 / width)
-
-    def add_squares(i, acc):
-        x = emb[pl.ds(pl.multiple_of(i * chunk, chunk), chunk), :] - mu
-        return acc + jnp.sum((x * x).reshape(chunk // 8, 8, block), axis=0)
-
-    total = lax.fori_loop(0, width // chunk, add_squares, jnp.zeros((8, block), F32), unroll=2)
+    shift_row = jnp.sum(mm(sums[...], pext[...]), axis=0, keepdims=True)
+    row = lax.broadcasted_iota(jnp.int32, (256 - pin, block), 0)
+    tail = pext[pin:256, :].astype(F32)
+    for n, part in enumerate(split3(shift_row)):
+        tail = jnp.where(row == 8 + n, part.astype(F32), tail)
+    px[0:pin, :] = pext[0:pin, :]
+    px[pin:256, :] = tail.astype(BF16)
+    step = width // 24
+    total = jnp.zeros((8, block), F32)
+    for n in range(24):
+        x = mm(sw[:, n * step : (n + 1) * step], px[...], TN)
+        emb[n * step : (n + 1) * step, :] = x
+        total = total + jnp.sum((x * x).reshape(step // 8, 8, block), axis=0)
     inv = lax.rsqrt(jnp.sum(total, axis=0, keepdims=True) * (1.0 / width) + ln_eps)
     inv_out[...] = jnp.broadcast_to(inv, (8, block))
+    chunk = 64
 
     def normalise(i, carry):
         at = pl.ds(pl.multiple_of(i * chunk, chunk), chunk)
-        n = (emb[at, :] - mu) * inv
-        emb[at, :] = n
         wide = lambda ref: jnp.concatenate([ref[at, :]] * (block // 128), 1)
-        hid_all[at, :] = (n * wide(sc) + wide(sh)).astype(BF16)
+        hid_all[at, :] = (emb[at, :] * inv * wide(sc) + wide(sh)).astype(BF16)
         return carry
 
-    lax.fori_loop(0, width // chunk, normalise, 0, unroll=2)
+    lax.fori_loop(0, width // chunk, normalise, 0, unroll=4)
     for g in range(16):
         at = pl.ds(pl.multiple_of(4 * rows * g + rows * j, 16), rows)
         hid[g * rows : (g + 1) * rows, :] = hid_all[at, :]
-        nrm[g * rows : (g + 1) * rows, :] = emb[at, :].astype(BF16)
+        nrm[g * rows : (g + 1) * rows, :] = (emb[at, :] * inv).astype(BF16)
 
     @pl.when(first)
     def _():
@@ -162,6 +165,8 @@
                 pltpu.VMEM((width, columns), BF16),
                 pltpu.VMEM((width, 128), F32),
                 pltpu.VMEM((width, 128), F32),
+                pltpu.VMEM((256, block), BF16),
+                pltpu.VMEM((8, 256), BF16),
                 pltpu.SemaphoreType.DMA((count,)),
             ],
         ),

time: 137 us -> 135 us (0.985)
  Pallas kernels: 50.5 us -> 47.7 us
    pallas_call x1, Pallas kernels: 21.3 us -> 18.6 us  [forward(): pl.pallas_call(forward_kernel, grid_spec=pltpu.PrefetchScalarGridSpec(num...]
  transfers between devices with their start and end apart: 23 -> 23, of which waited for: 10 -> 10; matrix products, arithmetic and copies ran while one was open for 2% -> 2% of each run, Pallas kernels for 20% -> 18%
where the time goes in v6:
time: 135 us
  Pallas kernels  47.7 us (35%)
  starting transfers between devices  46.9 us (35%)
  waiting for transfers between devices  27.6 us (20%)
  local copies, waits for them, and re-layouts  8.41 us (6%)
  other arithmetic  2.95 us (2%)
    ppermute x13, starting transfers between devices, xor(): return lax.ppermute(value, 'seq', [(a, a ^ mask) for a in range(seq)])  27.2 us
    pallas_call x1, Pallas kernels, attention(): pl.pallas_call(attention_kernel, grid_spec=pltpu.PrefetchScalarGridSpec(n...  19.7 us
    pallas_call x1, Pallas kernels, forward(): pl.pallas_call(forward_kernel, grid_spec=pltpu.PrefetchScalarGridSpec(num...  18.6 us
    ppermute x13, waiting for transfers between devices, xor(): return lax.ppermute(value, 'seq', [(a, a ^ mask) for a in range(seq)])  13 us
    ppermute x3, waiting for transfers between devices, per_device(): part = lax.ppermute(part.astype(BF16), 'seq', pairs)  7.48 us
    ppermute x3, starting transfers between devices, per_device(): weight[k] = lax.ppermute(weight[k], 'seq', pairs)  7.22 us
    ppermute x3, starting transfers between devices, per_device(): part = lax.ppermute(part.astype(BF16), 'seq', pairs)  6.73 us
    pallas_call x1, Pallas kernels, stem_part(): pl.pallas_call(stem_kernel, grid_spec=pltpu.PrefetchScalarGridSpec(num_sc...  6.26 us
  transfers between devices with their start and end apart: 23, of which 10 were waited for; matrix products, arithmetic and copies ran while one was open for 2% of the time, Pallas kernels for 18%

profile of v6, /device:TPU:1, one launch (start us, length us, event | category | flops | bytes accessed | tf_op | source)
XLA Modules:
  0.0 134.6 jit_solution(14545123347926158425)
XLA Ops:
  0.7 1.0 copy.30
  1.6 1.0 copy.31
  2.6 0.0 copy-start.10
  2.6 0.7 reshape.83
  3.3 0.7 collective-permute-start
  4.0 0.7 stack_reshape.8
  4.6 6.0 %collective-permute-start.1 = (bf16[2,64,256]{2,1,0:T(8,128)(2,1)S(1)}, bf16[2,64,256]{2,1,0:T(8,128)(2,1)S(1)}, u32[]{:S(2)}, u32[]{:S(2)}) collective-permute-start(bf16[2,64,256]{2,1,0:T(8,128)(2,1)S(1)} %pad_maximum_fusion.4), channel_id=1, source_target_pairs={{0,8},{4,12},{8,0},{12,4},{16,24},{20,28},{24,16},{28,20},{32,40},... | collective-permute-start | bytes 196616 | tf_op jit(solution)/shard_map/ppermute | solution.py:485
  10.7 2.0 %collective-permute-start.3 = (bf16[3,4,64,128]{3,2,1,0:T(8,128)(2,1)S(1)}, bf16[3,4,64,128]{3,2,1,0:T(8,128)(2,1)S(1)}, u32[]{:S(2)}, u32[]{:S(2)}) collective-permute-start(bf16[3,4,64,128]{3,2,1,0:T(8,128)(2,1)S(1)} %bitcast.85), channel_id=1, source_target_pairs={{0,4},{4,0},{8,12},{12,8},{16,20},{20,16},{24,28},{28,24},{32,36},... | collective-permute-start | bytes 589832 | tf_op jit(solution)/shard_map/ppermute | solution.py:485
  12.8 2.2 %collective-permute-start.2 = (bf16[4,64,256]{2,1,0:T(8,128)(2,1)S(1)}, bf16[4,64,256]{2,1,0:T(8,128)(2,1)S(1)}, u32[]{:S(2)}, u32[]{:S(2)}) collective-permute-start(bf16[4,64,256]{2,1,0:T(8,128)(2,1)S(1)} %pad_maximum_fusion.2), channel_id=1, source_target_pairs={{0,4},{4,0},{8,12},{12,8},{16,20},{20,16},{24,28},{28,24},{32,36},... | collective-permute-start | bytes 393224 | tf_op jit(solution)/shard_map/ppermute | solution.py:485
  15.0 0.6 pad_add_fusion.ids
  15.6 0.1 copy.36.lists
  15.8 0.2 collective-permute-done.2
  16.0 0.1 concatenate.26
  16.2 0.1 concatenate.27
  16.3 0.1 concatenate.28
  16.5 0.1 concatenate.30
  16.6 0.2 maximum_maximum_fusion
  16.8 0.7 copy.34
  17.6 1.0 copy.35.pext
  18.6 1.7 %collective-permute-start.4 = (bf16[2,3,4,64,128]{4,3,2,1,0:T(8,128)(2,1)S(1)}, bf16[2,3,4,64,128]{4,3,2,1,0:T(8,128)(2,1)S(1)}, u32[]{:S(2)}, u32[]{:S(2)}) collective-permute-start(bf16[2,3,4,64,128]{4,3,2,1,0:T(8,128)(2,1)S(1)} %pad_maximum_fusion.1), channel_id=1, source_target_pairs={{0,8},{4,12},{8,0},{12,4},{16,24},{20,28},{24,16},{28,20},{32,40},... | collective-permute-start | bytes 1179656 | tf_op jit(solution)/shard_map/ppermute | solution.py:485
  20.3 18.6 %forward.1 = (f32[1024,1152]{1,0:T(8,128)}, bf16[768,1024]{1,0:T(8,128)(2,1)}, bf16[768,1024]{1,0:T(8,128)(2,1)}, f32[8,1024]{1,0:T(8,128)}, f32[8,1152]{1,0:T(8,128)}, /*index=5*/f32[768,128]{1,0:T(8,128)}) custom-call(s32[3]{0:T(128)} %pad_add_fusion.ids, bf16[256,1024]{1,0:T(8,128)(2,1)} %copy.35.pext, bf16[192,3072]{1,0:T(8,128)(2,1)} %stem.1, ...), custom_call_target="tpu_custom_call" | custom-call | flops 8858370048 | bytes 25165824 | tf_op jit(solution)/shard_map/forward/pallas_call | solution.py:140
  38.9 0.1 pad_maximum_fusion.og
  39.0 0.0 slice-start
  39.0 0.9 copy-done.3
  39.9 19.7 %attention.1 = (bf16[3,1024,384]{2,1,0:T(8,128)(2,1)S(1)}, f32[2,8,1024]{2,1,0:T(8,128)S(1)}) custom-call(s32[3]{0:T(128)S(1)} %copy-done.5, s32[128,4]{1,0:T(8,128)S(1)} %copy.36.lists, f32[1024,1152]{1,0:T(8,128)} %get-tuple-element.43.pq.pk.pv, f32[1024,1152]{1,0:T(8,128)} %get-tuple-element.43.pq.pk.pv, f32[1024,1152]{1,0:T(8,128)} %get-tuple-element.43.pq.pk.pv, ...), custom_call_target="tpu_custom_call" | custom-call | flops 2013265920 | bytes 10485760 | tf_op jit(solution)/shard_map/attention/pallas_call | solution.py:321
  59.7 3.2 %weight_part.1 = (bf16[4,9,48,128]{3,2,1,0:T(8,128)(2,1)S(1)}, bf16[4,9,48,128]{3,2,1,0:T(8,128)(2,1)S(1)}, bf16[4,9,48,128]{3,2,1,0:T(8,128)(2,1)S(1)}, bf16[4,9,48,128]{3,2,1,0:T(8,128)(2,1)S(1)}) custom-call(s32[3]{0:T(128)S(1)} %copy-done.5, bf16[768,1024]{1,0:T(8,128)(2,1)S(1)} %copy-done.8, bf16[3,1024,384]{2,1,0:T(8,128)(2,1)S(1)} %get-tuple-element.46.mixed), custom_call_target="tpu_custom_call" | custom-call | flops 1811939328 | bytes 6291456 | tf_op jit(solution)/shard_map/weight_part/pallas_call | solution.py:378
  62.9 3.5 %collective-permute-start.8 = (bf16[4,9,48,128]{3,2,1,0:T(8,128)(2,1)S(1)}, bf16[4,9,48,128]{3,2,1,0:T(8,128)(2,1)S(1)}, u32[]{:S(2)}, u32[]{:S(2)}) collective-permute-start(bf16[4,9,48,128]{3,2,1,0:T(8,128)(2,1)S(1)} %get-tuple-element.56), channel_id=1, source_target_pairs={{0,64},{4,68},{8,72},{12,76},{16,80},{20,84},{24,88},{28,92},{32,9... | collective-permute-start | bytes 1327112 | tf_op jit(solution)/shard_map/ppermute | solution.py:533
  66.4 2.9 %collective-permute-start.9 = (bf16[4,9,48,128]{3,2,1,0:T(8,128)(2,1)S(1)}, bf16[4,9,48,128]{3,2,1,0:T(8,128)(2,1)S(1)}, u32[]{:S(2)}, u32[]{:S(2)}) collective-permute-start(bf16[4,9,48,128]{3,2,1,0:T(8,128)(2,1)S(1)} %get-tuple-element.57), channel_id=1, source_target_pairs={{0,128},{4,132},{8,136},{12,140},{16,144},{20,148},{24,152},{28,15... | collective-permute-start | bytes 1327112 | tf_op jit(solution)/shard_map/ppermute | solution.py:533
  69.3 6.3 %stem_part.1 = (f32[192,256]{1,0:T(8,128)S(1)}, bf16[192,256]{1,0:T(8,128)(2,1)S(1)}, bf16[192,256]{1,0:T(8,128)(2,1)S(1)}, bf16[192,256]{1,0:T(8,128)(2,1)S(1)}) custom-call(s32[3]{0:T(128)S(1)} %copy-done.5, bf16[9,16,4,48,128]{4,3,2,1,0:T(8,128)(2,1)S(1)} %bitcast.77, bf16[3,1024,384]{2,1,0:T(8,128)(2,1)S(1)} %get-tuple-element.46.mixed, ...), custom_call_target="tpu_custom_call" | custom-call | flops 1000 | bytes 1000 | tf_op jit(solution)/shard_map/stem_part/pallas_call | solution.py:431
  75.6 1.4 %collective-permute-start.5 = (bf16[192,256]{1,0:T(8,128)(2,1)S(1)}, bf16[192,256]{1,0:T(8,128)(2,1)S(1)}, u32[]{:S(2)}, u32[]{:S(2)}) collective-permute-start(bf16[192,256]{1,0:T(8,128)(2,1)S(1)} %get-tuple-element.53), channel_id=1, source_target_pairs={{0,1},{1,2},{2,3},{3,0},{4,5},{5,6},{6,7},{7,4},{8,9},{9,10},{10,1... | collective-permute-start | bytes 294920 | tf_op jit(solution)/shard_map/ppermute | solution.py:539
  76.9 2.6 %collective-permute-start.6 = (bf16[192,256]{1,0:T(8,128)(2,1)S(1)}, bf16[192,256]{1,0:T(8,128)(2,1)S(1)}, u32[]{:S(2)}, u32[]{:S(2)}) collective-permute-start(bf16[192,256]{1,0:T(8,128)(2,1)S(1)} %get-tuple-element.54), channel_id=1, source_target_pairs={{0,2},{1,3},{2,0},{3,1},{4,6},{5,7},{6,4},{7,5},{8,10},{9,11},{10,... | collective-permute-start | bytes 294920 | tf_op jit(solution)/shard_map/ppermute | solution.py:539
  79.5 1.1 collective-permute-start.7
  80.6 0.9 collective-permute-start.13
  81.5 2.0 %collective-permute-done.6 = bf16[192,256]{1,0:T(8,128)(2,1)S(1)} collective-permute-done((bf16[192,256]{1,0:T(8,128)(2,1)S(1)}, bf16[192,256]{1,0:T(8,128)(2,1)S(1)}, u32[]{:S(2)}, u32[]{:S(2)}) %collective-permute-start.6) | collective-permute-done | bytes 98336 | tf_op jit(solution)/shard_map/ppermute | solution.py:539
  83.6 0.3 collective-permute-done.7
  83.9 0.1 convert_add_fusion.1
  84.0 4.7 %collective-permute-done.9 = bf16[4,9,48,128]{3,2,1,0:T(8,128)(2,1)S(1)} collective-permute-done((bf16[4,9,48,128]{3,2,1,0:T(8,128)(2,1)S(1)}, bf16[4,9,48,128]{3,2,1,0:T(8,128)(2,1)S(1)}, u32[]{:S(2)}, u32[]{:S(2)}) %collective-permute-start.9) | collective-permute-done | bytes 442400 | tf_op jit(solution)/shard_map/ppermute | solution.py:533
  88.7 1.4 %collective-permute-start.10 = (bf16[192,256]{1,0:T(8,128)(2,1)S(1)}, bf16[192,256]{1,0:T(8,128)(2,1)S(1)}, u32[]{:S(2)}, u32[]{:S(2)}) collective-permute-start(bf16[192,256]{1,0:T(8,128)(2,1)S(1)} %reduce-precision_convert_fusion.1), channel_id=1, source_target_pairs={{0,16},{4,20},{8,24},{12,28},{16,0},{20,4},{24,8},{28,12},{32,48},... | collective-permute-start | bytes 294920 | tf_op jit(solution)/shard_map/ppermute | solution.py:485
  90.1 4.5 %collective-permute-start.11 = (bf16[192,256]{1,0:T(8,128)(2,1)S(1)}, bf16[192,256]{1,0:T(8,128)(2,1)S(1)}, u32[]{:S(2)}, u32[]{:S(2)}) collective-permute-start(bf16[192,256]{1,0:T(8,128)(2,1)S(1)} %reduce-precision_convert_fusion.1), channel_id=1, source_target_pairs={{0,32},{4,36},{8,40},{12,44},{16,48},{20,52},{24,56},{28,60},{32,0... | collective-permute-start | bytes 294920 | tf_op jit(solution)/shard_map/ppermute | solution.py:485
  94.6 3.5 %collective-permute-done.11 = bf16[192,256]{1,0:T(8,128)(2,1)S(1)} collective-permute-done((bf16[192,256]{1,0:T(8,128)(2,1)S(1)}, bf16[192,256]{1,0:T(8,128)(2,1)S(1)}, u32[]{:S(2)}, u32[]{:S(2)}) %collective-permute-start.11) | collective-permute-done | bytes 98336 | tf_op jit(solution)/shard_map/ppermute | solution.py:485
  98.1 5.0 %collective-permute-done.12 = bf16[192,256]{1,0:T(8,128)(2,1)S(1)} collective-permute-done((bf16[192,256]{1,0:T(8,128)(2,1)S(1)}, bf16[192,256]{1,0:T(8,128)(2,1)S(1)}, u32[]{:S(2)}, u32[]{:S(2)}) %collective-permute-start.12) | collective-permute-done | bytes 98336 | tf_op jit(solution)/shard_map/ppermute | solution.py:485
  103.1 0.1 add_add_fusion.1
  103.2 0.1 collective-permute-start.14
  103.3 1.4 %collective-permute-start.15 = (bf16[192,256]{1,0:T(8,128)(2,1)S(1)}, bf16[192,256]{1,0:T(8,128)(2,1)S(1)}, u32[]{:S(2)}, u32[]{:S(2)}) collective-permute-start(bf16[192,256]{1,0:T(8,128)(2,1)S(1)} %reduce-precision_convert_fusion), channel_id=1, source_target_pairs={{0,128},{4,132},{8,136},{12,140},{16,144},{20,148},{24,152},{28,15... | collective-permute-start | bytes 294920 | tf_op jit(solution)/shard_map/ppermute | solution.py:485
  104.8 2.4 %collective-permute-start.16 = (bf16[192,256]{1,0:T(8,128)(2,1)S(1)}, bf16[192,256]{1,0:T(8,128)(2,1)S(1)}, u32[]{:S(2)}, u32[]{:S(2)}) collective-permute-start(bf16[192,256]{1,0:T(8,128)(2,1)S(1)} %reduce-precision_convert_fusion), channel_id=1, source_target_pairs={{0,192},{4,196},{8,200},{12,204},{16,208},{20,212},{24,216},{28,22... | collective-permute-start | bytes 294920 | tf_op jit(solution)/shard_map/ppermute | solution.py:485
  107.2 0.2 convert_add_fusion
  107.4 0.1 fusion.3
  107.5 2.7 %collective-permute-start.17 = (bf16[9,48,128]{2,1,0:T(8,128)(2,1)S(1)}, bf16[9,48,128]{2,1,0:T(8,128)(2,1)S(1)}, u32[]{:S(2)}, u32[]{:S(2)}) collective-permute-start(bf16[9,48,128]{2,1,0:T(8,128)(2,1)S(1)} %get-tuple-element.75), channel_id=1, source_target_pairs={{0,16},{4,20},{8,24},{12,28},{16,32},{20,36},{24,40},{28,44},{32,4... | collective-permute-start | bytes 331784 | tf_op jit(solution)/shard_map/ppermute | solution.py:558
  110.2 4.0 %collective-permute-start.18 = (bf16[9,48,128]{2,1,0:T(8,128)(2,1)S(1)}, bf16[9,48,128]{2,1,0:T(8,128)(2,1)S(1)}, u32[]{:S(2)}, u32[]{:S(2)}) collective-permute-start(bf16[9,48,128]{2,1,0:T(8,128)(2,1)S(1)} %get-tuple-element.73), channel_id=1, source_target_pairs={{0,32},{4,36},{8,40},{12,44},{16,48},{20,52},{24,56},{28,60},{32,0... | collective-permute-start | bytes 331784 | tf_op jit(solution)/shard_map/ppermute | solution.py:558
  114.2 0.1 add_add_fusion
  114.3 2.2 %collective-permute-done.17 = bf16[9,48,128]{2,1,0:T(8,128)(2,1)S(1)} collective-permute-done((bf16[9,48,128]{2,1,0:T(8,128)(2,1)S(1)}, bf16[9,48,128]{2,1,0:T(8,128)(2,1)S(1)}, u32[]{:S(2)}, u32[]{:S(2)}) %collective-permute-start.17) | collective-permute-done | bytes 110624 | tf_op jit(solution)/shard_map/ppermute | solution.py:558
  116.5 5.2 %collective-permute-done.18 = bf16[9,48,128]{2,1,0:T(8,128)(2,1)S(1)} collective-permute-done((bf16[9,48,128]{2,1,0:T(8,128)(2,1)S(1)}, bf16[9,48,128]{2,1,0:T(8,128)(2,1)S(1)}, u32[]{:S(2)}, u32[]{:S(2)}) %collective-permute-start.18) | collective-permute-done | bytes 110624 | tf_op jit(solution)/shard_map/ppermute | solution.py:558
  121.8 3.8 %collective-permute-start.20 = (bf16[192,256]{1,0:T(8,128)(2,1)S(1)}, bf16[192,256]{1,0:T(8,128)(2,1)S(1)}, u32[]{:S(2)}, u32[]{:S(2)}) collective-permute-start(bf16[192,256]{1,0:T(8,128)(2,1)S(1)} %add_add_fusion), channel_id=1, source_target_pairs={{0,4},{4,0},{8,12},{12,8},{16,20},{20,16},{24,28},{28,24},{32,36},... | collective-permute-start | bytes 294920 | tf_op jit(solution)/shard_map/ppermute | solution.py:485
  125.5 1.6 %collective-permute-start.22 = (bf16[192,256]{1,0:T(8,128)(2,1)S(1)}, bf16[192,256]{1,0:T(8,128)(2,1)S(1)}, u32[]{:S(2)}, u32[]{:S(2)}) collective-permute-start(bf16[192,256]{1,0:T(8,128)(2,1)S(1)} %add_add_fusion), channel_id=1, source_target_pairs={{0,12},{4,8},{8,4},{12,0},{16,28},{20,24},{24,20},{28,16},{32,44},... | collective-permute-start | bytes 294920 | tf_op jit(solution)/shard_map/ppermute | solution.py:485
  127.2 0.7 fusion.1
  127.9 2.0 %collective-permute-done.21 = bf16[192,256]{1,0:T(8,128)(2,1)S(1)} collective-permute-done((bf16[192,256]{1,0:T(8,128)(2,1)S(1)}, bf16[192,256]{1,0:T(8,128)(2,1)S(1)}, u32[]{:S(2)}, u32[]{:S(2)}) %collective-permute-start.21) | collective-permute-done | bytes 98336 | tf_op jit(solution)/shard_map/ppermute | solution.py:485
  129.9 2.2 %collective-permute-done.22 = bf16[192,256]{1,0:T(8,128)(2,1)S(1)} collective-permute-done((bf16[192,256]{1,0:T(8,128)(2,1)S(1)}, bf16[192,256]{1,0:T(8,128)(2,1)S(1)}, u32[]{:S(2)}, u32[]{:S(2)}) %collective-permute-start.22) | collective-permute-done | bytes 98336 | tf_op jit(solution)/shard_map/ppermute | solution.py:485
  132.2 0.1 maximum_convert_fusion
  132.3 0.2 slice.67
  132.4 0.2 slice.68
  132.6 0.2 copy.42
  132.7 0.2 copy.43
  132.9 1.1 copy.44
  134.0 0.6 pad_maximum_fusion.5
  (53 shorter events, 0.3 us)
Async XLA Ops:
  0.6 10.1 %copy-start.9 = (bf16[256,3,128]{2,0,1:T(8,128)(2,1)S(1)}, bf16[256,3,128]{2,0,1:T(8,128)(2,1)}, u32[]{:S(2)}) copy-start(bf16[256,3,128]{2,0,1:T(8,128)(2,1)} %param.21) | copy-start | bytes 589828
  0.6 15.0 %copy-start.11 = (s32[128,4]{0,1:T(4,128)S(1)}, s32[128,4]{0,1:T(4,128)}, u32[]{:S(2)}) copy-start(s32[128,4]{0,1:T(4,128)} %param.20) | copy-start | bytes 6148
  2.6 14.0 %copy-start.10 = (bf16[64,8,1,64]{3,1,0,2:T(8,128)(2,1)S(1)}, bf16[64,8,1,64]{3,1,0,2:T(8,128)(2,1)}, u32[]{:S(2)}) copy-start(bf16[64,8,1,64]{3,1,0,2:T(8,128)(2,1)} %constant.112.clone.1) | copy-start | bytes 196612
  3.3 1.3 collective-permute-start
  4.6 8.1 %collective-permute-start.1 = (bf16[2,64,256]{2,1,0:T(8,128)(2,1)S(1)}, bf16[2,64,256]{2,1,0:T(8,128)(2,1)S(1)}, u32[]{:S(2)}, u32[]{:S(2)}) collective-permute-start(bf16[2,64,256]{2,1,0:T(8,128)(2,1)S(1)} %pad_maximum_fusion.4), channel_id=1, source_target_pairs={{0,8},{4,12},{8,0},{12,4},{16,24},{20,28},{24,16},{28,20},{32,40},... | collective-permute-start | bytes 196616 | tf_op jit(solution)/shard_map/ppermute | solution.py:485
  10.7 5.0 %collective-permute-start.3 = (bf16[3,4,64,128]{3,2,1,0:T(8,128)(2,1)S(1)}, bf16[3,4,64,128]{3,2,1,0:T(8,128)(2,1)S(1)}, u32[]{:S(2)}, u32[]{:S(2)}) collective-permute-start(bf16[3,4,64,128]{3,2,1,0:T(8,128)(2,1)S(1)} %bitcast.85), channel_id=1, source_target_pairs={{0,4},{4,0},{8,12},{12,8},{16,20},{20,16},{24,28},{28,24},{32,36},... | collective-permute-start | bytes 589832 | tf_op jit(solution)/shard_map/ppermute | solution.py:485
  12.8 3.2 %collective-permute-start.2 = (bf16[4,64,256]{2,1,0:T(8,128)(2,1)S(1)}, bf16[4,64,256]{2,1,0:T(8,128)(2,1)S(1)}, u32[]{:S(2)}, u32[]{:S(2)}) collective-permute-start(bf16[4,64,256]{2,1,0:T(8,128)(2,1)S(1)} %pad_maximum_fusion.2), channel_id=1, source_target_pairs={{0,4},{4,0},{8,12},{12,8},{16,20},{20,16},{24,28},{28,24},{32,36},... | collective-permute-start | bytes 393224 | tf_op jit(solution)/shard_map/ppermute | solution.py:485
  18.6 20.3 %collective-permute-start.4 = (bf16[2,3,4,64,128]{4,3,2,1,0:T(8,128)(2,1)S(1)}, bf16[2,3,4,64,128]{4,3,2,1,0:T(8,128)(2,1)S(1)}, u32[]{:S(2)}, u32[]{:S(2)}) collective-permute-start(bf16[2,3,4,64,128]{4,3,2,1,0:T(8,128)(2,1)S(1)} %pad_maximum_fusion.1), channel_id=1, source_target_pairs={{0,8},{4,12},{8,0},{12,4},{16,24},{20,28},{24,16},{28,20},{32,40},... | collective-permute-start | bytes 1179656 | tf_op jit(solution)/shard_map/ppermute | solution.py:485
  20.3 18.7 %copy-start.5 = (s32[3]{0:T(128)S(1)}, s32[3]{0:T(128)}, u32[]{:S(2)}) copy-start(s32[3]{0:T(128)} %pad_add_fusion.ids) | copy-start | bytes 40
  20.3 18.7 %copy-start.6 = (f32[128]{0:T(128)S(1)}, f32[128]{0:T(128)}, u32[]{:S(2)}) copy-start(f32[128]{0:T(128)} %param.18) | copy-start | bytes 1540
  20.3 18.7 %copy-start.7 = (f32[128]{0:T(128)S(1)}, f32[128]{0:T(128)}, u32[]{:S(2)}) copy-start(f32[128]{0:T(128)} %param.19) | copy-start | bytes 1540
  39.0 30.3 %slice-start = ((s8[7077888]{0:T(1024)(128)(4,1)}), s8[4194304]{0:T(1024)(128)(4,1)S(1)}, s32[]{:S(2)}) async-start(s8[7077888]{0:T(1024)(128)(4,1)} %bitcast.75), calls=%async_computation | async-start | bytes 8388608
  39.0 0.9 copy-start.3
  39.9 19.7 %copy-start.8 = (bf16[768,1024]{1,0:T(8,128)(2,1)S(1)}, bf16[768,1024]{1,0:T(8,128)(2,1)}, u32[]{:S(2)}) copy-start(bf16[768,1024]{1,0:T(8,128)(2,1)} %get-tuple-element.42.hid) | copy-start | bytes 4718596
  39.9 29.3 %slice-start.1 = ((s8[7077888]{0:T(1024)(128)(4,1)}), s8[2883584]{0:T(1024)(128)(4,1)S(1)}, s32[]{:S(2)}) async-start(s8[7077888]{0:T(1024)(128)(4,1)} %bitcast.75), calls=%async_computation.1 | async-start | bytes 5767168
  59.7 9.6 %copy-start = (bf16[256,1024]{1,0:T(8,128)(2,1)S(1)}, bf16[256,1024]{1,0:T(8,128)(2,1)}, u32[]{:S(2)}) copy-start(bf16[256,1024]{1,0:T(8,128)(2,1)} %copy.35.pext) | copy-start | bytes 1572868
  59.7 9.6 %copy-start.1 = (bf16[768,1024]{1,0:T(8,128)(2,1)S(1)}, bf16[768,1024]{1,0:T(8,128)(2,1)}, u32[]{:S(2)}) copy-start(bf16[768,1024]{1,0:T(8,128)(2,1)} %get-tuple-element.48.nrm) | copy-start | bytes 4718596
  59.7 9.6 %copy-start.2 = (f32[768,128]{1,0:T(8,128)S(1)}, f32[768,128]{1,0:T(8,128)}, u32[]{:S(2)}) copy-start(f32[768,128]{1,0:T(8,128)} %get-tuple-element.49.sc) | copy-start | bytes 1179652
  59.7 9.6 %copy-start.4 = (f32[8,1024]{1,0:T(8,128)S(1)}, f32[8,1024]{1,0:T(8,128)}, u32[]{:S(2)}) copy-start(f32[8,1024]{1,0:T(8,128)} %get-tuple-element.51.inv) | copy-start | bytes 98308
  62.9 21.0 %collective-permute-start.8 = (bf16[4,9,48,128]{3,2,1,0:T(8,128)(2,1)S(1)}, bf16[4,9,48,128]{3,2,1,0:T(8,128)(2,1)S(1)}, u32[]{:S(2)}, u32[]{:S(2)}) collective-permute-start(bf16[4,9,48,128]{3,2,1,0:T(8,128)(2,1)S(1)} %get-tuple-element.56), channel_id=1, source_target_pairs={{0,64},{4,68},{8,72},{12,76},{16,80},{20,84},{24,88},{28,92},{32,9... | collective-permute-start | bytes 1327112 | tf_op jit(solution)/shard_map/ppermute | solution.py:533
  66.4 22.3 %collective-permute-start.9 = (bf16[4,9,48,128]{3,2,1,0:T(8,128)(2,1)S(1)}, bf16[4,9,48,128]{3,2,1,0:T(8,128)(2,1)S(1)}, u32[]{:S(2)}, u32[]{:S(2)}) collective-permute-start(bf16[4,9,48,128]{3,2,1,0:T(8,128)(2,1)S(1)} %get-tuple-element.57), channel_id=1, source_target_pairs={{0,128},{4,132},{8,136},{12,140},{16,144},{20,148},{24,152},{28,15... | collective-permute-start | bytes 1327112 | tf_op jit(solution)/shard_map/ppermute | solution.py:533
  75.6 5.1 %collective-permute-start.5 = (bf16[192,256]{1,0:T(8,128)(2,1)S(1)}, bf16[192,256]{1,0:T(8,128)(2,1)S(1)}, u32[]{:S(2)}, u32[]{:S(2)}) collective-permute-start(bf16[192,256]{1,0:T(8,128)(2,1)S(1)} %get-tuple-element.53), channel_id=1, source_target_pairs={{0,1},{1,2},{2,3},{3,0},{4,5},{5,6},{6,7},{7,4},{8,9},{9,10},{10,1... | collective-permute-start | bytes 294920 | tf_op jit(solution)/shard_map/ppermute | solution.py:539
  76.9 6.6 %collective-permute-start.6 = (bf16[192,256]{1,0:T(8,128)(2,1)S(1)}, bf16[192,256]{1,0:T(8,128)(2,1)S(1)}, u32[]{:S(2)}, u32[]{:S(2)}) collective-permute-start(bf16[192,256]{1,0:T(8,128)(2,1)S(1)} %get-tuple-element.54), channel_id=1, source_target_pairs={{0,2},{1,3},{2,0},{3,1},{4,6},{5,7},{6,4},{7,5},{8,10},{9,11},{10,... | collective-permute-start | bytes 294920 | tf_op jit(solution)/shard_map/ppermute | solution.py:539
  79.5 4.3 %collective-permute-start.7 = (bf16[192,256]{1,0:T(8,128)(2,1)S(1)}, bf16[192,256]{1,0:T(8,128)(2,1)S(1)}, u32[]{:S(2)}, u32[]{:S(2)}) collective-permute-start(bf16[192,256]{1,0:T(8,128)(2,1)S(1)} %get-tuple-element.55), channel_id=1, source_target_pairs={{0,3},{1,0},{2,1},{3,2},{4,7},{5,4},{6,5},{7,6},{8,11},{9,8},{10,9... | collective-permute-start | bytes 294920 | tf_op jit(solution)/shard_map/ppermute | solution.py:539
  80.6 22.6 %collective-permute-start.13 = (bf16[4,9,48,128]{3,2,1,0:T(8,128)(2,1)S(1)}, bf16[4,9,48,128]{3,2,1,0:T(8,128)(2,1)S(1)}, u32[]{:S(2)}, u32[]{:S(2)}) collective-permute-start(bf16[4,9,48,128]{3,2,1,0:T(8,128)(2,1)S(1)} %get-tuple-element.61), channel_id=1, source_target_pairs={{0,192},{4,196},{8,200},{12,204},{16,208},{20,212},{24,216},{28,22... | collective-permute-start | bytes 1327112 | tf_op jit(solution)/shard_map/ppermute | solution.py:533
  88.7 5.9 %collective-permute-start.10 = (bf16[192,256]{1,0:T(8,128)(2,1)S(1)}, bf16[192,256]{1,0:T(8,128)(2,1)S(1)}, u32[]{:S(2)}, u32[]{:S(2)}) collective-permute-start(bf16[192,256]{1,0:T(8,128)(2,1)S(1)} %reduce-precision_convert_fusion.1), channel_id=1, source_target_pairs={{0,16},{4,20},{8,24},{12,28},{16,0},{20,4},{24,8},{28,12},{32,48},... | collective-permute-start | bytes 294920 | tf_op jit(solution)/shard_map/ppermute | solution.py:485
  90.1 8.0 %collective-permute-start.11 = (bf16[192,256]{1,0:T(8,128)(2,1)S(1)}, bf16[192,256]{1,0:T(8,128)(2,1)S(1)}, u32[]{:S(2)}, u32[]{:S(2)}) collective-permute-start(bf16[192,256]{1,0:T(8,128)(2,1)S(1)} %reduce-precision_convert_fusion.1), channel_id=1, source_target_pairs={{0,32},{4,36},{8,40},{12,44},{16,48},{20,52},{24,56},{28,60},{32,0... | collective-permute-start | bytes 294920 | tf_op jit(solution)/shard_map/ppermute | solution.py:485
  94.6 8.6 %collective-permute-start.12 = (bf16[192,256]{1,0:T(8,128)(2,1)S(1)}, bf16[192,256]{1,0:T(8,128)(2,1)S(1)}, u32[]{:S(2)}, u32[]{:S(2)}) collective-permute-start(bf16[192,256]{1,0:T(8,128)(2,1)S(1)} %reduce-precision_convert_fusion.1), channel_id=1, source_target_pairs={{0,48},{4,52},{8,56},{12,60},{16,32},{20,36},{24,40},{28,44},{32,1... | collective-permute-start | bytes 294920 | tf_op jit(solution)/shard_map/ppermute | solution.py:485
  103.2 11.0 %collective-permute-start.14 = (bf16[192,256]{1,0:T(8,128)(2,1)S(1)}, bf16[192,256]{1,0:T(8,128)(2,1)S(1)}, u32[]{:S(2)}, u32[]{:S(2)}) collective-permute-start(bf16[192,256]{1,0:T(8,128)(2,1)S(1)} %reduce-precision_convert_fusion), channel_id=1, source_target_pairs={{0,64},{4,68},{8,72},{12,76},{16,80},{20,84},{24,88},{28,92},{32,9... | collective-permute-start | bytes 294920 | tf_op jit(solution)/shard_map/ppermute | solution.py:485
  103.3 10.9 %collective-permute-start.15 = (bf16[192,256]{1,0:T(8,128)(2,1)S(1)}, bf16[192,256]{1,0:T(8,128)(2,1)S(1)}, u32[]{:S(2)}, u32[]{:S(2)}) collective-permute-start(bf16[192,256]{1,0:T(8,128)(2,1)S(1)} %reduce-precision_convert_fusion), channel_id=1, source_target_pairs={{0,128},{4,132},{8,136},{12,140},{16,144},{20,148},{24,152},{28,15... | collective-permute-start | bytes 294920 | tf_op jit(solution)/shard_map/ppermute | solution.py:485
  104.8 9.5 %collective-permute-start.16 = (bf16[192,256]{1,0:T(8,128)(2,1)S(1)}, bf16[192,256]{1,0:T(8,128)(2,1)S(1)}, u32[]{:S(2)}, u32[]{:S(2)}) collective-permute-start(bf16[192,256]{1,0:T(8,128)(2,1)S(1)} %reduce-precision_convert_fusion), channel_id=1, source_target_pairs={{0,192},{4,196},{8,200},{12,204},{16,208},{20,212},{24,216},{28,22... | collective-permute-start | bytes 294920 | tf_op jit(solution)/shard_map/ppermute | solution.py:485
  107.5 9.0 %collective-permute-start.17 = (bf16[9,48,128]{2,1,0:T(8,128)(2,1)S(1)}, bf16[9,48,128]{2,1,0:T(8,128)(2,1)S(1)}, u32[]{:S(2)}, u32[]{:S(2)}) collective-permute-start(bf16[9,48,128]{2,1,0:T(8,128)(2,1)S(1)} %get-tuple-element.75), channel_id=1, source_target_pairs={{0,16},{4,20},{8,24},{12,28},{16,32},{20,36},{24,40},{28,44},{32,4... | collective-permute-start | bytes 331784 | tf_op jit(solution)/shard_map/ppermute | solution.py:558
  110.2 11.6 %collective-permute-start.18 = (bf16[9,48,128]{2,1,0:T(8,128)(2,1)S(1)}, bf16[9,48,128]{2,1,0:T(8,128)(2,1)S(1)}, u32[]{:S(2)}, u32[]{:S(2)}) collective-permute-start(bf16[9,48,128]{2,1,0:T(8,128)(2,1)S(1)} %get-tuple-element.73), channel_id=1, source_target_pairs={{0,32},{4,36},{8,40},{12,44},{16,48},{20,52},{24,56},{28,60},{32,0... | collective-permute-start | bytes 331784 | tf_op jit(solution)/shard_map/ppermute | solution.py:558
  114.2 12.9 %collective-permute-start.19 = (bf16[9,48,128]{2,1,0:T(8,128)(2,1)S(1)}, bf16[9,48,128]{2,1,0:T(8,128)(2,1)S(1)}, u32[]{:S(2)}, u32[]{:S(2)}) collective-permute-start(bf16[9,48,128]{2,1,0:T(8,128)(2,1)S(1)} %get-tuple-element.74), channel_id=1, source_target_pairs={{0,48},{4,52},{8,56},{12,60},{16,0},{20,4},{24,8},{28,12},{32,16},... | collective-permute-start | bytes 331784 | tf_op jit(solution)/shard_map/ppermute | solution.py:558
  121.8 6.1 %collective-permute-start.20 = (bf16[192,256]{1,0:T(8,128)(2,1)S(1)}, bf16[192,256]{1,0:T(8,128)(2,1)S(1)}, u32[]{:S(2)}, u32[]{:S(2)}) collective-permute-start(bf16[192,256]{1,0:T(8,128)(2,1)S(1)} %add_add_fusion), channel_id=1, source_target_pairs={{0,4},{4,0},{8,12},{12,8},{16,20},{20,16},{24,28},{28,24},{32,36},... | collective-permute-start | bytes 294920 | tf_op jit(solution)/shard_map/ppermute | solution.py:485
  125.5 4.4 %collective-permute-start.21 = (bf16[192,256]{1,0:T(8,128)(2,1)S(1)}, bf16[192,256]{1,0:T(8,128)(2,1)S(1)}, u32[]{:S(2)}, u32[]{:S(2)}) collective-permute-start(bf16[192,256]{1,0:T(8,128)(2,1)S(1)} %add_add_fusion), channel_id=1, source_target_pairs={{0,8},{4,12},{8,0},{12,4},{16,24},{20,28},{24,16},{28,20},{32,40},... | collective-permute-start | bytes 294920 | tf_op jit(solution)/shard_map/ppermute | solution.py:485
  125.5 6.6 %collective-permute-start.22 = (bf16[192,256]{1,0:T(8,128)(2,1)S(1)}, bf16[192,256]{1,0:T(8,128)(2,1)S(1)}, u32[]{:S(2)}, u32[]{:S(2)}) collective-permute-start(bf16[192,256]{1,0:T(8,128)(2,1)S(1)} %add_add_fusion), channel_id=1, source_target_pairs={{0,12},{4,8},{8,4},{12,0},{16,28},{20,24},{24,20},{28,16},{32,44},... | collective-permute-start | bytes 294920 | tf_op jit(solution)/shard_map/ppermute | solution.py:485

commit v7 on v6

--- a/solution.py
+++ b/solution.py
@@ -524,6 +524,7 @@
     proj, hid, nrm, inv, wv, sc = forward(
         ids, pext, stem_weight, stem_bias[None], mod_scale[None], mod_shift[None], w9
     )
+    wv = pltpu.with_memory_space_constraint(wv, pltpu.HBM)
     mixed, means = attention(ids, tile_lists, proj, grads, q_gain[None], k_gain[None], wv)
     weight = list(weight_part(ids, hid, mixed, hd))
     stem = stem_part(ids, w9, mixed, nrm, sc, means, inv, pext)
@@ -544,9 +545,9 @@
         near, far, both = (xor(sent, mask).astype(F32) for mask in (low, high, low + high))
         return (held + near) + (far + both)
 
-    total, weight[1], weight[2] = lax.optimization_barrier((total, weight[1], weight[2]))
+    total, weight[1], weight[3] = lax.optimization_barrier((total, weight[1], weight[3]))
     total = quad_sum(total, 4, 8)
-    total, weight[3] = lax.optimization_barrier((total, weight[3]))
+    total, weight[2] = lax.optimization_barrier((total, weight[2]))
     weight_total = sum(part.astype(F32) for part in weight)
 
     zhi = g % 4

time: 135 us -> 129 us (0.956)
  waiting for transfers between devices: 27.6 us -> 20.8 us
    ppermute x3, waiting for transfers between devices: 4.7 us -> 0.01 us  [per_device(): weight[k] = lax.ppermute(weight[k], 'seq', pairs)]
    ppermute x13, starting transfers between devices: 27.2 us -> 28.9 us  [xor(): return lax.ppermute(value, 'seq', [(a, a ^ mask) for a in range(seq)])]
    unnamed x31 -> x29, local copies, waits for them, and re-layouts: 3.13 us -> 2.22 us
  transfers between devices with their start and end apart: 23 -> 23, of which waited for: 10 -> 8; matrix products, arithmetic and copies ran while one was open for 2% -> 2% of each run, Pallas kernels for 18% -> 19%
where the time goes in v7:
time: 129 us
  Pallas kernels  48.6 us (38%)
  starting transfers between devices  47.9 us (37%)
  waiting for transfers between devices  20.8 us (16%)
  local copies, waits for them, and re-layouts  7.5 us (6%)
  other arithmetic  2.99 us (2%)
    ppermute x13, starting transfers between devices, xor(): return lax.ppermute(value, 'seq', [(a, a ^ mask) for a in range(seq)])  28.9 us
    pallas_call x1, Pallas kernels, attention(): pl.pallas_call(attention_kernel, grid_spec=pltpu.PrefetchScalarGridSpec(n...  20.6 us
    pallas_call x1, Pallas kernels, forward(): pl.pallas_call(forward_kernel, grid_spec=pltpu.PrefetchScalarGridSpec(num...  18.6 us
    ppermute x13, waiting for transfers between devices, xor(): return lax.ppermute(value, 'seq', [(a, a ^ mask) for a in range(seq)])  12.4 us
    ppermute x3, starting transfers between devices, per_device(): part = lax.ppermute(part.astype(BF16), 'seq', pairs)  6.73 us
    ppermute x3, waiting for transfers between devices, per_device(): part = lax.ppermute(part.astype(BF16), 'seq', pairs)  6.73 us
    ppermute x3, starting transfers between devices, per_device(): weight[k] = lax.ppermute(weight[k], 'seq', pairs)  6.49 us
    pallas_call x1, Pallas kernels, stem_part(): pl.pallas_call(stem_kernel, grid_spec=pltpu.PrefetchScalarGridSpec(num_sc...  6.26 us
  transfers between devices with their start and end apart: 23, of which 8 were waited for; matrix products, arithmetic and copies ran while one was open for 2% of the time, Pallas kernels for 19%

profile of v7, /device:TPU:1, one launch (start us, length us, event | category | flops | bytes accessed | tf_op | source)
XLA Modules:
  0.0 128.8 jit_solution(2855916023379000430)
XLA Ops:
  0.7 1.0 copy.30
  1.6 1.0 copy.31
  2.6 0.0 copy-start.9
  2.6 0.7 reshape.83
  3.3 0.7 collective-permute-start
  4.0 0.7 stack_reshape.8
  4.6 0.0 collective-permute-done
  4.6 6.0 %collective-permute-start.1 = (bf16[2,64,256]{2,1,0:T(8,128)(2,1)S(1)}, bf16[2,64,256]{2,1,0:T(8,128)(2,1)S(1)}, u32[]{:S(2)}, u32[]{:S(2)}) collective-permute-start(bf16[2,64,256]{2,1,0:T(8,128)(2,1)S(1)} %pad_maximum_fusion.4), channel_id=1, source_target_pairs={{0,8},{4,12},{8,0},{12,4},{16,24},{20,28},{24,16},{28,20},{32,40},... | collective-permute-start | bytes 196616 | tf_op jit(solution)/shard_map/ppermute | solution.py:485
  10.7 2.0 %collective-permute-start.3 = (bf16[3,4,64,128]{3,2,1,0:T(8,128)(2,1)S(1)}, bf16[3,4,64,128]{3,2,1,0:T(8,128)(2,1)S(1)}, u32[]{:S(2)}, u32[]{:S(2)}) collective-permute-start(bf16[3,4,64,128]{3,2,1,0:T(8,128)(2,1)S(1)} %bitcast.85), channel_id=1, source_target_pairs={{0,4},{4,0},{8,12},{12,8},{16,20},{20,16},{24,28},{28,24},{32,36},... | collective-permute-start | bytes 589832 | tf_op jit(solution)/shard_map/ppermute | solution.py:485
  12.7 0.0 collective-permute-done.1
  12.8 2.2 %collective-permute-start.2 = (bf16[4,64,256]{2,1,0:T(8,128)(2,1)S(1)}, bf16[4,64,256]{2,1,0:T(8,128)(2,1)S(1)}, u32[]{:S(2)}, u32[]{:S(2)}) collective-permute-start(bf16[4,64,256]{2,1,0:T(8,128)(2,1)S(1)} %pad_maximum_fusion.2), channel_id=1, source_target_pairs={{0,4},{4,0},{8,12},{12,8},{16,20},{20,16},{24,28},{28,24},{32,36},... | collective-permute-start | bytes 393224 | tf_op jit(solution)/shard_map/ppermute | solution.py:485
  15.0 0.7 pad_add_fusion.ids
  15.7 0.1 copy.36.lists
  15.8 0.2 collective-permute-done.2
  16.0 0.1 concatenate.26
  16.2 0.1 concatenate.27
  16.3 0.1 concatenate.28
  16.5 0.1 concatenate.30
  16.6 0.2 maximum_maximum_fusion
  16.8 0.7 copy.34
  17.6 1.0 copy.35.pext
  18.6 1.7 %collective-permute-start.4 = (bf16[2,3,4,64,128]{4,3,2,1,0:T(8,128)(2,1)S(1)}, bf16[2,3,4,64,128]{4,3,2,1,0:T(8,128)(2,1)S(1)}, u32[]{:S(2)}, u32[]{:S(2)}) collective-permute-start(bf16[2,3,4,64,128]{4,3,2,1,0:T(8,128)(2,1)S(1)} %pad_maximum_fusion.1), channel_id=1, source_target_pairs={{0,8},{4,12},{8,0},{12,4},{16,24},{20,28},{24,16},{28,20},{32,40},... | collective-permute-start | bytes 1179656 | tf_op jit(solution)/shard_map/ppermute | solution.py:485
  20.3 18.6 %forward.1 = (f32[1024,1152]{1,0:T(8,128)}, bf16[768,1024]{1,0:T(8,128)(2,1)}, bf16[768,1024]{1,0:T(8,128)(2,1)}, f32[8,1024]{1,0:T(8,128)}, f32[8,1152]{1,0:T(8,128)}, /*index=5*/f32[768,128]{1,0:T(8,128)}) custom-call(s32[3]{0:T(128)} %pad_add_fusion.ids, bf16[256,1024]{1,0:T(8,128)(2,1)} %copy.35.pext, bf16[192,3072]{1,0:T(8,128)(2,1)} %stem.1, ...), custom_call_target="tpu_custom_call" | custom-call | flops 8858370048 | bytes 25165824 | tf_op jit(solution)/shard_map/forward/pallas_call | solution.py:140
  38.9 0.1 pad_maximum_fusion.og
  39.0 0.0 slice-start
  39.0 20.6 %attention.1 = (bf16[3,1024,384]{2,1,0:T(8,128)(2,1)S(1)}, f32[2,8,1024]{2,1,0:T(8,128)S(1)}) custom-call(s32[3]{0:T(128)S(1)} %copy-done.4, s32[128,4]{1,0:T(8,128)S(1)} %copy.36.lists, f32[1024,1152]{1,0:T(8,128)} %get-tuple-element.43.pq.pk.pv, f32[1024,1152]{1,0:T(8,128)} %get-tuple-element.43.pq.pk.pv, f32[1024,1152]{1,0:T(8,128)} %get-tuple-element.43.pq.pk.pv, ...), custom_call_target="tpu_custom_call" | custom-call | flops 2013265920 | bytes 10485760 | tf_op jit(solution)/shard_map/attention/pallas_call | solution.py:321
  59.6 0.0 copy-start
  59.7 3.2 %weight_part.1 = (bf16[4,9,48,128]{3,2,1,0:T(8,128)(2,1)S(1)}, bf16[4,9,48,128]{3,2,1,0:T(8,128)(2,1)S(1)}, bf16[4,9,48,128]{3,2,1,0:T(8,128)(2,1)S(1)}, bf16[4,9,48,128]{3,2,1,0:T(8,128)(2,1)S(1)}) custom-call(s32[3]{0:T(128)S(1)} %copy-done.4, bf16[768,1024]{1,0:T(8,128)(2,1)S(1)} %copy-done.7, bf16[3,1024,384]{2,1,0:T(8,128)(2,1)S(1)} %get-tuple-element.46.mixed), custom_call_target="tpu_custom_call" | custom-call | flops 1811939328 | bytes 6291456 | tf_op jit(solution)/shard_map/weight_part/pallas_call | solution.py:378
  62.9 3.5 %collective-permute-start.8 = (bf16[4,9,48,128]{3,2,1,0:T(8,128)(2,1)S(1)}, bf16[4,9,48,128]{3,2,1,0:T(8,128)(2,1)S(1)}, u32[]{:S(2)}, u32[]{:S(2)}) collective-permute-start(bf16[4,9,48,128]{3,2,1,0:T(8,128)(2,1)S(1)} %get-tuple-element.56), channel_id=1, source_target_pairs={{0,64},{4,68},{8,72},{12,76},{16,80},{20,84},{24,88},{28,92},{32,9... | collective-permute-start | bytes 1327112 | tf_op jit(solution)/shard_map/ppermute | solution.py:534
  66.4 1.6 %collective-permute-start.9 = (bf16[4,9,48,128]{3,2,1,0:T(8,128)(2,1)S(1)}, bf16[4,9,48,128]{3,2,1,0:T(8,128)(2,1)S(1)}, u32[]{:S(2)}, u32[]{:S(2)}) collective-permute-start(bf16[4,9,48,128]{3,2,1,0:T(8,128)(2,1)S(1)} %get-tuple-element.57), channel_id=1, source_target_pairs={{0,192},{4,196},{8,200},{12,204},{16,208},{20,212},{24,216},{28,22... | collective-permute-start | bytes 1327112 | tf_op jit(solution)/shard_map/ppermute | solution.py:534
  68.1 6.3 %stem_part.1 = (f32[192,256]{1,0:T(8,128)S(1)}, bf16[192,256]{1,0:T(8,128)(2,1)S(1)}, bf16[192,256]{1,0:T(8,128)(2,1)S(1)}, bf16[192,256]{1,0:T(8,128)(2,1)S(1)}) custom-call(s32[3]{0:T(128)S(1)} %copy-done.4, bf16[9,16,4,48,128]{4,3,2,1,0:T(8,128)(2,1)S(1)} %bitcast.77, bf16[3,1024,384]{2,1,0:T(8,128)(2,1)S(1)} %get-tuple-element.46.mixed, ...), custom_call_target="tpu_custom_call" | custom-call | flops 1000 | bytes 1000 | tf_op jit(solution)/shard_map/stem_part/pallas_call | solution.py:431
  74.3 1.4 %collective-permute-start.5 = (bf16[192,256]{1,0:T(8,128)(2,1)S(1)}, bf16[192,256]{1,0:T(8,128)(2,1)S(1)}, u32[]{:S(2)}, u32[]{:S(2)}) collective-permute-start(bf16[192,256]{1,0:T(8,128)(2,1)S(1)} %get-tuple-element.53), channel_id=1, source_target_pairs={{0,1},{1,2},{2,3},{3,0},{4,5},{5,6},{6,7},{7,4},{8,9},{9,10},{10,1... | collective-permute-start | bytes 294920 | tf_op jit(solution)/shard_map/ppermute | solution.py:540
  75.7 2.6 %collective-permute-start.6 = (bf16[192,256]{1,0:T(8,128)(2,1)S(1)}, bf16[192,256]{1,0:T(8,128)(2,1)S(1)}, u32[]{:S(2)}, u32[]{:S(2)}) collective-permute-start(bf16[192,256]{1,0:T(8,128)(2,1)S(1)} %get-tuple-element.54), channel_id=1, source_target_pairs={{0,2},{1,3},{2,0},{3,1},{4,6},{5,7},{6,4},{7,5},{8,10},{9,11},{10,... | collective-permute-start | bytes 294920 | tf_op jit(solution)/shard_map/ppermute | solution.py:540
  78.3 1.1 collective-permute-start.7
  79.4 1.4 %collective-permute-start.13 = (bf16[4,9,48,128]{3,2,1,0:T(8,128)(2,1)S(1)}, bf16[4,9,48,128]{3,2,1,0:T(8,128)(2,1)S(1)}, u32[]{:S(2)}, u32[]{:S(2)}) collective-permute-start(bf16[4,9,48,128]{3,2,1,0:T(8,128)(2,1)S(1)} %get-tuple-element.60), channel_id=1, source_target_pairs={{0,128},{4,132},{8,136},{12,140},{16,144},{20,148},{24,152},{28,15... | collective-permute-start | bytes 1327112 | tf_op jit(solution)/shard_map/ppermute | solution.py:534
  80.7 1.6 %collective-permute-done.6 = bf16[192,256]{1,0:T(8,128)(2,1)S(1)} collective-permute-done((bf16[192,256]{1,0:T(8,128)(2,1)S(1)}, bf16[192,256]{1,0:T(8,128)(2,1)S(1)}, u32[]{:S(2)}, u32[]{:S(2)}) %collective-permute-start.6) | collective-permute-done | bytes 98336 | tf_op jit(solution)/shard_map/ppermute | solution.py:540
  82.3 0.1 convert_add_fusion.1
  82.4 2.5 %collective-permute-start.10 = (bf16[192,256]{1,0:T(8,128)(2,1)S(1)}, bf16[192,256]{1,0:T(8,128)(2,1)S(1)}, u32[]{:S(2)}, u32[]{:S(2)}) collective-permute-start(bf16[192,256]{1,0:T(8,128)(2,1)S(1)} %reduce-precision_convert_fusion.1), channel_id=1, source_target_pairs={{0,16},{4,20},{8,24},{12,28},{16,0},{20,4},{24,8},{28,12},{32,48},... | collective-permute-start | bytes 294920 | tf_op jit(solution)/shard_map/ppermute | solution.py:485
  84.9 5.1 %collective-permute-start.11 = (bf16[192,256]{1,0:T(8,128)(2,1)S(1)}, bf16[192,256]{1,0:T(8,128)(2,1)S(1)}, u32[]{:S(2)}, u32[]{:S(2)}) collective-permute-start(bf16[192,256]{1,0:T(8,128)(2,1)S(1)} %reduce-precision_convert_fusion.1), channel_id=1, source_target_pairs={{0,32},{4,36},{8,40},{12,44},{16,48},{20,52},{24,56},{28,60},{32,0... | collective-permute-start | bytes 294920 | tf_op jit(solution)/shard_map/ppermute | solution.py:485
  90.0 3.3 %collective-permute-done.11 = bf16[192,256]{1,0:T(8,128)(2,1)S(1)} collective-permute-done((bf16[192,256]{1,0:T(8,128)(2,1)S(1)}, bf16[192,256]{1,0:T(8,128)(2,1)S(1)}, u32[]{:S(2)}, u32[]{:S(2)}) %collective-permute-start.11) | collective-permute-done | bytes 98336 | tf_op jit(solution)/shard_map/ppermute | solution.py:485
  93.3 4.7 %collective-permute-done.12 = bf16[192,256]{1,0:T(8,128)(2,1)S(1)} collective-permute-done((bf16[192,256]{1,0:T(8,128)(2,1)S(1)}, bf16[192,256]{1,0:T(8,128)(2,1)S(1)}, u32[]{:S(2)}, u32[]{:S(2)}) %collective-permute-start.12) | collective-permute-done | bytes 98336 | tf_op jit(solution)/shard_map/ppermute | solution.py:485
  98.0 0.1 add_add_fusion.1
  98.1 0.1 collective-permute-start.14
  98.2 1.6 %collective-permute-start.15 = (bf16[192,256]{1,0:T(8,128)(2,1)S(1)}, bf16[192,256]{1,0:T(8,128)(2,1)S(1)}, u32[]{:S(2)}, u32[]{:S(2)}) collective-permute-start(bf16[192,256]{1,0:T(8,128)(2,1)S(1)} %reduce-precision_convert_fusion), channel_id=1, source_target_pairs={{0,128},{4,132},{8,136},{12,140},{16,144},{20,148},{24,152},{28,15... | collective-permute-start | bytes 294920 | tf_op jit(solution)/shard_map/ppermute | solution.py:485
  99.9 2.2 %collective-permute-start.16 = (bf16[192,256]{1,0:T(8,128)(2,1)S(1)}, bf16[192,256]{1,0:T(8,128)(2,1)S(1)}, u32[]{:S(2)}, u32[]{:S(2)}) collective-permute-start(bf16[192,256]{1,0:T(8,128)(2,1)S(1)} %reduce-precision_convert_fusion), channel_id=1, source_target_pairs={{0,192},{4,196},{8,200},{12,204},{16,208},{20,212},{24,216},{28,22... | collective-permute-start | bytes 294920 | tf_op jit(solution)/shard_map/ppermute | solution.py:485
  102.1 0.2 convert_add_fusion
  102.3 0.1 fusion.3
  102.3 2.7 %collective-permute-start.17 = (bf16[9,48,128]{2,1,0:T(8,128)(2,1)S(1)}, bf16[9,48,128]{2,1,0:T(8,128)(2,1)S(1)}, u32[]{:S(2)}, u32[]{:S(2)}) collective-permute-start(bf16[9,48,128]{2,1,0:T(8,128)(2,1)S(1)} %get-tuple-element.75), channel_id=1, source_target_pairs={{0,16},{4,20},{8,24},{12,28},{16,32},{20,36},{24,40},{28,44},{32,4... | collective-permute-start | bytes 331784 | tf_op jit(solution)/shard_map/ppermute | solution.py:559
  105.0 4.0 %collective-permute-start.18 = (bf16[9,48,128]{2,1,0:T(8,128)(2,1)S(1)}, bf16[9,48,128]{2,1,0:T(8,128)(2,1)S(1)}, u32[]{:S(2)}, u32[]{:S(2)}) collective-permute-start(bf16[9,48,128]{2,1,0:T(8,128)(2,1)S(1)} %get-tuple-element.73), channel_id=1, source_target_pairs={{0,32},{4,36},{8,40},{12,44},{16,48},{20,52},{24,56},{28,60},{32,0... | collective-permute-start | bytes 331784 | tf_op jit(solution)/shard_map/ppermute | solution.py:559
  109.1 0.1 add_add_fusion
  109.2 2.0 %collective-permute-done.17 = bf16[9,48,128]{2,1,0:T(8,128)(2,1)S(1)} collective-permute-done((bf16[9,48,128]{2,1,0:T(8,128)(2,1)S(1)}, bf16[9,48,128]{2,1,0:T(8,128)(2,1)S(1)}, u32[]{:S(2)}, u32[]{:S(2)}) %collective-permute-start.17) | collective-permute-done | bytes 110624 | tf_op jit(solution)/shard_map/ppermute | solution.py:559
  111.1 4.7 %collective-permute-done.18 = bf16[9,48,128]{2,1,0:T(8,128)(2,1)S(1)} collective-permute-done((bf16[9,48,128]{2,1,0:T(8,128)(2,1)S(1)}, bf16[9,48,128]{2,1,0:T(8,128)(2,1)S(1)}, u32[]{:S(2)}, u32[]{:S(2)}) %collective-permute-start.18) | collective-permute-done | bytes 110624 | tf_op jit(solution)/shard_map/ppermute | solution.py:559
  115.9 3.8 %collective-permute-start.20 = (bf16[192,256]{1,0:T(8,128)(2,1)S(1)}, bf16[192,256]{1,0:T(8,128)(2,1)S(1)}, u32[]{:S(2)}, u32[]{:S(2)}) collective-permute-start(bf16[192,256]{1,0:T(8,128)(2,1)S(1)} %add_add_fusion), channel_id=1, source_target_pairs={{0,4},{4,0},{8,12},{12,8},{16,20},{20,16},{24,28},{28,24},{32,36},... | collective-permute-start | bytes 294920 | tf_op jit(solution)/shard_map/ppermute | solution.py:485
  119.7 1.6 %collective-permute-start.22 = (bf16[192,256]{1,0:T(8,128)(2,1)S(1)}, bf16[192,256]{1,0:T(8,128)(2,1)S(1)}, u32[]{:S(2)}, u32[]{:S(2)}) collective-permute-start(bf16[192,256]{1,0:T(8,128)(2,1)S(1)} %add_add_fusion), channel_id=1, source_target_pairs={{0,12},{4,8},{8,4},{12,0},{16,28},{20,24},{24,20},{28,16},{32,44},... | collective-permute-start | bytes 294920 | tf_op jit(solution)/shard_map/ppermute | solution.py:485
  121.3 0.7 fusion.1
  122.1 2.0 %collective-permute-done.21 = bf16[192,256]{1,0:T(8,128)(2,1)S(1)} collective-permute-done((bf16[192,256]{1,0:T(8,128)(2,1)S(1)}, bf16[192,256]{1,0:T(8,128)(2,1)S(1)}, u32[]{:S(2)}, u32[]{:S(2)}) %collective-permute-start.21) | collective-permute-done | bytes 98336 | tf_op jit(solution)/shard_map/ppermute | solution.py:485
  124.1 2.2 %collective-permute-done.22 = bf16[192,256]{1,0:T(8,128)(2,1)S(1)} collective-permute-done((bf16[192,256]{1,0:T(8,128)(2,1)S(1)}, bf16[192,256]{1,0:T(8,128)(2,1)S(1)}, u32[]{:S(2)}, u32[]{:S(2)}) %collective-permute-start.22) | collective-permute-done | bytes 98336 | tf_op jit(solution)/shard_map/ppermute | solution.py:485
  126.4 0.1 maximum_convert_fusion
  126.4 0.2 slice.67
  126.6 0.2 slice.68
  126.8 0.2 copy.42
  126.9 0.2 copy.43
  127.1 1.1 copy.44
  128.2 0.6 pad_maximum_fusion.5
  (51 shorter events, 0.3 us)
Async XLA Ops:
  0.6 10.1 %copy-start.8 = (bf16[256,3,128]{2,0,1:T(8,128)(2,1)S(1)}, bf16[256,3,128]{2,0,1:T(8,128)(2,1)}, u32[]{:S(2)}) copy-start(bf16[256,3,128]{2,0,1:T(8,128)(2,1)} %param.21) | copy-start | bytes 589828
  0.6 15.0 %copy-start.10 = (s32[128,4]{0,1:T(4,128)S(1)}, s32[128,4]{0,1:T(4,128)}, u32[]{:S(2)}) copy-start(s32[128,4]{0,1:T(4,128)} %param.20) | copy-start | bytes 6148
  2.6 14.0 %copy-start.9 = (bf16[64,8,1,64]{3,1,0,2:T(8,128)(2,1)S(1)}, bf16[64,8,1,64]{3,1,0,2:T(8,128)(2,1)}, u32[]{:S(2)}) copy-start(bf16[64,8,1,64]{3,1,0,2:T(8,128)(2,1)} %constant.112.clone.1) | copy-start | bytes 196612
  3.3 1.3 %collective-permute-start = (bf16[64,256]{1,0:T(8,128)(2,1)S(1)}, bf16[64,256]{1,0:T(8,128)(2,1)S(1)}, u32[]{:S(2)}, u32[]{:S(2)}) collective-permute-start(bf16[64,256]{1,0:T(8,128)(2,1)S(1)} %reshape.83), channel_id=1, source_target_pairs={{8,16},{12,20},{16,8},{20,12},{24,32},{28,36},{32,24},{36,28},{40,... | collective-permute-start | bytes 98312 | tf_op jit(solution)/shard_map/ppermute | solution.py:492
  4.6 8.1 %collective-permute-start.1 = (bf16[2,64,256]{2,1,0:T(8,128)(2,1)S(1)}, bf16[2,64,256]{2,1,0:T(8,128)(2,1)S(1)}, u32[]{:S(2)}, u32[]{:S(2)}) collective-permute-start(bf16[2,64,256]{2,1,0:T(8,128)(2,1)S(1)} %pad_maximum_fusion.4), channel_id=1, source_target_pairs={{0,8},{4,12},{8,0},{12,4},{16,24},{20,28},{24,16},{28,20},{32,40},... | collective-permute-start | bytes 196616 | tf_op jit(solution)/shard_map/ppermute | solution.py:485
  10.7 5.0 %collective-permute-start.3 = (bf16[3,4,64,128]{3,2,1,0:T(8,128)(2,1)S(1)}, bf16[3,4,64,128]{3,2,1,0:T(8,128)(2,1)S(1)}, u32[]{:S(2)}, u32[]{:S(2)}) collective-permute-start(bf16[3,4,64,128]{3,2,1,0:T(8,128)(2,1)S(1)} %bitcast.85), channel_id=1, source_target_pairs={{0,4},{4,0},{8,12},{12,8},{16,20},{20,16},{24,28},{28,24},{32,36},... | collective-permute-start | bytes 589832 | tf_op jit(solution)/shard_map/ppermute | solution.py:485
  12.8 3.2 %collective-permute-start.2 = (bf16[4,64,256]{2,1,0:T(8,128)(2,1)S(1)}, bf16[4,64,256]{2,1,0:T(8,128)(2,1)S(1)}, u32[]{:S(2)}, u32[]{:S(2)}) collective-permute-start(bf16[4,64,256]{2,1,0:T(8,128)(2,1)S(1)} %pad_maximum_fusion.2), channel_id=1, source_target_pairs={{0,4},{4,0},{8,12},{12,8},{16,20},{20,16},{24,28},{28,24},{32,36},... | collective-permute-start | bytes 393224 | tf_op jit(solution)/shard_map/ppermute | solution.py:485
  18.6 20.3 %collective-permute-start.4 = (bf16[2,3,4,64,128]{4,3,2,1,0:T(8,128)(2,1)S(1)}, bf16[2,3,4,64,128]{4,3,2,1,0:T(8,128)(2,1)S(1)}, u32[]{:S(2)}, u32[]{:S(2)}) collective-permute-start(bf16[2,3,4,64,128]{4,3,2,1,0:T(8,128)(2,1)S(1)} %pad_maximum_fusion.1), channel_id=1, source_target_pairs={{0,8},{4,12},{8,0},{12,4},{16,24},{20,28},{24,16},{28,20},{32,40},... | collective-permute-start | bytes 1179656 | tf_op jit(solution)/shard_map/ppermute | solution.py:485
  20.3 18.7 %copy-start.4 = (s32[3]{0:T(128)S(1)}, s32[3]{0:T(128)}, u32[]{:S(2)}) copy-start(s32[3]{0:T(128)} %pad_add_fusion.ids) | copy-start | bytes 40
  20.3 18.7 %copy-start.5 = (f32[128]{0:T(128)S(1)}, f32[128]{0:T(128)}, u32[]{:S(2)}) copy-start(f32[128]{0:T(128)} %param.18) | copy-start | bytes 1540
  20.3 18.7 %copy-start.6 = (f32[128]{0:T(128)S(1)}, f32[128]{0:T(128)}, u32[]{:S(2)}) copy-start(f32[128]{0:T(128)} %param.19) | copy-start | bytes 1540
  39.0 29.0 %slice-start = ((s8[7077888]{0:T(1024)(128)(4,1)}), s8[4194304]{0:T(1024)(128)(4,1)S(1)}, s32[]{:S(2)}) async-start(s8[7077888]{0:T(1024)(128)(4,1)} %bitcast.75), calls=%async_computation | async-start | bytes 8388608
  39.0 20.6 %copy-start.7 = (bf16[768,1024]{1,0:T(8,128)(2,1)S(1)}, bf16[768,1024]{1,0:T(8,128)(2,1)}, u32[]{:S(2)}) copy-start(bf16[768,1024]{1,0:T(8,128)(2,1)} %get-tuple-element.42.hid) | copy-start | bytes 4718596
  39.0 29.0 %slice-start.1 = ((s8[7077888]{0:T(1024)(128)(4,1)}), s8[2883584]{0:T(1024)(128)(4,1)S(1)}, s32[]{:S(2)}) async-start(s8[7077888]{0:T(1024)(128)(4,1)} %bitcast.75), calls=%async_computation.1 | async-start | bytes 5767168
  59.6 8.4 %copy-start = (bf16[256,1024]{1,0:T(8,128)(2,1)S(1)}, bf16[256,1024]{1,0:T(8,128)(2,1)}, u32[]{:S(2)}) copy-start(bf16[256,1024]{1,0:T(8,128)(2,1)} %copy.35.pext) | copy-start | bytes 1572868
  59.6 8.4 %copy-start.1 = (bf16[768,1024]{1,0:T(8,128)(2,1)S(1)}, bf16[768,1024]{1,0:T(8,128)(2,1)}, u32[]{:S(2)}) copy-start(bf16[768,1024]{1,0:T(8,128)(2,1)} %get-tuple-element.48.nrm) | copy-start | bytes 4718596
  59.7 8.4 %copy-start.2 = (f32[768,128]{1,0:T(8,128)S(1)}, f32[768,128]{1,0:T(8,128)}, u32[]{:S(2)}) copy-start(f32[768,128]{1,0:T(8,128)} %get-tuple-element.49.sc) | copy-start | bytes 1179652
  59.7 8.4 %copy-start.3 = (f32[8,1024]{1,0:T(8,128)S(1)}, f32[8,1024]{1,0:T(8,128)}, u32[]{:S(2)}) copy-start(f32[8,1024]{1,0:T(8,128)} %get-tuple-element.51.inv) | copy-start | bytes 98308
  62.9 19.5 %collective-permute-start.8 = (bf16[4,9,48,128]{3,2,1,0:T(8,128)(2,1)S(1)}, bf16[4,9,48,128]{3,2,1,0:T(8,128)(2,1)S(1)}, u32[]{:S(2)}, u32[]{:S(2)}) collective-permute-start(bf16[4,9,48,128]{3,2,1,0:T(8,128)(2,1)S(1)} %get-tuple-element.56), channel_id=1, source_target_pairs={{0,64},{4,68},{8,72},{12,76},{16,80},{20,84},{24,88},{28,92},{32,9... | collective-permute-start | bytes 1327112 | tf_op jit(solution)/shard_map/ppermute | solution.py:534
  66.4 16.0 %collective-permute-start.9 = (bf16[4,9,48,128]{3,2,1,0:T(8,128)(2,1)S(1)}, bf16[4,9,48,128]{3,2,1,0:T(8,128)(2,1)S(1)}, u32[]{:S(2)}, u32[]{:S(2)}) collective-permute-start(bf16[4,9,48,128]{3,2,1,0:T(8,128)(2,1)S(1)} %get-tuple-element.57), channel_id=1, source_target_pairs={{0,192},{4,196},{8,200},{12,204},{16,208},{20,212},{24,216},{28,22... | collective-permute-start | bytes 1327112 | tf_op jit(solution)/shard_map/ppermute | solution.py:534
  74.3 5.1 %collective-permute-start.5 = (bf16[192,256]{1,0:T(8,128)(2,1)S(1)}, bf16[192,256]{1,0:T(8,128)(2,1)S(1)}, u32[]{:S(2)}, u32[]{:S(2)}) collective-permute-start(bf16[192,256]{1,0:T(8,128)(2,1)S(1)} %get-tuple-element.53), channel_id=1, source_target_pairs={{0,1},{1,2},{2,3},{3,0},{4,5},{5,6},{6,7},{7,4},{8,9},{9,10},{10,1... | collective-permute-start | bytes 294920 | tf_op jit(solution)/shard_map/ppermute | solution.py:540
  75.7 6.7 %collective-permute-start.6 = (bf16[192,256]{1,0:T(8,128)(2,1)S(1)}, bf16[192,256]{1,0:T(8,128)(2,1)S(1)}, u32[]{:S(2)}, u32[]{:S(2)}) collective-permute-start(bf16[192,256]{1,0:T(8,128)(2,1)S(1)} %get-tuple-element.54), channel_id=1, source_target_pairs={{0,2},{1,3},{2,0},{3,1},{4,6},{5,7},{6,4},{7,5},{8,10},{9,11},{10,... | collective-permute-start | bytes 294920 | tf_op jit(solution)/shard_map/ppermute | solution.py:540
  78.3 4.0 %collective-permute-start.7 = (bf16[192,256]{1,0:T(8,128)(2,1)S(1)}, bf16[192,256]{1,0:T(8,128)(2,1)S(1)}, u32[]{:S(2)}, u32[]{:S(2)}) collective-permute-start(bf16[192,256]{1,0:T(8,128)(2,1)S(1)} %get-tuple-element.55), channel_id=1, source_target_pairs={{0,3},{1,0},{2,1},{3,2},{4,7},{5,4},{6,5},{7,6},{8,11},{9,8},{10,9... | collective-permute-start | bytes 294920 | tf_op jit(solution)/shard_map/ppermute | solution.py:540
  79.4 18.7 %collective-permute-start.13 = (bf16[4,9,48,128]{3,2,1,0:T(8,128)(2,1)S(1)}, bf16[4,9,48,128]{3,2,1,0:T(8,128)(2,1)S(1)}, u32[]{:S(2)}, u32[]{:S(2)}) collective-permute-start(bf16[4,9,48,128]{3,2,1,0:T(8,128)(2,1)S(1)} %get-tuple-element.60), channel_id=1, source_target_pairs={{0,128},{4,132},{8,136},{12,140},{16,144},{20,148},{24,152},{28,15... | collective-permute-start | bytes 1327112 | tf_op jit(solution)/shard_map/ppermute | solution.py:534
  82.4 7.6 %collective-permute-start.10 = (bf16[192,256]{1,0:T(8,128)(2,1)S(1)}, bf16[192,256]{1,0:T(8,128)(2,1)S(1)}, u32[]{:S(2)}, u32[]{:S(2)}) collective-permute-start(bf16[192,256]{1,0:T(8,128)(2,1)S(1)} %reduce-precision_convert_fusion.1), channel_id=1, source_target_pairs={{0,16},{4,20},{8,24},{12,28},{16,0},{20,4},{24,8},{28,12},{32,48},... | collective-permute-start | bytes 294920 | tf_op jit(solution)/shard_map/ppermute | solution.py:485
  84.9 8.4 %collective-permute-start.11 = (bf16[192,256]{1,0:T(8,128)(2,1)S(1)}, bf16[192,256]{1,0:T(8,128)(2,1)S(1)}, u32[]{:S(2)}, u32[]{:S(2)}) collective-permute-start(bf16[192,256]{1,0:T(8,128)(2,1)S(1)} %reduce-precision_convert_fusion.1), channel_id=1, source_target_pairs={{0,32},{4,36},{8,40},{12,44},{16,48},{20,52},{24,56},{28,60},{32,0... | collective-permute-start | bytes 294920 | tf_op jit(solution)/shard_map/ppermute | solution.py:485
  90.0 8.0 %collective-permute-start.12 = (bf16[192,256]{1,0:T(8,128)(2,1)S(1)}, bf16[192,256]{1,0:T(8,128)(2,1)S(1)}, u32[]{:S(2)}, u32[]{:S(2)}) collective-permute-start(bf16[192,256]{1,0:T(8,128)(2,1)S(1)} %reduce-precision_convert_fusion.1), channel_id=1, source_target_pairs={{0,48},{4,52},{8,56},{12,60},{16,32},{20,36},{24,40},{28,44},{32,1... | collective-permute-start | bytes 294920 | tf_op jit(solution)/shard_map/ppermute | solution.py:485
  98.1 11.0 %collective-permute-start.14 = (bf16[192,256]{1,0:T(8,128)(2,1)S(1)}, bf16[192,256]{1,0:T(8,128)(2,1)S(1)}, u32[]{:S(2)}, u32[]{:S(2)}) collective-permute-start(bf16[192,256]{1,0:T(8,128)(2,1)S(1)} %reduce-precision_convert_fusion), channel_id=1, source_target_pairs={{0,64},{4,68},{8,72},{12,76},{16,80},{20,84},{24,88},{28,92},{32,9... | collective-permute-start | bytes 294920 | tf_op jit(solution)/shard_map/ppermute | solution.py:485
  98.2 10.8 %collective-permute-start.15 = (bf16[192,256]{1,0:T(8,128)(2,1)S(1)}, bf16[192,256]{1,0:T(8,128)(2,1)S(1)}, u32[]{:S(2)}, u32[]{:S(2)}) collective-permute-start(bf16[192,256]{1,0:T(8,128)(2,1)S(1)} %reduce-precision_convert_fusion), channel_id=1, source_target_pairs={{0,128},{4,132},{8,136},{12,140},{16,144},{20,148},{24,152},{28,15... | collective-permute-start | bytes 294920 | tf_op jit(solution)/shard_map/ppermute | solution.py:485
  99.9 9.2 %collective-permute-start.16 = (bf16[192,256]{1,0:T(8,128)(2,1)S(1)}, bf16[192,256]{1,0:T(8,128)(2,1)S(1)}, u32[]{:S(2)}, u32[]{:S(2)}) collective-permute-start(bf16[192,256]{1,0:T(8,128)(2,1)S(1)} %reduce-precision_convert_fusion), channel_id=1, source_target_pairs={{0,192},{4,196},{8,200},{12,204},{16,208},{20,212},{24,216},{28,22... | collective-permute-start | bytes 294920 | tf_op jit(solution)/shard_map/ppermute | solution.py:485
  102.3 8.8 %collective-permute-start.17 = (bf16[9,48,128]{2,1,0:T(8,128)(2,1)S(1)}, bf16[9,48,128]{2,1,0:T(8,128)(2,1)S(1)}, u32[]{:S(2)}, u32[]{:S(2)}) collective-permute-start(bf16[9,48,128]{2,1,0:T(8,128)(2,1)S(1)} %get-tuple-element.75), channel_id=1, source_target_pairs={{0,16},{4,20},{8,24},{12,28},{16,32},{20,36},{24,40},{28,44},{32,4... | collective-permute-start | bytes 331784 | tf_op jit(solution)/shard_map/ppermute | solution.py:559
  105.0 10.8 %collective-permute-start.18 = (bf16[9,48,128]{2,1,0:T(8,128)(2,1)S(1)}, bf16[9,48,128]{2,1,0:T(8,128)(2,1)S(1)}, u32[]{:S(2)}, u32[]{:S(2)}) collective-permute-start(bf16[9,48,128]{2,1,0:T(8,128)(2,1)S(1)} %get-tuple-element.73), channel_id=1, source_target_pairs={{0,32},{4,36},{8,40},{12,44},{16,48},{20,52},{24,56},{28,60},{32,0... | collective-permute-start | bytes 331784 | tf_op jit(solution)/shard_map/ppermute | solution.py:559
  109.1 12.2 %collective-permute-start.19 = (bf16[9,48,128]{2,1,0:T(8,128)(2,1)S(1)}, bf16[9,48,128]{2,1,0:T(8,128)(2,1)S(1)}, u32[]{:S(2)}, u32[]{:S(2)}) collective-permute-start(bf16[9,48,128]{2,1,0:T(8,128)(2,1)S(1)} %get-tuple-element.74), channel_id=1, source_target_pairs={{0,48},{4,52},{8,56},{12,60},{16,0},{20,4},{24,8},{28,12},{32,16},... | collective-permute-start | bytes 331784 | tf_op jit(solution)/shard_map/ppermute | solution.py:559
  115.9 6.2 %collective-permute-start.20 = (bf16[192,256]{1,0:T(8,128)(2,1)S(1)}, bf16[192,256]{1,0:T(8,128)(2,1)S(1)}, u32[]{:S(2)}, u32[]{:S(2)}) collective-permute-start(bf16[192,256]{1,0:T(8,128)(2,1)S(1)} %add_add_fusion), channel_id=1, source_target_pairs={{0,4},{4,0},{8,12},{12,8},{16,20},{20,16},{24,28},{28,24},{32,36},... | collective-permute-start | bytes 294920 | tf_op jit(solution)/shard_map/ppermute | solution.py:485
  119.7 4.4 %collective-permute-start.21 = (bf16[192,256]{1,0:T(8,128)(2,1)S(1)}, bf16[192,256]{1,0:T(8,128)(2,1)S(1)}, u32[]{:S(2)}, u32[]{:S(2)}) collective-permute-start(bf16[192,256]{1,0:T(8,128)(2,1)S(1)} %add_add_fusion), channel_id=1, source_target_pairs={{0,8},{4,12},{8,0},{12,4},{16,24},{20,28},{24,16},{28,20},{32,40},... | collective-permute-start | bytes 294920 | tf_op jit(solution)/shard_map/ppermute | solution.py:485
  119.7 6.6 %collective-permute-start.22 = (bf16[192,256]{1,0:T(8,128)(2,1)S(1)}, bf16[192,256]{1,0:T(8,128)(2,1)S(1)}, u32[]{:S(2)}, u32[]{:S(2)}) collective-permute-start(bf16[192,256]{1,0:T(8,128)(2,1)S(1)} %add_add_fusion), channel_id=1, source_target_pairs={{0,12},{4,8},{8,4},{12,0},{16,28},{20,24},{24,20},{28,16},{32,44},... | collective-permute-start | bytes 294920 | tf_op jit(solution)/shard_map/ppermute | solution.py:485

commit v8 on v7

--- a/solution.py
+++ b/solution.py
@@ -559,7 +559,7 @@
             part = lax.ppermute(part.astype(BF16), "seq", pairs)
         parts.append(part)
     total = quad_sum(total, 16, 32)
-    total, parts[1], parts[2] = lax.optimization_barrier((total, parts[1], parts[2]))
+    total, parts[1], parts[3] = lax.optimization_barrier((total, parts[1], parts[3]))
     weight_grad = sum(part.astype(F32) for part in parts)
     weight_grad = jnp.transpose(weight_grad.reshape(3, heads, rows, hd), (2, 0, 1, 3))
 

time: 129 us -> 128 us (level); the launches traced: 129 us -> 126 us
  waiting for transfers between devices: 20.8 us -> 15.8 us
  starting transfers between devices: 47.9 us -> 50 us
    ppermute x3, waiting for transfers between devices: 6.73 us -> 0.01 us  [per_device(): part = lax.ppermute(part.astype(BF16), 'seq', pairs)]
    ppermute x3, waiting for transfers between devices: 1.62 us -> 5.48 us  [per_device(): total = total + lax.ppermute(stem[k], 'head', pairs).astype(F32)]
    ppermute x3, starting transfers between devices: 6.73 us -> 9.02 us  [per_device(): part = lax.ppermute(part.astype(BF16), 'seq', pairs)]
    ppermute x13, waiting for transfers between devices: 12.4 us -> 10.3 us  [xor(): return lax.ppermute(value, 'seq', [(a, a ^ mask) for a in range(seq)])]
  transfers between devices with their start and end apart: 23 -> 23, of which waited for: 8 -> 8; matrix products, arithmetic and copies ran while one was open for 2% -> 2% of each run, Pallas kernels for 19% -> 20%
where the time goes in v8:
time: 128 us; the launch traced here: 126 us
  starting transfers between devices  50 us (39%)
  Pallas kernels  48.6 us (38%)
  waiting for transfers between devices  15.8 us (12%)
  local copies, waits for them, and re-layouts  7.49 us (6%)
  other arithmetic  2.99 us (2%)
    ppermute x13, starting transfers between devices, xor(): return lax.ppermute(value, 'seq', [(a, a ^ mask) for a in range(seq)])  30 us
    pallas_call x1, Pallas kernels, attention(): pl.pallas_call(attention_kernel, grid_spec=pltpu.PrefetchScalarGridSpec(n...  20.6 us
    pallas_call x1, Pallas kernels, forward(): pl.pallas_call(forward_kernel, grid_spec=pltpu.PrefetchScalarGridSpec(num...  18.6 us
    ppermute x13, waiting for transfers between devices, xor(): return lax.ppermute(value, 'seq', [(a, a ^ mask) for a in range(seq)])  10.3 us
    ppermute x3, starting transfers between devices, per_device(): part = lax.ppermute(part.astype(BF16), 'seq', pairs)  9.02 us
    ppermute x3, starting transfers between devices, per_device(): weight[k] = lax.ppermute(weight[k], 'seq', pairs)  6.48 us
    pallas_call x1, Pallas kernels, stem_part(): pl.pallas_call(stem_kernel, grid_spec=pltpu.PrefetchScalarGridSpec(num_sc...  6.25 us
    ppermute x3, waiting for transfers between devices, per_device(): total = total + lax.ppermute(stem[k], 'head', pairs).astype(F32)  5.48 us
  transfers between devices with their start and end apart: 23, of which 8 were waited for; matrix products, arithmetic and copies ran while one was open for 2% of the time, Pallas kernels for 20%

profile of v8, /device:TPU:1, one launch (start us, length us, event | category | flops | bytes accessed | tf_op | source)
XLA Modules:
  0.0 125.9 jit_solution(12368474755783894643)
XLA Ops:
  0.7 1.0 copy.30
  1.6 1.0 copy.31
  2.6 0.0 copy-start.9
  2.6 0.7 reshape.83
  3.3 0.7 collective-permute-start
  4.0 0.7 stack_reshape.8
  4.6 0.0 collective-permute-done
  4.6 6.0 %collective-permute-start.1 = (bf16[2,64,256]{2,1,0:T(8,128)(2,1)S(1)}, bf16[2,64,256]{2,1,0:T(8,128)(2,1)S(1)}, u32[]{:S(2)}, u32[]{:S(2)}) collective-permute-start(bf16[2,64,256]{2,1,0:T(8,128)(2,1)S(1)} %pad_maximum_fusion.4), channel_id=1, source_target_pairs={{0,8},{4,12},{8,0},{12,4},{16,24},{20,28},{24,16},{28,20},{32,40},... | collective-permute-start | bytes 196616 | tf_op jit(solution)/shard_map/ppermute | solution.py:485
  10.7 2.0 %collective-permute-start.3 = (bf16[3,4,64,128]{3,2,1,0:T(8,128)(2,1)S(1)}, bf16[3,4,64,128]{3,2,1,0:T(8,128)(2,1)S(1)}, u32[]{:S(2)}, u32[]{:S(2)}) collective-permute-start(bf16[3,4,64,128]{3,2,1,0:T(8,128)(2,1)S(1)} %bitcast.85), channel_id=1, source_target_pairs={{0,4},{4,0},{8,12},{12,8},{16,20},{20,16},{24,28},{28,24},{32,36},... | collective-permute-start | bytes 589832 | tf_op jit(solution)/shard_map/ppermute | solution.py:485
  12.7 0.0 collective-permute-done.1
  12.8 2.2 %collective-permute-start.2 = (bf16[4,64,256]{2,1,0:T(8,128)(2,1)S(1)}, bf16[4,64,256]{2,1,0:T(8,128)(2,1)S(1)}, u32[]{:S(2)}, u32[]{:S(2)}) collective-permute-start(bf16[4,64,256]{2,1,0:T(8,128)(2,1)S(1)} %pad_maximum_fusion.2), channel_id=1, source_target_pairs={{0,4},{4,0},{8,12},{12,8},{16,20},{20,16},{24,28},{28,24},{32,36},... | collective-permute-start | bytes 393224 | tf_op jit(solution)/shard_map/ppermute | solution.py:485
  15.0 0.7 pad_add_fusion.ids
  15.7 0.1 copy.36.lists
  15.8 0.2 collective-permute-done.2
  16.0 0.1 concatenate.30
  16.2 0.1 concatenate.28
  16.3 0.1 concatenate.27
  16.5 0.1 concatenate.26
  16.6 0.2 maximum_maximum_fusion
  16.8 0.7 copy.34
  17.6 1.0 copy.35.pext
  18.6 1.7 %collective-permute-start.4 = (bf16[2,3,4,64,128]{4,3,2,1,0:T(8,128)(2,1)S(1)}, bf16[2,3,4,64,128]{4,3,2,1,0:T(8,128)(2,1)S(1)}, u32[]{:S(2)}, u32[]{:S(2)}) collective-permute-start(bf16[2,3,4,64,128]{4,3,2,1,0:T(8,128)(2,1)S(1)} %pad_maximum_fusion.1), channel_id=1, source_target_pairs={{0,8},{4,12},{8,0},{12,4},{16,24},{20,28},{24,16},{28,20},{32,40},... | collective-permute-start | bytes 1179656 | tf_op jit(solution)/shard_map/ppermute | solution.py:485
  20.3 18.6 %forward.1 = (f32[1024,1152]{1,0:T(8,128)}, bf16[768,1024]{1,0:T(8,128)(2,1)}, bf16[768,1024]{1,0:T(8,128)(2,1)}, f32[8,1024]{1,0:T(8,128)}, f32[8,1152]{1,0:T(8,128)}, /*index=5*/f32[768,128]{1,0:T(8,128)}) custom-call(s32[3]{0:T(128)} %pad_add_fusion.ids, bf16[256,1024]{1,0:T(8,128)(2,1)} %copy.35.pext, bf16[192,3072]{1,0:T(8,128)(2,1)} %stem.1, ...), custom_call_target="tpu_custom_call" | custom-call | flops 8858370048 | bytes 25165824 | tf_op jit(solution)/shard_map/forward/pallas_call | solution.py:140
  38.9 0.1 pad_maximum_fusion.og
  39.0 0.0 slice-start
  39.0 20.6 %attention.1 = (bf16[3,1024,384]{2,1,0:T(8,128)(2,1)S(1)}, f32[2,8,1024]{2,1,0:T(8,128)S(1)}) custom-call(s32[3]{0:T(128)S(1)} %copy-done.4, s32[128,4]{1,0:T(8,128)S(1)} %copy.36.lists, f32[1024,1152]{1,0:T(8,128)} %get-tuple-element.43.pq.pk.pv, f32[1024,1152]{1,0:T(8,128)} %get-tuple-element.43.pq.pk.pv, f32[1024,1152]{1,0:T(8,128)} %get-tuple-element.43.pq.pk.pv, ...), custom_call_target="tpu_custom_call" | custom-call | flops 2013265920 | bytes 10485760 | tf_op jit(solution)/shard_map/attention/pallas_call | solution.py:321
  59.6 0.0 copy-start
  59.7 3.2 %weight_part.1 = (bf16[4,9,48,128]{3,2,1,0:T(8,128)(2,1)S(1)}, bf16[4,9,48,128]{3,2,1,0:T(8,128)(2,1)S(1)}, bf16[4,9,48,128]{3,2,1,0:T(8,128)(2,1)S(1)}, bf16[4,9,48,128]{3,2,1,0:T(8,128)(2,1)S(1)}) custom-call(s32[3]{0:T(128)S(1)} %copy-done.4, bf16[768,1024]{1,0:T(8,128)(2,1)S(1)} %copy-done.7, bf16[3,1024,384]{2,1,0:T(8,128)(2,1)S(1)} %get-tuple-element.46.mixed), custom_call_target="tpu_custom_call" | custom-call | flops 1811939328 | bytes 6291456 | tf_op jit(solution)/shard_map/weight_part/pallas_call | solution.py:378
  62.9 3.5 %collective-permute-start.8 = (bf16[4,9,48,128]{3,2,1,0:T(8,128)(2,1)S(1)}, bf16[4,9,48,128]{3,2,1,0:T(8,128)(2,1)S(1)}, u32[]{:S(2)}, u32[]{:S(2)}) collective-permute-start(bf16[4,9,48,128]{3,2,1,0:T(8,128)(2,1)S(1)} %get-tuple-element.56), channel_id=1, source_target_pairs={{0,64},{4,68},{8,72},{12,76},{16,80},{20,84},{24,88},{28,92},{32,9... | collective-permute-start | bytes 1327112 | tf_op jit(solution)/shard_map/ppermute | solution.py:534
  66.3 1.7 %collective-permute-start.9 = (bf16[4,9,48,128]{3,2,1,0:T(8,128)(2,1)S(1)}, bf16[4,9,48,128]{3,2,1,0:T(8,128)(2,1)S(1)}, u32[]{:S(2)}, u32[]{:S(2)}) collective-permute-start(bf16[4,9,48,128]{3,2,1,0:T(8,128)(2,1)S(1)} %get-tuple-element.57), channel_id=1, source_target_pairs={{0,192},{4,196},{8,200},{12,204},{16,208},{20,212},{24,216},{28,22... | collective-permute-start | bytes 1327112 | tf_op jit(solution)/shard_map/ppermute | solution.py:534
  68.1 6.2 %stem_part.1 = (f32[192,256]{1,0:T(8,128)S(1)}, bf16[192,256]{1,0:T(8,128)(2,1)S(1)}, bf16[192,256]{1,0:T(8,128)(2,1)S(1)}, bf16[192,256]{1,0:T(8,128)(2,1)S(1)}) custom-call(s32[3]{0:T(128)S(1)} %copy-done.4, bf16[9,16,4,48,128]{4,3,2,1,0:T(8,128)(2,1)S(1)} %bitcast.77, bf16[3,1024,384]{2,1,0:T(8,128)(2,1)S(1)} %get-tuple-element.46.mixed, ...), custom_call_target="tpu_custom_call" | custom-call | flops 1000 | bytes 1000 | tf_op jit(solution)/shard_map/stem_part/pallas_call | solution.py:431
  74.4 2.8 %collective-permute-start.7 = (bf16[192,256]{1,0:T(8,128)(2,1)S(1)}, bf16[192,256]{1,0:T(8,128)(2,1)S(1)}, u32[]{:S(2)}, u32[]{:S(2)}) collective-permute-start(bf16[192,256]{1,0:T(8,128)(2,1)S(1)} %get-tuple-element.55), channel_id=1, source_target_pairs={{0,3},{1,0},{2,1},{3,2},{4,7},{5,4},{6,5},{7,6},{8,11},{9,8},{10,9... | collective-permute-start | bytes 294920 | tf_op jit(solution)/shard_map/ppermute | solution.py:540
  77.2 0.3 collective-permute-start.6
  77.5 0.7 collective-permute-start.5
  78.2 0.6 collective-permute-done.7
  78.8 1.3 %collective-permute-start.13 = (bf16[4,9,48,128]{3,2,1,0:T(8,128)(2,1)S(1)}, bf16[4,9,48,128]{3,2,1,0:T(8,128)(2,1)S(1)}, u32[]{:S(2)}, u32[]{:S(2)}) collective-permute-start(bf16[4,9,48,128]{3,2,1,0:T(8,128)(2,1)S(1)} %get-tuple-element.60), channel_id=1, source_target_pairs={{0,128},{4,132},{8,136},{12,140},{16,144},{20,148},{24,152},{28,15... | collective-permute-start | bytes 1327112 | tf_op jit(solution)/shard_map/ppermute | solution.py:534
  80.1 2.1 %collective-permute-done.6 = bf16[192,256]{1,0:T(8,128)(2,1)S(1)} collective-permute-done((bf16[192,256]{1,0:T(8,128)(2,1)S(1)}, bf16[192,256]{1,0:T(8,128)(2,1)S(1)}, u32[]{:S(2)}, u32[]{:S(2)}) %collective-permute-start.6) | collective-permute-done | bytes 98336 | tf_op jit(solution)/shard_map/ppermute | solution.py:540
  82.3 2.8 %collective-permute-done.5 = bf16[192,256]{1,0:T(8,128)(2,1)S(1)} collective-permute-done((bf16[192,256]{1,0:T(8,128)(2,1)S(1)}, bf16[192,256]{1,0:T(8,128)(2,1)S(1)}, u32[]{:S(2)}, u32[]{:S(2)}) %collective-permute-start.5) | collective-permute-done | bytes 98336 | tf_op jit(solution)/shard_map/ppermute | solution.py:540
  85.1 3.4 %collective-permute-start.12 = (bf16[192,256]{1,0:T(8,128)(2,1)S(1)}, bf16[192,256]{1,0:T(8,128)(2,1)S(1)}, u32[]{:S(2)}, u32[]{:S(2)}) collective-permute-start(bf16[192,256]{1,0:T(8,128)(2,1)S(1)} %reduce-precision_convert_fusion.1), channel_id=1, source_target_pairs={{0,48},{4,52},{8,56},{12,60},{16,32},{20,36},{24,40},{28,44},{32,1... | collective-permute-start | bytes 294920 | tf_op jit(solution)/shard_map/ppermute | solution.py:485
  88.5 0.6 collective-permute-start.11
  89.1 1.7 %collective-permute-start.10 = (bf16[192,256]{1,0:T(8,128)(2,1)S(1)}, bf16[192,256]{1,0:T(8,128)(2,1)S(1)}, u32[]{:S(2)}, u32[]{:S(2)}) collective-permute-start(bf16[192,256]{1,0:T(8,128)(2,1)S(1)} %reduce-precision_convert_fusion.1), channel_id=1, source_target_pairs={{0,16},{4,20},{8,24},{12,28},{16,0},{20,4},{24,8},{28,12},{32,48},... | collective-permute-start | bytes 294920 | tf_op jit(solution)/shard_map/ppermute | solution.py:485
  90.8 0.3 collective-permute-done.12
  91.1 5.5 %collective-permute-done.11 = bf16[192,256]{1,0:T(8,128)(2,1)S(1)} collective-permute-done((bf16[192,256]{1,0:T(8,128)(2,1)S(1)}, bf16[192,256]{1,0:T(8,128)(2,1)S(1)}, u32[]{:S(2)}, u32[]{:S(2)}) %collective-permute-start.11) | collective-permute-done | bytes 98336 | tf_op jit(solution)/shard_map/ppermute | solution.py:485
  96.6 0.1 add_add_fusion.1
  96.7 2.3 %collective-permute-start.16 = (bf16[192,256]{1,0:T(8,128)(2,1)S(1)}, bf16[192,256]{1,0:T(8,128)(2,1)S(1)}, u32[]{:S(2)}, u32[]{:S(2)}) collective-permute-start(bf16[192,256]{1,0:T(8,128)(2,1)S(1)} %reduce-precision_convert_fusion), channel_id=1, source_target_pairs={{0,192},{4,196},{8,200},{12,204},{16,208},{20,212},{24,216},{28,22... | collective-permute-start | bytes 294920 | tf_op jit(solution)/shard_map/ppermute | solution.py:485
  99.0 1.0 collective-permute-start.14
  100.0 0.2 convert_add_fusion
  100.3 0.1 fusion.4
  100.3 2.2 %collective-permute-start.17 = (bf16[9,48,128]{2,1,0:T(8,128)(2,1)S(1)}, bf16[9,48,128]{2,1,0:T(8,128)(2,1)S(1)}, u32[]{:S(2)}, u32[]{:S(2)}) collective-permute-start(bf16[9,48,128]{2,1,0:T(8,128)(2,1)S(1)} %get-tuple-element.75), channel_id=1, source_target_pairs={{0,16},{4,20},{8,24},{12,28},{16,32},{20,36},{24,40},{28,44},{32,4... | collective-permute-start | bytes 331784 | tf_op jit(solution)/shard_map/ppermute | solution.py:559
  102.5 2.4 %collective-permute-start.18 = (bf16[9,48,128]{2,1,0:T(8,128)(2,1)S(1)}, bf16[9,48,128]{2,1,0:T(8,128)(2,1)S(1)}, u32[]{:S(2)}, u32[]{:S(2)}) collective-permute-start(bf16[9,48,128]{2,1,0:T(8,128)(2,1)S(1)} %get-tuple-element.74), channel_id=1, source_target_pairs={{0,48},{4,52},{8,56},{12,60},{16,0},{20,4},{24,8},{28,12},{32,16},... | collective-permute-start | bytes 331784 | tf_op jit(solution)/shard_map/ppermute | solution.py:559
  104.9 4.4 %collective-permute-start.19 = (bf16[9,48,128]{2,1,0:T(8,128)(2,1)S(1)}, bf16[9,48,128]{2,1,0:T(8,128)(2,1)S(1)}, u32[]{:S(2)}, u32[]{:S(2)}) collective-permute-start(bf16[9,48,128]{2,1,0:T(8,128)(2,1)S(1)} %get-tuple-element.73), channel_id=1, source_target_pairs={{0,32},{4,36},{8,40},{12,44},{16,48},{20,52},{24,56},{28,60},{32,0... | collective-permute-start | bytes 331784 | tf_op jit(solution)/shard_map/ppermute | solution.py:559
  109.4 0.1 add_add_fusion
  109.4 7.2 %collective-permute-start.20 = (bf16[192,256]{1,0:T(8,128)(2,1)S(1)}, bf16[192,256]{1,0:T(8,128)(2,1)S(1)}, u32[]{:S(2)}, u32[]{:S(2)}) collective-permute-start(bf16[192,256]{1,0:T(8,128)(2,1)S(1)} %add_add_fusion), channel_id=1, source_target_pairs={{0,4},{4,0},{8,12},{12,8},{16,20},{20,16},{24,28},{28,24},{32,36},... | collective-permute-start | bytes 294920 | tf_op jit(solution)/shard_map/ppermute | solution.py:485
  116.7 1.6 %collective-permute-start.22 = (bf16[192,256]{1,0:T(8,128)(2,1)S(1)}, bf16[192,256]{1,0:T(8,128)(2,1)S(1)}, u32[]{:S(2)}, u32[]{:S(2)}) collective-permute-start(bf16[192,256]{1,0:T(8,128)(2,1)S(1)} %add_add_fusion), channel_id=1, source_target_pairs={{0,12},{4,8},{8,4},{12,0},{16,28},{20,24},{24,20},{28,16},{32,44},... | collective-permute-start | bytes 294920 | tf_op jit(solution)/shard_map/ppermute | solution.py:485
  118.3 0.7 fusion.1
  119.1 2.2 %collective-permute-done.21 = bf16[192,256]{1,0:T(8,128)(2,1)S(1)} collective-permute-done((bf16[192,256]{1,0:T(8,128)(2,1)S(1)}, bf16[192,256]{1,0:T(8,128)(2,1)S(1)}, u32[]{:S(2)}, u32[]{:S(2)}) %collective-permute-start.21) | collective-permute-done | bytes 98336 | tf_op jit(solution)/shard_map/ppermute | solution.py:485
  121.3 2.1 %collective-permute-done.22 = bf16[192,256]{1,0:T(8,128)(2,1)S(1)} collective-permute-done((bf16[192,256]{1,0:T(8,128)(2,1)S(1)}, bf16[192,256]{1,0:T(8,128)(2,1)S(1)}, u32[]{:S(2)}, u32[]{:S(2)}) %collective-permute-start.22) | collective-permute-done | bytes 98336 | tf_op jit(solution)/shard_map/ppermute | solution.py:485
  123.5 0.1 maximum_convert_fusion
  123.6 0.2 slice.68
  123.7 0.2 slice.67
  123.9 1.1 copy.44
  125.0 0.1 copy.43
  125.1 0.2 copy.42
  125.3 0.6 pad_maximum_fusion.5
  (51 shorter events, 0.4 us)
Async XLA Ops:
  0.6 10.1 %copy-start.8 = (bf16[256,3,128]{2,0,1:T(8,128)(2,1)S(1)}, bf16[256,3,128]{2,0,1:T(8,128)(2,1)}, u32[]{:S(2)}) copy-start(bf16[256,3,128]{2,0,1:T(8,128)(2,1)} %param.21) | copy-start | bytes 589828
  0.6 15.0 %copy-start.10 = (s32[128,4]{0,1:T(4,128)S(1)}, s32[128,4]{0,1:T(4,128)}, u32[]{:S(2)}) copy-start(s32[128,4]{0,1:T(4,128)} %param.20) | copy-start | bytes 6148
  2.6 14.0 %copy-start.9 = (bf16[64,8,1,64]{3,1,0,2:T(8,128)(2,1)S(1)}, bf16[64,8,1,64]{3,1,0,2:T(8,128)(2,1)}, u32[]{:S(2)}) copy-start(bf16[64,8,1,64]{3,1,0,2:T(8,128)(2,1)} %constant.112.clone.1) | copy-start | bytes 196612
  3.3 1.3 %collective-permute-start = (bf16[64,256]{1,0:T(8,128)(2,1)S(1)}, bf16[64,256]{1,0:T(8,128)(2,1)S(1)}, u32[]{:S(2)}, u32[]{:S(2)}) collective-permute-start(bf16[64,256]{1,0:T(8,128)(2,1)S(1)} %reshape.83), channel_id=1, source_target_pairs={{8,16},{12,20},{16,8},{20,12},{24,32},{28,36},{32,24},{36,28},{40,... | collective-permute-start | bytes 98312 | tf_op jit(solution)/shard_map/ppermute | solution.py:492
  4.6 8.1 %collective-permute-start.1 = (bf16[2,64,256]{2,1,0:T(8,128)(2,1)S(1)}, bf16[2,64,256]{2,1,0:T(8,128)(2,1)S(1)}, u32[]{:S(2)}, u32[]{:S(2)}) collective-permute-start(bf16[2,64,256]{2,1,0:T(8,128)(2,1)S(1)} %pad_maximum_fusion.4), channel_id=1, source_target_pairs={{0,8},{4,12},{8,0},{12,4},{16,24},{20,28},{24,16},{28,20},{32,40},... | collective-permute-start | bytes 196616 | tf_op jit(solution)/shard_map/ppermute | solution.py:485
  10.7 5.0 %collective-permute-start.3 = (bf16[3,4,64,128]{3,2,1,0:T(8,128)(2,1)S(1)}, bf16[3,4,64,128]{3,2,1,0:T(8,128)(2,1)S(1)}, u32[]{:S(2)}, u32[]{:S(2)}) collective-permute-start(bf16[3,4,64,128]{3,2,1,0:T(8,128)(2,1)S(1)} %bitcast.85), channel_id=1, source_target_pairs={{0,4},{4,0},{8,12},{12,8},{16,20},{20,16},{24,28},{28,24},{32,36},... | collective-permute-start | bytes 589832 | tf_op jit(solution)/shard_map/ppermute | solution.py:485
  12.8 3.2 %collective-permute-start.2 = (bf16[4,64,256]{2,1,0:T(8,128)(2,1)S(1)}, bf16[4,64,256]{2,1,0:T(8,128)(2,1)S(1)}, u32[]{:S(2)}, u32[]{:S(2)}) collective-permute-start(bf16[4,64,256]{2,1,0:T(8,128)(2,1)S(1)} %pad_maximum_fusion.2), channel_id=1, source_target_pairs={{0,4},{4,0},{8,12},{12,8},{16,20},{20,16},{24,28},{28,24},{32,36},... | collective-permute-start | bytes 393224 | tf_op jit(solution)/shard_map/ppermute | solution.py:485
  18.6 20.3 %collective-permute-start.4 = (bf16[2,3,4,64,128]{4,3,2,1,0:T(8,128)(2,1)S(1)}, bf16[2,3,4,64,128]{4,3,2,1,0:T(8,128)(2,1)S(1)}, u32[]{:S(2)}, u32[]{:S(2)}) collective-permute-start(bf16[2,3,4,64,128]{4,3,2,1,0:T(8,128)(2,1)S(1)} %pad_maximum_fusion.1), channel_id=1, source_target_pairs={{0,8},{4,12},{8,0},{12,4},{16,24},{20,28},{24,16},{28,20},{32,40},... | collective-permute-start | bytes 1179656 | tf_op jit(solution)/shard_map/ppermute | solution.py:485
  20.3 18.7 %copy-start.4 = (s32[3]{0:T(128)S(1)}, s32[3]{0:T(128)}, u32[]{:S(2)}) copy-start(s32[3]{0:T(128)} %pad_add_fusion.ids) | copy-start | bytes 40
  20.3 18.7 %copy-start.5 = (f32[128]{0:T(128)S(1)}, f32[128]{0:T(128)}, u32[]{:S(2)}) copy-start(f32[128]{0:T(128)} %param.18) | copy-start | bytes 1540
  20.3 18.7 %copy-start.6 = (f32[128]{0:T(128)S(1)}, f32[128]{0:T(128)}, u32[]{:S(2)}) copy-start(f32[128]{0:T(128)} %param.19) | copy-start | bytes 1540
  39.0 29.1 %slice-start = ((s8[7077888]{0:T(1024)(128)(4,1)}), s8[4194304]{0:T(1024)(128)(4,1)S(1)}, s32[]{:S(2)}) async-start(s8[7077888]{0:T(1024)(128)(4,1)} %bitcast.75), calls=%async_computation | async-start | bytes 8388608
  39.0 20.6 %copy-start.7 = (bf16[768,1024]{1,0:T(8,128)(2,1)S(1)}, bf16[768,1024]{1,0:T(8,128)(2,1)}, u32[]{:S(2)}) copy-start(bf16[768,1024]{1,0:T(8,128)(2,1)} %get-tuple-element.42.hid) | copy-start | bytes 4718596
  39.0 29.0 %slice-start.1 = ((s8[7077888]{0:T(1024)(128)(4,1)}), s8[2883584]{0:T(1024)(128)(4,1)S(1)}, s32[]{:S(2)}) async-start(s8[7077888]{0:T(1024)(128)(4,1)} %bitcast.75), calls=%async_computation.1 | async-start | bytes 5767168
  59.6 8.4 %copy-start = (bf16[256,1024]{1,0:T(8,128)(2,1)S(1)}, bf16[256,1024]{1,0:T(8,128)(2,1)}, u32[]{:S(2)}) copy-start(bf16[256,1024]{1,0:T(8,128)(2,1)} %copy.35.pext) | copy-start | bytes 1572868
  59.7 8.4 %copy-start.1 = (bf16[768,1024]{1,0:T(8,128)(2,1)S(1)}, bf16[768,1024]{1,0:T(8,128)(2,1)}, u32[]{:S(2)}) copy-start(bf16[768,1024]{1,0:T(8,128)(2,1)} %get-tuple-element.48.nrm) | copy-start | bytes 4718596
  59.7 8.4 %copy-start.2 = (f32[768,128]{1,0:T(8,128)S(1)}, f32[768,128]{1,0:T(8,128)}, u32[]{:S(2)}) copy-start(f32[768,128]{1,0:T(8,128)} %get-tuple-element.49.sc) | copy-start | bytes 1179652
  59.7 8.4 %copy-start.3 = (f32[8,1024]{1,0:T(8,128)S(1)}, f32[8,1024]{1,0:T(8,128)}, u32[]{:S(2)}) copy-start(f32[8,1024]{1,0:T(8,128)} %get-tuple-element.51.inv) | copy-start | bytes 98308
  62.9 22.2 %collective-permute-start.8 = (bf16[4,9,48,128]{3,2,1,0:T(8,128)(2,1)S(1)}, bf16[4,9,48,128]{3,2,1,0:T(8,128)(2,1)S(1)}, u32[]{:S(2)}, u32[]{:S(2)}) collective-permute-start(bf16[4,9,48,128]{3,2,1,0:T(8,128)(2,1)S(1)} %get-tuple-element.56), channel_id=1, source_target_pairs={{0,64},{4,68},{8,72},{12,76},{16,80},{20,84},{24,88},{28,92},{32,9... | collective-permute-start | bytes 1327112 | tf_op jit(solution)/shard_map/ppermute | solution.py:534
  66.3 18.7 %collective-permute-start.9 = (bf16[4,9,48,128]{3,2,1,0:T(8,128)(2,1)S(1)}, bf16[4,9,48,128]{3,2,1,0:T(8,128)(2,1)S(1)}, u32[]{:S(2)}, u32[]{:S(2)}) collective-permute-start(bf16[4,9,48,128]{3,2,1,0:T(8,128)(2,1)S(1)} %get-tuple-element.57), channel_id=1, source_target_pairs={{0,192},{4,196},{8,200},{12,204},{16,208},{20,212},{24,216},{28,22... | collective-permute-start | bytes 1327112 | tf_op jit(solution)/shard_map/ppermute | solution.py:534
  74.4 4.5 %collective-permute-start.7 = (bf16[192,256]{1,0:T(8,128)(2,1)S(1)}, bf16[192,256]{1,0:T(8,128)(2,1)S(1)}, u32[]{:S(2)}, u32[]{:S(2)}) collective-permute-start(bf16[192,256]{1,0:T(8,128)(2,1)S(1)} %get-tuple-element.55), channel_id=1, source_target_pairs={{0,3},{1,0},{2,1},{3,2},{4,7},{5,4},{6,5},{7,6},{8,11},{9,8},{10,9... | collective-permute-start | bytes 294920 | tf_op jit(solution)/shard_map/ppermute | solution.py:540
  77.2 5.1 %collective-permute-start.6 = (bf16[192,256]{1,0:T(8,128)(2,1)S(1)}, bf16[192,256]{1,0:T(8,128)(2,1)S(1)}, u32[]{:S(2)}, u32[]{:S(2)}) collective-permute-start(bf16[192,256]{1,0:T(8,128)(2,1)S(1)} %get-tuple-element.54), channel_id=1, source_target_pairs={{0,2},{1,3},{2,0},{3,1},{4,6},{5,7},{6,4},{7,5},{8,10},{9,11},{10,... | collective-permute-start | bytes 294920 | tf_op jit(solution)/shard_map/ppermute | solution.py:540
  77.5 7.5 %collective-permute-start.5 = (bf16[192,256]{1,0:T(8,128)(2,1)S(1)}, bf16[192,256]{1,0:T(8,128)(2,1)S(1)}, u32[]{:S(2)}, u32[]{:S(2)}) collective-permute-start(bf16[192,256]{1,0:T(8,128)(2,1)S(1)} %get-tuple-element.53), channel_id=1, source_target_pairs={{0,1},{1,2},{2,3},{3,0},{4,5},{5,6},{6,7},{7,4},{8,9},{9,10},{10,1... | collective-permute-start | bytes 294920 | tf_op jit(solution)/shard_map/ppermute | solution.py:540
  78.8 17.8 %collective-permute-start.13 = (bf16[4,9,48,128]{3,2,1,0:T(8,128)(2,1)S(1)}, bf16[4,9,48,128]{3,2,1,0:T(8,128)(2,1)S(1)}, u32[]{:S(2)}, u32[]{:S(2)}) collective-permute-start(bf16[4,9,48,128]{3,2,1,0:T(8,128)(2,1)S(1)} %get-tuple-element.60), channel_id=1, source_target_pairs={{0,128},{4,132},{8,136},{12,140},{16,144},{20,148},{24,152},{28,15... | collective-permute-start | bytes 1327112 | tf_op jit(solution)/shard_map/ppermute | solution.py:534
  85.1 6.0 %collective-permute-start.12 = (bf16[192,256]{1,0:T(8,128)(2,1)S(1)}, bf16[192,256]{1,0:T(8,128)(2,1)S(1)}, u32[]{:S(2)}, u32[]{:S(2)}) collective-permute-start(bf16[192,256]{1,0:T(8,128)(2,1)S(1)} %reduce-precision_convert_fusion.1), channel_id=1, source_target_pairs={{0,48},{4,52},{8,56},{12,60},{16,32},{20,36},{24,40},{28,44},{32,1... | collective-permute-start | bytes 294920 | tf_op jit(solution)/shard_map/ppermute | solution.py:485
  88.5 8.1 %collective-permute-start.11 = (bf16[192,256]{1,0:T(8,128)(2,1)S(1)}, bf16[192,256]{1,0:T(8,128)(2,1)S(1)}, u32[]{:S(2)}, u32[]{:S(2)}) collective-permute-start(bf16[192,256]{1,0:T(8,128)(2,1)S(1)} %reduce-precision_convert_fusion.1), channel_id=1, source_target_pairs={{0,32},{4,36},{8,40},{12,44},{16,48},{20,52},{24,56},{28,60},{32,0... | collective-permute-start | bytes 294920 | tf_op jit(solution)/shard_map/ppermute | solution.py:485
  89.1 7.5 %collective-permute-start.10 = (bf16[192,256]{1,0:T(8,128)(2,1)S(1)}, bf16[192,256]{1,0:T(8,128)(2,1)S(1)}, u32[]{:S(2)}, u32[]{:S(2)}) collective-permute-start(bf16[192,256]{1,0:T(8,128)(2,1)S(1)} %reduce-precision_convert_fusion.1), channel_id=1, source_target_pairs={{0,16},{4,20},{8,24},{12,28},{16,0},{20,4},{24,8},{28,12},{32,48},... | collective-permute-start | bytes 294920 | tf_op jit(solution)/shard_map/ppermute | solution.py:485
  96.7 8.2 %collective-permute-start.16 = (bf16[192,256]{1,0:T(8,128)(2,1)S(1)}, bf16[192,256]{1,0:T(8,128)(2,1)S(1)}, u32[]{:S(2)}, u32[]{:S(2)}) collective-permute-start(bf16[192,256]{1,0:T(8,128)(2,1)S(1)} %reduce-precision_convert_fusion), channel_id=1, source_target_pairs={{0,192},{4,196},{8,200},{12,204},{16,208},{20,212},{24,216},{28,22... | collective-permute-start | bytes 294920 | tf_op jit(solution)/shard_map/ppermute | solution.py:485
  99.0 10.3 %collective-permute-start.15 = (bf16[192,256]{1,0:T(8,128)(2,1)S(1)}, bf16[192,256]{1,0:T(8,128)(2,1)S(1)}, u32[]{:S(2)}, u32[]{:S(2)}) collective-permute-start(bf16[192,256]{1,0:T(8,128)(2,1)S(1)} %reduce-precision_convert_fusion), channel_id=1, source_target_pairs={{0,128},{4,132},{8,136},{12,140},{16,144},{20,148},{24,152},{28,15... | collective-permute-start | bytes 294920 | tf_op jit(solution)/shard_map/ppermute | solution.py:485
  99.0 10.3 %collective-permute-start.14 = (bf16[192,256]{1,0:T(8,128)(2,1)S(1)}, bf16[192,256]{1,0:T(8,128)(2,1)S(1)}, u32[]{:S(2)}, u32[]{:S(2)}) collective-permute-start(bf16[192,256]{1,0:T(8,128)(2,1)S(1)} %reduce-precision_convert_fusion), channel_id=1, source_target_pairs={{0,64},{4,68},{8,72},{12,76},{16,80},{20,84},{24,88},{28,92},{32,9... | collective-permute-start | bytes 294920 | tf_op jit(solution)/shard_map/ppermute | solution.py:485
  100.3 9.1 %collective-permute-start.17 = (bf16[9,48,128]{2,1,0:T(8,128)(2,1)S(1)}, bf16[9,48,128]{2,1,0:T(8,128)(2,1)S(1)}, u32[]{:S(2)}, u32[]{:S(2)}) collective-permute-start(bf16[9,48,128]{2,1,0:T(8,128)(2,1)S(1)} %get-tuple-element.75), channel_id=1, source_target_pairs={{0,16},{4,20},{8,24},{12,28},{16,32},{20,36},{24,40},{28,44},{32,4... | collective-permute-start | bytes 331784 | tf_op jit(solution)/shard_map/ppermute | solution.py:559
  102.5 6.9 %collective-permute-start.18 = (bf16[9,48,128]{2,1,0:T(8,128)(2,1)S(1)}, bf16[9,48,128]{2,1,0:T(8,128)(2,1)S(1)}, u32[]{:S(2)}, u32[]{:S(2)}) collective-permute-start(bf16[9,48,128]{2,1,0:T(8,128)(2,1)S(1)} %get-tuple-element.74), channel_id=1, source_target_pairs={{0,48},{4,52},{8,56},{12,60},{16,0},{20,4},{24,8},{28,12},{32,16},... | collective-permute-start | bytes 331784 | tf_op jit(solution)/shard_map/ppermute | solution.py:559
  104.9 13.4 %collective-permute-start.19 = (bf16[9,48,128]{2,1,0:T(8,128)(2,1)S(1)}, bf16[9,48,128]{2,1,0:T(8,128)(2,1)S(1)}, u32[]{:S(2)}, u32[]{:S(2)}) collective-permute-start(bf16[9,48,128]{2,1,0:T(8,128)(2,1)S(1)} %get-tuple-element.73), channel_id=1, source_target_pairs={{0,32},{4,36},{8,40},{12,44},{16,48},{20,52},{24,56},{28,60},{32,0... | collective-permute-start | bytes 331784 | tf_op jit(solution)/shard_map/ppermute | solution.py:559
  109.4 9.6 %collective-permute-start.20 = (bf16[192,256]{1,0:T(8,128)(2,1)S(1)}, bf16[192,256]{1,0:T(8,128)(2,1)S(1)}, u32[]{:S(2)}, u32[]{:S(2)}) collective-permute-start(bf16[192,256]{1,0:T(8,128)(2,1)S(1)} %add_add_fusion), channel_id=1, source_target_pairs={{0,4},{4,0},{8,12},{12,8},{16,20},{20,16},{24,28},{28,24},{32,36},... | collective-permute-start | bytes 294920 | tf_op jit(solution)/shard_map/ppermute | solution.py:485
  116.7 4.6 %collective-permute-start.21 = (bf16[192,256]{1,0:T(8,128)(2,1)S(1)}, bf16[192,256]{1,0:T(8,128)(2,1)S(1)}, u32[]{:S(2)}, u32[]{:S(2)}) collective-permute-start(bf16[192,256]{1,0:T(8,128)(2,1)S(1)} %add_add_fusion), channel_id=1, source_target_pairs={{0,8},{4,12},{8,0},{12,4},{16,24},{20,28},{24,16},{28,20},{32,40},... | collective-permute-start | bytes 294920 | tf_op jit(solution)/shard_map/ppermute | solution.py:485
  116.7 6.8 %collective-permute-start.22 = (bf16[192,256]{1,0:T(8,128)(2,1)S(1)}, bf16[192,256]{1,0:T(8,128)(2,1)S(1)}, u32[]{:S(2)}, u32[]{:S(2)}) collective-permute-start(bf16[192,256]{1,0:T(8,128)(2,1)S(1)} %add_add_fusion), channel_id=1, source_target_pairs={{0,12},{4,8},{8,4},{12,0},{16,28},{20,24},{24,20},{28,16},{32,44},... | collective-permute-start | bytes 294920 | tf_op jit(solution)/shard_map/ppermute | solution.py:485

commit v9 on v8

--- a/solution.py
+++ b/solution.py
@@ -559,7 +559,7 @@
             part = lax.ppermute(part.astype(BF16), "seq", pairs)
         parts.append(part)
     total = quad_sum(total, 16, 32)
-    total, parts[1], parts[3] = lax.optimization_barrier((total, parts[1], parts[3]))
+    total, parts[1] = lax.optimization_barrier((total, parts[1]))
     weight_grad = sum(part.astype(F32) for part in parts)
     weight_grad = jnp.transpose(weight_grad.reshape(3, heads, rows, hd), (2, 0, 1, 3))
 

time: 128 us -> 126 us (0.984); the launches traced: 126 us -> 126 us
    ppermute x3, waiting for transfers between devices: 5.48 us -> 1.63 us  [per_device(): total = total + lax.ppermute(stem[k], 'head', pairs).astype(F32)]
    ppermute x13, waiting for transfers between devices: 10.3 us -> 12.7 us  [xor(): return lax.ppermute(value, 'seq', [(a, a ^ mask) for a in range(seq)])]
    ppermute x3, starting transfers between devices: 9.02 us -> 6.73 us  [per_device(): part = lax.ppermute(part.astype(BF16), 'seq', pairs)]
    ppermute x3, waiting for transfers between devices: 0.01 us -> 2.05 us  [per_device(): part = lax.ppermute(part.astype(BF16), 'seq', pairs)]
  transfers between devices with their start and end apart: 23 -> 23, of which waited for: 8 -> 7; matrix products, arithmetic and copies ran while one was open for 2% -> 2% of each run, Pallas kernels for 20% -> 20%
where the time goes in v9:
time: 126 us
  starting transfers between devices  49.7 us (39%)
  Pallas kernels  48.6 us (39%)
  waiting for transfers between devices  16.4 us (13%)
  local copies, waits for them, and re-layouts  7.5 us (6%)
  other arithmetic  2.99 us (2%)
    ppermute x13, starting transfers between devices, xor(): return lax.ppermute(value, 'seq', [(a, a ^ mask) for a in range(seq)])  30.8 us
    pallas_call x1, Pallas kernels, attention(): pl.pallas_call(attention_kernel, grid_spec=pltpu.PrefetchScalarGridSpec(n...  20.6 us
    pallas_call x1, Pallas kernels, forward(): pl.pallas_call(forward_kernel, grid_spec=pltpu.PrefetchScalarGridSpec(num...  18.6 us
    ppermute x13, waiting for transfers between devices, xor(): return lax.ppermute(value, 'seq', [(a, a ^ mask) for a in range(seq)])  12.7 us
    ppermute x3, starting transfers between devices, per_device(): part = lax.ppermute(part.astype(BF16), 'seq', pairs)  6.73 us
    ppermute x3, starting transfers between devices, per_device(): weight[k] = lax.ppermute(weight[k], 'seq', pairs)  6.48 us
    pallas_call x1, Pallas kernels, stem_part(): pl.pallas_call(stem_kernel, grid_spec=pltpu.PrefetchScalarGridSpec(num_sc...  6.25 us
    ppermute x3, starting transfers between devices, per_device(): total = total + lax.ppermute(stem[k], 'head', pairs).astype(F32)  5.06 us
  transfers between devices with their start and end apart: 23, of which 7 were waited for; matrix products, arithmetic and copies ran while one was open for 2% of the time, Pallas kernels for 20%

profile of v9, /device:TPU:1, one launch (start us, length us, event | category | flops | bytes accessed | tf_op | source)
XLA Modules:
  0.0 126.2 jit_solution(11493860656664412970)
XLA Ops:
  0.7 1.0 copy.30
  1.6 1.0 copy.31
  2.6 0.0 copy-start.9
  2.6 0.7 reshape.83
  3.3 0.7 collective-permute-start
  4.0 0.7 stack_reshape.8
  4.6 6.0 %collective-permute-start.1 = (bf16[2,64,256]{2,1,0:T(8,128)(2,1)S(1)}, bf16[2,64,256]{2,1,0:T(8,128)(2,1)S(1)}, u32[]{:S(2)}, u32[]{:S(2)}) collective-permute-start(bf16[2,64,256]{2,1,0:T(8,128)(2,1)S(1)} %pad_maximum_fusion.4), channel_id=1, source_target_pairs={{0,8},{4,12},{8,0},{12,4},{16,24},{20,28},{24,16},{28,20},{32,40},... | collective-permute-start | bytes 196616 | tf_op jit(solution)/shard_map/ppermute | solution.py:485
  10.7 2.0 %collective-permute-start.3 = (bf16[3,4,64,128]{3,2,1,0:T(8,128)(2,1)S(1)}, bf16[3,4,64,128]{3,2,1,0:T(8,128)(2,1)S(1)}, u32[]{:S(2)}, u32[]{:S(2)}) collective-permute-start(bf16[3,4,64,128]{3,2,1,0:T(8,128)(2,1)S(1)} %bitcast.85), channel_id=1, source_target_pairs={{0,4},{4,0},{8,12},{12,8},{16,20},{20,16},{24,28},{28,24},{32,36},... | collective-permute-start | bytes 589832 | tf_op jit(solution)/shard_map/ppermute | solution.py:485
  12.7 0.0 collective-permute-done.1
  12.8 2.2 %collective-permute-start.2 = (bf16[4,64,256]{2,1,0:T(8,128)(2,1)S(1)}, bf16[4,64,256]{2,1,0:T(8,128)(2,1)S(1)}, u32[]{:S(2)}, u32[]{:S(2)}) collective-permute-start(bf16[4,64,256]{2,1,0:T(8,128)(2,1)S(1)} %pad_maximum_fusion.2), channel_id=1, source_target_pairs={{0,4},{4,0},{8,12},{12,8},{16,20},{20,16},{24,28},{28,24},{32,36},... | collective-permute-start | bytes 393224 | tf_op jit(solution)/shard_map/ppermute | solution.py:485
  15.0 0.7 pad_add_fusion.ids
  15.7 0.1 copy.36.lists
  15.8 0.0 collective-permute-done.3
  15.8 0.2 collective-permute-done.2
  16.0 0.1 concatenate.26
  16.2 0.1 concatenate.27
  16.3 0.1 concatenate.28
  16.5 0.1 concatenate.30
  16.6 0.2 maximum_maximum_fusion
  16.8 0.7 copy.34
  17.6 1.0 copy.35.pext
  18.6 1.7 %collective-permute-start.4 = (bf16[2,3,4,64,128]{4,3,2,1,0:T(8,128)(2,1)S(1)}, bf16[2,3,4,64,128]{4,3,2,1,0:T(8,128)(2,1)S(1)}, u32[]{:S(2)}, u32[]{:S(2)}) collective-permute-start(bf16[2,3,4,64,128]{4,3,2,1,0:T(8,128)(2,1)S(1)} %pad_maximum_fusion.1), channel_id=1, source_target_pairs={{0,8},{4,12},{8,0},{12,4},{16,24},{20,28},{24,16},{28,20},{32,40},... | collective-permute-start | bytes 1179656 | tf_op jit(solution)/shard_map/ppermute | solution.py:485
  20.3 18.6 %forward.1 = (f32[1024,1152]{1,0:T(8,128)}, bf16[768,1024]{1,0:T(8,128)(2,1)}, bf16[768,1024]{1,0:T(8,128)(2,1)}, f32[8,1024]{1,0:T(8,128)}, f32[8,1152]{1,0:T(8,128)}, /*index=5*/f32[768,128]{1,0:T(8,128)}) custom-call(s32[3]{0:T(128)} %pad_add_fusion.ids, bf16[256,1024]{1,0:T(8,128)(2,1)} %copy.35.pext, bf16[192,3072]{1,0:T(8,128)(2,1)} %stem.1, ...), custom_call_target="tpu_custom_call" | custom-call | flops 8858370048 | bytes 25165824 | tf_op jit(solution)/shard_map/forward/pallas_call | solution.py:140
  38.9 0.1 pad_maximum_fusion.og
  39.0 0.0 slice-start
  39.0 0.0 slice-start.1
  39.0 20.6 %attention.1 = (bf16[3,1024,384]{2,1,0:T(8,128)(2,1)S(1)}, f32[2,8,1024]{2,1,0:T(8,128)S(1)}) custom-call(s32[3]{0:T(128)S(1)} %copy-done.4, s32[128,4]{1,0:T(8,128)S(1)} %copy.36.lists, f32[1024,1152]{1,0:T(8,128)} %get-tuple-element.42.pq.pk.pv, f32[1024,1152]{1,0:T(8,128)} %get-tuple-element.42.pq.pk.pv, f32[1024,1152]{1,0:T(8,128)} %get-tuple-element.42.pq.pk.pv, ...), custom_call_target="tpu_custom_call" | custom-call | flops 2013265920 | bytes 10485760 | tf_op jit(solution)/shard_map/attention/pallas_call | solution.py:321
  59.6 0.0 copy-start
  59.7 3.2 %weight_part.1 = (bf16[4,9,48,128]{3,2,1,0:T(8,128)(2,1)S(1)}, bf16[4,9,48,128]{3,2,1,0:T(8,128)(2,1)S(1)}, bf16[4,9,48,128]{3,2,1,0:T(8,128)(2,1)S(1)}, bf16[4,9,48,128]{3,2,1,0:T(8,128)(2,1)S(1)}) custom-call(s32[3]{0:T(128)S(1)} %copy-done.4, bf16[768,1024]{1,0:T(8,128)(2,1)S(1)} %copy-done.7, bf16[3,1024,384]{2,1,0:T(8,128)(2,1)S(1)} %get-tuple-element.45.mixed), custom_call_target="tpu_custom_call" | custom-call | flops 1811939328 | bytes 6291456 | tf_op jit(solution)/shard_map/weight_part/pallas_call | solution.py:378
  62.9 3.5 %collective-permute-start.8 = (bf16[4,9,48,128]{3,2,1,0:T(8,128)(2,1)S(1)}, bf16[4,9,48,128]{3,2,1,0:T(8,128)(2,1)S(1)}, u32[]{:S(2)}, u32[]{:S(2)}) collective-permute-start(bf16[4,9,48,128]{3,2,1,0:T(8,128)(2,1)S(1)} %get-tuple-element.55), channel_id=1, source_target_pairs={{0,64},{4,68},{8,72},{12,76},{16,80},{20,84},{24,88},{28,92},{32,9... | collective-permute-start | bytes 1327112 | tf_op jit(solution)/shard_map/ppermute | solution.py:534
  66.4 1.6 %collective-permute-start.9 = (bf16[4,9,48,128]{3,2,1,0:T(8,128)(2,1)S(1)}, bf16[4,9,48,128]{3,2,1,0:T(8,128)(2,1)S(1)}, u32[]{:S(2)}, u32[]{:S(2)}) collective-permute-start(bf16[4,9,48,128]{3,2,1,0:T(8,128)(2,1)S(1)} %get-tuple-element.56), channel_id=1, source_target_pairs={{0,192},{4,196},{8,200},{12,204},{16,208},{20,212},{24,216},{28,22... | collective-permute-start | bytes 1327112 | tf_op jit(solution)/shard_map/ppermute | solution.py:534
  68.0 6.3 %stem_part.1 = (f32[192,256]{1,0:T(8,128)S(1)}, bf16[192,256]{1,0:T(8,128)(2,1)S(1)}, bf16[192,256]{1,0:T(8,128)(2,1)S(1)}, bf16[192,256]{1,0:T(8,128)(2,1)S(1)}) custom-call(s32[3]{0:T(128)S(1)} %copy-done.4, bf16[9,16,4,48,128]{4,3,2,1,0:T(8,128)(2,1)S(1)} %bitcast.77, bf16[3,1024,384]{2,1,0:T(8,128)(2,1)S(1)} %get-tuple-element.45.mixed, ...), custom_call_target="tpu_custom_call" | custom-call | flops 1000 | bytes 1000 | tf_op jit(solution)/shard_map/stem_part/pallas_call | solution.py:431
  74.3 1.4 %collective-permute-start.5 = (bf16[192,256]{1,0:T(8,128)(2,1)S(1)}, bf16[192,256]{1,0:T(8,128)(2,1)S(1)}, u32[]{:S(2)}, u32[]{:S(2)}) collective-permute-start(bf16[192,256]{1,0:T(8,128)(2,1)S(1)} %get-tuple-element.52), channel_id=1, source_target_pairs={{0,1},{1,2},{2,3},{3,0},{4,5},{5,6},{6,7},{7,4},{8,9},{9,10},{10,1... | collective-permute-start | bytes 294920 | tf_op jit(solution)/shard_map/ppermute | solution.py:540
  75.7 2.6 %collective-permute-start.6 = (bf16[192,256]{1,0:T(8,128)(2,1)S(1)}, bf16[192,256]{1,0:T(8,128)(2,1)S(1)}, u32[]{:S(2)}, u32[]{:S(2)}) collective-permute-start(bf16[192,256]{1,0:T(8,128)(2,1)S(1)} %get-tuple-element.53), channel_id=1, source_target_pairs={{0,2},{1,3},{2,0},{3,1},{4,6},{5,7},{6,4},{7,5},{8,10},{9,11},{10,... | collective-permute-start | bytes 294920 | tf_op jit(solution)/shard_map/ppermute | solution.py:540
  78.3 1.1 collective-permute-start.7
  79.4 1.4 %collective-permute-start.13 = (bf16[4,9,48,128]{3,2,1,0:T(8,128)(2,1)S(1)}, bf16[4,9,48,128]{3,2,1,0:T(8,128)(2,1)S(1)}, u32[]{:S(2)}, u32[]{:S(2)}) collective-permute-start(bf16[4,9,48,128]{3,2,1,0:T(8,128)(2,1)S(1)} %get-tuple-element.59), channel_id=1, source_target_pairs={{0,128},{4,132},{8,136},{12,140},{16,144},{20,148},{24,152},{28,15... | collective-permute-start | bytes 1327112 | tf_op jit(solution)/shard_map/ppermute | solution.py:534
  80.7 1.6 %collective-permute-done.6 = bf16[192,256]{1,0:T(8,128)(2,1)S(1)} collective-permute-done((bf16[192,256]{1,0:T(8,128)(2,1)S(1)}, bf16[192,256]{1,0:T(8,128)(2,1)S(1)}, u32[]{:S(2)}, u32[]{:S(2)}) %collective-permute-start.6) | collective-permute-done | bytes 98336 | tf_op jit(solution)/shard_map/ppermute | solution.py:540
  82.3 0.1 convert_add_fusion.1
  82.4 2.5 %collective-permute-start.10 = (bf16[192,256]{1,0:T(8,128)(2,1)S(1)}, bf16[192,256]{1,0:T(8,128)(2,1)S(1)}, u32[]{:S(2)}, u32[]{:S(2)}) collective-permute-start(bf16[192,256]{1,0:T(8,128)(2,1)S(1)} %reduce-precision_convert_fusion.1), channel_id=1, source_target_pairs={{0,16},{4,20},{8,24},{12,28},{16,0},{20,4},{24,8},{28,12},{32,48},... | collective-permute-start | bytes 294920 | tf_op jit(solution)/shard_map/ppermute | solution.py:485
  84.9 5.1 %collective-permute-start.11 = (bf16[192,256]{1,0:T(8,128)(2,1)S(1)}, bf16[192,256]{1,0:T(8,128)(2,1)S(1)}, u32[]{:S(2)}, u32[]{:S(2)}) collective-permute-start(bf16[192,256]{1,0:T(8,128)(2,1)S(1)} %reduce-precision_convert_fusion.1), channel_id=1, source_target_pairs={{0,32},{4,36},{8,40},{12,44},{16,48},{20,52},{24,56},{28,60},{32,0... | collective-permute-start | bytes 294920 | tf_op jit(solution)/shard_map/ppermute | solution.py:485
  90.1 3.3 %collective-permute-done.11 = bf16[192,256]{1,0:T(8,128)(2,1)S(1)} collective-permute-done((bf16[192,256]{1,0:T(8,128)(2,1)S(1)}, bf16[192,256]{1,0:T(8,128)(2,1)S(1)}, u32[]{:S(2)}, u32[]{:S(2)}) %collective-permute-start.11) | collective-permute-done | bytes 98336 | tf_op jit(solution)/shard_map/ppermute | solution.py:485
  93.4 4.7 %collective-permute-done.12 = bf16[192,256]{1,0:T(8,128)(2,1)S(1)} collective-permute-done((bf16[192,256]{1,0:T(8,128)(2,1)S(1)}, bf16[192,256]{1,0:T(8,128)(2,1)S(1)}, u32[]{:S(2)}, u32[]{:S(2)}) %collective-permute-start.12) | collective-permute-done | bytes 98336 | tf_op jit(solution)/shard_map/ppermute | solution.py:485
  98.1 0.1 add_add_fusion.1
  98.2 0.1 collective-permute-start.14
  98.3 1.6 %collective-permute-start.15 = (bf16[192,256]{1,0:T(8,128)(2,1)S(1)}, bf16[192,256]{1,0:T(8,128)(2,1)S(1)}, u32[]{:S(2)}, u32[]{:S(2)}) collective-permute-start(bf16[192,256]{1,0:T(8,128)(2,1)S(1)} %reduce-precision_convert_fusion), channel_id=1, source_target_pairs={{0,128},{4,132},{8,136},{12,140},{16,144},{20,148},{24,152},{28,15... | collective-permute-start | bytes 294920 | tf_op jit(solution)/shard_map/ppermute | solution.py:485
  99.9 2.2 %collective-permute-start.16 = (bf16[192,256]{1,0:T(8,128)(2,1)S(1)}, bf16[192,256]{1,0:T(8,128)(2,1)S(1)}, u32[]{:S(2)}, u32[]{:S(2)}) collective-permute-start(bf16[192,256]{1,0:T(8,128)(2,1)S(1)} %reduce-precision_convert_fusion), channel_id=1, source_target_pairs={{0,192},{4,196},{8,200},{12,204},{16,208},{20,212},{24,216},{28,22... | collective-permute-start | bytes 294920 | tf_op jit(solution)/shard_map/ppermute | solution.py:485
  102.1 0.2 convert_add_fusion
  102.3 0.1 fusion.2
  102.4 2.5 %collective-permute-start.17 = (bf16[9,48,128]{2,1,0:T(8,128)(2,1)S(1)}, bf16[9,48,128]{2,1,0:T(8,128)(2,1)S(1)}, u32[]{:S(2)}, u32[]{:S(2)}) collective-permute-start(bf16[9,48,128]{2,1,0:T(8,128)(2,1)S(1)} %get-tuple-element.71), channel_id=1, source_target_pairs={{0,16},{4,20},{8,24},{12,28},{16,32},{20,36},{24,40},{28,44},{32,4... | collective-permute-start | bytes 331784 | tf_op jit(solution)/shard_map/ppermute | solution.py:559
  104.9 4.2 %collective-permute-start.18 = (bf16[9,48,128]{2,1,0:T(8,128)(2,1)S(1)}, bf16[9,48,128]{2,1,0:T(8,128)(2,1)S(1)}, u32[]{:S(2)}, u32[]{:S(2)}) collective-permute-start(bf16[9,48,128]{2,1,0:T(8,128)(2,1)S(1)} %get-tuple-element.73), channel_id=1, source_target_pairs={{0,32},{4,36},{8,40},{12,44},{16,48},{20,52},{24,56},{28,60},{32,0... | collective-permute-start | bytes 331784 | tf_op jit(solution)/shard_map/ppermute | solution.py:559
  109.1 0.1 add_add_fusion
  109.2 2.0 %collective-permute-done.17 = bf16[9,48,128]{2,1,0:T(8,128)(2,1)S(1)} collective-permute-done((bf16[9,48,128]{2,1,0:T(8,128)(2,1)S(1)}, bf16[9,48,128]{2,1,0:T(8,128)(2,1)S(1)}, u32[]{:S(2)}, u32[]{:S(2)}) %collective-permute-start.17) | collective-permute-done | bytes 110624 | tf_op jit(solution)/shard_map/ppermute | solution.py:559
  111.3 3.7 %collective-permute-start.20 = (bf16[192,256]{1,0:T(8,128)(2,1)S(1)}, bf16[192,256]{1,0:T(8,128)(2,1)S(1)}, u32[]{:S(2)}, u32[]{:S(2)}) collective-permute-start(bf16[192,256]{1,0:T(8,128)(2,1)S(1)} %add_add_fusion), channel_id=1, source_target_pairs={{0,4},{4,0},{8,12},{12,8},{16,20},{20,16},{24,28},{28,24},{32,36},... | collective-permute-start | bytes 294920 | tf_op jit(solution)/shard_map/ppermute | solution.py:485
  114.9 3.6 %collective-permute-start.21 = (bf16[192,256]{1,0:T(8,128)(2,1)S(1)}, bf16[192,256]{1,0:T(8,128)(2,1)S(1)}, u32[]{:S(2)}, u32[]{:S(2)}) collective-permute-start(bf16[192,256]{1,0:T(8,128)(2,1)S(1)} %add_add_fusion), channel_id=1, source_target_pairs={{0,8},{4,12},{8,0},{12,4},{16,24},{20,28},{24,16},{28,20},{32,40},... | collective-permute-start | bytes 294920 | tf_op jit(solution)/shard_map/ppermute | solution.py:485
  118.5 0.8 fusion.1
  119.3 2.4 %collective-permute-done.21 = bf16[192,256]{1,0:T(8,128)(2,1)S(1)} collective-permute-done((bf16[192,256]{1,0:T(8,128)(2,1)S(1)}, bf16[192,256]{1,0:T(8,128)(2,1)S(1)}, u32[]{:S(2)}, u32[]{:S(2)}) %collective-permute-start.21) | collective-permute-done | bytes 98336 | tf_op jit(solution)/shard_map/ppermute | solution.py:485
  121.7 2.1 %collective-permute-done.22 = bf16[192,256]{1,0:T(8,128)(2,1)S(1)} collective-permute-done((bf16[192,256]{1,0:T(8,128)(2,1)S(1)}, bf16[192,256]{1,0:T(8,128)(2,1)S(1)}, u32[]{:S(2)}, u32[]{:S(2)}) %collective-permute-start.22) | collective-permute-done | bytes 98336 | tf_op jit(solution)/shard_map/ppermute | solution.py:485
  123.8 0.1 maximum_convert_fusion
  123.9 0.2 slice.67
  124.1 0.2 slice.68
  124.2 0.2 copy.42
  124.4 0.2 copy.43
  124.5 1.1 copy.44
  125.6 0.6 pad_maximum_fusion.5
  (51 shorter events, 0.3 us)
Async XLA Ops:
  0.6 10.1 %copy-start.8 = (bf16[256,3,128]{2,0,1:T(8,128)(2,1)S(1)}, bf16[256,3,128]{2,0,1:T(8,128)(2,1)}, u32[]{:S(2)}) copy-start(bf16[256,3,128]{2,0,1:T(8,128)(2,1)} %param.21) | copy-start | bytes 589828
  0.6 15.0 %copy-start.10 = (s32[128,4]{0,1:T(4,128)S(1)}, s32[128,4]{0,1:T(4,128)}, u32[]{:S(2)}) copy-start(s32[128,4]{0,1:T(4,128)} %param.20) | copy-start | bytes 6148
  2.6 14.0 %copy-start.9 = (bf16[64,8,1,64]{3,1,0,2:T(8,128)(2,1)S(1)}, bf16[64,8,1,64]{3,1,0,2:T(8,128)(2,1)}, u32[]{:S(2)}) copy-start(bf16[64,8,1,64]{3,1,0,2:T(8,128)(2,1)} %constant.112.clone.1) | copy-start | bytes 196612
  3.3 1.3 %collective-permute-start = (bf16[64,256]{1,0:T(8,128)(2,1)S(1)}, bf16[64,256]{1,0:T(8,128)(2,1)S(1)}, u32[]{:S(2)}, u32[]{:S(2)}) collective-permute-start(bf16[64,256]{1,0:T(8,128)(2,1)S(1)} %reshape.83), channel_id=1, source_target_pairs={{8,16},{12,20},{16,8},{20,12},{24,32},{28,36},{32,24},{36,28},{40,... | collective-permute-start | bytes 98312 | tf_op jit(solution)/shard_map/ppermute | solution.py:492
  4.6 8.1 %collective-permute-start.1 = (bf16[2,64,256]{2,1,0:T(8,128)(2,1)S(1)}, bf16[2,64,256]{2,1,0:T(8,128)(2,1)S(1)}, u32[]{:S(2)}, u32[]{:S(2)}) collective-permute-start(bf16[2,64,256]{2,1,0:T(8,128)(2,1)S(1)} %pad_maximum_fusion.4), channel_id=1, source_target_pairs={{0,8},{4,12},{8,0},{12,4},{16,24},{20,28},{24,16},{28,20},{32,40},... | collective-permute-start | bytes 196616 | tf_op jit(solution)/shard_map/ppermute | solution.py:485
  10.7 5.0 %collective-permute-start.3 = (bf16[3,4,64,128]{3,2,1,0:T(8,128)(2,1)S(1)}, bf16[3,4,64,128]{3,2,1,0:T(8,128)(2,1)S(1)}, u32[]{:S(2)}, u32[]{:S(2)}) collective-permute-start(bf16[3,4,64,128]{3,2,1,0:T(8,128)(2,1)S(1)} %bitcast.85), channel_id=1, source_target_pairs={{0,4},{4,0},{8,12},{12,8},{16,20},{20,16},{24,28},{28,24},{32,36},... | collective-permute-start | bytes 589832 | tf_op jit(solution)/shard_map/ppermute | solution.py:485
  12.8 3.2 %collective-permute-start.2 = (bf16[4,64,256]{2,1,0:T(8,128)(2,1)S(1)}, bf16[4,64,256]{2,1,0:T(8,128)(2,1)S(1)}, u32[]{:S(2)}, u32[]{:S(2)}) collective-permute-start(bf16[4,64,256]{2,1,0:T(8,128)(2,1)S(1)} %pad_maximum_fusion.2), channel_id=1, source_target_pairs={{0,4},{4,0},{8,12},{12,8},{16,20},{20,16},{24,28},{28,24},{32,36},... | collective-permute-start | bytes 393224 | tf_op jit(solution)/shard_map/ppermute | solution.py:485
  18.6 20.3 %collective-permute-start.4 = (bf16[2,3,4,64,128]{4,3,2,1,0:T(8,128)(2,1)S(1)}, bf16[2,3,4,64,128]{4,3,2,1,0:T(8,128)(2,1)S(1)}, u32[]{:S(2)}, u32[]{:S(2)}) collective-permute-start(bf16[2,3,4,64,128]{4,3,2,1,0:T(8,128)(2,1)S(1)} %pad_maximum_fusion.1), channel_id=1, source_target_pairs={{0,8},{4,12},{8,0},{12,4},{16,24},{20,28},{24,16},{28,20},{32,40},... | collective-permute-start | bytes 1179656 | tf_op jit(solution)/shard_map/ppermute | solution.py:485
  20.3 18.7 %copy-start.4 = (s32[3]{0:T(128)S(1)}, s32[3]{0:T(128)}, u32[]{:S(2)}) copy-start(s32[3]{0:T(128)} %pad_add_fusion.ids) | copy-start | bytes 40
  20.3 18.7 %copy-start.5 = (f32[128]{0:T(128)S(1)}, f32[128]{0:T(128)}, u32[]{:S(2)}) copy-start(f32[128]{0:T(128)} %param.18) | copy-start | bytes 1540
  20.3 18.7 %copy-start.6 = (f32[128]{0:T(128)S(1)}, f32[128]{0:T(128)}, u32[]{:S(2)}) copy-start(f32[128]{0:T(128)} %param.19) | copy-start | bytes 1540
  39.0 29.0 %slice-start = ((s8[7077888]{0:T(1024)(128)(4,1)}), s8[4194304]{0:T(1024)(128)(4,1)S(1)}, s32[]{:S(2)}) async-start(s8[7077888]{0:T(1024)(128)(4,1)} %bitcast.75), calls=%async_computation | async-start | bytes 8388608
  39.0 20.6 %copy-start.7 = (bf16[768,1024]{1,0:T(8,128)(2,1)S(1)}, bf16[768,1024]{1,0:T(8,128)(2,1)}, u32[]{:S(2)}) copy-start(bf16[768,1024]{1,0:T(8,128)(2,1)} %get-tuple-element.41.hid) | copy-start | bytes 4718596
  39.0 29.0 %slice-start.1 = ((s8[7077888]{0:T(1024)(128)(4,1)}), s8[2883584]{0:T(1024)(128)(4,1)S(1)}, s32[]{:S(2)}) async-start(s8[7077888]{0:T(1024)(128)(4,1)} %bitcast.75), calls=%async_computation.1 | async-start | bytes 5767168
  59.6 8.4 %copy-start = (bf16[256,1024]{1,0:T(8,128)(2,1)S(1)}, bf16[256,1024]{1,0:T(8,128)(2,1)}, u32[]{:S(2)}) copy-start(bf16[256,1024]{1,0:T(8,128)(2,1)} %copy.35.pext) | copy-start | bytes 1572868
  59.6 8.4 %copy-start.1 = (bf16[768,1024]{1,0:T(8,128)(2,1)S(1)}, bf16[768,1024]{1,0:T(8,128)(2,1)}, u32[]{:S(2)}) copy-start(bf16[768,1024]{1,0:T(8,128)(2,1)} %get-tuple-element.47.nrm) | copy-start | bytes 4718596
  59.6 8.4 %copy-start.2 = (f32[768,128]{1,0:T(8,128)S(1)}, f32[768,128]{1,0:T(8,128)}, u32[]{:S(2)}) copy-start(f32[768,128]{1,0:T(8,128)} %get-tuple-element.48.sc) | copy-start | bytes 1179652
  59.7 8.4 %copy-start.3 = (f32[8,1024]{1,0:T(8,128)S(1)}, f32[8,1024]{1,0:T(8,128)}, u32[]{:S(2)}) copy-start(f32[8,1024]{1,0:T(8,128)} %get-tuple-element.50.inv) | copy-start | bytes 98308
  62.9 19.5 %collective-permute-start.8 = (bf16[4,9,48,128]{3,2,1,0:T(8,128)(2,1)S(1)}, bf16[4,9,48,128]{3,2,1,0:T(8,128)(2,1)S(1)}, u32[]{:S(2)}, u32[]{:S(2)}) collective-permute-start(bf16[4,9,48,128]{3,2,1,0:T(8,128)(2,1)S(1)} %get-tuple-element.55), channel_id=1, source_target_pairs={{0,64},{4,68},{8,72},{12,76},{16,80},{20,84},{24,88},{28,92},{32,9... | collective-permute-start | bytes 1327112 | tf_op jit(solution)/shard_map/ppermute | solution.py:534
  66.4 16.0 %collective-permute-start.9 = (bf16[4,9,48,128]{3,2,1,0:T(8,128)(2,1)S(1)}, bf16[4,9,48,128]{3,2,1,0:T(8,128)(2,1)S(1)}, u32[]{:S(2)}, u32[]{:S(2)}) collective-permute-start(bf16[4,9,48,128]{3,2,1,0:T(8,128)(2,1)S(1)} %get-tuple-element.56), channel_id=1, source_target_pairs={{0,192},{4,196},{8,200},{12,204},{16,208},{20,212},{24,216},{28,22... | collective-permute-start | bytes 1327112 | tf_op jit(solution)/shard_map/ppermute | solution.py:534
  74.3 5.1 %collective-permute-start.5 = (bf16[192,256]{1,0:T(8,128)(2,1)S(1)}, bf16[192,256]{1,0:T(8,128)(2,1)S(1)}, u32[]{:S(2)}, u32[]{:S(2)}) collective-permute-start(bf16[192,256]{1,0:T(8,128)(2,1)S(1)} %get-tuple-element.52), channel_id=1, source_target_pairs={{0,1},{1,2},{2,3},{3,0},{4,5},{5,6},{6,7},{7,4},{8,9},{9,10},{10,1... | collective-permute-start | bytes 294920 | tf_op jit(solution)/shard_map/ppermute | solution.py:540
  75.7 6.7 %collective-permute-start.6 = (bf16[192,256]{1,0:T(8,128)(2,1)S(1)}, bf16[192,256]{1,0:T(8,128)(2,1)S(1)}, u32[]{:S(2)}, u32[]{:S(2)}) collective-permute-start(bf16[192,256]{1,0:T(8,128)(2,1)S(1)} %get-tuple-element.53), channel_id=1, source_target_pairs={{0,2},{1,3},{2,0},{3,1},{4,6},{5,7},{6,4},{7,5},{8,10},{9,11},{10,... | collective-permute-start | bytes 294920 | tf_op jit(solution)/shard_map/ppermute | solution.py:540
  78.3 4.0 %collective-permute-start.7 = (bf16[192,256]{1,0:T(8,128)(2,1)S(1)}, bf16[192,256]{1,0:T(8,128)(2,1)S(1)}, u32[]{:S(2)}, u32[]{:S(2)}) collective-permute-start(bf16[192,256]{1,0:T(8,128)(2,1)S(1)} %get-tuple-element.54), channel_id=1, source_target_pairs={{0,3},{1,0},{2,1},{3,2},{4,7},{5,4},{6,5},{7,6},{8,11},{9,8},{10,9... | collective-permute-start | bytes 294920 | tf_op jit(solution)/shard_map/ppermute | solution.py:540
  79.4 18.8 %collective-permute-start.13 = (bf16[4,9,48,128]{3,2,1,0:T(8,128)(2,1)S(1)}, bf16[4,9,48,128]{3,2,1,0:T(8,128)(2,1)S(1)}, u32[]{:S(2)}, u32[]{:S(2)}) collective-permute-start(bf16[4,9,48,128]{3,2,1,0:T(8,128)(2,1)S(1)} %get-tuple-element.59), channel_id=1, source_target_pairs={{0,128},{4,132},{8,136},{12,140},{16,144},{20,148},{24,152},{28,15... | collective-permute-start | bytes 1327112 | tf_op jit(solution)/shard_map/ppermute | solution.py:534
  82.4 7.6 %collective-permute-start.10 = (bf16[192,256]{1,0:T(8,128)(2,1)S(1)}, bf16[192,256]{1,0:T(8,128)(2,1)S(1)}, u32[]{:S(2)}, u32[]{:S(2)}) collective-permute-start(bf16[192,256]{1,0:T(8,128)(2,1)S(1)} %reduce-precision_convert_fusion.1), channel_id=1, source_target_pairs={{0,16},{4,20},{8,24},{12,28},{16,0},{20,4},{24,8},{28,12},{32,48},... | collective-permute-start | bytes 294920 | tf_op jit(solution)/shard_map/ppermute | solution.py:485
  84.9 8.4 %collective-permute-start.11 = (bf16[192,256]{1,0:T(8,128)(2,1)S(1)}, bf16[192,256]{1,0:T(8,128)(2,1)S(1)}, u32[]{:S(2)}, u32[]{:S(2)}) collective-permute-start(bf16[192,256]{1,0:T(8,128)(2,1)S(1)} %reduce-precision_convert_fusion.1), channel_id=1, source_target_pairs={{0,32},{4,36},{8,40},{12,44},{16,48},{20,52},{24,56},{28,60},{32,0... | collective-permute-start | bytes 294920 | tf_op jit(solution)/shard_map/ppermute | solution.py:485
  90.1 8.0 %collective-permute-start.12 = (bf16[192,256]{1,0:T(8,128)(2,1)S(1)}, bf16[192,256]{1,0:T(8,128)(2,1)S(1)}, u32[]{:S(2)}, u32[]{:S(2)}) collective-permute-start(bf16[192,256]{1,0:T(8,128)(2,1)S(1)} %reduce-precision_convert_fusion.1), channel_id=1, source_target_pairs={{0,48},{4,52},{8,56},{12,60},{16,32},{20,36},{24,40},{28,44},{32,1... | collective-permute-start | bytes 294920 | tf_op jit(solution)/shard_map/ppermute | solution.py:485
  98.2 11.0 %collective-permute-start.14 = (bf16[192,256]{1,0:T(8,128)(2,1)S(1)}, bf16[192,256]{1,0:T(8,128)(2,1)S(1)}, u32[]{:S(2)}, u32[]{:S(2)}) collective-permute-start(bf16[192,256]{1,0:T(8,128)(2,1)S(1)} %reduce-precision_convert_fusion), channel_id=1, source_target_pairs={{0,64},{4,68},{8,72},{12,76},{16,80},{20,84},{24,88},{28,92},{32,9... | collective-permute-start | bytes 294920 | tf_op jit(solution)/shard_map/ppermute | solution.py:485
  98.3 10.9 %collective-permute-start.15 = (bf16[192,256]{1,0:T(8,128)(2,1)S(1)}, bf16[192,256]{1,0:T(8,128)(2,1)S(1)}, u32[]{:S(2)}, u32[]{:S(2)}) collective-permute-start(bf16[192,256]{1,0:T(8,128)(2,1)S(1)} %reduce-precision_convert_fusion), channel_id=1, source_target_pairs={{0,128},{4,132},{8,136},{12,140},{16,144},{20,148},{24,152},{28,15... | collective-permute-start | bytes 294920 | tf_op jit(solution)/shard_map/ppermute | solution.py:485
  99.9 9.3 %collective-permute-start.16 = (bf16[192,256]{1,0:T(8,128)(2,1)S(1)}, bf16[192,256]{1,0:T(8,128)(2,1)S(1)}, u32[]{:S(2)}, u32[]{:S(2)}) collective-permute-start(bf16[192,256]{1,0:T(8,128)(2,1)S(1)} %reduce-precision_convert_fusion), channel_id=1, source_target_pairs={{0,192},{4,196},{8,200},{12,204},{16,208},{20,212},{24,216},{28,22... | collective-permute-start | bytes 294920 | tf_op jit(solution)/shard_map/ppermute | solution.py:485
  102.4 8.9 %collective-permute-start.17 = (bf16[9,48,128]{2,1,0:T(8,128)(2,1)S(1)}, bf16[9,48,128]{2,1,0:T(8,128)(2,1)S(1)}, u32[]{:S(2)}, u32[]{:S(2)}) collective-permute-start(bf16[9,48,128]{2,1,0:T(8,128)(2,1)S(1)} %get-tuple-element.71), channel_id=1, source_target_pairs={{0,16},{4,20},{8,24},{12,28},{16,32},{20,36},{24,40},{28,44},{32,4... | collective-permute-start | bytes 331784 | tf_op jit(solution)/shard_map/ppermute | solution.py:559
  104.9 13.6 %collective-permute-start.18 = (bf16[9,48,128]{2,1,0:T(8,128)(2,1)S(1)}, bf16[9,48,128]{2,1,0:T(8,128)(2,1)S(1)}, u32[]{:S(2)}, u32[]{:S(2)}) collective-permute-start(bf16[9,48,128]{2,1,0:T(8,128)(2,1)S(1)} %get-tuple-element.73), channel_id=1, source_target_pairs={{0,32},{4,36},{8,40},{12,44},{16,48},{20,52},{24,56},{28,60},{32,0... | collective-permute-start | bytes 331784 | tf_op jit(solution)/shard_map/ppermute | solution.py:559
  109.1 9.4 %collective-permute-start.19 = (bf16[9,48,128]{2,1,0:T(8,128)(2,1)S(1)}, bf16[9,48,128]{2,1,0:T(8,128)(2,1)S(1)}, u32[]{:S(2)}, u32[]{:S(2)}) collective-permute-start(bf16[9,48,128]{2,1,0:T(8,128)(2,1)S(1)} %get-tuple-element.72), channel_id=1, source_target_pairs={{0,48},{4,52},{8,56},{12,60},{16,0},{20,4},{24,8},{28,12},{32,16},... | collective-permute-start | bytes 331784 | tf_op jit(solution)/shard_map/ppermute | solution.py:559
  111.3 8.0 %collective-permute-start.20 = (bf16[192,256]{1,0:T(8,128)(2,1)S(1)}, bf16[192,256]{1,0:T(8,128)(2,1)S(1)}, u32[]{:S(2)}, u32[]{:S(2)}) collective-permute-start(bf16[192,256]{1,0:T(8,128)(2,1)S(1)} %add_add_fusion), channel_id=1, source_target_pairs={{0,4},{4,0},{8,12},{12,8},{16,20},{20,16},{24,28},{28,24},{32,36},... | collective-permute-start | bytes 294920 | tf_op jit(solution)/shard_map/ppermute | solution.py:485
  114.9 6.7 %collective-permute-start.21 = (bf16[192,256]{1,0:T(8,128)(2,1)S(1)}, bf16[192,256]{1,0:T(8,128)(2,1)S(1)}, u32[]{:S(2)}, u32[]{:S(2)}) collective-permute-start(bf16[192,256]{1,0:T(8,128)(2,1)S(1)} %add_add_fusion), channel_id=1, source_target_pairs={{0,8},{4,12},{8,0},{12,4},{16,24},{20,28},{24,16},{28,20},{32,40},... | collective-permute-start | bytes 294920 | tf_op jit(solution)/shard_map/ppermute | solution.py:485
  118.5 5.3 %collective-permute-start.22 = (bf16[192,256]{1,0:T(8,128)(2,1)S(1)}, bf16[192,256]{1,0:T(8,128)(2,1)S(1)}, u32[]{:S(2)}, u32[]{:S(2)}) collective-permute-start(bf16[192,256]{1,0:T(8,128)(2,1)S(1)} %add_add_fusion), channel_id=1, source_target_pairs={{0,12},{4,8},{8,4},{12,0},{16,28},{20,24},{24,20},{28,16},{32,44},... | collective-permute-start | bytes 294920 | tf_op jit(solution)/shard_map/ppermute | solution.py:485
